TPU v7x, 32 devices: a whole 2x2x4 slice. The times are simulated.
32 devices in a mesh: dp: 4 (over y, x), expert: 8 (over z, core).
Axes of the slice: x: 2, y: 2, z: 4, core: 2. Of those that a mesh axis runs over, the one named last changes fastest.
Arguments:
- images: float32 [128, 197, 512], P(('dp', 'expert')), may hold values from -6 to 6
- cotangent: float32 [128, 197, 512], P(('dp', 'expert')), may hold values from -6 to 6
- routes: int32 [2, 128, 197, 2], P(None, ('dp', 'expert')), may hold values from 0 to 15, all different within a row
- query_weight: float32 [2, 512, 512], P(None, 'dp'), may hold values from -0.25 to 0.25
- key_weight: float32 [2, 512, 512], P(None, 'dp'), may hold values from -0.25 to 0.25
- value_weight: float32 [2, 512, 512], P(None, 'dp'), may hold values from -0.25 to 0.25
- output_weight: float32 [2, 512, 512], P(None, 'dp'), may hold values from -2 to 2
- router_weight: float32 [2, 512, 16], P(None, 'dp'), may hold values from -0.1875 to 0.1875
- query_bias: float32 [2, 512], P(None, 'dp'), may hold values from -1.2 to 1.2
- value_bias: float32 [2, 512], P(None, 'dp'), may hold values from -1.2 to 1.2
- output_bias: float32 [2, 512], P(None, 'dp'), may hold values from -1.2 to 1.2
- attend_gain: float32 [2, 512], P(None, 'dp'), may hold values from 0.5 to 1.5
- attend_shift: float32 [2, 512], P(None, 'dp'), may hold values from -0.6 to 0.6
- expert_gain: float32 [2, 512], P(None, 'dp'), may hold values from 0.5 to 1.5
- expert_shift: float32 [2, 512], P(None, 'dp'), may hold values from -0.6 to 0.6
- inner_weight: float32 [2, 16, 512, 2048], P(None, 'expert', 'dp'), may hold values from -0.25 to 0.25
- inner_bias: float32 [2, 16, 2048], P(None, 'expert', 'dp'), may hold values from -0.6 to 0.6
- outer_weight: float32 [2, 16, 2048, 512], P(None, 'expert', 'dp'), may hold values from -0.1875 to 0.1875
- outer_bias: float32 [2, 16, 512], P(None, 'expert', 'dp'), may hold values from -0.6 to 0.6
Outputs:
- layer_output: float32 [128, 197, 512], P(('dp', 'expert'))
- images_gradient: float32 [128, 197, 512], P(('dp', 'expert'))
- query_weight_gradient: float32 [2, 512, 512], P(None, 'dp')
- key_weight_gradient: float32 [2, 512, 512], P(None, 'dp')
- value_weight_gradient: float32 [2, 512, 512], P(None, 'dp')
- output_weight_gradient: float32 [2, 512, 512], P(None, 'dp')
- router_weight_gradient: float32 [2, 512, 16], P(None, 'dp')
- query_bias_gradient: float32 [2, 512], P(None, 'dp')
- value_bias_gradient: float32 [2, 512], P(None, 'dp')
- output_bias_gradient: float32 [2, 512], P(None, 'dp')
- attend_gain_gradient: float32 [2, 512], P(None, 'dp')
- attend_shift_gradient: float32 [2, 512], P(None, 'dp')
- expert_gain_gradient: float32 [2, 512], P(None, 'dp')
- expert_shift_gradient: float32 [2, 512], P(None, 'dp')
- inner_weight_gradient: float32 [2, 16, 512, 2048], P(None, 'expert', 'dp')
- inner_bias_gradient: float32 [2, 16, 2048], P(None, 'expert', 'dp')
- outer_weight_gradient: float32 [2, 16, 2048, 512], P(None, 'expert', 'dp')
- outer_bias_gradient: float32 [2, 16, 512], P(None, 'expert', 'dp')
All inputs are finite; a program needn't handle non-finite values.
Results may differ from a plain program's by a relative error of at most 0.015.
Values may be sent and summed in bfloat16 or wider, within the bound.
A program may use at most 320 MiB of HBM per device.

v0:
```python
import jax
import jax.numpy as jnp
from jax import lax
from jax.sharding import PartitionSpec as P

HEADS = 8
HEAD_DIM = 64
LAYERS = 2


EPSILON = 1e-06


def normalize(rows, gain, shift):
    mean_value = jnp.mean(rows, axis=-1, keepdims=True)
    centered = rows - mean_value
    variance = jnp.mean(centered * centered, axis=-1, keepdims=True)
    scale = lax.rsqrt(variance + EPSILON)
    unit = centered * scale
    return (unit * gain + shift, unit, scale)


def normalize_back(upstream, unit, scale, gain):
    along = upstream * gain
    inner = (
        along
        - jnp.mean(along, axis=-1, keepdims=True)
        - unit * jnp.mean(along * unit, axis=-1, keepdims=True)
    )
    return (inner * scale, jnp.sum(upstream * unit, axis=0), jnp.sum(upstream, axis=0))


def lowered(item, layer):
    return item[layer].astype(jnp.bfloat16)


def fetch_dense(masters, layer):
    return (
        lax.all_gather(lowered(masters[0], layer), "dp", axis=0, tiled=True),
        lax.all_gather(lowered(masters[1], layer), "dp", axis=0, tiled=True),
        lax.all_gather(lowered(masters[2], layer), "dp", axis=0, tiled=True),
        lax.all_gather(lowered(masters[3], layer), "dp", axis=0, tiled=True),
        lax.all_gather(lowered(masters[4], layer), "dp", axis=0, tiled=True),
        lax.all_gather(lowered(masters[5], layer), "dp", axis=0, tiled=True),
        lax.all_gather(lowered(masters[6], layer), "dp", axis=0, tiled=True),
        lax.all_gather(lowered(masters[7], layer), "dp", axis=0, tiled=True),
        lax.all_gather(lowered(masters[8], layer), "dp", axis=0, tiled=True),
        lax.all_gather(lowered(masters[9], layer), "dp", axis=0, tiled=True),
        lax.all_gather(lowered(masters[10], layer), "dp", axis=0, tiled=True),
        lax.all_gather(lowered(masters[11], layer), "dp", axis=0, tiled=True),
    )


def fetch_expert(masters, layer):
    return (
        lax.all_gather(lowered(masters[0], layer), "dp", axis=1, tiled=True),
        lax.all_gather(lowered(masters[1], layer), "dp", axis=1, tiled=True),
        lax.all_gather(lowered(masters[2], layer), "dp", axis=1, tiled=True),
        lax.all_gather(lowered(masters[3], layer), "dp", axis=1, tiled=True),
    )


def forward_layer(rows, routes_here, dense, expert):
    (
        query_weight,
        key_weight,
        value_weight,
        output_weight,
        router_weight,
        query_bias,
        value_bias,
        output_bias,
        attend_gain,
        attend_shift,
        expert_gain,
        expert_shift,
    ) = dense
    inner_weight, inner_bias, outer_weight, outer_bias = expert
    images_here = routes_here.shape[0]
    length = routes_here.shape[1]
    tokens_here = rows.shape[0]
    width = rows.shape[1]
    shape4 = (images_here, length, HEADS, HEAD_DIM)
    factor = HEAD_DIM ** (-0.5)
    normed, unit_one, scale_one = normalize(
        rows, attend_gain.astype(jnp.float32), attend_shift.astype(jnp.float32)
    )
    normed_low = normed.astype(jnp.bfloat16)
    queries = (
        jnp.dot(normed_low, query_weight, preferred_element_type=jnp.float32)
        + query_bias.astype(jnp.float32)
    ).astype(jnp.bfloat16)
    keys = jnp.dot(normed_low, key_weight, preferred_element_type=jnp.float32).astype(jnp.bfloat16)
    values = (
        jnp.dot(normed_low, value_weight, preferred_element_type=jnp.float32)
        + value_bias.astype(jnp.float32)
    ).astype(jnp.bfloat16)
    scores = (
        jnp.einsum(
            "iqhe,ikhe->ihqk",
            queries.reshape(shape4),
            keys.reshape(shape4),
            preferred_element_type=jnp.float32,
        )
        * factor
    )
    highest = jnp.max(scores, axis=-1, keepdims=True)
    expo = jnp.exp(scores - highest)
    total = jnp.sum(expo, axis=-1, keepdims=True)
    attention = (expo / total).astype(jnp.bfloat16)
    logsum = highest + jnp.log(total)
    mixed = jnp.einsum(
        "ihqk,ikhe->iqhe", attention, values.reshape(shape4), preferred_element_type=jnp.float32
    )
    context = mixed.reshape(tokens_here, width).astype(jnp.bfloat16)
    branch = jnp.dot(
        context, output_weight, preferred_element_type=jnp.float32
    ) + output_bias.astype(jnp.float32)
    middle = rows + branch
    hidden_full, unit_two, scale_two = normalize(
        middle, expert_gain.astype(jnp.float32), expert_shift.astype(jnp.float32)
    )
    hidden = hidden_full.astype(jnp.bfloat16)
    logits = jnp.dot(hidden, router_weight, preferred_element_type=jnp.float32)
    experts_all = logits.shape[1]
    pairs = routes_here.reshape(tokens_here, 2)
    chosen = jnp.take_along_axis(logits, pairs, axis=1)
    gates = jax.nn.softmax(chosen, axis=1)
    pair_experts = pairs.reshape(-1)
    table = (pair_experts[:, None] == jnp.arange(experts_all, dtype=jnp.int32)[None, :]).astype(
        jnp.int32
    )
    before = jnp.cumsum(table, axis=0) - table
    slot = jnp.sum(before * table, axis=1)
    capacity = (10 * tokens_here // (4 * experts_all) + 7) // 8 * 8
    valid = slot < capacity
    slots_all = experts_all * capacity
    dest = jnp.where(valid, pair_experts * capacity + slot, slots_all)
    pair_rows = jnp.repeat(hidden, 2, axis=0)
    buffer = jnp.zeros((slots_all, width), jnp.bfloat16).at[dest].set(pair_rows, mode="drop")
    owners = lax.axis_size("expert")
    local = experts_all // owners
    received = lax.all_to_all(
        buffer.reshape(owners, local * capacity, width),
        "expert",
        split_axis=0,
        concat_axis=0,
        tiled=True,
    )
    arrived = received.reshape(owners, local, capacity, width)
    inner = (
        jnp.einsum("sjcd,jdf->sjcf", arrived, inner_weight, preferred_element_type=jnp.float32)
        + inner_bias.astype(jnp.float32)[None, :, None, :]
    )
    activated = jax.nn.gelu(inner, approximate=False).astype(jnp.bfloat16)
    produced = (
        jnp.einsum("sjcf,jfd->sjcd", activated, outer_weight, preferred_element_type=jnp.float32)
        + outer_bias.astype(jnp.float32)[None, :, None, :]
    ).astype(jnp.bfloat16)
    returned = lax.all_to_all(
        produced.reshape(owners, local * capacity, width),
        "expert",
        split_axis=0,
        concat_axis=0,
        tiled=True,
    )
    back_rows = returned.reshape(slots_all, width)
    safe_dest = jnp.minimum(dest, slots_all - 1)
    picked = back_rows[safe_dest].astype(jnp.float32)
    valid_float = valid.astype(jnp.float32)
    weight = gates.reshape(-1) * valid_float
    mixture = jnp.sum((picked * weight[:, None]).reshape(tokens_here, 2, width), axis=1)
    saved = {
        "unit_one": unit_one,
        "scale_one": scale_one,
        "normed_low": normed_low,
        "queries": queries,
        "keys": keys,
        "values": values,
        "logsum": logsum,
        "context": context,
        "unit_two": unit_two,
        "scale_two": scale_two,
        "hidden": hidden,
        "gates": gates,
        "valid_float": valid_float,
        "dest": dest,
        "safe_dest": safe_dest,
        "arrived": arrived,
        "inner": inner,
        "back_rows": back_rows,
        "pairs": pairs,
        "shape4": shape4,
    }
    return (middle + mixture, saved)


def backward_layer(upstream, saved, dense, expert):
    (
        query_weight,
        key_weight,
        value_weight,
        output_weight,
        router_weight,
        query_bias,
        value_bias,
        output_bias,
        attend_gain,
        attend_shift,
        expert_gain,
        expert_shift,
    ) = dense
    inner_weight, inner_bias, outer_weight, outer_bias = expert
    tokens_here, width = upstream.shape
    shape4 = saved["shape4"]
    factor = HEAD_DIM ** (-0.5)
    gates = saved["gates"]
    valid_float = saved["valid_float"]
    back_rows = saved["back_rows"]
    slots_all = back_rows.shape[0]
    experts_all = router_weight.shape[1]
    owners = lax.axis_size("expert")
    local = experts_all // owners
    capacity = slots_all // experts_all
    pair_up = jnp.repeat(upstream, 2, axis=0)
    picked = back_rows[saved["safe_dest"]].astype(jnp.float32)
    gate_grad = (valid_float * jnp.sum(picked * pair_up, axis=1)).reshape(tokens_here, 2)
    chosen_grad = gates * (gate_grad - jnp.sum(gates * gate_grad, axis=1, keepdims=True))
    route_table = (
        saved["pairs"][:, :, None] == jnp.arange(experts_all, dtype=jnp.int32)[None, None, :]
    ).astype(jnp.float32)
    logit_grad = jnp.sum(route_table * chosen_grad[:, :, None], axis=1).astype(jnp.bfloat16)
    weight = gates.reshape(-1) * valid_float
    slot_grad = (pair_up * weight[:, None]).astype(jnp.bfloat16)
    grad_buffer = (
        jnp.zeros((slots_all, width), jnp.bfloat16).at[saved["dest"]].set(slot_grad, mode="drop")
    )
    sent = lax.all_to_all(
        grad_buffer.reshape(owners, local * capacity, width),
        "expert",
        split_axis=0,
        concat_axis=0,
        tiled=True,
    )
    sent = sent.reshape(owners, local, capacity, width)
    activated_full, gelu_pull = jax.vjp(
        lambda value: jax.nn.gelu(value, approximate=False), saved["inner"]
    )
    activated = activated_full.astype(jnp.bfloat16)
    outer_weight_grad = jnp.einsum(
        "sjcf,sjcd->jfd", activated, sent, preferred_element_type=jnp.float32
    )
    outer_bias_grad = jnp.sum(sent.astype(jnp.float32), axis=(0, 2))
    activated_grad = jnp.einsum(
        "sjcd,jfd->sjcf", sent, outer_weight, preferred_element_type=jnp.float32
    )
    inner_grad = gelu_pull(activated_grad)[0].astype(jnp.bfloat16)
    arrived = saved["arrived"]
    inner_weight_grad = jnp.einsum(
        "sjcd,sjcf->jdf", arrived, inner_grad, preferred_element_type=jnp.float32
    )
    inner_bias_grad = jnp.sum(inner_grad.astype(jnp.float32), axis=(0, 2))
    arrived_grad = jnp.einsum(
        "sjcf,jdf->sjcd", inner_grad, inner_weight, preferred_element_type=jnp.float32
    ).astype(jnp.bfloat16)
    came_back = lax.all_to_all(
        arrived_grad.reshape(owners, local * capacity, width),
        "expert",
        split_axis=0,
        concat_axis=0,
        tiled=True,
    )
    came_back = came_back.reshape(slots_all, width)
    pair_hidden = came_back[saved["safe_dest"]].astype(jnp.float32) * valid_float[:, None]
    hidden = saved["hidden"]
    hidden_grad = jnp.sum(pair_hidden.reshape(tokens_here, 2, width), axis=1)
    hidden_grad = hidden_grad + jnp.einsum(
        "te,de->td", logit_grad, router_weight, preferred_element_type=jnp.float32
    )
    router_weight_grad = jnp.einsum(
        "td,te->de", hidden, logit_grad, preferred_element_type=jnp.float32
    )
    middle_norm_grad, expert_gain_grad, expert_shift_grad = normalize_back(
        hidden_grad, saved["unit_two"], saved["scale_two"], expert_gain.astype(jnp.float32)
    )
    middle_grad = upstream + middle_norm_grad
    branch_grad = middle_grad.astype(jnp.bfloat16)
    context = saved["context"]
    output_weight_grad = jnp.einsum(
        "td,te->de", context, branch_grad, preferred_element_type=jnp.float32
    )
    output_bias_grad = jnp.sum(branch_grad.astype(jnp.float32), axis=0)
    context_grad = jnp.einsum(
        "te,de->td", branch_grad, output_weight, preferred_element_type=jnp.float32
    ).astype(jnp.bfloat16)
    context_heads = context_grad.reshape(shape4)
    queries4 = saved["queries"].reshape(shape4)
    keys4 = saved["keys"].reshape(shape4)
    values4 = saved["values"].reshape(shape4)
    scores = (
        jnp.einsum("iqhe,ikhe->ihqk", queries4, keys4, preferred_element_type=jnp.float32) * factor
    )
    attention_full = jnp.exp(scores - saved["logsum"])
    attention_low = attention_full.astype(jnp.bfloat16)
    prob_grad = jnp.einsum(
        "iqhe,ikhe->ihqk", context_heads, values4, preferred_element_type=jnp.float32
    )
    delta = jnp.sum(attention_full * prob_grad, axis=-1, keepdims=True)
    score_grad = (attention_full * (prob_grad - delta)).astype(jnp.bfloat16)
    values_grad = (
        jnp.einsum(
            "ihqk,iqhe->ikhe", attention_low, context_heads, preferred_element_type=jnp.float32
        )
        .astype(jnp.bfloat16)
        .reshape(tokens_here, width)
    )
    queries_grad = (
        (
            jnp.einsum("ihqk,ikhe->iqhe", score_grad, keys4, preferred_element_type=jnp.float32)
            * factor
        )
        .astype(jnp.bfloat16)
        .reshape(tokens_here, width)
    )
    keys_grad = (
        (
            jnp.einsum("ihqk,iqhe->ikhe", score_grad, queries4, preferred_element_type=jnp.float32)
            * factor
        )
        .astype(jnp.bfloat16)
        .reshape(tokens_here, width)
    )
    normed_low = saved["normed_low"]
    query_weight_grad = jnp.einsum(
        "td,te->de", normed_low, queries_grad, preferred_element_type=jnp.float32
    )
    key_weight_grad = jnp.einsum(
        "td,te->de", normed_low, keys_grad, preferred_element_type=jnp.float32
    )
    value_weight_grad = jnp.einsum(
        "td,te->de", normed_low, values_grad, preferred_element_type=jnp.float32
    )
    query_bias_grad = jnp.sum(queries_grad.astype(jnp.float32), axis=0)
    value_bias_grad = jnp.sum(values_grad.astype(jnp.float32), axis=0)
    normed_grad = jnp.einsum(
        "te,de->td", queries_grad, query_weight, preferred_element_type=jnp.float32
    )
    normed_grad = normed_grad + jnp.einsum(
        "te,de->td", keys_grad, key_weight, preferred_element_type=jnp.float32
    )
    normed_grad = normed_grad + jnp.einsum(
        "te,de->td", values_grad, value_weight, preferred_element_type=jnp.float32
    )
    rows_norm_grad, attend_gain_grad, attend_shift_grad = normalize_back(
        normed_grad, saved["unit_one"], saved["scale_one"], attend_gain.astype(jnp.float32)
    )
    rows_grad = middle_grad + rows_norm_grad
    dense_local = (
        query_weight_grad,
        key_weight_grad,
        value_weight_grad,
        output_weight_grad,
        router_weight_grad,
        query_bias_grad,
        value_bias_grad,
        output_bias_grad,
        attend_gain_grad,
        attend_shift_grad,
        expert_gain_grad,
        expert_shift_grad,
    )
    expert_local = (inner_weight_grad, inner_bias_grad, outer_weight_grad, outer_bias_grad)
    return (rows_grad, dense_local, expert_local)


def shards(
    images,
    cotangent,
    routes,
    query_weight,
    key_weight,
    value_weight,
    output_weight,
    router_weight,
    query_bias,
    value_bias,
    output_bias,
    attend_gain,
    attend_shift,
    expert_gain,
    expert_shift,
    inner_weight,
    inner_bias,
    outer_weight,
    outer_bias,
):
    dense_masters = (
        query_weight,
        key_weight,
        value_weight,
        output_weight,
        router_weight,
        query_bias,
        value_bias,
        output_bias,
        attend_gain,
        attend_shift,
        expert_gain,
        expert_shift,
    )
    expert_masters = (inner_weight, inner_bias, outer_weight, outer_bias)
    rows = images.reshape(images.shape[0] * images.shape[1], images.shape[2])
    saved_layers = []
    dense_kept = []
    expert_kept = []
    for layer in range(LAYERS):
        dense = fetch_dense(dense_masters, layer)
        expert = fetch_expert(expert_masters, layer)
        rows, saved = forward_layer(rows, routes[layer], dense, expert)
        saved_layers.append(saved)
        dense_kept.append(dense)
        expert_kept.append(expert)
    result = rows.reshape(images.shape)
    upstream = cotangent.reshape(rows.shape)
    dense_grads = [None] * LAYERS
    expert_grads = [None] * LAYERS
    for layer in reversed(range(LAYERS)):
        dense = dense_kept[layer]
        expert = expert_kept[layer]
        upstream, dense_local, expert_local = backward_layer(
            upstream, saved_layers[layer], dense, expert
        )
        expert_grads[layer] = (
            lax.psum_scatter(
                expert_local[0].astype(jnp.bfloat16), "dp", scatter_dimension=1, tiled=True
            ).astype(jnp.float32),
            lax.psum_scatter(
                expert_local[1].astype(jnp.bfloat16), "dp", scatter_dimension=1, tiled=True
            ).astype(jnp.float32),
            lax.psum_scatter(
                expert_local[2].astype(jnp.bfloat16), "dp", scatter_dimension=1, tiled=True
            ).astype(jnp.float32),
            lax.psum_scatter(
                expert_local[3].astype(jnp.bfloat16), "dp", scatter_dimension=1, tiled=True
            ).astype(jnp.float32),
        )
        summed = lax.psum(
            (
                dense_local[0],
                dense_local[1],
                dense_local[2],
                dense_local[3],
                dense_local[4],
                dense_local[5],
                dense_local[6],
                dense_local[7],
                dense_local[8],
                dense_local[9],
                dense_local[10],
                dense_local[11],
            ),
            ("dp", "expert"),
        )
        share_rows = summed[0].shape[0] // lax.axis_size("dp")
        first_row = lax.axis_index("dp") * share_rows
        dense_grads[layer] = tuple(
            (lax.dynamic_slice_in_dim(item, first_row, share_rows, 0) for item in summed)
        )
    images_grad = upstream.reshape(images.shape)
    dense_out = [
        jnp.stack([dense_grads[layer][number] for layer in range(LAYERS)]) for number in range(12)
    ]
    expert_out = [
        jnp.stack([expert_grads[layer][number] for layer in range(LAYERS)]) for number in range(4)
    ]
    return (
        result,
        images_grad,
        dense_out[0],
        dense_out[1],
        dense_out[2],
        dense_out[3],
        dense_out[4],
        dense_out[5],
        dense_out[6],
        dense_out[7],
        dense_out[8],
        dense_out[9],
        dense_out[10],
        dense_out[11],
        expert_out[0],
        expert_out[1],
        expert_out[2],
        expert_out[3],
    )


def solution(mesh):
    return jax.shard_map(
        shards,
        mesh=mesh,
        in_specs=(
            P(("dp", "expert"), None, None),
            P(("dp", "expert"), None, None),
            P(None, ("dp", "expert"), None, None),
            P(None, "dp", None),
            P(None, "dp", None),
            P(None, "dp", None),
            P(None, "dp", None),
            P(None, "dp", None),
            P(None, "dp"),
            P(None, "dp"),
            P(None, "dp"),
            P(None, "dp"),
            P(None, "dp"),
            P(None, "dp"),
            P(None, "dp"),
            P(None, "expert", "dp", None),
            P(None, "expert", "dp"),
            P(None, "expert", "dp", None),
            P(None, "expert", "dp"),
        ),
        out_specs=(
            P(("dp", "expert"), None, None),
            P(("dp", "expert"), None, None),
            P(None, "dp", None),
            P(None, "dp", None),
            P(None, "dp", None),
            P(None, "dp", None),
            P(None, "dp", None),
            P(None, "dp"),
            P(None, "dp"),
            P(None, "dp"),
            P(None, "dp"),
            P(None, "dp"),
            P(None, "dp"),
            P(None, "dp"),
            P(None, "expert", "dp", None),
            P(None, "expert", "dp"),
            P(None, "expert", "dp", None),
            P(None, "expert", "dp"),
        ),
        check_vma=False,
    )
```

profile of v0, /device:TPU:0, one launch (start us, length us, event | category | flops | bytes accessed | tf_op | source)
XLA Modules:
  0.0 1716.6 jit_solution(18229086670945239742)
XLA Ops:
  166.1 12.4 scatter_custom_fusion
  203.8 28.7 %all-to-all-done = bf16[8,256,512]{2,1,0:T(8,128)(2,1)S(1)} async-done(((bf16[8,256,512]{2,1,0:T(8,128)(2,1)}), bf16[8,256,512]{2,1,0:T(8,128)(2,1)S(1)}, u32[]{:S(2)}, u32[]{:S(2)}) %all-to-all-start) | async-done | bytes 2097184 | tf_op jit(solution)/shard_map/all_to_all | solution.py:143
  232.5 44.5 %fusion.19 = (bf16[8,2,128,2048]{3,2,0,1:T(8,128)(2,1)}, f32[8,2,128,2048]{3,2,0,1:T(8,128)}, f32[2,8,128,2048]{3,2,1,0:T(8,128)}) fusion(f32[2,2048]{1,0:T(2,128)S(1)} %bitcast_convert_fusion.5, bf16[1,2,512,2048]{3,2,1,0:T(8,128)(2,1)} %all-gather.37.cloned.1.call-done, bf16[8,2,128,512]{3,2,1,0:T(8,128)(2,1)S(1)} %bitcast.540), kind=kOutput, calls=%fused_computation.45 | convolution fusion | flops 4571791360 | bytes 48250880 | tf_op jit(solution)/shard_map/sjcd,jdf->sjcf/dot_general | solution.py:152
  304.9 20.1 %gather_fusion.4 = f32[1576]{0:T(1024)S(1)} fusion(f32[788,16]{0,1:T(8,128)S(1)} %fusion.158, s32[1576]{0:T(1024)S(1)} %reshape.831), kind=kCustom, calls=%fused_computation.clone | custom fusion | bytes 25216 | tf_op jit(solution)/shard_map/jit(take_along_axis)/gather | solution.py:127
  442.5 17.6 %multiply_reduce_fusion.9 = f32[788,512]{1,0:T(8,128)S(1)} fusion(f32[788,2,512]{2,1,0:T(2,128)S(1)} %reshape.689, f32[788,2]{1,0:T(8,128)} %broadcast_select_fusion.3), kind=kLoop, calls=%fused_computation.127 | loop fusion | flops 1210368 | bytes 4847776 | tf_op jit(solution)/shard_map/reduce_sum | solution.py:172
  496.6 12.6 scatter_custom_fusion.1
  529.8 33.4 %all-to-all-done.2 = bf16[8,256,512]{2,1,0:T(8,128)(2,1)S(1)} async-done(((bf16[8,256,512]{2,1,0:T(8,128)(2,1)}), bf16[8,256,512]{2,1,0:T(8,128)(2,1)S(1)}, u32[]{:S(2)}, u32[]{:S(2)}) %all-to-all-start.2) | async-done | bytes 2097184 | tf_op jit(solution)/shard_map/all_to_all | solution.py:143
  563.2 44.4 %fusion.17 = (bf16[8,2,128,2048]{3,2,0,1:T(8,128)(2,1)}, f32[8,2,128,2048]{3,2,0,1:T(8,128)}, f32[2,8,128,2048]{3,2,1,0:T(8,128)}) fusion(f32[2,2048]{1,0:T(2,128)S(1)} %bitcast_convert_fusion.4, bf16[1,2,512,2048]{3,2,1,0:T(8,128)(2,1)} %all-gather.41.cloned.1.call-done, bf16[8,2,128,512]{3,2,1,0:T(8,128)(2,1)S(1)} %bitcast.542), kind=kOutput, calls=%fused_computation.38 | convolution fusion | flops 4571791360 | bytes 48250880 | tf_op jit(solution)/shard_map/sjcd,jdf->sjcf/dot_general | solution.py:152
  649.2 20.1 %gather_fusion.5 = f32[1576]{0:T(1024)S(1)} fusion(f32[788,16]{0,1:T(8,128)S(1)} %fusion.155, s32[1576]{0:T(1024)S(1)} %reshape.836), kind=kCustom, calls=%fused_computation.1.clone | custom fusion | bytes 25216 | tf_op jit(solution)/shard_map/jit(take_along_axis)/gather | solution.py:127
  685.0 17.0 scatter_custom_fusion.2
  702.0 53.2 %all_to_all.40 = bf16[8,256,512]{2,1,0:T(8,128)(2,1)S(1)} all-to-all(bf16[8,256,512]{2,1,0:T(8,128)(2,1)} %bitcast.538), channel_id=1, replica_groups=mesh['dp'=4,'expert'=8] {'expert'}, dimensions={0} | all-to-all | bytes 4194304 | tf_op jit(solution)/shard_map/all_to_all | solution.py:238
  755.2 19.8 %fusion.205 = (bf16[2,2048]{1,0:T(2,128)(2,1)}, bf16[8,2,128,2048]{3,2,0,1:T(8,128)(2,1)}) fusion(f32[8,2,128,2048]{3,2,0,1:T(8,128)} %get-tuple-element.162, bf16[1,2,2048,512]{3,2,1,0:T(8,128)(2,1)} %all-gather.43.cloned.1.call-done, bf16[8,2,128,512]{3,2,1,0:T(8,128)(2,1)S(1)} %bitcast.530, f32[2,8,128,2048]{3,2,1,0:T(8,128)} %get-tuple-element.215, ...), kind=kOutput, calls=%fused_computation.402 | convolution fusion | flops 4362072064 | bytes 48259072 | tf_op jit(solution)/shard_map/sjcd,jfd->sjcf/dot_general | solution.py:254
  803.8 34.7 %all-to-all-done.5 = bf16[8,256,512]{2,1,0:T(8,128)(2,1)S(1)} async-done(((bf16[8,256,512]{2,1,0:T(8,128)(2,1)}), bf16[8,256,512]{2,1,0:T(8,128)(2,1)S(1)}, u32[]{:S(2)}, u32[]{:S(2)}) %all-to-all-start.5) | async-done | bytes 2097184 | tf_op jit(solution)/shard_map/all_to_all | solution.py:266
  848.2 17.6 %multiply_reduce_fusion.7 = f32[788,512]{1,0:T(8,128)S(1)} fusion(f32[788,2,512]{2,1,0:T(2,128)S(1)} %reshape.692, f32[788,2]{1,0:T(8,128)} %convert_element_type.559), kind=kLoop, calls=%fused_computation.124 | loop fusion | flops 1210368 | bytes 4847776 | tf_op jit(solution)/shard_map/reduce_sum | solution.py:276
  927.3 16.8 scatter_custom_fusion.3
  944.1 53.9 %all_to_all.41 = bf16[8,256,512]{2,1,0:T(8,128)(2,1)} all-to-all(bf16[8,256,512]{2,1,0:T(8,128)(2,1)} %bitcast.539), channel_id=1, replica_groups=mesh['dp'=4,'expert'=8] {'expert'}, dimensions={0} | all-to-all | bytes 4194304 | tf_op jit(solution)/shard_map/all_to_all | solution.py:238
  998.1 19.8 %fusion.206 = (bf16[2,2048]{1,0:T(2,128)(2,1)}, bf16[8,2,128,2048]{3,2,0,1:T(8,128)(2,1)}) fusion(f32[8,2,128,2048]{3,2,0,1:T(8,128)} %get-tuple-element.166, bf16[1,2,2048,512]{3,2,1,0:T(8,128)(2,1)} %all-gather.39.cloned.1.call-done, bf16[8,2,128,512]{3,2,1,0:T(8,128)(2,1)} %bitcast.532, f32[2,8,128,2048]{3,2,1,0:T(8,128)} %get-tuple-element.210, ...), kind=kOutput, calls=%fused_computation.403 | convolution fusion | flops 4362072064 | bytes 48259072 | tf_op jit(solution)/shard_map/sjcd,jfd->sjcf/dot_general | solution.py:254
  1091.0 17.6 %multiply_reduce_fusion.5 = f32[788,512]{1,0:T(8,128)S(1)} fusion(f32[788,2,512]{2,1,0:T(2,128)S(1)} %reshape.693, f32[788,2]{1,0:T(8,128)} %convert_element_type.578), kind=kLoop, calls=%fused_computation.121 | loop fusion | flops 1210368 | bytes 4847776 | tf_op jit(solution)/shard_map/reduce_sum | solution.py:276
  1229.7 62.3 %all-reduce.7.cloned.1.call-done = (f32[512,16]{0,1:T(8,128)}, f32[512,16]{0,1:T(8,128)}, f32[512]{0:T(512)}, f32[512]{0:T(512)}, f32[512]{0:T(512)}, /*index=5*...) async-done(((f32[512,16]{0,1:T(8,128)}, f32[512,16]{0,1:T(8,128)}, ...) | async-done | bytes 94224 | tf_op jit(solution)/shard_map/psum | solution.py:447
  1308.3 173.5 %all-reduce.9.cloned.1.call-done = (f32[512,512]{1,0:T(8,128)}, f32[512,512]{1,0:T(8,128)}, f32[512,512]{1,0:T(8,128)}, f32[512,512]{1,0:T(8,128)}, f32[512,512]...) async-done(((f32[512,512]{1,0:T(8,128)}, f32[512,512]{1,0:T(8,128)}, f32[512,512]{1,0:T(8,128)}, f32[512,512]{1,0:T(8,128)}, ...) | async-done | bytes 8388624 | tf_op jit(solution)/shard_map/psum | solution.py:447
  1492.9 45.5 %reduce-scatter.23.cloned.1.call-done = bf16[2,512,512]{2,1,0:T(8,128)(2,1)} async-done(((bf16[2,2048,512]{2,1,0:T(8,128)(2,1)}), bf16[2,512,512]{2,1,0:T(8,128)(2,1)}) %reduce-scatter.23.cloned.1.call-update) | async-done | bytes 1048592 | tf_op jit(solution)/shard_map/reduce_scatter | solution.py:440
  1538.4 55.5 %reduce-scatter.21.cloned.1.call-done = bf16[2,512,512]{2,1,0:T(8,128)(2,1)} async-done(((bf16[2,2048,512]{2,1,0:T(8,128)(2,1)}), bf16[2,512,512]{2,1,0:T(8,128)(2,1)}) %reduce-scatter.21.cloned.1.call-update) | async-done | bytes 1048592 | tf_op jit(solution)/shard_map/reduce_scatter | solution.py:440
  1597.8 52.7 %reduce-scatter.19.cloned.1.call-done = bf16[2,128,2048]{2,1,0:T(8,128)(2,1)} async-done(((bf16[2,512,2048]{2,1,0:T(8,128)(2,1)}), bf16[2,128,2048]{2,1,0:T(8,128)(2,1)}) %reduce-scatter.19.cloned.1.call-update) | async-done | bytes 1048592 | tf_op jit(solution)/shard_map/reduce_scatter | solution.py:434
  1650.5 55.5 %reduce-scatter.17.cloned.1.call-done = bf16[2,128,2048]{2,1,0:T(8,128)(2,1)} async-done(((bf16[2,512,2048]{2,1,0:T(8,128)(2,1)}), bf16[2,128,2048]{2,1,0:T(8,128)(2,1)}) %reduce-scatter.17.cloned.1.call-update) | async-done | bytes 1048592 | tf_op jit(solution)/shard_map/reduce_scatter | solution.py:434
  (748 shorter events, 770.8 us)
Async XLA Ops:
  7.2 225.3 %all-gather.37.cloned.1.call-start = ((), (), s32[]{:S(2)}) async-start(), calls=%async_computation.20 | async-start | bytes 5242880 | tf_op jit(solution)/shard_map/all_gather | solution.py:56
  24.0 136.1 %copy-start.7 = (f32[788,512]{1,0:T(8,128)}, f32[788,512]{1,0:T(8,128)S(1)}, u32[]{:S(2)}) copy-start(f32[788,512]{1,0:T(8,128)S(1)} %reshape.643) | copy-start | bytes 4841476
  162.4 141.6 %copy-start.23 = (bf16[788,512]{1,0:T(8,128)(2,1)}, bf16[788,512]{1,0:T(8,128)(2,1)S(1)}, u32[]{:S(2)}) copy-start(bf16[788,512]{1,0:T(8,128)(2,1)S(1)} %add_convert_fusion.6) | copy-start | bytes 2420740
  178.5 54.0 %all-to-all-start = ((bf16[8,256,512]{2,1,0:T(8,128)(2,1)}), bf16[8,256,512]{2,1,0:T(8,128)(2,1)S(1)}, u32[]{:S(2)}, u32[]{:S(2)}) async-start(bf16[8,256,512]{2,1,0:T(8,128)(2,1)} %bitcast.13), calls=%async_computation | async-start | bytes 4194304 | tf_op jit(solution)/shard_map/all_to_all | solution.py:143
  183.4 93.6 %all-gather.39.cloned.1.call-start = ((), (), s32[]{:S(2)}) async-start(), calls=%async_computation.21 | async-start | bytes 5242880 | tf_op jit(solution)/shard_map/all_gather | solution.py:58
  287.7 145.2 %all-to-all-start.1 = ((bf16[8,256,512]{2,1,0:T(8,128)(2,1)}), bf16[8,256,512]{2,1,0:T(8,128)(2,1)S(1)}, u32[]{:S(2)}, u32[]{:S(2)}) async-start(bf16[8,256,512]{2,1,0:T(8,128)(2,1)} %bitcast.534), calls=%async_computation.1 | async-start | bytes 4194304 | tf_op jit(solution)/shard_map/all_to_all | solution.py:160
  291.4 238.4 %all-gather.41.cloned.1.call-start = ((), (), s32[]{:S(2)}) async-start(), calls=%async_computation.22 | async-start | bytes 5242880 | tf_op jit(solution)/shard_map/all_gather | solution.py:56
  334.2 126.6 %copy-start.135 = (f32[1,512]{1,0:T(1,128)}, f32[1,512]{1,0:T(1,128)S(1)}, u32[]{:S(2)}) copy-start(f32[1,512]{1,0:T(1,128)S(1)} %convert_element_type.616) | copy-start | bytes 6148
  494.0 154.3 %copy-start.25 = (bf16[788,512]{1,0:T(8,128)(2,1)}, bf16[788,512]{1,0:T(8,128)(2,1)S(1)}, u32[]{:S(2)}) copy-start(bf16[788,512]{1,0:T(8,128)(2,1)S(1)} %add_convert_fusion.2) | copy-start | bytes 2420740
  509.2 54.0 %all-to-all-start.2 = ((bf16[8,256,512]{2,1,0:T(8,128)(2,1)}), bf16[8,256,512]{2,1,0:T(8,128)(2,1)S(1)}, u32[]{:S(2)}, u32[]{:S(2)}) async-start(bf16[8,256,512]{2,1,0:T(8,128)(2,1)} %bitcast.43), calls=%async_computation.2 | async-start | bytes 4194304 | tf_op jit(solution)/shard_map/all_to_all | solution.py:143
  514.1 93.5 %all-gather.43.cloned.1.call-start = ((), (), s32[]{:S(2)}) async-start(), calls=%async_computation.23 | async-start | bytes 5242880 | tf_op jit(solution)/shard_map/all_gather | solution.py:58
  618.3 53.0 %all-to-all-start.3 = ((bf16[8,256,512]{2,1,0:T(8,128)(2,1)}), bf16[8,256,512]{2,1,0:T(8,128)(2,1)S(1)}, u32[]{:S(2)}, u32[]{:S(2)}) async-start(bf16[8,256,512]{2,1,0:T(8,128)(2,1)} %bitcast.536), calls=%async_computation.3 | async-start | bytes 4194304 | tf_op jit(solution)/shard_map/all_to_all | solution.py:160
  785.6 52.9 %all-to-all-start.5 = ((bf16[8,256,512]{2,1,0:T(8,128)(2,1)}), bf16[8,256,512]{2,1,0:T(8,128)(2,1)S(1)}, u32[]{:S(2)}, u32[]{:S(2)}) async-start(bf16[8,256,512]{2,1,0:T(8,128)(2,1)} %bitcast.537), calls=%async_computation.5 | async-start | bytes 4194304 | tf_op jit(solution)/shard_map/all_to_all | solution.py:266
  1028.5 52.7 %all-to-all-start.7 = ((bf16[8,256,512]{2,1,0:T(8,128)(2,1)}), bf16[8,256,512]{2,1,0:T(8,128)(2,1)S(1)}, u32[]{:S(2)}, u32[]{:S(2)}) async-start(bf16[8,256,512]{2,1,0:T(8,128)(2,1)} %bitcast.535), calls=%async_computation.7 | async-start | bytes 4194304 | tf_op jit(solution)/shard_map/all_to_all | solution.py:266
  1032.3 179.0 %reduce-scatter.31.cloned.1.call-start = ((), (), s32[]{:S(2)}) async-start(), calls=%async_computation.27 | async-start | bytes 163840
  1041.4 170.7 %reduce-scatter.27.cloned.1.call-start = ((), (), s32[]{:S(2)}) async-start(), calls=%async_computation.25 | async-start | bytes 655360
  1043.4 176.3 %reduce-scatter.29.cloned.1.call-start = ((), (), s32[]{:S(2)}) async-start(), calls=%async_computation.26 | async-start | bytes 163840
  1066.7 154.4 %reduce-scatter.25.cloned.1.call-start = ((), (), s32[]{:S(2)}) async-start(), calls=%async_computation.24 | async-start | bytes 655360
  1070.0 222.0 %all-reduce.7.cloned.1.call-start = ((), (), s32[]{:S(2)}) async-start(), calls=%async_computation.28 | async-start | bytes 188416 | tf_op jit(solution)/shard_map/psum | solution.py:447
  1164.9 316.8 %all-reduce.9.cloned.1.call-start = ((), (), s32[]{:S(2)}) async-start(), calls=%async_computation.29 | async-start | bytes 16777216 | tf_op jit(solution)/shard_map/psum | solution.py:447
  1168.2 370.3 %reduce-scatter.23.cloned.1.call-start = ((), (), s32[]{:S(2)}) async-start(), calls=%async_computation.19 | async-start | bytes 5242880 | tf_op jit(solution)/shard_map/reduce_scatter | solution.py:440
  1178.8 415.1 %reduce-scatter.21.cloned.1.call-start = ((), (), s32[]{:S(2)}) async-start(), calls=%async_computation.18 | async-start | bytes 5242880 | tf_op jit(solution)/shard_map/reduce_scatter | solution.py:440
  1189.7 460.8 %reduce-scatter.19.cloned.1.call-start = ((), (), s32[]{:S(2)}) async-start(), calls=%async_computation.17 | async-start | bytes 5242880 | tf_op jit(solution)/shard_map/reduce_scatter | solution.py:434
  1200.4 505.6 %reduce-scatter.17.cloned.1.call-start = ((), (), s32[]{:S(2)}) async-start(), calls=%async_computation.16 | async-start | bytes 5242880 | tf_op jit(solution)/shard_map/reduce_scatter | solution.py:434
  (168 other events, 2648.2 us)
Sparse Core Ops, SparseCore 0:
  11.3 58.9 all-gather.36
  187.6 53.5 all-gather.38
  294.7 53.5 all-gather.40
  516.5 53.2 all-gather.42
  1041.6 24.2 reduce-scatter.30
  1068.8 24.7 reduce-scatter.26
  1096.3 23.8 reduce-scatter.28
  1123.2 24.7 reduce-scatter.24
  1165.1 126.8 all-reduce.6
  1299.4 182.3 all-reduce.8
  1485.6 52.7 reduce-scatter.22
  1541.3 52.6 reduce-scatter.20
  1597.8 52.6 reduce-scatter.18
  1653.3 52.6 reduce-scatter.16
where the time goes:
time: 1730 us; the launch traced here: 1720 us
  waiting for transfers between devices  556 us (32%)
  blocking collectives  344 us (20%)
  matrix products  297 us (17%)
  local copies, waits for them, and re-layouts  295 us (17%)
  other arithmetic  182 us (11%)
  starting transfers between devices  26.4 us (2%)
    psum x2, waiting for transfers between devices, shards(): lax.psum((dense_local[0], dense_local[1], dense_local[2], dense_local[3],...  236 us
    reduce_scatter x2, waiting for transfers between devices, shards(): lax.psum_scatter(expert_local[0].astype(jnp.bfloat16), 'dp', scatter_dime...  108 us
    all_to_all x2, blocking collectives, backward_layer(): lax.all_to_all(grad_buffer.reshape(owners, local * capacity, width), 'exp...  107 us
    reduce_scatter x2, waiting for transfers between devices, shards(): lax.psum_scatter(expert_local[2].astype(jnp.bfloat16), 'dp', scatter_dime...  101 us
    dot_general x2, matrix products, forward_layer(): jnp.einsum('sjcd,jdf->sjcf', arrived, inner_weight, preferred_element_typ...  88.9 us
    all_to_all x2, waiting for transfers between devices, forward_layer(): lax.all_to_all(buffer.reshape(owners, local * capacity, width), 'expert',...  62.1 us
    all_to_all x2, waiting for transfers between devices, backward_layer(): lax.all_to_all(arrived_grad.reshape(owners, local * capacity, width), 'ex...  45.9 us
    gather x6, local copies, waits for them, and re-layouts, forward_layer(): chosen = jnp.take_along_axis(logits, pairs, axis=1)  43.3 us
  transfers between devices with their start and end apart: 20, of which 11 were waited for; matrix products, arithmetic and copies ran while one was open for 31% of the time, Pallas kernels for 0%

commit v1 on v0

v1 whole, which is shorter than its diff:
```python
import functools

import jax
import jax.numpy as jnp
from jax import lax
from jax.experimental import pallas as pl
from jax.experimental.pallas import tpu as pltpu
from jax.sharding import PartitionSpec as P

HEADS = 8
HEAD_DIM = 64
LAYERS = 2
EPSILON = 1e-06
FACTOR = HEAD_DIM**-0.5
VEC_AT = 64
BIAS_AT = 72
MISC = 128
FF_BLOCK = 512
VMEM = 56 * 1024 * 1024

F32 = jnp.float32
BF16 = jnp.bfloat16


def dot(a, b):
    return jnp.dot(a, b, preferred_element_type=F32)


def dot_nt(a, b):
    return lax.dot_general(a, b, (((1,), (1,)), ((), ())), preferred_element_type=F32)


def dot_tn(a, b):
    return lax.dot_general(a, b, (((0,), (0,)), ((), ())), preferred_element_type=F32)


def standardize(rows):
    mean_value = jnp.mean(rows, axis=-1, keepdims=True)
    centered = rows - mean_value
    variance = jnp.mean(centered * centered, axis=-1, keepdims=True)
    scale = lax.rsqrt(variance + EPSILON)
    return centered * scale, scale


def standardize_back(upstream, unit, scale, gain):
    along = upstream * gain
    inner = (
        along
        - jnp.mean(along, axis=-1, keepdims=True)
        - unit * jnp.mean(along * unit, axis=-1, keepdims=True)
    )
    return inner * scale


def vectors_of(misc_ref):
    turned = misc_ref[...].astype(F32).T
    return [turned[VEC_AT + n : VEC_AT + n + 1, :] for n in range(7)]


def pick(dest, buffers):
    total = None
    for number, buffer in enumerate(buffers):
        count = buffer.shape[0]
        lanes = lax.broadcasted_iota(jnp.int32, (dest.shape[0], count), 1)
        chosen = (dest - number * count == lanes).astype(F32).astype(BF16)
        part = dot(chosen, buffer[...])
        total = part if total is None else total + part
    return total


def spread(dest_rows, sources, outs, first):
    half = outs[0].shape[0]
    step = 256
    length = dest_rows[0].shape[1]
    for number, out in enumerate(outs):
        for start in range(0, half, step):
            slots = lax.broadcasted_iota(jnp.int32, (step, length), 0) + (number * half + start)
            if len(sources) == 1:
                hit = (slots == dest_rows[0]) | (slots == dest_rows[1])
                block = dot(hit.astype(F32).astype(BF16), sources[0])
            else:
                block = dot((slots == dest_rows[0]).astype(F32).astype(BF16), sources[0])
                block = block + dot((slots == dest_rows[1]).astype(F32).astype(BF16), sources[1])
            block = block.astype(BF16)

            @pl.when(first)
            def _(out=out, start=start, block=block):
                out[start : start + step, :] = block

            @pl.when(jnp.logical_not(first))
            def _(out=out, start=start, block=block):
                out[start : start + step, :] += block


def lane_masks(length):
    lanes = lax.broadcasted_iota(jnp.int32, (length, 2 * HEAD_DIM), 1)
    return (lanes < HEAD_DIM).astype(F32).astype(BF16), (lanes >= HEAD_DIM).astype(F32).astype(BF16)


def attend_body(
    rows, routes_ref, drow_ref, wq, wk, wv, wo, misc,
    t_ref, q_ref, k_ref, v_ref, o_ref, lse_ref, gates_ref, outs,
):
    length = rows.shape[0]
    qb, vb, ob, again, ashift, egain, eshift = vectors_of(misc)
    unit, _ = standardize(rows)
    low = (unit * again + ashift).astype(BF16)
    queries = (dot(low, wq[...]) + qb).astype(BF16)
    keys = dot(low, wk[...]).astype(BF16)
    values = (dot(low, wv[...]) + vb).astype(BF16)
    q_ref[0] = queries
    k_ref[0] = keys
    v_ref[0] = values
    masks = lane_masks(length)
    lanes = lax.broadcasted_iota(jnp.int32, (length, MISC), 1)
    first_half = lax.broadcasted_iota(jnp.int32, (length, 2 * HEAD_DIM), 1) < HEAD_DIM
    sums = jnp.zeros((length, MISC), F32)
    for pair in range(HEADS // 2):
        cols = slice(pair * 2 * HEAD_DIM, (pair + 1) * 2 * HEAD_DIM)
        mixed = []
        for side in range(2):
            scores = dot_nt(queries[:, cols] * (masks[side] * FACTOR), keys[:, cols])
            highest = jnp.max(scores, axis=-1, keepdims=True)
            expo = jnp.exp(scores - highest)
            total = jnp.sum(expo, axis=-1, keepdims=True)
            attention = (expo * (1.0 / total)).astype(BF16)
            sums = jnp.where(lanes == 2 * pair + side, highest + jnp.log(total), sums)
            mixed.append(dot(attention, values[:, cols]))
        o_ref[0, :, cols] = jnp.where(first_half, mixed[0], mixed[1]).astype(BF16)
    lse_ref[0] = sums
    middle = rows + (dot(o_ref[0], wo[...]) + ob)
    t_ref[0] = middle
    unit_two, _ = standardize(middle)
    hidden = (unit_two * egain + eshift).astype(BF16)
    logits = dot(hidden, misc[...])
    pair_experts = routes_ref[0]
    zero = jnp.sum(jnp.where(lanes == pair_experts[:, 0:1], logits, 0.0), axis=-1, keepdims=True)
    one = jnp.sum(jnp.where(lanes == pair_experts[:, 1:2], logits, 0.0), axis=-1, keepdims=True)
    gate_zero = 1.0 / (1.0 + jnp.exp(one - zero))
    gate_one = 1.0 / (1.0 + jnp.exp(zero - one))
    gates_ref[0, :, 0:1] = gate_zero
    gates_ref[0, :, 1:2] = gate_one
    drow = drow_ref[0]
    spread([drow[0:1, :], drow[1:2, :]], [hidden], outs, pl.program_id(0) == 0)


def combine_body(middle, gates_ref, dcol_ref, back, yzero_ref, yone_ref):
    dest = dcol_ref[0]
    gates = gates_ref[0]
    zero = pick(dest[:, 0:1], back)
    one = pick(dest[:, 1:2], back)
    if yzero_ref is not None:
        yzero_ref[0] = zero.astype(BF16)
        yone_ref[0] = one.astype(BF16)
    return middle + (gates[:, 0:1] * zero + gates[:, 1:2] * one), zero, one


def grads_body(upstream, zero, one, gates_ref, routes_ref, drow_ref, dz_ref, outs):
    length = upstream.shape[0]
    gates = gates_ref[0]
    gate_zero, gate_one = gates[:, 0:1], gates[:, 1:2]
    grad_zero = jnp.sum(zero * upstream, axis=-1, keepdims=True)
    grad_one = jnp.sum(one * upstream, axis=-1, keepdims=True)
    along = gate_zero * grad_zero + gate_one * grad_one
    lanes = lax.broadcasted_iota(jnp.int32, (length, MISC), 1)
    pair_experts = routes_ref[0]
    dz = jnp.where(lanes == pair_experts[:, 0:1], gate_zero * (grad_zero - along), 0.0)
    dz = dz + jnp.where(lanes == pair_experts[:, 1:2], gate_one * (grad_one - along), 0.0)
    dz_ref[0] = dz.astype(BF16)
    drow = drow_ref[0]
    spread(
        [drow[0:1, :], drow[1:2, :]],
        [(gate_zero * upstream).astype(BF16), (gate_one * upstream).astype(BF16)],
        outs,
        pl.program_id(0) == 0,
    )


def first_kernel(rows, routes, drow, wq, wk, wv, wo, misc, *outs):
    attend_body(rows[0], routes, drow, wq, wk, wv, wo, misc, *outs[:7], outs[7:])


def next_kernel(
    middle, gates, dcol, back_a, back_b, routes, drow, wq, wk, wv, wo, misc, rows_ref, yzero, yone, *outs
):
    rows, _, _ = combine_body(middle[0], gates, dcol, (back_a, back_b), yzero, yone)
    rows_ref[0] = rows
    attend_body(rows, routes, drow, wq, wk, wv, wo, misc, *outs[:7], outs[7:])


def turn_kernel(middle, gates, dcol, back_a, back_b, cotangent, routes, drow, result, dz, out_a, out_b):
    rows, zero, one = combine_body(middle[0], gates, dcol, (back_a, back_b), None, None)
    result[0] = rows
    grads_body(cotangent[0], zero, one, gates, routes, drow, dz, (out_a, out_b))


def back_kernel(
    upstream, rows, middle, q_ref, k_ref, v_ref, o_ref, lse_ref, dz_ref, dcol, came_a, came_b,
    wq, wk, wv, wo, misc, *rest,
):
    if len(rest) > 3:
        yzero, yone, gates_below, routes_below, drow_below, grad_ref, wgrad, dz_below, out_a, out_b, vgrad = rest
    else:
        grad_ref, wgrad, vgrad = rest
    first = pl.program_id(0) == 0
    length = rows.shape[1]
    width = rows.shape[2]
    qb, vb, ob, again, ashift, egain, eshift = vectors_of(misc)

    @pl.when(first)
    def _():
        wgrad[...] = jnp.zeros_like(wgrad)
        vgrad[...] = jnp.zeros_like(vgrad)

    def add_vector(number, value):
        vgrad[VEC_AT + number : VEC_AT + number + 1, :] += jnp.sum(value, axis=0, keepdims=True)

    unit_two, scale_two = standardize(middle[0])
    hidden = (unit_two * egain + eshift).astype(BF16)
    dz = dz_ref[0]
    dest = dcol[0]
    dhidden = dot_nt(dz, misc[...])
    for number, came in enumerate((came_a, came_b)):
        count = came.shape[0]
        lanes = lax.broadcasted_iota(jnp.int32, (length, count), 1) + number * count
        hit = (dest[:, 0:1] == lanes) | (dest[:, 1:2] == lanes)
        dhidden = dhidden + dot(hit.astype(F32).astype(BF16), came[...])
    wgrad[:, 4 * width :] += dot_tn(hidden, dz)
    add_vector(5, dhidden * unit_two)
    add_vector(6, dhidden)
    dmiddle = upstream[0] + standardize_back(dhidden, unit_two, scale_two, egain)
    dbranch = dmiddle.astype(BF16)
    wgrad[:, 3 * width : 4 * width] += dot_tn(o_ref[0], dbranch)
    add_vector(2, dbranch.astype(F32))
    dcontext = dot_nt(dbranch, wo[...]).astype(BF16)
    masks = lane_masks(length)
    first_half = lax.broadcasted_iota(jnp.int32, (length, 2 * HEAD_DIM), 1) < HEAD_DIM
    dqs, dks, dvs = [], [], []
    for pair in range(HEADS // 2):
        cols = slice(pair * 2 * HEAD_DIM, (pair + 1) * 2 * HEAD_DIM)
        keys = k_ref[0, :, cols]
        values = v_ref[0, :, cols]
        queries = q_ref[0, :, cols]
        dvalues, dqueries, dkeys = None, [], None
        for side in range(2):
            own_queries = queries * (masks[side] * FACTOR)
            own_context = dcontext[:, cols] * masks[side]
            scores = dot_nt(own_queries, keys)
            number = 2 * pair + side
            attention = jnp.exp(scores - lse_ref[0, :, number : number + 1])
            prob = dot_nt(own_context, values)
            weighed = attention * prob
            delta = jnp.sum(weighed, axis=-1, keepdims=True)
            dscores = (weighed - attention * delta).astype(BF16)
            dvalue = dot_tn(attention.astype(BF16), own_context)
            dkey = dot_tn(dscores, own_queries)
            dvalues = dvalue if dvalues is None else dvalues + dvalue
            dkeys = dkey if dkeys is None else dkeys + dkey
            dqueries.append(dot(dscores, keys))
        dqs.append((jnp.where(first_half, dqueries[0], dqueries[1]) * FACTOR).astype(BF16))
        dks.append(dkeys.astype(BF16))
        dvs.append(dvalues.astype(BF16))
    dq = jnp.concatenate(dqs, axis=1)
    dk = jnp.concatenate(dks, axis=1)
    dv = jnp.concatenate(dvs, axis=1)
    unit, scale = standardize(rows[0])
    low = (unit * again + ashift).astype(BF16)
    wgrad[:, 0:width] += dot_tn(low, dq)
    wgrad[:, width : 2 * width] += dot_tn(low, dk)
    wgrad[:, 2 * width : 3 * width] += dot_tn(low, dv)
    add_vector(0, dq.astype(F32))
    add_vector(1, dv.astype(F32))
    dlow = dot_nt(dq, wq[...]) + dot_nt(dk, wk[...]) + dot_nt(dv, wv[...])
    add_vector(3, dlow * unit)
    add_vector(4, dlow)
    grad = dmiddle + standardize_back(dlow, unit, scale, again)
    grad_ref[0] = grad
    if len(rest) > 3:
        grads_body(
            grad, yzero[0].astype(F32), yone[0].astype(F32), gates_below, routes_below, drow_below, dz_below,
            (out_a, out_b),
        )

    @pl.when(pl.program_id(0) == pl.num_programs(0) - 1)
    def _():
        wgrad[:, 4 * width :] += vgrad[...].T


def per_image(array):
    return pl.BlockSpec((1,) + array.shape[1:], lambda i: (i,) + (0,) * (len(array.shape) - 1))


def whole(array):
    return pl.BlockSpec(array.shape, lambda i: (0,) * len(array.shape))


def packed_specs(packed):
    width = packed.shape[0]
    specs = [pl.BlockSpec((width, width), lambda i, n=n: (0, n)) for n in range(4)]
    return specs + [pl.BlockSpec((width, MISC), lambda i: (0, 4 * width // MISC))]


def call(body, grid, inputs, outputs, scratch=(), flops=0, aliases=None):
    moved = sum(a.size * a.dtype.itemsize for a, _ in inputs)
    shapes = [jax.ShapeDtypeStruct(s, t) for s, t, _ in outputs]
    moved += sum(s.size * s.dtype.itemsize for s in shapes)
    return pl.pallas_call(
        body,
        grid=grid,
        in_specs=[s for _, s in inputs],
        out_specs=[s for _, _, s in outputs],
        out_shape=shapes,
        scratch_shapes=list(scratch),
        compiler_params=pltpu.CompilerParams(vmem_limit_bytes=VMEM),
        cost_estimate=pl.CostEstimate(flops=flops, bytes_accessed=moved, transcendentals=0),
    )(*[a for a, _ in inputs])


def images_out(images, length, columns, kind):
    shape = (images, length, columns)
    return (shape, kind, pl.BlockSpec((1, length, columns), lambda i: (i, 0, 0)))


def slots_out(half, width):
    return [((half, width), BF16, pl.BlockSpec((half, width), lambda i: (0, 0)))] * 2


def attend_outputs(images, length, width, half):
    return [
        images_out(images, length, width, F32),
        images_out(images, length, width, BF16),
        images_out(images, length, width, BF16),
        images_out(images, length, width, BF16),
        images_out(images, length, width, BF16),
        images_out(images, length, MISC, F32),
        images_out(images, length, 2, F32),
    ] + slots_out(half, width)


def gelu(value):
    return 0.5 * value * (1.0 + lax.erf(value * 0.7071067811865476))


def expert_kernel(x_ref, w1_ref, b1_ref, w2_ref, b2_ref, y_ref, acc):
    step = pl.program_id(0)
    rows = x_ref.shape[0]
    chunk = 256
    for start in range(0, rows, chunk):
        part = slice(start, start + chunk)
        inner = dot(x_ref[part, :], w1_ref[0]) + b1_ref[0]
        term = dot(gelu(inner).astype(BF16), w2_ref[0])

        @pl.when(step == 0)
        def _(part=part, term=term):
            acc[part, :] = term + b2_ref[0]

        @pl.when(step > 0)
        def _(part=part, term=term):
            acc[part, :] += term

    @pl.when(step == pl.num_programs(0) - 1)
    def _():
        y_ref[...] = acc[...].astype(BF16)


def slope_kernel(x_ref, w1_ref, b1_ref, g_ref, s_ref):
    rows = x_ref.shape[0]
    chunk = 256
    for start in range(0, rows, chunk):
        part = slice(start, start + chunk)
        inner = dot(x_ref[part, :], w1_ref[0]) + b1_ref[0]
        normal = 0.5 * (1.0 + lax.erf(inner * 0.7071067811865476))
        g_ref[part, :] = (inner * normal).astype(BF16)
        s_ref[part, :] = (normal + inner * (jnp.exp(-0.5 * inner * inner) * 0.3989422804014327)).astype(BF16)


def expert_back_kernel(dy_ref, s_ref, w1_ref, w2_ref, du_ref, dx_ref, acc):
    step = pl.program_id(0)
    rows = dy_ref.shape[0]
    chunk = 256
    for start in range(0, rows, chunk):
        part = slice(start, start + chunk)
        dg = dot_nt(dy_ref[part, :], w2_ref[0])
        du = (dg * s_ref[part, :].astype(F32)).astype(BF16)
        du_ref[part, :] = du
        term = dot_nt(du, w1_ref[0])

        @pl.when(step == 0)
        def _(part=part, term=term):
            acc[part, :] = term

        @pl.when(step > 0)
        def _(part=part, term=term):
            acc[part, :] += term

    @pl.when(step == pl.num_programs(0) - 1)
    def _():
        dx_ref[...] = acc[...].astype(BF16)


def expert_weight_kernel(x_ref, g_ref, du_ref, dy_ref, dw1_ref, dw2_ref, db1_ref, db2_ref):
    dw1_ref[...] = dot_tn(x_ref[...], du_ref[...]).astype(BF16)
    dw2_ref[...] = dot_tn(g_ref[...], dy_ref[...]).astype(BF16)
    db1_ref[...] = jnp.sum(du_ref[...].astype(F32), axis=0, keepdims=True)

    @pl.when(pl.program_id(0) == 0)
    def _():
        db2_ref[...] = jnp.sum(dy_ref[...].astype(F32), axis=0, keepdims=True)


def inner_specs(j, width, ff):
    return (
        pl.BlockSpec((1, width, FF_BLOCK), lambda f: (j, 0, f)),
        pl.BlockSpec((1, 1, FF_BLOCK), lambda f: (j, 0, f)),
        pl.BlockSpec((1, FF_BLOCK, width), lambda f: (j, f, 0)),
        pl.BlockSpec((1, 1, width), lambda f: (j, 0, 0)),
    )


def columns_of(rows, ff):
    return ((rows, ff), BF16, pl.BlockSpec((rows, FF_BLOCK), lambda f: (0, f)))


def expert_forward(x, expert, j):
    w1, b1, w2, b2 = expert
    rows, width = x.shape
    ff = w1.shape[2]
    i1, i2, i3, i4 = inner_specs(j, width, ff)
    return call(
        expert_kernel, (ff // FF_BLOCK,),
        [(x, whole(x)), (w1, i1), (b1, i2), (w2, i3), (b2, i4)],
        [((rows, width), BF16, pl.BlockSpec((rows, width), lambda f: (0, 0)))],
        [pltpu.VMEM((rows, width), F32)],
        flops=4 * rows * width * ff,
    )[0]


def expert_slopes(x, expert, j):
    w1, b1, w2, b2 = expert
    rows, width = x.shape
    ff = w1.shape[2]
    i1, i2, _, _ = inner_specs(j, width, ff)
    return call(
        slope_kernel, (ff // FF_BLOCK,), [(x, whole(x)), (w1, i1), (b1, i2)],
        [columns_of(rows, ff), columns_of(rows, ff)],
        flops=2 * rows * width * ff,
    )


def expert_backward(dy, slopes, expert, j):
    w1, b1, w2, b2 = expert
    rows, width = dy.shape
    ff = w1.shape[2]
    i1, _, i3, _ = inner_specs(j, width, ff)
    by_columns = pl.BlockSpec((rows, FF_BLOCK), lambda f: (0, f))
    return call(
        expert_back_kernel, (ff // FF_BLOCK,),
        [(dy, whole(dy)), (slopes, by_columns), (w1, i1), (w2, i3)],
        [columns_of(rows, ff), ((rows, width), BF16, pl.BlockSpec((rows, width), lambda f: (0, 0)))],
        [pltpu.VMEM((rows, width), F32)],
        flops=4 * rows * width * ff,
    )


def expert_weight_grads(x, g, du, dy):
    rows, width = x.shape
    ff = g.shape[1]
    by_columns = pl.BlockSpec((rows, FF_BLOCK), lambda f: (0, f))
    return call(
        expert_weight_kernel, (ff // FF_BLOCK,),
        [(x, whole(x)), (g, by_columns), (du, by_columns), (dy, whole(dy))],
        [
            ((width, ff), BF16, pl.BlockSpec((width, FF_BLOCK), lambda f: (0, f))),
            ((ff, width), BF16, pl.BlockSpec((FF_BLOCK, width), lambda f: (f, 0))),
            ((1, ff), F32, pl.BlockSpec((1, FF_BLOCK), lambda f: (0, f))),
            ((1, width), F32, pl.BlockSpec((1, width), lambda f: (0, 0))),
        ],
        flops=4 * rows * width * ff,
    )


def destinations(routes, experts_all, owners):
    layers, images, length, _ = routes.shape
    tokens = images * length
    pairs = routes.reshape(layers, tokens, 2)
    hot = (pairs[..., None] == jnp.arange(experts_all, dtype=jnp.int32)).astype(F32)
    counts = (hot[:, :, 0] + hot[:, :, 1]).astype(BF16)
    earlier = (jnp.arange(tokens)[:, None] > jnp.arange(tokens)[None, :]).astype(BF16)
    before = jnp.einsum("ts,lse->lte", earlier, counts, preferred_element_type=F32)
    slot = jnp.sum(before[:, :, None, :] * hot, axis=-1).astype(jnp.int32)
    capacity = (10 * tokens // (4 * experts_all) + 7) // 8 * 8
    local = experts_all // owners
    row = ((pairs % local) * owners + pairs // local) * capacity + slot
    dest = jnp.where(slot < capacity, row, -1)
    return dest.reshape(layers, images, length, 2), capacity


def exchange(array):
    owners = lax.axis_size("expert")
    rows, width = array.shape
    swapped = lax.all_to_all(
        array.reshape(owners, rows // owners, width), "expert", split_axis=0, concat_axis=0, tiled=True
    )
    return swapped.reshape(rows, width)


def shards(
    images, cotangent, routes, query_weight, key_weight, value_weight, output_weight, router_weight, query_bias,
    value_bias, output_bias, attend_gain, attend_shift, expert_gain, expert_shift, inner_weight, inner_bias,
    outer_weight, outer_bias,
):
    count, length, width = images.shape
    parts = lax.axis_size("dp")
    owners = lax.axis_size("expert")
    experts_all = router_weight.shape[2]
    local = inner_weight.shape[1]
    ff = inner_weight.shape[3]
    share = width // parts
    tokens = count * length
    squares = (query_weight, key_weight, value_weight, output_weight)
    vectors = (query_bias, value_bias, output_bias, attend_gain, attend_shift, expert_gain, expert_shift)
    bias_columns = ff // width + 1

    biases = jnp.concatenate(
        [inner_bias.reshape(LAYERS, local, ff // width, share), outer_bias.reshape(LAYERS, local, 1, share)], axis=2
    )
    biases = biases.reshape(LAYERS * local * bias_columns, share).T

    packed = []
    for layer in range(LAYERS):
        misc = [router_weight[layer], jnp.zeros((share, VEC_AT - experts_all), F32)]
        misc += [jnp.stack([v[layer] for v in vectors], axis=1), jnp.zeros((share, BIAS_AT - VEC_AT - 7), F32)]
        if layer == 0:
            misc += [biases, jnp.zeros((share, MISC - BIAS_AT - biases.shape[1]), F32)]
        else:
            misc += [jnp.zeros((share, MISC - BIAS_AT), F32)]
        mine = jnp.concatenate([s[layer] for s in squares] + misc, axis=1).astype(BF16)
        packed.append(lax.all_gather(mine, "dp", axis=0, tiled=True))
    spare = packed[0][:, 4 * width + BIAS_AT : 4 * width + BIAS_AT + biases.shape[1]].astype(F32)
    spare = spare.reshape(parts, share, LAYERS, local, bias_columns)
    inner_biases = jnp.transpose(spare[..., :-1], (2, 3, 0, 4, 1)).reshape(LAYERS, local, 1, ff)
    outer_biases = jnp.transpose(spare[..., -1:], (2, 3, 4, 0, 1)).reshape(LAYERS, local, 1, width)
    experts = []
    for layer in range(LAYERS):
        experts.append((
            lax.all_gather(inner_weight[layer].astype(BF16), "dp", axis=1, tiled=True),
            inner_biases[layer],
            lax.all_gather(outer_weight[layer].astype(BF16), "dp", axis=1, tiled=True),
            outer_biases[layer],
        ))

    dcol, capacity = destinations(routes, experts_all, owners)
    drow = jnp.transpose(dcol, (0, 1, 3, 2))
    half = owners * capacity
    dense_flops = 8 * tokens * width * width + 4 * tokens * half * width

    saved = []
    back = None
    rows = images
    for layer in range(LAYERS):
        weights = [(packed[layer], s) for s in packed_specs(packed[layer])]
        routing = [(routes[layer], per_image(routes[layer])), (drow[layer], per_image(drow[layer]))]
        outputs = attend_outputs(count, length, width, half)
        if layer == 0:
            done = call(
                first_kernel, (count,), [(rows, per_image(rows))] + routing + weights, outputs, flops=dense_flops
            )
            picked = None
        else:
            before = saved[-1]
            done = call(
                next_kernel, (count,),
                [
                    (before["middle"], per_image(before["middle"])),
                    (before["gates"], per_image(before["gates"])),
                    (dcol[layer - 1], per_image(dcol[layer - 1])),
                    (back[0], whole(back[0])),
                    (back[1], whole(back[1])),
                ] + routing + weights,
                [
                    images_out(count, length, width, F32),
                    images_out(count, length, width, BF16),
                    images_out(count, length, width, BF16),
                ] + outputs,
                flops=dense_flops,
            )
            rows, *picked = done[:3]
            done = done[3:]
            before["picked"] = picked
        middle, queries, keys, values, context, sums, gates = done[:7]
        arrived = [exchange(item) for item in done[7:]]
        produced = [expert_forward(arrived[j], experts[layer], j) for j in range(local)]
        back = [exchange(item) for item in produced]
        slopes = [expert_slopes(arrived[j], experts[layer], j) for j in range(local)]
        saved.append({
            "rows": rows, "middle": middle, "attend": (queries, keys, values, context, sums), "gates": gates,
            "arrived": arrived, "slopes": slopes,
        })

    last = saved[-1]
    result, dz, *sent = call(
        turn_kernel, (count,),
        [(last["middle"], per_image(last["middle"])), (last["gates"], per_image(last["gates"]))]
        + [(dcol[-1], per_image(dcol[-1])), (back[0], whole(back[0])), (back[1], whole(back[1]))]
        + [(cotangent, per_image(cotangent)), (routes[-1], per_image(routes[-1])), (drow[-1], per_image(drow[-1]))],
        [images_out(count, length, width, F32), images_out(count, length, MISC, BF16)] + slots_out(half, width),
        flops=dense_flops,
    )
    upstream = cotangent
    dense_grads = [None] * LAYERS
    bias_grads = [None] * LAYERS
    inner_grads = [None] * LAYERS
    outer_grads = [None] * LAYERS
    for layer in reversed(range(LAYERS)):
        kept = saved[layer]
        dys = [exchange(item) for item in sent]
        dus, dxs = [], []
        for j in range(local):
            du, dx = expert_backward(dys[j], kept["slopes"][j][1], experts[layer], j)
            dus.append(du)
            dxs.append(dx)
        came = [exchange(item) for item in dxs]
        grads = [
            expert_weight_grads(kept["arrived"][j], kept["slopes"][j][0], dus[j], dys[j]) for j in range(local)
        ]
        inner_grads[layer] = [lax.psum_scatter(g[0], "dp", scatter_dimension=0, tiled=True) for g in grads]
        outer_grads[layer] = [lax.psum_scatter(g[1], "dp", scatter_dimension=0, tiled=True) for g in grads]
        bias_grads[layer] = [
            jnp.concatenate([g[2].reshape(parts, ff // parts), g[3].reshape(parts, share)], axis=1) for g in grads
        ]
        weights = [(packed[layer], s) for s in packed_specs(packed[layer])]
        inputs = [upstream, kept["rows"], kept["middle"], *kept["attend"], dz, dcol[layer]]
        inputs = [(a, per_image(a)) for a in inputs] + [(a, whole(a)) for a in came] + weights
        outputs = [
            images_out(count, length, width, F32),
            (
                (width, 4 * width + MISC), F32,
                pl.BlockSpec((width, 4 * width + MISC), lambda i: (0, 0)),
            ),
        ]
        if layer > 0:
            below = saved[layer - 1]
            extra = [*below["picked"], below["gates"], routes[layer - 1], drow[layer - 1]]
            inputs += [(a, per_image(a)) for a in extra]
            outputs += [images_out(count, length, MISC, BF16)] + slots_out(half, width)
        done = call(
            back_kernel, (count,), inputs, outputs, [pltpu.VMEM((MISC, width), F32)], flops=3 * dense_flops
        )
        upstream, wgrad = done[:2]
        if layer > 0:
            dz, *sent = done[2:]
        mine = lax.psum_scatter(wgrad, "dp", scatter_dimension=0, tiled=True)
        dense_grads[layer] = lax.psum(mine, "expert")

    small = jnp.stack([jnp.stack(b, axis=1) for b in bias_grads], axis=1)
    small = lax.psum_scatter(small, "dp", scatter_dimension=0, tiled=False)
    inner_bias_grad = small[:, :, : ff // parts]
    outer_bias_grad = small[:, :, ff // parts :]
    both = jnp.stack(dense_grads)
    square_grads = [both[:, :, n * width : (n + 1) * width] for n in range(4)]
    tail = both[:, :, 4 * width :]
    return (
        rows_out(result, images),
        upstream,
        *square_grads,
        tail[:, :, :experts_all],
        *[tail[:, :, VEC_AT + n] for n in range(7)],
        jnp.stack([jnp.stack(g) for g in inner_grads]).astype(F32),
        inner_bias_grad,
        jnp.stack([jnp.stack(g) for g in outer_grads]).astype(F32),
        outer_bias_grad,
    )


def rows_out(result, images):
    return result.reshape(images.shape)


def solution(mesh):
    both = P(("dp", "expert"), None, None)
    square = P(None, "dp", None)
    vector = P(None, "dp")
    matrix = P(None, "expert", "dp", None)
    bias = P(None, "expert", "dp")
    grads = (square,) * 5 + (vector,) * 7 + (matrix, bias, matrix, bias)
    return jax.shard_map(
        shards,
        mesh=mesh,
        in_specs=(both, both, P(None, ("dp", "expert"), None, None)) + grads,
        out_specs=(both, both) + grads,
        check_vma=False,
    )
```

time: 1730 us -> 1170 us (0.68)
  Pallas kernels: 0 us -> 306 us
  matrix products: 297 us -> 0.37 us
  local copies, waits for them, and re-layouts: 295 us -> 33.6 us
  other arithmetic: 182 us -> 22.2 us
  blocking collectives: 344 us -> 200 us
    pallas_call x0 -> x21, Pallas kernels: none -> 306 us  [call(): pl.pallas_call(body, grid=grid, in_specs=[s for _, s in inputs], out_spec...]
    dot_general x54 -> x1, matrix products: 297 us -> 0.37 us  [destinations(): jnp.einsum('ts,lse->lte', earlier, counts, preferred_element_type=F32)]
    all_gather x28 -> x0, blocking collectives: 237 us -> none  [the longest x2 22.4 us: fetch_dense(): lax.all_gather(lowered(masters[1], layer), 'dp', axis=0, tiled=True)]
    psum x2 -> x1, waiting for transfers between devices: 236 us -> 64.4 us  [shards(): dense_grads[layer] = lax.psum(mine, 'expert')]
    all_gather x4 -> x6, waiting for transfers between devices: 0.04 us -> 88.5 us  [the longest x2 63.9 us: shards(): lax.all_gather(outer_weight[layer].astype(BF16), 'dp', axis=1, tiled=True)]
    reduce_sum x28 -> x1, other arithmetic: 85 us -> 0.07 us  [destinations(): slot = jnp.sum(before[:, :, None, :] * hot, axis=-1).astype(jnp.int32)]
    all_to_all x2 -> x6, blocking collectives: 107 us -> 184 us  [exchange(): lax.all_to_all(array.reshape(owners, rows // owners, width), 'expert', sp...]
    reduce_scatter x4 -> x10, waiting for transfers between devices: 209 us -> 285 us  [the longest x4 147 us: shards(): lax.psum_scatter(g[1], 'dp', scatter_dimension=0, tiled=True)]
  transfers between devices with their start and end apart: 20 -> 27, of which waited for: 11 -> 21; matrix products, arithmetic and copies ran while one was open for 31% -> 4% of each run, Pallas kernels for 0% -> 21%
where the time goes in v1:
time: 1170 us; the launch traced here: 1160 us
  waiting for transfers between devices  540 us (46%)
  Pallas kernels  306 us (26%)
  blocking collectives  200 us (17%)
  starting transfers between devices  39.1 us (3%)
  local copies, waits for them, and re-layouts  33.6 us (3%)
  other arithmetic  22.2 us (2%)
  between operations  15.4 us (1%)
    pallas_call x21, Pallas kernels, call(): pl.pallas_call(body, grid=grid, in_specs=[s for _, s in inputs], out_spec...  306 us
    all_to_all x6, blocking collectives, exchange(): lax.all_to_all(array.reshape(owners, rows // owners, width), 'expert', sp...  184 us
    reduce_scatter x4, waiting for transfers between devices, shards(): lax.psum_scatter(g[1], 'dp', scatter_dimension=0, tiled=True)  147 us
    reduce_scatter x4, waiting for transfers between devices, shards(): lax.psum_scatter(g[0], 'dp', scatter_dimension=0, tiled=True)  138 us
    all_to_all x10, waiting for transfers between devices, exchange(): lax.all_to_all(array.reshape(owners, rows // owners, width), 'expert', sp...  98.5 us
    psum x1, waiting for transfers between devices, shards(): dense_grads[layer] = lax.psum(mine, 'expert')  64.4 us
    all_gather x2, waiting for transfers between devices, shards(): lax.all_gather(outer_weight[layer].astype(BF16), 'dp', axis=1, tiled=True)  63.9 us
    all_to_all x10, starting transfers between devices, exchange(): lax.all_to_all(array.reshape(owners, rows // owners, width), 'expert', sp...  37.9 us
  transfers between devices with their start and end apart: 27, of which 21 were waited for; matrix products, arithmetic and copies ran while one was open for 4% of the time, Pallas kernels for 21%

profile of v1, /device:TPU:0, one launch (start us, length us, event | category | flops | bytes accessed | tf_op | source)
XLA Modules:
  0.0 1156.2 jit_solution(1481382654029568242)
XLA Ops:
  28.2 24.6 %all-gather.11.cloned.1.call-done.wq.wk.wv.wo.misc = bf16[512,2176]{1,0:T(8,128)(2,1)} async-done(((bf16[128,2176]{1,0:T(8,128)(2,1)}), bf16[512,2176]{1,0:T(8,128)(2,1)}) %all-gather.11.cloned.1.call-update) | async-done | bytes 2228240 | tf_op jit(solution)/shard_map/all_gather | solution.py:538
  52.8 20.6 %shard_map.322 = (f32[4,197,512]{2,1,0:T(8,128)}, bf16[4,197,512]{2,1,0:T(8,128)(2,1)}, bf16[4,197,512]{2,1,0:T(8,128)(2,1)}, bf16[4,197,512]{2,1,0:T(8,128)(2,1...) custom-call(f32[4,197,512]{2,1,0:T(8,128)} %copy.163.rows, ...), custom_call_target="tpu_custom_call" | custom-call | flops 3305111552 | bytes 20115936 | tf_op jit(solution)/shard_map/pallas_call | solution.py:307
  73.4 31.3 %all_to_all.80 = bf16[8,128,512]{2,1,0:T(8,128)(2,1)} all-to-all(bf16[8,128,512]{2,1,0:T(8,128)(2,1)} %bitcast.198), channel_id=1, replica_groups=mesh['dp'=4,'expert'=8] {'expert'}, dimensions={0} | all-to-all | bytes 2097152 | tf_op jit(solution)/shard_map/all_to_all | solution.py:501
  110.7 52.0 %all-gather.17.cloned.1.call-done = bf16[1,2,2048,512]{3,2,1,0:T(8,128)(2,1)} async-done(((bf16[1,2,512,512]{3,2,1,0:T(8,128)(2,1)}), bf16[1,2,2048,512]{3,2,1,0:T(8,128)(2,1)}) %all-gather.17.cloned.1.call-update) | async-done | bytes 4194320 | tf_op jit(solution)/shard_map/all_gather | solution.py:548
  212.0 24.3 %all-to-all-done.1 = bf16[8,128,512]{2,1,0:T(8,128)(2,1)S(1)} async-done(((bf16[8,128,512]{2,1,0:T(8,128)(2,1)}), bf16[8,128,512]{2,1,0:T(8,128)(2,1)S(1)}, u32[]{:S(2)}, u32[]{:S(2)}) %all-to-all-start.1) | async-done | bytes 1048608 | tf_op jit(solution)/shard_map/all_to_all | solution.py:501
  237.4 26.0 %shard_map.325 = (f32[4,197,512]{2,1,0:T(8,128)}, bf16[4,197,512]{2,1,0:T(8,128)(2,1)}, bf16[4,197,512]{2,1,0:T(8,128)(2,1)}, f32[4,197,512]{2,1,0:T(8,128)}, bf...) custom-call(f32[4,197,512]{2,1,0:T(8,128)} %get-tuple-element.82.mid, ...), custom_call_target="tpu_custom_call" | custom-call | flops 3305111552 | bytes 25453344 | tf_op jit(solution)/shard_map/pallas_call | solution.py:307
  263.3 30.8 %all_to_all.81 = bf16[8,128,512]{2,1,0:T(8,128)(2,1)} all-to-all(bf16[8,128,512]{2,1,0:T(8,128)(2,1)} %bitcast.194), channel_id=1, replica_groups=mesh['dp'=4,'expert'=8] {'expert'}, dimensions={0} | all-to-all | bytes 2097152 | tf_op jit(solution)/shard_map/all_to_all | solution.py:501
  361.8 23.8 %all-to-all-done.5 = bf16[8,128,512]{2,1,0:T(8,128)(2,1)} async-done(((bf16[8,128,512]{2,1,0:T(8,128)(2,1)}), bf16[8,128,512]{2,1,0:T(8,128)(2,1)}, u32[]{:S(2)}, u32[]{:S(2)}) %all-to-all-start.5) | async-done | bytes 1048608 | tf_op jit(solution)/shard_map/all_to_all | solution.py:501
  385.6 18.6 %shard_map.328 = (f32[4,197,512]{2,1,0:T(8,128)}, bf16[4,197,128]{2,1,0:T(8,128)(2,1)}, bf16[1024,512]{1,0:T(8,128)(2,1)}, bf16[1024,512]{1,0:T(8,128)(2,1)}) custom-call(f32[4,197,512]{2,1,0:T(8,128)} %get-tuple-element.86.middle, f32[4,197,2]{2,1,0:T(8,128)} %get-tuple-element.87.gates, s32[4,197,2]{2,1,0:T(8,128)} %copy.180.dcol, ...), custom_call_target="tpu_custom_call" | custom-call | flops 3305111552 | bytes 9262720 | tf_op jit(solution)/shard_map/pallas_call | solution.py:307
  404.2 30.8 %all_to_all.82 = bf16[8,128,512]{2,1,0:T(8,128)(2,1)} all-to-all(bf16[8,128,512]{2,1,0:T(8,128)(2,1)} %bitcast.199), channel_id=1, replica_groups=mesh['dp'=4,'expert'=8] {'expert'}, dimensions={0} | all-to-all | bytes 2097152 | tf_op jit(solution)/shard_map/all_to_all | solution.py:501
  495.2 31.0 %all_to_all.83 = bf16[8,128,512]{2,1,0:T(8,128)(2,1)} all-to-all(bf16[8,128,512]{2,1,0:T(8,128)(2,1)} %bitcast.196), channel_id=1, replica_groups=mesh['dp'=4,'expert'=8] {'expert'}, dimensions={0} | all-to-all | bytes 2097152 | tf_op jit(solution)/shard_map/all_to_all | solution.py:501
  526.2 39.6 %shard_map.333 = (f32[4,197,512]{2,1,0:T(8,128)}, f32[512,2176]{1,0:T(8,128)}, bf16[4,197,128]{2,1,0:T(8,128)(2,1)}, bf16[1024,512]{1,0:T(8,128)(2,1)}, bf16[1024,512]{1,0:T(8,128)(2,1)}) custom-call(f32[4,197,512]{2,1,0:T(8,128)} %copy.181.cotangent.upstream, f32[4,197,512]{2,1,0:T(8,128)} %get-tuple-element.91.rows, ...), custom_call_target="tpu_custom_call" | custom-call | flops 9915334656 | bytes 31920768 | tf_op jit(solution)/shard_map/pallas_call | solution.py:307
  567.1 29.7 %all_to_all.84 = bf16[8,128,512]{2,1,0:T(8,128)(2,1)} all-to-all(bf16[8,128,512]{2,1,0:T(8,128)(2,1)S(1)} %bitcast.185), channel_id=1, replica_groups=mesh['dp'=4,'expert'=8] {'expert'}, dimensions={0} | all-to-all | bytes 2097152 | tf_op jit(solution)/shard_map/all_to_all | solution.py:501
  656.9 30.8 %all_to_all.85 = bf16[8,128,512]{2,1,0:T(8,128)(2,1)} all-to-all(bf16[8,128,512]{2,1,0:T(8,128)(2,1)} %bitcast.197), channel_id=1, replica_groups=mesh['dp'=4,'expert'=8] {'expert'}, dimensions={0} | all-to-all | bytes 2097152 | tf_op jit(solution)/shard_map/all_to_all | solution.py:501
  687.8 28.0 %shard_map.338 = (f32[4,197,512]{2,1,0:T(8,128)}, f32[512,2176]{1,0:T(8,128)}) custom-call(f32[4,197,512]{2,1,0:T(8,128)} %get-tuple-element.106.upstream, f32[4,197,512]{2,1,0:T(8,128)} %copy.163.rows, f32[4,197,512]{2,1,0:T(8,128)} %get-tuple-element.82.middle, bf16[4,197,512]{2,1,0:T(8,128)(2,1)} %get-tuple-element.107.q_ref, ...), custom_call_target="tpu_custom_call" | custom-call | flops 9915334656 | bytes 27989152 | tf_op jit(solution)/shard_map/pallas_call | solution.py:307
  781.3 26.1 %reduce-scatter.19.cloned.1.call-done = bf16[128,2048]{1,0:T(8,128)(2,1)} async-done(((bf16[512,2048]{1,0:T(8,128)(2,1)}), bf16[128,2048]{1,0:T(8,128)(2,1)}) %reduce-scatter.19.cloned.1.call-update) | async-done | bytes 524304 | tf_op jit(solution)/shard_map/reduce_scatter | solution.py:626
  807.4 38.9 %reduce-scatter.21.cloned.1.call-done = bf16[128,2048]{1,0:T(8,128)(2,1)} async-done(((bf16[512,2048]{1,0:T(8,128)(2,1)}), bf16[128,2048]{1,0:T(8,128)(2,1)}) %reduce-scatter.21.cloned.1.call-update) | async-done | bytes 524304 | tf_op jit(solution)/shard_map/reduce_scatter | solution.py:626
  847.6 36.9 %reduce-scatter.27.cloned.1.call-done = bf16[512,512]{1,0:T(8,128)(2,1)} async-done(((bf16[2048,512]{1,0:T(8,128)(2,1)}), bf16[512,512]{1,0:T(8,128)(2,1)}) %reduce-scatter.27.cloned.1.call-update) | async-done | bytes 524304 | tf_op jit(solution)/shard_map/reduce_scatter | solution.py:627
  884.5 38.3 %reduce-scatter.29.cloned.1.call-done = bf16[512,512]{1,0:T(8,128)(2,1)} async-done(((bf16[2048,512]{1,0:T(8,128)(2,1)}), bf16[512,512]{1,0:T(8,128)(2,1)}) %reduce-scatter.29.cloned.1.call-update) | async-done | bytes 524304 | tf_op jit(solution)/shard_map/reduce_scatter | solution.py:627
  927.8 33.3 %reduce-scatter.23.cloned.1.call-done = bf16[512,512]{1,0:T(8,128)(2,1)} async-done(((bf16[2048,512]{1,0:T(8,128)(2,1)}), bf16[512,512]{1,0:T(8,128)(2,1)}) %reduce-scatter.23.cloned.1.call-update) | async-done | bytes 524304 | tf_op jit(solution)/shard_map/reduce_scatter | solution.py:627
  961.0 38.3 %reduce-scatter.25.cloned.1.call-done = bf16[512,512]{1,0:T(8,128)(2,1)} async-done(((bf16[2048,512]{1,0:T(8,128)(2,1)}), bf16[512,512]{1,0:T(8,128)(2,1)}) %reduce-scatter.25.cloned.1.call-update) | async-done | bytes 524304 | tf_op jit(solution)/shard_map/reduce_scatter | solution.py:627
  1002.9 34.5 %reduce-scatter.15.cloned.1.call-done = bf16[128,2048]{1,0:T(8,128)(2,1)} async-done(((bf16[512,2048]{1,0:T(8,128)(2,1)}), bf16[128,2048]{1,0:T(8,128)(2,1)}) %reduce-scatter.15.cloned.1.call-update) | async-done | bytes 524304 | tf_op jit(solution)/shard_map/reduce_scatter | solution.py:626
  1037.4 38.9 %reduce-scatter.17.cloned.1.call-done = bf16[128,2048]{1,0:T(8,128)(2,1)} async-done(((bf16[512,2048]{1,0:T(8,128)(2,1)}), bf16[128,2048]{1,0:T(8,128)(2,1)}) %reduce-scatter.17.cloned.1.call-update) | async-done | bytes 524304 | tf_op jit(solution)/shard_map/reduce_scatter | solution.py:626
  1079.9 64.4 %all-reduce.4.cloned.1.call-done = (f32[1,128,2176]{2,1,0:T(8,128)}, f32[1,128,2176]{2,1,0:T(8,128)}) async-done(((f32[1,128,2176]{2,1,0:T(8,128)}, f32[1,128,2176]{2,1,0:T(8,128)}), (f32[1,128,2176]{2,1,0:T(8,128)}, f32[1,128,2176]{2,1,0:T(8,128)})) %all-reduce.4.cloned.1.call-update) | async-done | bytes 2228240 | tf_op jit(solution)/shard_map/psum | solution.py:653
  (265 shorter events, 349.3 us)
Async XLA Ops:
  7.3 45.5 %all-gather.11.cloned.1.call-start = ((), (), s32[]{:S(2)}) async-start(), calls=%async_computation.26 | async-start | bytes 2785280 | tf_op jit(solution)/shard_map/all_gather | solution.py:538
  13.5 97.2 %all-gather.15.cloned.1.call-start = ((), (), s32[]{:S(2)}) async-start(), calls=%async_computation.38 | async-start | bytes 5242880 | tf_op jit(solution)/shard_map/all_gather | solution.py:546
  17.5 145.1 %all-gather.17.cloned.1.call-start = ((), (), s32[]{:S(2)}) async-start(), calls=%async_computation.39 | async-start | bytes 5242880 | tf_op jit(solution)/shard_map/all_gather | solution.py:548
  21.5 190.5 %all-gather.13.cloned.1.call-start = ((), (), s32[]{:S(2)}) async-start(), calls=%async_computation.27 | async-start | bytes 2785280 | tf_op jit(solution)/shard_map/all_gather | solution.py:538
  23.6 274.7 %all-gather.19.cloned.1.call-start = ((), (), s32[]{:S(2)}) async-start(), calls=%async_computation.40 | async-start | bytes 5242880 | tf_op jit(solution)/shard_map/all_gather | solution.py:546
  104.7 70.2 %all-to-all-start = ((bf16[8,128,512]{2,1,0:T(8,128)(2,1)}), bf16[8,128,512]{2,1,0:T(8,128)(2,1)S(1)}, u32[]{:S(2)}, u32[]{:S(2)}) async-start(bf16[8,128,512]{2,1,0:T(8,128)(2,1)} %bitcast.181), calls=%async_computation | async-start | bytes 2097152 | tf_op jit(solution)/shard_map/all_to_all | solution.py:501
  174.9 31.2 %all-to-all-start.3 = ((bf16[8,128,512]{2,1,0:T(8,128)(2,1)}), bf16[8,128,512]{2,1,0:T(8,128)(2,1)S(1)}, u32[]{:S(2)}, u32[]{:S(2)}) async-start(bf16[8,128,512]{2,1,0:T(8,128)(2,1)} %bitcast.190), calls=%async_computation.3 | async-start | bytes 2097152 | tf_op jit(solution)/shard_map/all_to_all | solution.py:501
  179.5 130.7 %all-gather.21.cloned.1.call-start = ((), (), s32[]{:S(2)}) async-start(), calls=%async_computation.41 | async-start | bytes 5242880 | tf_op jit(solution)/shard_map/all_gather | solution.py:548
  206.1 30.3 %all-to-all-start.1 = ((bf16[8,128,512]{2,1,0:T(8,128)(2,1)}), bf16[8,128,512]{2,1,0:T(8,128)(2,1)S(1)}, u32[]{:S(2)}, u32[]{:S(2)}) async-start(bf16[8,128,512]{2,1,0:T(8,128)(2,1)} %bitcast.186), calls=%async_computation.1 | async-start | bytes 2097152 | tf_op jit(solution)/shard_map/all_to_all | solution.py:501
  324.2 30.1 %all-to-all-start.7 = ((bf16[8,128,512]{2,1,0:T(8,128)(2,1)}), bf16[8,128,512]{2,1,0:T(8,128)(2,1)S(1)}, u32[]{:S(2)}, u32[]{:S(2)}) async-start(bf16[8,128,512]{2,1,0:T(8,128)(2,1)} %bitcast.195), calls=%async_computation.7 | async-start | bytes 2097152 | tf_op jit(solution)/shard_map/all_to_all | solution.py:501
  354.3 31.2 %all-to-all-start.5 = ((bf16[8,128,512]{2,1,0:T(8,128)(2,1)}), bf16[8,128,512]{2,1,0:T(8,128)(2,1)}, u32[]{:S(2)}, u32[]{:S(2)}) async-start(bf16[8,128,512]{2,1,0:T(8,128)(2,1)} %bitcast.193), calls=%async_computation.5 | async-start | bytes 2097152 | tf_op jit(solution)/shard_map/all_to_all | solution.py:501
  435.1 30.1 %all-to-all-start.8 = ((bf16[8,128,512]{2,1,0:T(8,128)(2,1)}), bf16[8,128,512]{2,1,0:T(8,128)(2,1)S(1)}, u32[]{:S(2)}, u32[]{:S(2)}) async-start(bf16[8,128,512]{2,1,0:T(8,128)(2,1)} %bitcast.191), calls=%async_computation.8 | async-start | bytes 2097152 | tf_op jit(solution)/shard_map/all_to_all | solution.py:501
  465.2 30.1 %all-to-all-start.11 = ((bf16[8,128,512]{2,1,0:T(8,128)(2,1)}), bf16[8,128,512]{2,1,0:T(8,128)(2,1)S(1)}, u32[]{:S(2)}, u32[]{:S(2)}) async-start(bf16[8,128,512]{2,1,0:T(8,128)(2,1)} %bitcast.187), calls=%async_computation.11 | async-start | bytes 2097152 | tf_op jit(solution)/shard_map/all_to_all | solution.py:501
  468.7 312.6 %reduce-scatter.13.cloned.1.call-start = ((), (), s32[]{:S(2)}) async-start(), calls=%async_computation.29 | async-start | bytes 5570560 | tf_op jit(solution)/shard_map/reduce_scatter | solution.py:652
  630.4 150.9 %reduce-scatter.11.cloned.1.call-start = ((), (), s32[]{:S(2)}) async-start(), calls=%async_computation.28 | async-start | bytes 5570560 | tf_op jit(solution)/shard_map/reduce_scatter | solution.py:652
  715.8 91.6 %reduce-scatter.19.cloned.1.call-start = ((), (), s32[]{:S(2)}) async-start(), calls=%async_computation.32 | async-start | bytes 2621440 | tf_op jit(solution)/shard_map/reduce_scatter | solution.py:626
  725.8 120.5 %reduce-scatter.21.cloned.1.call-start = ((), (), s32[]{:S(2)}) async-start(), calls=%async_computation.33 | async-start | bytes 2621440 | tf_op jit(solution)/shard_map/reduce_scatter | solution.py:626
  735.5 149.0 %reduce-scatter.27.cloned.1.call-start = ((), (), s32[]{:S(2)}) async-start(), calls=%async_computation.36 | async-start | bytes 2621440 | tf_op jit(solution)/shard_map/reduce_scatter | solution.py:627
  736.2 186.6 %reduce-scatter.29.cloned.1.call-start = ((), (), s32[]{:S(2)}) async-start(), calls=%async_computation.37 | async-start | bytes 2621440 | tf_op jit(solution)/shard_map/reduce_scatter | solution.py:627
  736.8 224.2 %reduce-scatter.23.cloned.1.call-start = ((), (), s32[]{:S(2)}) async-start(), calls=%async_computation.34 | async-start | bytes 2621440 | tf_op jit(solution)/shard_map/reduce_scatter | solution.py:627
  746.3 253.1 %reduce-scatter.25.cloned.1.call-start = ((), (), s32[]{:S(2)}) async-start(), calls=%async_computation.35 | async-start | bytes 2621440 | tf_op jit(solution)/shard_map/reduce_scatter | solution.py:627
  756.4 281.0 %reduce-scatter.15.cloned.1.call-start = ((), (), s32[]{:S(2)}) async-start(), calls=%async_computation.30 | async-start | bytes 2621440 | tf_op jit(solution)/shard_map/reduce_scatter | solution.py:626
  757.0 319.3 %reduce-scatter.17.cloned.1.call-start = ((), (), s32[]{:S(2)}) async-start(), calls=%async_computation.31 | async-start | bytes 2621440 | tf_op jit(solution)/shard_map/reduce_scatter | solution.py:626
  757.6 386.6 %all-reduce.4.cloned.1.call-start = ((), (), s32[]{:S(2)}) async-start(), calls=%async_computation.42 | async-start | bytes 4456448 | tf_op jit(solution)/shard_map/psum | solution.py:653
  (38 other events, 342.2 us)
Sparse Core Ops, SparseCore 0:
  13.6 39.1 all-gather.10
  55.2 52.7 all-gather.14
  109.9 52.6 all-gather.16
  164.3 36.5 all-gather.12
  203.1 52.6 all-gather.18
  257.6 52.6 all-gather.20
  566.0 52.7 reduce-scatter.12
  715.9 52.8 reduce-scatter.10
  771.7 35.6 reduce-scatter.18
  811.1 35.1 reduce-scatter.20
  849.3 35.1 reduce-scatter.26
  887.6 35.1 reduce-scatter.28
  925.8 35.1 reduce-scatter.22
  964.1 35.1 reduce-scatter.24
  1002.2 35.1 reduce-scatter.14
  1041.1 35.1 reduce-scatter.16
  1078.5 65.6 all-reduce.3

commit v2 on v1

--- a/solution.py
+++ b/solution.py
@@ -198,10 +198,11 @@
     upstream, rows, middle, q_ref, k_ref, v_ref, o_ref, lse_ref, dz_ref, dcol, came_a, came_b,
     wq, wk, wv, wo, misc, *rest,
 ):
-    if len(rest) > 3:
-        yzero, yone, gates_below, routes_below, drow_below, grad_ref, wgrad, dz_below, out_a, out_b, vgrad = rest
+    bias, *rest = rest
+    if len(rest) > 4:
+        yzero, yone, gates_below, routes_below, drow_below, grad_ref, sent, dz_below, out_a, out_b, wgrad, vgrad = rest
     else:
-        grad_ref, wgrad, vgrad = rest
+        grad_ref, sent, wgrad, vgrad = rest
     first = pl.program_id(0) == 0
     length = rows.shape[1]
     width = rows.shape[2]
@@ -275,7 +276,7 @@
     add_vector(4, dlow)
     grad = dmiddle + standardize_back(dlow, unit, scale, again)
     grad_ref[0] = grad
-    if len(rest) > 3:
+    if len(rest) > 4:
         grads_body(
             grad, yzero[0].astype(F32), yone[0].astype(F32), gates_below, routes_below, drow_below, dz_below,
             (out_a, out_b),
@@ -284,6 +285,8 @@
     @pl.when(pl.program_id(0) == pl.num_programs(0) - 1)
     def _():
         wgrad[:, 4 * width :] += vgrad[...].T
+        sent[:, : 4 * width + MISC] = wgrad[...].astype(BF16)
+        sent[:, 4 * width + MISC :] = bias[...]
 
 
 def per_image(array):
@@ -341,14 +344,19 @@
     return 0.5 * value * (1.0 + lax.erf(value * 0.7071067811865476))
 
 
+def block_of(ref):
+    return ref[...].reshape(-1, ref.shape[-1])
+
+
 def expert_kernel(x_ref, w1_ref, b1_ref, w2_ref, b2_ref, y_ref, acc):
     step = pl.program_id(0)
+    w1, w2 = block_of(w1_ref), block_of(w2_ref)
     rows = x_ref.shape[0]
     chunk = 256
     for start in range(0, rows, chunk):
         part = slice(start, start + chunk)
-        inner = dot(x_ref[part, :], w1_ref[0]) + b1_ref[0]
-        term = dot(gelu(inner).astype(BF16), w2_ref[0])
+        inner = dot(x_ref[part, :], w1) + b1_ref[0]
+        term = dot(gelu(inner).astype(BF16), w2)
 
         @pl.when(step == 0)
         def _(part=part, term=term):
@@ -365,10 +373,11 @@
 
 def slope_kernel(x_ref, w1_ref, b1_ref, g_ref, s_ref):
     rows = x_ref.shape[0]
+    w1 = block_of(w1_ref)
     chunk = 256
     for start in range(0, rows, chunk):
         part = slice(start, start + chunk)
-        inner = dot(x_ref[part, :], w1_ref[0]) + b1_ref[0]
+        inner = dot(x_ref[part, :], w1) + b1_ref[0]
         normal = 0.5 * (1.0 + lax.erf(inner * 0.7071067811865476))
         g_ref[part, :] = (inner * normal).astype(BF16)
         s_ref[part, :] = (normal + inner * (jnp.exp(-0.5 * inner * inner) * 0.3989422804014327)).astype(BF16)
@@ -376,14 +385,15 @@
 
 def expert_back_kernel(dy_ref, s_ref, w1_ref, w2_ref, du_ref, dx_ref, acc):
     step = pl.program_id(0)
+    w1, w2 = block_of(w1_ref), block_of(w2_ref)
     rows = dy_ref.shape[0]
     chunk = 256
     for start in range(0, rows, chunk):
         part = slice(start, start + chunk)
-        dg = dot_nt(dy_ref[part, :], w2_ref[0])
+        dg = dot_nt(dy_ref[part, :], w2)
         du = (dg * s_ref[part, :].astype(F32)).astype(BF16)
         du_ref[part, :] = du
-        term = dot_nt(du, w1_ref[0])
+        term = dot_nt(du, w1)
 
         @pl.when(step == 0)
         def _(part=part, term=term):
@@ -398,21 +408,34 @@
         dx_ref[...] = acc[...].astype(BF16)
 
 
-def expert_weight_kernel(x_ref, g_ref, du_ref, dy_ref, dw1_ref, dw2_ref, db1_ref, db2_ref):
-    dw1_ref[...] = dot_tn(x_ref[...], du_ref[...]).astype(BF16)
-    dw2_ref[...] = dot_tn(g_ref[...], dy_ref[...]).astype(BF16)
+def expert_weight_kernel(x_ref, g_ref, du_ref, dy_ref, out_ref, db1_ref, db2_ref):
+    step = pl.program_id(0)
+    parts, rows, _ = out_ref.shape
+    width = x_ref.shape[1]
+    share = width // parts
+    dw1 = dot_tn(x_ref[...], du_ref[...]).astype(BF16)
+    place = pl.ds(pl.multiple_of(step * share, share), share)
+    for part in range(parts):
+        out_ref[part, place, :] = dw1[part * share : (part + 1) * share, :]
+    dw2 = dot_tn(g_ref[...], dy_ref[...]).astype(BF16)
+    take = rows // 2
+    each = FF_BLOCK // take
+    for part in range(each):
+        out_ref[step * each + part, take:, :] = dw2[part * take : (part + 1) * take, :]
     db1_ref[...] = jnp.sum(du_ref[...].astype(F32), axis=0, keepdims=True)
 
-    @pl.when(pl.program_id(0) == 0)
+    @pl.when(step == 0)
     def _():
         db2_ref[...] = jnp.sum(dy_ref[...].astype(F32), axis=0, keepdims=True)
 
 
-def inner_specs(j, width, ff):
+def inner_specs(packed, j):
+    parts, _, rows, width = packed.shape
+    share, take = width // parts, rows // 2
     return (
-        pl.BlockSpec((1, width, FF_BLOCK), lambda f: (j, 0, f)),
+        pl.BlockSpec((parts, 1, share, width), lambda f: (0, j, f, 0)),
         pl.BlockSpec((1, 1, FF_BLOCK), lambda f: (j, 0, f)),
-        pl.BlockSpec((1, FF_BLOCK, width), lambda f: (j, f, 0)),
+        pl.BlockSpec((FF_BLOCK // take, 1, take, width), lambda f: (f, j, 1, 0)),
         pl.BlockSpec((1, 1, width), lambda f: (j, 0, 0)),
     )
 
@@ -422,13 +445,13 @@
 
 
 def expert_forward(x, expert, j):
-    w1, b1, w2, b2 = expert
+    packed, b1, b2 = expert
     rows, width = x.shape
-    ff = w1.shape[2]
-    i1, i2, i3, i4 = inner_specs(j, width, ff)
+    ff = b1.shape[2]
+    i1, i2, i3, i4 = inner_specs(packed, j)
     return call(
         expert_kernel, (ff // FF_BLOCK,),
-        [(x, whole(x)), (w1, i1), (b1, i2), (w2, i3), (b2, i4)],
+        [(x, whole(x)), (packed, i1), (b1, i2), (packed, i3), (b2, i4)],
         [((rows, width), BF16, pl.BlockSpec((rows, width), lambda f: (0, 0)))],
         [pltpu.VMEM((rows, width), F32)],
         flops=4 * rows * width * ff,
@@ -436,42 +459,42 @@
 
 
 def expert_slopes(x, expert, j):
-    w1, b1, w2, b2 = expert
+    packed, b1, b2 = expert
     rows, width = x.shape
-    ff = w1.shape[2]
-    i1, i2, _, _ = inner_specs(j, width, ff)
+    ff = b1.shape[2]
+    i1, i2, _, _ = inner_specs(packed, j)
     return call(
-        slope_kernel, (ff // FF_BLOCK,), [(x, whole(x)), (w1, i1), (b1, i2)],
+        slope_kernel, (ff // FF_BLOCK,), [(x, whole(x)), (packed, i1), (b1, i2)],
         [columns_of(rows, ff), columns_of(rows, ff)],
         flops=2 * rows * width * ff,
     )
 
 
 def expert_backward(dy, slopes, expert, j):
-    w1, b1, w2, b2 = expert
+    packed, b1, b2 = expert
     rows, width = dy.shape
-    ff = w1.shape[2]
-    i1, _, i3, _ = inner_specs(j, width, ff)
+    ff = b1.shape[2]
+    i1, _, i3, _ = inner_specs(packed, j)
     by_columns = pl.BlockSpec((rows, FF_BLOCK), lambda f: (0, f))
     return call(
         expert_back_kernel, (ff // FF_BLOCK,),
-        [(dy, whole(dy)), (slopes, by_columns), (w1, i1), (w2, i3)],
+        [(dy, whole(dy)), (slopes, by_columns), (packed, i1), (packed, i3)],
         [columns_of(rows, ff), ((rows, width), BF16, pl.BlockSpec((rows, width), lambda f: (0, 0)))],
         [pltpu.VMEM((rows, width), F32)],
         flops=4 * rows * width * ff,
     )
 
 
-def expert_weight_grads(x, g, du, dy):
+def expert_weight_grads(x, g, du, dy, parts):
     rows, width = x.shape
     ff = g.shape[1]
     by_columns = pl.BlockSpec((rows, FF_BLOCK), lambda f: (0, f))
+    packed = (parts, 2 * ff // parts, width)
     return call(
         expert_weight_kernel, (ff // FF_BLOCK,),
         [(x, whole(x)), (g, by_columns), (du, by_columns), (dy, whole(dy))],
         [
-            ((width, ff), BF16, pl.BlockSpec((width, FF_BLOCK), lambda f: (0, f))),
-            ((ff, width), BF16, pl.BlockSpec((FF_BLOCK, width), lambda f: (f, 0))),
+            (packed, BF16, pl.BlockSpec(packed, lambda f: (0, 0, 0))),
             ((1, ff), F32, pl.BlockSpec((1, FF_BLOCK), lambda f: (0, f))),
             ((1, width), F32, pl.BlockSpec((1, width), lambda f: (0, 0))),
         ],
@@ -520,13 +543,15 @@
     squares = (query_weight, key_weight, value_weight, output_weight)
     vectors = (query_bias, value_bias, output_bias, attend_gain, attend_shift, expert_gain, expert_shift)
     bias_columns = ff // width + 1
+    bias_room = -(-experts_all * bias_columns // MISC) * MISC
 
     biases = jnp.concatenate(
-        [inner_bias.reshape(LAYERS, local, ff // width, share), outer_bias.reshape(LAYERS, local, 1, share)], axis=2
-    )
-    biases = biases.reshape(LAYERS * local * bias_columns, share).T
+        [inner_bias.reshape(LAYERS, local, share, ff // width), outer_bias.reshape(LAYERS, local, share, 1)], axis=3
+    )
+    biases = jnp.transpose(biases, (2, 0, 1, 3)).reshape(share, LAYERS * local * bias_columns)
 
     packed = []
+    experts = []
     for layer in range(LAYERS):
         misc = [router_weight[layer], jnp.zeros((share, VEC_AT - experts_all), F32)]
         misc += [jnp.stack([v[layer] for v in vectors], axis=1), jnp.zeros((share, BIAS_AT - VEC_AT - 7), F32)]
@@ -536,18 +561,14 @@
             misc += [jnp.zeros((share, MISC - BIAS_AT), F32)]
         mine = jnp.concatenate([s[layer] for s in squares] + misc, axis=1).astype(BF16)
         packed.append(lax.all_gather(mine, "dp", axis=0, tiled=True))
+        mine = jnp.transpose(inner_weight[layer].reshape(local, share, ff // FF_BLOCK, FF_BLOCK), (0, 2, 1, 3))
+        mine = jnp.concatenate([mine.reshape(local, ff // parts, width), outer_weight[layer]], axis=1).astype(BF16)
+        experts.append(lax.all_gather(mine, "dp", axis=0, tiled=False))
     spare = packed[0][:, 4 * width + BIAS_AT : 4 * width + BIAS_AT + biases.shape[1]].astype(F32)
-    spare = spare.reshape(parts, share, LAYERS, local, bias_columns)
-    inner_biases = jnp.transpose(spare[..., :-1], (2, 3, 0, 4, 1)).reshape(LAYERS, local, 1, ff)
-    outer_biases = jnp.transpose(spare[..., -1:], (2, 3, 4, 0, 1)).reshape(LAYERS, local, 1, width)
-    experts = []
-    for layer in range(LAYERS):
-        experts.append((
-            lax.all_gather(inner_weight[layer].astype(BF16), "dp", axis=1, tiled=True),
-            inner_biases[layer],
-            lax.all_gather(outer_weight[layer].astype(BF16), "dp", axis=1, tiled=True),
-            outer_biases[layer],
-        ))
+    spare = jnp.transpose(spare.reshape(width, LAYERS, local, bias_columns), (1, 2, 0, 3))
+    inner_biases = spare[..., :-1].reshape(LAYERS, local, 1, ff)
+    outer_biases = spare[..., -1].reshape(LAYERS, local, 1, width)
+    experts = [(experts[n], inner_biases[n], outer_biases[n]) for n in range(LAYERS)]
 
     dcol, capacity = destinations(routes, experts_all, owners)
     drow = jnp.transpose(dcol, (0, 1, 3, 2))
@@ -592,6 +613,7 @@
         produced = [expert_forward(arrived[j], experts[layer], j) for j in range(local)]
         back = [exchange(item) for item in produced]
         slopes = [expert_slopes(arrived[j], experts[layer], j) for j in range(local)]
+        back, slopes = lax.optimization_barrier((back, slopes))
         saved.append({
             "rows": rows, "middle": middle, "attend": (queries, keys, values, context, sums), "gates": gates,
             "arrived": arrived, "slopes": slopes,
@@ -608,34 +630,42 @@
     )
     upstream = cotangent
     dense_grads = [None] * LAYERS
-    bias_grads = [None] * LAYERS
-    inner_grads = [None] * LAYERS
-    outer_grads = [None] * LAYERS
+    finished = []
+    waiting = []
     for layer in reversed(range(LAYERS)):
         kept = saved[layer]
         dys = [exchange(item) for item in sent]
-        dus, dxs = [], []
+        dxs, grads, came, reduced = [], [], [], []
         for j in range(local):
+            dys[j], done = lax.optimization_barrier((dys[j], waiting[j : j + 1]))
+            finished += done
             du, dx = expert_backward(dys[j], kept["slopes"][j][1], experts[layer], j)
-            dus.append(du)
             dxs.append(dx)
+            grad = expert_weight_grads(kept["arrived"][j], kept["slopes"][j][0], du, dys[j], parts)
+            grads.append(grad)
+            reduced.append(lax.psum_scatter(grad[0], "dp", scatter_dimension=0, tiled=False))
+            if j + 1 < local:
+                dys[j + 1], grad = lax.optimization_barrier((dys[j + 1], grad))
+                grads[j] = grad
         came = [exchange(item) for item in dxs]
-        grads = [
-            expert_weight_grads(kept["arrived"][j], kept["slopes"][j][0], dus[j], dys[j]) for j in range(local)
+        waiting = reduced
+        own = [
+            jnp.concatenate([g[1].reshape(width, ff // width), g[2].reshape(width, 1)], axis=1) for g in grads
         ]
-        inner_grads[layer] = [lax.psum_scatter(g[0], "dp", scatter_dimension=0, tiled=True) for g in grads]
-        outer_grads[layer] = [lax.psum_scatter(g[1], "dp", scatter_dimension=0, tiled=True) for g in grads]
-        bias_grads[layer] = [
-            jnp.concatenate([g[2].reshape(parts, ff // parts), g[3].reshape(parts, share)], axis=1) for g in grads
-        ]
+        first_column = lax.axis_index("expert") * (local * bias_columns)
+        bias = lax.dynamic_update_slice(
+            jnp.zeros((width, bias_room), F32), jnp.concatenate(own, axis=1), (0, first_column)
+        ).astype(BF16)
+        came, bias = lax.optimization_barrier((came, bias))
         weights = [(packed[layer], s) for s in packed_specs(packed[layer])]
         inputs = [upstream, kept["rows"], kept["middle"], *kept["attend"], dz, dcol[layer]]
         inputs = [(a, per_image(a)) for a in inputs] + [(a, whole(a)) for a in came] + weights
+        inputs += [(bias, whole(bias))]
         outputs = [
             images_out(count, length, width, F32),
             (
-                (width, 4 * width + MISC), F32,
-                pl.BlockSpec((width, 4 * width + MISC), lambda i: (0, 0)),
+                (width, 4 * width + MISC + bias_room), BF16,
+                pl.BlockSpec((width, 4 * width + MISC + bias_room), lambda i: (0, 0)),
             ),
         ]
         if layer > 0:
@@ -644,36 +674,37 @@
             inputs += [(a, per_image(a)) for a in extra]
             outputs += [images_out(count, length, MISC, BF16)] + slots_out(half, width)
         done = call(
-            back_kernel, (count,), inputs, outputs, [pltpu.VMEM((MISC, width), F32)], flops=3 * dense_flops
+            back_kernel, (count,), inputs, outputs,
+            [pltpu.VMEM((width, 4 * width + MISC), F32), pltpu.VMEM((MISC, width), F32)], flops=3 * dense_flops,
         )
         upstream, wgrad = done[:2]
         if layer > 0:
             dz, *sent = done[2:]
         mine = lax.psum_scatter(wgrad, "dp", scatter_dimension=0, tiled=True)
         dense_grads[layer] = lax.psum(mine, "expert")
-
-    small = jnp.stack([jnp.stack(b, axis=1) for b in bias_grads], axis=1)
-    small = lax.psum_scatter(small, "dp", scatter_dimension=0, tiled=False)
-    inner_bias_grad = small[:, :, : ff // parts]
-    outer_bias_grad = small[:, :, ff // parts :]
-    both = jnp.stack(dense_grads)
+    expert_grads = [waiting, finished]
+
+    both = jnp.stack(dense_grads).astype(F32)
     square_grads = [both[:, :, n * width : (n + 1) * width] for n in range(4)]
-    tail = both[:, :, 4 * width :]
+    tail = both[:, :, 4 * width : 4 * width + MISC]
+    own = lax.dynamic_slice_in_dim(
+        both[:, :, 4 * width + MISC :], lax.axis_index("expert") * (local * bias_columns), local * bias_columns, 2
+    )
+    own = jnp.transpose(own.reshape(LAYERS, share, local, bias_columns), (0, 2, 1, 3))
+    pieces = jnp.stack([jnp.stack(g) for g in expert_grads])
+    inner_grad = pieces[:, :, : ff // parts].reshape(LAYERS, local, ff // FF_BLOCK, share, FF_BLOCK)
+    inner_grad = jnp.transpose(inner_grad, (0, 1, 3, 2, 4)).reshape(inner_weight.shape)
     return (
-        rows_out(result, images),
+        result,
         upstream,
         *square_grads,
         tail[:, :, :experts_all],
         *[tail[:, :, VEC_AT + n] for n in range(7)],
-        jnp.stack([jnp.stack(g) for g in inner_grads]).astype(F32),
-        inner_bias_grad,
-        jnp.stack([jnp.stack(g) for g in outer_grads]).astype(F32),
-        outer_bias_grad,
-    )
-
-
-def rows_out(result, images):
-    return result.reshape(images.shape)
+        inner_grad.astype(F32),
+        own[..., :-1].reshape(LAYERS, local, ff // parts),
+        pieces[:, :, ff // parts :].astype(F32),
+        own[..., -1],
+    )
 
 
 def solution(mesh):

time: 1170 us -> 980 us (0.84)
  waiting for transfers between devices: 540 us -> 356 us
  blocking collectives: 200 us -> 183 us
  local copies, waits for them, and re-layouts: 33.6 us -> 48.4 us
    reduce_scatter x8 -> x0, waiting for transfers between devices: 285 us -> none  [the longest x4 147 us: shards(): lax.psum_scatter(g[1], 'dp', scatter_dimension=0, tiled=True)]
    unnamed x17 -> x15, waiting for transfers between devices: 3.45 us -> 105 us
    reduce_scatter x2, waiting for transfers between devices: 0.01 us -> 35.4 us  [shards(): mine = lax.psum_scatter(wgrad, 'dp', scatter_dimension=0, tiled=True)]
    all_gather x4 -> x2, waiting for transfers between devices: 63.9 us -> 31.7 us  [shards(): experts.append(lax.all_gather(mine, 'dp', axis=0, tiled=False))]
    unnamed x1 -> x0, blocking collectives: 15.4 us -> none
  transfers between devices with their start and end apart: 27 -> 21, of which waited for: 21 -> 15; matrix products, arithmetic and copies ran while one was open for 4% -> 5% of each run, Pallas kernels for 21% -> 27%
where the time goes in v2:
time: 980 us; the launch traced here: 969 us
  waiting for transfers between devices  356 us (36%)
  Pallas kernels  305 us (31%)
  blocking collectives  183 us (19%)
  local copies, waits for them, and re-layouts  48.4 us (5%)
  starting transfers between devices  38.9 us (4%)
  other arithmetic  22 us (2%)
  between operations  15.3 us (2%)
    pallas_call x21, Pallas kernels, call(): pl.pallas_call(body, grid=grid, in_specs=[s for _, s in inputs], out_spec...  305 us
    all_to_all x6, blocking collectives, exchange(): lax.all_to_all(array.reshape(owners, rows // owners, width), 'expert', sp...  183 us
    all_to_all x10, waiting for transfers between devices, exchange(): lax.all_to_all(array.reshape(owners, rows // owners, width), 'expert', sp...  108 us
    unnamed x15, waiting for transfers between devices  105 us
    psum x1, waiting for transfers between devices, shards(): dense_grads[layer] = lax.psum(mine, 'expert')  54.3 us
    all_to_all x10, starting transfers between devices, exchange(): lax.all_to_all(array.reshape(owners, rows // owners, width), 'expert', sp...  38.2 us
    reduce_scatter x2, waiting for transfers between devices, shards(): mine = lax.psum_scatter(wgrad, 'dp', scatter_dimension=0, tiled=True)  35.4 us
    all_gather x2, waiting for transfers between devices, shards(): experts.append(lax.all_gather(mine, 'dp', axis=0, tiled=False))  31.7 us
  transfers between devices with their start and end apart: 21, of which 15 were waited for; matrix products, arithmetic and copies ran while one was open for 5% of the time, Pallas kernels for 27%

profile of v2, /device:TPU:0, one launch (start us, length us, event | category | flops | bytes accessed | tf_op | source)
XLA Modules:
  0.0 969.3 jit_solution(12674123739541731339)
XLA Ops:
  35.1 20.8 %all-gather.5.cloned.1.call-done.wq.wk.wv.wo.misc = bf16[512,2176]{1,0:T(8,128)(2,1)} async-done(((bf16[128,2176]{1,0:T(8,128)(2,1)}), bf16[512,2176]{1,0:T(8,128)(2,1)}) %all-gather.5.cloned.1.call-update) | async-done | bytes 2228240 | tf_op jit(solution)/shard_map/all_gather | solution.py:563
  55.9 20.5 %shard_map.322 = (f32[4,197,512]{2,1,0:T(8,128)}, bf16[4,197,512]{2,1,0:T(8,128)(2,1)}, bf16[4,197,512]{2,1,0:T(8,128)(2,1)}, bf16[4,197,512]{2,1,0:T(8,128)(2,1...) custom-call(f32[4,197,512]{2,1,0:T(8,128)} %copy.328.rows, ...), custom_call_target="tpu_custom_call" | custom-call | flops 3305111552 | bytes 20115936 | tf_op jit(solution)/shard_map/pallas_call | solution.py:310
  76.5 31.3 %all_to_all.80 = bf16[8,128,512]{2,1,0:T(8,128)(2,1)} all-to-all(bf16[8,128,512]{2,1,0:T(8,128)(2,1)} %bitcast.213), channel_id=1, replica_groups=mesh['dp'=4,'expert'=8] {'expert'}, dimensions={0} | all-to-all | bytes 2097152 | tf_op jit(solution)/shard_map/all_to_all | solution.py:524
  114.4 31.7 %all-gather.7.cloned.1.call-done.w1_ref.w2_ref = bf16[4,2,1024,512]{3,2,1,0:T(8,128)(2,1)} async-done(((bf16[1,2,1024,512]{3,2,1,0:T(8,128)(2,1)}), bf16[4,2,1024,512]{3,2,1,0:T(8,128)(2,1)}) %all-gather.7.cloned.1.call-update) | async-done | bytes 8388624 | tf_op jit(solution)/shard_map/all_gather | solution.py:566
  175.6 14.2 %all-to-all-done.1 = bf16[8,128,512]{2,1,0:T(8,128)(2,1)S(1)} async-done(((bf16[8,128,512]{2,1,0:T(8,128)(2,1)}), bf16[8,128,512]{2,1,0:T(8,128)(2,1)S(1)}, u32[]{:S(2)}, u32[]{:S(2)}) %all-to-all-start.1) | async-done | bytes 1048608 | tf_op jit(solution)/shard_map/all_to_all | solution.py:524
  220.8 26.0 %shard_map.327 = (f32[4,197,512]{2,1,0:T(8,128)}, bf16[4,197,512]{2,1,0:T(8,128)(2,1)}, bf16[4,197,512]{2,1,0:T(8,128)(2,1)}, f32[4,197,512]{2,1,0:T(8,128)}, bf...) custom-call(f32[4,197,512]{2,1,0:T(8,128)} %get-tuple-element.106.mi, ...), custom_call_target="tpu_custom_call" | custom-call | flops 3305111552 | bytes 25453344 | tf_op jit(solution)/shard_map/pallas_call | solution.py:310
  246.8 30.8 %all_to_all.81 = bf16[8,128,512]{2,1,0:T(8,128)(2,1)} all-to-all(bf16[8,128,512]{2,1,0:T(8,128)(2,1)} %bitcast.212), channel_id=1, replica_groups=mesh['dp'=4,'expert'=8] {'expert'}, dimensions={0} | all-to-all | bytes 2097152 | tf_op jit(solution)/shard_map/all_to_all | solution.py:524
  294.7 13.0 %all-to-all-done.6 = bf16[8,128,512]{2,1,0:T(8,128)(2,1)S(1)} async-done(((bf16[8,128,512]{2,1,0:T(8,128)(2,1)}), bf16[8,128,512]{2,1,0:T(8,128)(2,1)S(1)}, u32[]{:S(2)}, u32[]{:S(2)}) %all-to-all-start.6) | async-done | bytes 1048608 | tf_op jit(solution)/shard_map/all_to_all | solution.py:524
  324.1 14.1 %all-to-all-done.5 = bf16[8,128,512]{2,1,0:T(8,128)(2,1)S(1)} async-done(((bf16[8,128,512]{2,1,0:T(8,128)(2,1)}), bf16[8,128,512]{2,1,0:T(8,128)(2,1)S(1)}, u32[]{:S(2)}, u32[]{:S(2)}) %all-to-all-start.5) | async-done | bytes 1048608 | tf_op jit(solution)/shard_map/all_to_all | solution.py:524
  369.1 18.6 %shard_map.332 = (f32[4,197,512]{2,1,0:T(8,128)}, bf16[4,197,128]{2,1,0:T(8,128)(2,1)}, bf16[1024,512]{1,0:T(8,128)(2,1)}, bf16[1024,512]{1,0:T(8,128)(2,1)}) custom-call(f32[4,197,512]{2,1,0:T(8,128)} %get-tuple-element.116.middle, f32[4,197,2]{2,1,0:T(8,128)} %get-tuple-element.117.gates, s32[4,197,2]{2,1,0:T(8,128)} %copy.356.dcol, ...), custom_call_target="tpu_custom_call" | custom-call | flops 3305111552 | bytes 9262720 | tf_op jit(solution)/shard_map/pallas_call | solution.py:310
  387.7 30.8 %all_to_all.82 = bf16[8,128,512]{2,1,0:T(8,128)(2,1)} all-to-all(bf16[8,128,512]{2,1,0:T(8,128)(2,1)} %bitcast.214), channel_id=1, replica_groups=mesh['dp'=4,'expert'=8] {'expert'}, dimensions={0} | all-to-all | bytes 2097152 | tf_op jit(solution)/shard_map/all_to_all | solution.py:524
  442.5 29.9 %all_to_all.83 = bf16[8,128,512]{2,1,0:T(8,128)(2,1)} all-to-all(bf16[8,128,512]{2,1,0:T(8,128)(2,1)S(1)} %bitcast.208), channel_id=1, replica_groups=mesh['dp'=4,'expert'=8] {'expert'}, dimensions={0} | all-to-all | bytes 2097152 | tf_op jit(solution)/shard_map/all_to_all | solution.py:524
  496.4 29.8 %all_to_all.84 = bf16[8,128,512]{2,1,0:T(8,128)(2,1)} all-to-all(bf16[8,128,512]{2,1,0:T(8,128)(2,1)S(1)} %bitcast.206), channel_id=1, replica_groups=mesh['dp'=4,'expert'=8] {'expert'}, dimensions={0} | all-to-all | bytes 2097152 | tf_op jit(solution)/shard_map/all_to_all | solution.py:524
  533.3 23.0 %all-to-all-done.11 = bf16[8,128,512]{2,1,0:T(8,128)(2,1)S(1)} async-done(((bf16[8,128,512]{2,1,0:T(8,128)(2,1)}), bf16[8,128,512]{2,1,0:T(8,128)(2,1)S(1)}, u32[]{:S(2)}, u32[]{:S(2)}) %all-to-all-start.11) | async-done | bytes 1048608 | tf_op jit(solution)/shard_map/all_to_all | solution.py:524
  557.2 39.2 %shard_map.337 = (f32[4,197,512]{2,1,0:T(8,128)}, bf16[512,2304]{1,0:T(8,128)(2,1)}, bf16[4,197,128]{2,1,0:T(8,128)(2,1)}, bf16[1024,512]{1,0:T(8,128)(2,1)}, bf16[1024,512]{1,0:T(8,128)(2,1)}) custom-call(f32[4,197,512]{2,1,0:T(8,128)} %copy.357.cotangent.upstream, f32[4,197,512]{2,1,0:T(8,128)} %get-tuple-element.127.rows, ...), custom_call_target="tpu_custom_call" | custom-call | flops 9915334656 | bytes 29954688 | tf_op jit(solution)/shard_map/pallas_call | solution.py:310
  596.5 30.8 %all_to_all.85 = bf16[8,128,512]{2,1,0:T(8,128)(2,1)} all-to-all(bf16[8,128,512]{2,1,0:T(8,128)(2,1)} %bitcast.211), channel_id=1, replica_groups=mesh['dp'=4,'expert'=8] {'expert'}, dimensions={0} | all-to-all | bytes 2097152 | tf_op jit(solution)/shard_map/all_to_all | solution.py:524
  631.9 12.8 %shard_map.338 = (bf16[1024,2048]{1,0:T(8,128)(2,1)}, bf16[1024,512]{1,0:T(8,128)(2,1)}) custom-call(bf16[1024,512]{1,0:T(8,128)(2,1)} %bitcast.189, bf16[1024,2048]{1,0:T(8,128)(2,1)} %get-tuple-element.166.s_ref, bf16[4,2,1024,512]{3,2,1,0:T(8,128)(2,1)} %all-gather.7.cloned.1.call-done.w1_ref.w2_ref, ...), custom_call_target="tpu_custom_call" | custom-call | flops 4294967296 | bytes 27262976 | tf_op jit(solution)/shard_map/pallas_call | solution.py:310
  644.7 12.9 %all-to-all-done.14 = bf16[8,128,512]{2,1,0:T(8,128)(2,1)S(1)} async-done(((bf16[8,128,512]{2,1,0:T(8,128)(2,1)}), bf16[8,128,512]{2,1,0:T(8,128)(2,1)S(1)}, u32[]{:S(2)}, u32[]{:S(2)}) %all-to-all-start.14) | async-done | bytes 1048608 | tf_op jit(solution)/shard_map/all_to_all | solution.py:524
  671.3 12.8 %shard_map.340 = (bf16[1024,2048]{1,0:T(8,128)(2,1)}, bf16[1024,512]{1,0:T(8,128)(2,1)}) custom-call(bf16[1024,512]{1,0:T(8,128)(2,1)} %bitcast.187, bf16[1024,2048]{1,0:T(8,128)(2,1)} %get-tuple-element.177.s_ref, bf16[4,2,1024,512]{3,2,1,0:T(8,128)(2,1)} %all-gather.7.cloned.1.call-done.w1_ref.w2_ref, ...), custom_call_target="tpu_custom_call" | custom-call | flops 4294967296 | bytes 27262976 | tf_op jit(solution)/shard_map/pallas_call | solution.py:310
  718.7 27.5 %shard_map.342 = (f32[4,197,512]{2,1,0:T(8,128)}, bf16[512,2304]{1,0:T(8,128)(2,1)}) custom-call(f32[4,197,512]{2,1,0:T(8,128)} %get-tuple-element.157.upstream, f32[4,197,512]{2,1,0:T(8,128)} %copy.328.rows, f32[4,197,512]{2,1,0:T(8,128)} %get-tuple-element.106.middle, bf16[4,197,512]{2,1,0:T(8,128)(2,1)} %get-tuple-element.158.q_ref, ...), custom_call_target="tpu_custom_call" | custom-call | flops 9915334656 | bytes 26023072 | tf_op jit(solution)/shard_map/pallas_call | solution.py:310
  746.3 35.4 %reduce-scatter.15.cloned.1.call-done = bf16[128,2304]{1,0:T(8,128)(2,1)} async-done(((bf16[512,2304]{1,0:T(8,128)(2,1)}), bf16[128,2304]{1,0:T(8,128)(2,1)}) %reduce-scatter.15.cloned.1.call-update) | async-done | bytes 589840 | tf_op jit(solution)/shard_map/reduce_scatter | solution.py:683
  789.6 54.3 %all-reduce.7.cloned.1.call-done = (bf16[1,128,2304]{2,1,0:T(8,128)(2,1)}, bf16[1,128,2304]{2,1,0:T(8,128)(2,1)}) async-done(((bf16[1,128,2304]{2,1,0:T(8,128)(2,1)}, bf16[1,128,2304]{2,1,0:T(8,128)(2,1)}), (bf16[1,128,2304]{2,1,0:T(8,128)(2,1)}, bf16[1,128,2304]{2,1,0:T(8,128)(2,1)})) %all-reduce.7.cloned.1.call-update) | async-done | bytes 1179664 | tf_op jit(solution)/shard_map/psum | solution.py:684
  851.8 47.2 %reduce-scatter.25.cloned.1.call-done = bf16[1,1024,512]{2,1,0:T(8,128)(2,1)} async-done(((bf16[4,1024,512]{2,1,0:T(8,128)(2,1)}), bf16[1,1024,512]{2,1,0:T(8,128)(2,1)}) %reduce-scatter.25.cloned.1.call-update) | async-done | bytes 1048592
  899.0 56.0 %reduce-scatter.23.cloned.1.call-done = bf16[1,1024,512]{2,1,0:T(8,128)(2,1)} async-done(((bf16[4,1024,512]{2,1,0:T(8,128)(2,1)}), bf16[1,1024,512]{2,1,0:T(8,128)(2,1)}) %reduce-scatter.23.cloned.1.call-update) | async-done | bytes 1048592
  (284 shorter events, 290.2 us)
Async XLA Ops:
  7.3 48.6 %all-gather.5.cloned.1.call-start = ((), (), s32[]{:S(2)}) async-start(), calls=%async_computation.22 | async-start | bytes 2785280 | tf_op jit(solution)/shard_map/all_gather | solution.py:563
  16.7 129.4 %all-gather.7.cloned.1.call-start = ((), (), s32[]{:S(2)}) async-start(), calls=%async_computation.23 | async-start | bytes 10485760 | tf_op jit(solution)/shard_map/all_gather | solution.py:566
  25.7 194.2 %all-gather.9.cloned.1.call-start = ((), (), s32[]{:S(2)}) async-start(), calls=%async_computation.24 | async-start | bytes 2785280 | tf_op jit(solution)/shard_map/all_gather | solution.py:563
  27.8 254.6 %all-gather.11.cloned.1.call-start = ((), (), s32[]{:S(2)}) async-start(), calls=%async_computation.25 | async-start | bytes 10485760 | tf_op jit(solution)/shard_map/all_gather | solution.py:566
  107.8 50.6 %all-to-all-start.2 = ((bf16[8,128,512]{2,1,0:T(8,128)(2,1)}), bf16[8,128,512]{2,1,0:T(8,128)(2,1)S(1)}, u32[]{:S(2)}, u32[]{:S(2)}) async-start(bf16[8,128,512]{2,1,0:T(8,128)(2,1)} %bitcast.207), calls=%async_computation.2 | async-start | bytes 2097152 | tf_op jit(solution)/shard_map/all_to_all | solution.py:524
  158.4 31.4 %all-to-all-start.1 = ((bf16[8,128,512]{2,1,0:T(8,128)(2,1)}), bf16[8,128,512]{2,1,0:T(8,128)(2,1)S(1)}, u32[]{:S(2)}, u32[]{:S(2)}) async-start(bf16[8,128,512]{2,1,0:T(8,128)(2,1)} %bitcast.182), calls=%async_computation.1 | async-start | bytes 2097152 | tf_op jit(solution)/shard_map/all_to_all | solution.py:524
  189.8 30.1 %all-to-all-start.3 = ((bf16[8,128,512]{2,1,0:T(8,128)(2,1)}), bf16[8,128,512]{2,1,0:T(8,128)(2,1)S(1)}, u32[]{:S(2)}, u32[]{:S(2)}) async-start(bf16[8,128,512]{2,1,0:T(8,128)(2,1)} %bitcast.180), calls=%async_computation.3 | async-start | bytes 2097152 | tf_op jit(solution)/shard_map/all_to_all | solution.py:524
  277.6 30.1 %all-to-all-start.6 = ((bf16[8,128,512]{2,1,0:T(8,128)(2,1)}), bf16[8,128,512]{2,1,0:T(8,128)(2,1)S(1)}, u32[]{:S(2)}, u32[]{:S(2)}) async-start(bf16[8,128,512]{2,1,0:T(8,128)(2,1)} %bitcast.210), calls=%async_computation.6 | async-start | bytes 2097152 | tf_op jit(solution)/shard_map/all_to_all | solution.py:524
  307.7 30.5 %all-to-all-start.5 = ((bf16[8,128,512]{2,1,0:T(8,128)(2,1)}), bf16[8,128,512]{2,1,0:T(8,128)(2,1)S(1)}, u32[]{:S(2)}, u32[]{:S(2)}) async-start(bf16[8,128,512]{2,1,0:T(8,128)(2,1)} %bitcast.183), calls=%async_computation.5 | async-start | bytes 2097152 | tf_op jit(solution)/shard_map/all_to_all | solution.py:524
  338.2 30.9 %all-to-all-start.7 = ((bf16[8,128,512]{2,1,0:T(8,128)(2,1)}), bf16[8,128,512]{2,1,0:T(8,128)(2,1)}, u32[]{:S(2)}, u32[]{:S(2)}) async-start(bf16[8,128,512]{2,1,0:T(8,128)(2,1)} %bitcast.181), calls=%async_computation.7 | async-start | bytes 2097152 | tf_op jit(solution)/shard_map/all_to_all | solution.py:524
  342.5 289.4 %reduce-scatter.19.cloned.1.call-start = ((), (), s32[]{:S(2)}) async-start(), calls=%async_computation.28 | async-start | bytes 5242880
  441.3 230.0 %reduce-scatter.21.cloned.1.call-start = ((), (), s32[]{:S(2)}) async-start(), calls=%async_computation.29 | async-start | bytes 5242880
  495.2 35.3 %copy-start.35 = (f32[1,2048]{1,0:T(1,128)S(1)}, f32[1,2048]{1,0:T(1,128)}, u32[]{:S(2)}) copy-start(f32[1,2048]{1,0:T(1,128)} %get-tuple-element.150) | copy-start | bytes 24580
  496.4 35.1 %copy-start.36 = (f32[1,512]{1,0:T(1,128)S(1)}, f32[1,512]{1,0:T(1,128)}, u32[]{:S(2)}) copy-start(f32[1,512]{1,0:T(1,128)} %get-tuple-element.147) | copy-start | bytes 6148
  496.4 35.3 %copy-start.33 = (f32[1,2048]{1,0:T(1,128)S(1)}, f32[1,2048]{1,0:T(1,128)}, u32[]{:S(2)}) copy-start(f32[1,2048]{1,0:T(1,128)} %get-tuple-element.146) | copy-start | bytes 24580
  526.2 30.1 %all-to-all-start.11 = ((bf16[8,128,512]{2,1,0:T(8,128)(2,1)}), bf16[8,128,512]{2,1,0:T(8,128)(2,1)S(1)}, u32[]{:S(2)}, u32[]{:S(2)}) async-start(bf16[8,128,512]{2,1,0:T(8,128)(2,1)} %bitcast.64), calls=%async_computation.11 | async-start | bytes 2097152 | tf_op jit(solution)/shard_map/all_to_all | solution.py:524
  627.3 30.3 %all-to-all-start.14 = ((bf16[8,128,512]{2,1,0:T(8,128)(2,1)}), bf16[8,128,512]{2,1,0:T(8,128)(2,1)S(1)}, u32[]{:S(2)}, u32[]{:S(2)}) async-start(bf16[8,128,512]{2,1,0:T(8,128)(2,1)} %bitcast.203), calls=%async_computation.14 | async-start | bytes 2097152 | tf_op jit(solution)/shard_map/all_to_all | solution.py:524
  631.1 115.2 %reduce-scatter.17.cloned.1.call-start = ((), (), s32[]{:S(2)}) async-start(), calls=%async_computation.27 | async-start | bytes 2949120 | tf_op jit(solution)/shard_map/reduce_scatter | solution.py:683
  657.6 30.1 %all-to-all-start.13 = ((bf16[8,128,512]{2,1,0:T(8,128)(2,1)}), bf16[8,128,512]{2,1,0:T(8,128)(2,1)S(1)}, u32[]{:S(2)}, u32[]{:S(2)}) async-start(bf16[8,128,512]{2,1,0:T(8,128)(2,1)} %bitcast.209), calls=%async_computation.13 | async-start | bytes 2097152 | tf_op jit(solution)/shard_map/all_to_all | solution.py:524
  687.7 30.1 %all-to-all-start.15 = ((bf16[8,128,512]{2,1,0:T(8,128)(2,1)}), bf16[8,128,512]{2,1,0:T(8,128)(2,1)S(1)}, u32[]{:S(2)}, u32[]{:S(2)}) async-start(bf16[8,128,512]{2,1,0:T(8,128)(2,1)} %bitcast.204), calls=%async_computation.15 | async-start | bytes 2097152 | tf_op jit(solution)/shard_map/all_to_all | solution.py:524
  691.2 90.5 %reduce-scatter.15.cloned.1.call-start = ((), (), s32[]{:S(2)}) async-start(), calls=%async_computation.26 | async-start | bytes 2949120 | tf_op jit(solution)/shard_map/reduce_scatter | solution.py:683
  746.3 97.7 %all-reduce.7.cloned.1.call-start = ((), (), s32[]{:S(2)}) async-start(), calls=%async_computation.32 | async-start | bytes 2359296 | tf_op jit(solution)/shard_map/psum | solution.py:684
  781.7 117.3 %reduce-scatter.25.cloned.1.call-start = ((), (), s32[]{:S(2)}) async-start(), calls=%async_computation.31 | async-start | bytes 5242880
  782.3 172.6 %reduce-scatter.23.cloned.1.call-start = ((), (), s32[]{:S(2)}) async-start(), calls=%async_computation.30 | async-start | bytes 5242880
  (47 other events, 275.5 us)
Sparse Core Ops, SparseCore 0:
  16.8 39.1 all-gather.4
  58.3 87.6 all-gather.6
  147.9 36.4 all-gather.8
  186.6 87.5 all-gather.10
  441.4 50.6 reduce-scatter.18
  495.8 52.6 reduce-scatter.20
  635.0 37.8 reduce-scatter.16
  746.4 35.2 reduce-scatter.14
  784.1 59.7 all-reduce.6
  847.3 51.6 reduce-scatter.24
  902.2 52.6 reduce-scatter.22

commit v3 on v2

--- a/solution.py
+++ b/solution.py
@@ -181,26 +181,26 @@
 
 
 def next_kernel(
-    middle, gates, dcol, back_a, back_b, routes, drow, wq, wk, wv, wo, misc, rows_ref, yzero, yone, *outs
+    middle, gates, dcol, back, routes, drow, wq, wk, wv, wo, misc, rows_ref, yzero, yone, *outs
 ):
-    rows, _, _ = combine_body(middle[0], gates, dcol, (back_a, back_b), yzero, yone)
+    rows, _, _ = combine_body(middle[0], gates, dcol, (back,), yzero, yone)
     rows_ref[0] = rows
     attend_body(rows, routes, drow, wq, wk, wv, wo, misc, *outs[:7], outs[7:])
 
 
-def turn_kernel(middle, gates, dcol, back_a, back_b, cotangent, routes, drow, result, dz, out_a, out_b):
-    rows, zero, one = combine_body(middle[0], gates, dcol, (back_a, back_b), None, None)
+def turn_kernel(middle, gates, dcol, back, cotangent, routes, drow, result, dz, out):
+    rows, zero, one = combine_body(middle[0], gates, dcol, (back,), None, None)
     result[0] = rows
-    grads_body(cotangent[0], zero, one, gates, routes, drow, dz, (out_a, out_b))
+    grads_body(cotangent[0], zero, one, gates, routes, drow, dz, (out,))
 
 
 def back_kernel(
-    upstream, rows, middle, q_ref, k_ref, v_ref, o_ref, lse_ref, dz_ref, dcol, came_a, came_b,
+    upstream, rows, middle, q_ref, k_ref, v_ref, o_ref, lse_ref, dz_ref, dcol, came,
     wq, wk, wv, wo, misc, *rest,
 ):
     bias, *rest = rest
     if len(rest) > 4:
-        yzero, yone, gates_below, routes_below, drow_below, grad_ref, sent, dz_below, out_a, out_b, wgrad, vgrad = rest
+        yzero, yone, gates_below, routes_below, drow_below, grad_ref, sent, dz_below, out, wgrad, vgrad = rest
     else:
         grad_ref, sent, wgrad, vgrad = rest
     first = pl.program_id(0) == 0
@@ -221,11 +221,9 @@
     dz = dz_ref[0]
     dest = dcol[0]
     dhidden = dot_nt(dz, misc[...])
-    for number, came in enumerate((came_a, came_b)):
-        count = came.shape[0]
-        lanes = lax.broadcasted_iota(jnp.int32, (length, count), 1) + number * count
-        hit = (dest[:, 0:1] == lanes) | (dest[:, 1:2] == lanes)
-        dhidden = dhidden + dot(hit.astype(F32).astype(BF16), came[...])
+    lanes = lax.broadcasted_iota(jnp.int32, (length, came.shape[0]), 1)
+    hit = (dest[:, 0:1] == lanes) | (dest[:, 1:2] == lanes)
+    dhidden = dhidden + dot(hit.astype(F32).astype(BF16), came[...])
     wgrad[:, 4 * width :] += dot_tn(hidden, dz)
     add_vector(5, dhidden * unit_two)
     add_vector(6, dhidden)
@@ -279,7 +277,7 @@
     if len(rest) > 4:
         grads_body(
             grad, yzero[0].astype(F32), yone[0].astype(F32), gates_below, routes_below, drow_below, dz_below,
-            (out_a, out_b),
+            (out,),
         )
 
     @pl.when(pl.program_id(0) == pl.num_programs(0) - 1)
@@ -324,11 +322,11 @@
     return (shape, kind, pl.BlockSpec((1, length, columns), lambda i: (i, 0, 0)))
 
 
-def slots_out(half, width):
-    return [((half, width), BF16, pl.BlockSpec((half, width), lambda i: (0, 0)))] * 2
-
-
-def attend_outputs(images, length, width, half):
+def slots_out(slots, width):
+    return [((slots, width), BF16, pl.BlockSpec((slots, width), lambda i: (0, 0)))]
+
+
+def attend_outputs(images, length, width, slots):
     return [
         images_out(images, length, width, F32),
         images_out(images, length, width, BF16),
@@ -337,168 +335,342 @@
         images_out(images, length, width, BF16),
         images_out(images, length, MISC, F32),
         images_out(images, length, 2, F32),
-    ] + slots_out(half, width)
-
-
-def gelu(value):
-    return 0.5 * value * (1.0 + lax.erf(value * 0.7071067811865476))
-
-
-def block_of(ref):
-    return ref[...].reshape(-1, ref.shape[-1])
-
-
-def expert_kernel(x_ref, w1_ref, b1_ref, w2_ref, b2_ref, y_ref, acc):
-    step = pl.program_id(0)
-    w1, w2 = block_of(w1_ref), block_of(w2_ref)
-    rows = x_ref.shape[0]
-    chunk = 256
-    for start in range(0, rows, chunk):
-        part = slice(start, start + chunk)
-        inner = dot(x_ref[part, :], w1) + b1_ref[0]
-        term = dot(gelu(inner).astype(BF16), w2)
-
-        @pl.when(step == 0)
-        def _(part=part, term=term):
-            acc[part, :] = term + b2_ref[0]
-
-        @pl.when(step > 0)
-        def _(part=part, term=term):
-            acc[part, :] += term
-
-    @pl.when(step == pl.num_programs(0) - 1)
-    def _():
-        y_ref[...] = acc[...].astype(BF16)
-
-
-def slope_kernel(x_ref, w1_ref, b1_ref, g_ref, s_ref):
-    rows = x_ref.shape[0]
-    w1 = block_of(w1_ref)
-    chunk = 256
-    for start in range(0, rows, chunk):
-        part = slice(start, start + chunk)
-        inner = dot(x_ref[part, :], w1) + b1_ref[0]
-        normal = 0.5 * (1.0 + lax.erf(inner * 0.7071067811865476))
-        g_ref[part, :] = (inner * normal).astype(BF16)
-        s_ref[part, :] = (normal + inner * (jnp.exp(-0.5 * inner * inner) * 0.3989422804014327)).astype(BF16)
-
-
-def expert_back_kernel(dy_ref, s_ref, w1_ref, w2_ref, du_ref, dx_ref, acc):
-    step = pl.program_id(0)
-    w1, w2 = block_of(w1_ref), block_of(w2_ref)
-    rows = dy_ref.shape[0]
-    chunk = 256
-    for start in range(0, rows, chunk):
-        part = slice(start, start + chunk)
-        dg = dot_nt(dy_ref[part, :], w2)
-        du = (dg * s_ref[part, :].astype(F32)).astype(BF16)
-        du_ref[part, :] = du
-        term = dot_nt(du, w1)
-
-        @pl.when(step == 0)
-        def _(part=part, term=term):
-            acc[part, :] = term
-
-        @pl.when(step > 0)
-        def _(part=part, term=term):
-            acc[part, :] += term
-
-    @pl.when(step == pl.num_programs(0) - 1)
-    def _():
-        dx_ref[...] = acc[...].astype(BF16)
-
-
-def expert_weight_kernel(x_ref, g_ref, du_ref, dy_ref, out_ref, db1_ref, db2_ref):
-    step = pl.program_id(0)
-    parts, rows, _ = out_ref.shape
-    width = x_ref.shape[1]
-    share = width // parts
-    dw1 = dot_tn(x_ref[...], du_ref[...]).astype(BF16)
-    place = pl.ds(pl.multiple_of(step * share, share), share)
-    for part in range(parts):
-        out_ref[part, place, :] = dw1[part * share : (part + 1) * share, :]
-    dw2 = dot_tn(g_ref[...], dy_ref[...]).astype(BF16)
-    take = rows // 2
+    ] + slots_out(slots, width)
+
+
+ROOT_HALF = 0.7071067811865476
+ROOT_TWO_PI_INVERSE = 0.3989422804014327
+MESH = pl.DeviceIdType.MESH
+
+
+def order_of(count):
+    return sorted(range(1, count), key=lambda k: -min(k, count - k))
+
+
+class Swap:
+    def __init__(self, sent, arrived, made, back, sems):
+        self.sent, self.arrived, self.made, self.back = sent, arrived, made, back
+        self.out_send, self.out_recv, self.home_send, self.home_recv, self.own = sems
+        self.local, self.count = arrived.shape[0], arrived.shape[1]
+        self.me = lax.axis_index("expert")
+
+    def greet(self):
+        barrier = pltpu.get_barrier_semaphore()
+        for k in range(1, self.count):
+            peer = lax.rem(self.me + k, self.count)
+            pl.semaphore_signal(barrier, inc=1, device_id={"expert": peer}, device_id_type=MESH)
+        pl.semaphore_wait(barrier, self.count - 1)
+
+    def outward(self, j, k, peer):
+        return pltpu.make_async_remote_copy(
+            src_ref=self.sent.at[j, peer], dst_ref=self.arrived.at[j, self.me],
+            send_sem=self.out_send.at[j, k], recv_sem=self.out_recv.at[j, k],
+            device_id={"expert": peer}, device_id_type=MESH,
+        )
+
+    def homeward(self, j, k, peer):
+        return pltpu.make_async_remote_copy(
+            src_ref=self.made.at[j, peer], dst_ref=self.back.at[j, self.me],
+            send_sem=self.home_send.at[j, k], recv_sem=self.home_recv.at[j, k],
+            device_id={"expert": peer}, device_id_type=MESH,
+        )
+
+    def own_out(self, j):
+        return pltpu.make_async_copy(self.sent.at[j, self.me], self.arrived.at[j, self.me], self.own.at[j])
+
+    def own_home(self, j):
+        return pltpu.make_async_copy(self.made.at[j, self.me], self.back.at[j, self.me], self.own.at[self.local + j])
+
+    def send_all(self):
+        for j in range(self.local):
+            for k in order_of(self.count):
+                self.outward(j, k, lax.rem(self.me + k, self.count)).start()
+            self.own_out(j).start()
+
+    def chip(self, turn):
+        chips = self.count // 2
+        return lax.rem(self.me // 2 - turn + chips, chips)
+
+    def wait_chip(self, j, chip):
+        for core in range(2):
+            source = 2 * chip + core
+            k = lax.rem(self.me - source + self.count, self.count)
+
+            @pl.when(source != self.me)
+            def _(k=k, source=source):
+                pltpu.make_async_remote_copy(
+                    src_ref=self.arrived.at[j, source], dst_ref=self.arrived.at[j, source],
+                    send_sem=self.out_send.at[j, k], recv_sem=self.out_recv.at[j, k],
+                    device_id={"expert": source}, device_id_type=MESH,
+                ).wait_recv()
+
+            @pl.when(source == self.me)
+            def _():
+                self.own_out(j).wait()
+
+    def send_home(self, j, chip):
+        for core in range(2):
+            peer = 2 * chip + core
+            k = lax.rem(peer - self.me + self.count, self.count)
+
+            @pl.when(peer != self.me)
+            def _(k=k, peer=peer):
+                self.homeward(j, k, peer).start()
+
+            @pl.when(peer == self.me)
+            def _():
+                self.own_home(j).start()
+
+    def finish(self):
+        for j in range(self.local):
+            self.own_home(j).wait()
+            for k in range(1, self.count):
+                peer = lax.rem(self.me + k, self.count)
+                self.outward(j, k, peer).wait_send()
+                self.homeward(j, k, peer).wait()
+
+
+def weight_blocks(weights, j, f):
+    _, parts, rows, width = weights.shape
+    share, take = width // parts, rows // 2
     each = FF_BLOCK // take
-    for part in range(each):
-        out_ref[step * each + part, take:, :] = dw2[part * take : (part + 1) * take, :]
-    db1_ref[...] = jnp.sum(du_ref[...].astype(F32), axis=0, keepdims=True)
-
-    @pl.when(step == 0)
-    def _():
-        db2_ref[...] = jnp.sum(dy_ref[...].astype(F32), axis=0, keepdims=True)
-
-
-def inner_specs(packed, j):
-    parts, _, rows, width = packed.shape
-    share, take = width // parts, rows // 2
-    return (
-        pl.BlockSpec((parts, 1, share, width), lambda f: (0, j, f, 0)),
-        pl.BlockSpec((1, 1, FF_BLOCK), lambda f: (j, 0, f)),
-        pl.BlockSpec((FF_BLOCK // take, 1, take, width), lambda f: (f, j, 1, 0)),
-        pl.BlockSpec((1, 1, width), lambda f: (j, 0, 0)),
+    first = weights[j, :, f * share : (f + 1) * share, :].reshape(width, width)
+    second = weights[j, f * each : (f + 1) * each, take:, :].reshape(FF_BLOCK, width)
+    return first, second
+
+
+def expert_kernel(
+    sent, packed, b1, b2, back, arrived_out, g_out, s_out,
+    arrived, made, weights, g_stage, s_stage, out_send, out_recv, home_send, home_recv, own, load, stores, last,
+):
+    swap = Swap(sent, arrived, made, back, (out_send, out_recv, home_send, home_recv, own))
+    local, count, capacity, width = arrived.shape
+    chips = count // 2
+    rows = 2 * capacity
+    ff = g_out.shape[2]
+    loads = [pltpu.make_async_copy(packed.at[:, j], weights.at[j], load.at[j]) for j in range(local)]
+    for copy in loads:
+        copy.start()
+    swap.greet()
+    swap.send_all()
+
+    def kept(j, slot, chip):
+        place = pl.ds(pl.multiple_of(chip * rows, rows), rows)
+        return (
+            pltpu.make_async_copy(g_stage.at[slot], g_out.at[j, place, :], stores.at[0, slot]),
+            pltpu.make_async_copy(s_stage.at[slot], s_out.at[j, place, :], stores.at[1, slot]),
+        )
+
+    for j in range(local):
+        loads[j].wait()
+
+        def chip_step(turn, carry, j=j):
+            chip = swap.chip(turn)
+            slot = lax.rem(turn, 2)
+            swap.wait_chip(j, chip)
+
+            @pl.when(j * chips + turn >= 2)
+            def _():
+                for copy in kept(j, slot, chip):
+                    copy.wait()
+
+            x = arrived[j, pl.ds(2 * chip, 2)].reshape(rows, width)
+            total = jnp.broadcast_to(b2[j], (rows, width))
+            for f in range(ff // FF_BLOCK):
+                cols = slice(f * FF_BLOCK, (f + 1) * FF_BLOCK)
+                first, second = weight_blocks(weights, j, f)
+                inner = dot(x, first) + b1[j, :, cols]
+                normal = 0.5 * (1.0 + lax.erf(inner * ROOT_HALF))
+                g = (inner * normal).astype(BF16)
+                density = jnp.exp(-0.5 * inner * inner) * ROOT_TWO_PI_INVERSE
+                g_stage[slot, :, cols] = g
+                s_stage[slot, :, cols] = (normal + inner * density).astype(BF16)
+                total = total + dot(g, second)
+            made[j, pl.ds(2 * chip, 2)] = total.astype(BF16).reshape(2, capacity, width)
+            swap.send_home(j, chip)
+            for copy in kept(j, slot, chip):
+                copy.start()
+            return carry
+
+        lax.fori_loop(0, chips, chip_step, 0)
+    final = pltpu.make_async_copy(arrived, arrived_out, last)
+    final.start()
+    for slot in range(2):
+        for copy in kept(0, slot, 0):
+            copy.wait()
+    swap.finish()
+    final.wait()
+
+
+def expert_back_kernel(
+    sent, packed, arrived_x, g_in, s_in, back, out, db1, db2,
+    arrived, made, weights, x, du, s_stage, g_stage, first_stage, second_stage,
+    out_send, out_recv, home_send, home_recv, own, load, fetch, stores,
+):
+    swap = Swap(sent, arrived, made, back, (out_send, out_recv, home_send, home_recv, own))
+    local, count, capacity, width = arrived.shape
+    chips = count // 2
+    rows = 2 * capacity
+    ff = g_in.shape[2]
+    blocks = ff // FF_BLOCK
+    _, parts, all_rows, _ = weights.shape
+    share, take = width // parts, all_rows // 2
+    each = FF_BLOCK // take
+    loads = [pltpu.make_async_copy(packed.at[:, j], weights.at[j], load.at[j]) for j in range(local)]
+    loads.append(pltpu.make_async_copy(arrived_x, x, load.at[local]))
+    for copy in loads:
+        copy.start()
+
+    def slopes(j, turn):
+        slot = lax.rem(turn, 2)
+        place = pl.ds(pl.multiple_of(swap.chip(turn) * rows, rows), rows)
+        return pltpu.make_async_copy(s_in.at[j, place, :], s_stage.at[slot], fetch.at[0, slot])
+
+    def activations(j, f):
+        return pltpu.make_async_copy(
+            g_in.at[j, :, f * FF_BLOCK : (f + 1) * FF_BLOCK], g_stage.at[f % 2], fetch.at[1, f % 2]
+        )
+
+    def results(j, f):
+        return (
+            pltpu.make_async_copy(
+                first_stage.at[f % 2], out.at[:, j, f * share : (f + 1) * share, :], stores.at[0, f % 2]
+            ),
+            pltpu.make_async_copy(
+                second_stage.at[f % 2], out.at[f * each : (f + 1) * each, j, take:, :], stores.at[1, f % 2]
+            ),
+        )
+
+    slopes(0, 0).start()
+    swap.greet()
+    swap.send_all()
+    for j in range(local):
+        loads[j].wait()
+        activations(j, 0).start()
+
+        def chip_step(turn, carry, j=j):
+            chip = swap.chip(turn)
+            slot = lax.rem(turn, 2)
+
+            @pl.when(turn + 1 < chips)
+            def _():
+                slopes(j, turn + 1).start()
+
+            swap.wait_chip(j, chip)
+            slopes(j, turn).wait()
+            dy = arrived[j, pl.ds(2 * chip, 2)].reshape(rows, width)
+            place = pl.ds(pl.multiple_of(chip * rows, rows), rows)
+            total = jnp.zeros((rows, width), F32)
+            for f in range(blocks):
+                cols = slice(f * FF_BLOCK, (f + 1) * FF_BLOCK)
+                first, second = weight_blocks(weights, j, f)
+                part = (dot_nt(dy, second) * s_stage[slot, :, cols].astype(F32)).astype(BF16)
+                du[place, cols] = part
+                total = total + dot_nt(part, first)
+            made[j, pl.ds(2 * chip, 2)] = total.astype(BF16).reshape(2, capacity, width)
+            swap.send_home(j, chip)
+            return carry
+
+        lax.fori_loop(0, chips, chip_step, 0)
+        if j + 1 < local:
+            slopes(j + 1, 0).start()
+        if j == 0:
+            loads[local].wait()
+        dy = arrived[j].reshape(count * capacity, width)
+        db2[j] = jnp.sum(dy.astype(F32), axis=0, keepdims=True)
+        for f in range(blocks):
+            cols = slice(f * FF_BLOCK, (f + 1) * FF_BLOCK)
+            if f + 1 < blocks:
+                activations(j, f + 1).start()
+            if j > 0 or f > 1:
+                for copy in results(j, f):
+                    copy.wait()
+            part = du[:, cols]
+            grad = dot_tn(x[j].reshape(count * capacity, width), part).astype(BF16)
+            first_stage[f % 2] = grad.reshape(parts, share, width)
+            db1[j, :, cols] = jnp.sum(part.astype(F32), axis=0, keepdims=True)
+            activations(j, f).wait()
+            grad = dot_tn(g_stage[f % 2], dy).astype(BF16)
+            second_stage[f % 2] = grad.reshape(each, take, width)
+            for copy in results(j, f):
+                copy.start()
+    for f in range(2):
+        for copy in results(0, f):
+            copy.wait()
+    swap.finish()
+
+
+def swap_sems(local, count):
+    pairs = [pltpu.SemaphoreType.DMA((local, count))] * 4
+    return pairs + [pltpu.SemaphoreType.DMA((2 * local,))]
+
+
+def expert_call(body, inputs, outputs, scratch, number, flops):
+    def spec(held):
+        return pl.BlockSpec(memory_space=pltpu.VMEM if held else pl.ANY)
+
+    shapes = [jax.ShapeDtypeStruct(s, t) for s, t, _ in outputs]
+    moved = sum(a.size * a.dtype.itemsize for a, _ in inputs) + sum(s.size * s.dtype.itemsize for s in shapes)
+    return pl.pallas_call(
+        body,
+        in_specs=[spec(held) for _, held in inputs],
+        out_specs=[spec(held) for _, _, held in outputs],
+        out_shape=shapes,
+        scratch_shapes=scratch,
+        compiler_params=pltpu.CompilerParams(
+            collective_id=number, has_side_effects=True, vmem_limit_bytes=VMEM
+        ),
+        cost_estimate=pl.CostEstimate(flops=flops, bytes_accessed=moved, transcendentals=0),
+    )(*[a for a, _ in inputs])
+
+
+def expert_forward(sent, expert, number):
+    packed, b1, b2 = expert
+    local, count, capacity, width = sent.shape
+    ff = b1.shape[2]
+    rows = 2 * capacity
+    slots = (local, count * capacity, ff)
+    return expert_call(
+        expert_kernel,
+        [(sent, False), (packed, False), (b1, True), (b2, True)],
+        [(sent.shape, BF16, False), (sent.shape, BF16, False), (slots, BF16, False), (slots, BF16, False)],
+        [
+            pltpu.VMEM(sent.shape, BF16), pltpu.VMEM(sent.shape, BF16),
+            pltpu.VMEM((local, packed.shape[0], *packed.shape[2:]), BF16),
+            pltpu.VMEM((2, rows, ff), BF16), pltpu.VMEM((2, rows, ff), BF16),
+        ] + swap_sems(local, count) + [
+            pltpu.SemaphoreType.DMA((local,)), pltpu.SemaphoreType.DMA((2, 2)), pltpu.SemaphoreType.DMA,
+        ],
+        number,
+        4 * local * count * capacity * width * ff,
     )
 
 
-def columns_of(rows, ff):
-    return ((rows, ff), BF16, pl.BlockSpec((rows, FF_BLOCK), lambda f: (0, f)))
-
-
-def expert_forward(x, expert, j):
+def expert_backward(sent, expert, arrived, g, s, number):
     packed, b1, b2 = expert
-    rows, width = x.shape
+    local, count, capacity, width = sent.shape
     ff = b1.shape[2]
-    i1, i2, i3, i4 = inner_specs(packed, j)
-    return call(
-        expert_kernel, (ff // FF_BLOCK,),
-        [(x, whole(x)), (packed, i1), (b1, i2), (packed, i3), (b2, i4)],
-        [((rows, width), BF16, pl.BlockSpec((rows, width), lambda f: (0, 0)))],
-        [pltpu.VMEM((rows, width), F32)],
-        flops=4 * rows * width * ff,
-    )[0]
-
-
-def expert_slopes(x, expert, j):
-    packed, b1, b2 = expert
-    rows, width = x.shape
-    ff = b1.shape[2]
-    i1, i2, _, _ = inner_specs(packed, j)
-    return call(
-        slope_kernel, (ff // FF_BLOCK,), [(x, whole(x)), (packed, i1), (b1, i2)],
-        [columns_of(rows, ff), columns_of(rows, ff)],
-        flops=2 * rows * width * ff,
-    )
-
-
-def expert_backward(dy, slopes, expert, j):
-    packed, b1, b2 = expert
-    rows, width = dy.shape
-    ff = b1.shape[2]
-    i1, _, i3, _ = inner_specs(packed, j)
-    by_columns = pl.BlockSpec((rows, FF_BLOCK), lambda f: (0, f))
-    return call(
-        expert_back_kernel, (ff // FF_BLOCK,),
-        [(dy, whole(dy)), (slopes, by_columns), (packed, i1), (packed, i3)],
-        [columns_of(rows, ff), ((rows, width), BF16, pl.BlockSpec((rows, width), lambda f: (0, 0)))],
-        [pltpu.VMEM((rows, width), F32)],
-        flops=4 * rows * width * ff,
-    )
-
-
-def expert_weight_grads(x, g, du, dy, parts):
-    rows, width = x.shape
-    ff = g.shape[1]
-    by_columns = pl.BlockSpec((rows, FF_BLOCK), lambda f: (0, f))
-    packed = (parts, 2 * ff // parts, width)
-    return call(
-        expert_weight_kernel, (ff // FF_BLOCK,),
-        [(x, whole(x)), (g, by_columns), (du, by_columns), (dy, whole(dy))],
+    rows = 2 * capacity
+    parts, _, all_rows, _ = packed.shape
+    share, take = width // parts, all_rows // 2
+    return expert_call(
+        expert_back_kernel,
+        [(sent, False), (packed, False), (arrived, False), (g, False), (s, False)],
         [
-            (packed, BF16, pl.BlockSpec(packed, lambda f: (0, 0, 0))),
-            ((1, ff), F32, pl.BlockSpec((1, FF_BLOCK), lambda f: (0, f))),
-            ((1, width), F32, pl.BlockSpec((1, width), lambda f: (0, 0))),
+            (sent.shape, BF16, False), (packed.shape, BF16, False),
+            (b1.shape, F32, True), (b2.shape, F32, True),
         ],
-        flops=4 * rows * width * ff,
+        [
+            pltpu.VMEM(sent.shape, BF16), pltpu.VMEM(sent.shape, BF16),
+            pltpu.VMEM((local, parts, all_rows, width), BF16), pltpu.VMEM(sent.shape, BF16),
+            pltpu.VMEM((count * capacity, ff), BF16), pltpu.VMEM((2, rows, ff), BF16),
+            pltpu.VMEM((2, count * capacity, FF_BLOCK), BF16), pltpu.VMEM((2, parts, share, width), BF16),
+            pltpu.VMEM((2, FF_BLOCK // take, take, width), BF16),
+        ] + swap_sems(local, count) + [
+            pltpu.SemaphoreType.DMA((local + 1,)), pltpu.SemaphoreType.DMA((2, 2)), pltpu.SemaphoreType.DMA((2, 2)),
+        ],
+        number,
+        8 * local * count * capacity * width * ff,
     )
 
 
@@ -516,15 +688,6 @@
     row = ((pairs % local) * owners + pairs // local) * capacity + slot
     dest = jnp.where(slot < capacity, row, -1)
     return dest.reshape(layers, images, length, 2), capacity
-
-
-def exchange(array):
-    owners = lax.axis_size("expert")
-    rows, width = array.shape
-    swapped = lax.all_to_all(
-        array.reshape(owners, rows // owners, width), "expert", split_axis=0, concat_axis=0, tiled=True
-    )
-    return swapped.reshape(rows, width)
 
 
 def shards(
@@ -572,8 +735,8 @@
 
     dcol, capacity = destinations(routes, experts_all, owners)
     drow = jnp.transpose(dcol, (0, 1, 3, 2))
-    half = owners * capacity
-    dense_flops = 8 * tokens * width * width + 4 * tokens * half * width
+    slots = experts_all * capacity
+    dense_flops = 8 * tokens * width * width + 4 * tokens * slots * width
 
     saved = []
     back = None
@@ -581,7 +744,7 @@
     for layer in range(LAYERS):
         weights = [(packed[layer], s) for s in packed_specs(packed[layer])]
         routing = [(routes[layer], per_image(routes[layer])), (drow[layer], per_image(drow[layer]))]
-        outputs = attend_outputs(count, length, width, half)
+        outputs = attend_outputs(count, length, width, slots)
         if layer == 0:
             done = call(
                 first_kernel, (count,), [(rows, per_image(rows))] + routing + weights, outputs, flops=dense_flops
@@ -595,8 +758,7 @@
                     (before["middle"], per_image(before["middle"])),
                     (before["gates"], per_image(before["gates"])),
                     (dcol[layer - 1], per_image(dcol[layer - 1])),
-                    (back[0], whole(back[0])),
-                    (back[1], whole(back[1])),
+                    (back, whole(back)),
                 ] + routing + weights,
                 [
                     images_out(count, length, width, F32),
@@ -609,23 +771,21 @@
             done = done[3:]
             before["picked"] = picked
         middle, queries, keys, values, context, sums, gates = done[:7]
-        arrived = [exchange(item) for item in done[7:]]
-        produced = [expert_forward(arrived[j], experts[layer], j) for j in range(local)]
-        back = [exchange(item) for item in produced]
-        slopes = [expert_slopes(arrived[j], experts[layer], j) for j in range(local)]
-        back, slopes = lax.optimization_barrier((back, slopes))
+        sent = done[7].reshape(local, owners, capacity, width)
+        back, arrived, g, s = expert_forward(sent, experts[layer], layer)
+        back = back.reshape(slots, width)
         saved.append({
             "rows": rows, "middle": middle, "attend": (queries, keys, values, context, sums), "gates": gates,
-            "arrived": arrived, "slopes": slopes,
+            "experts": (arrived, g, s),
         })
 
     last = saved[-1]
-    result, dz, *sent = call(
+    result, dz, sent = call(
         turn_kernel, (count,),
         [(last["middle"], per_image(last["middle"])), (last["gates"], per_image(last["gates"]))]
-        + [(dcol[-1], per_image(dcol[-1])), (back[0], whole(back[0])), (back[1], whole(back[1]))]
+        + [(dcol[-1], per_image(dcol[-1])), (back, whole(back))]
         + [(cotangent, per_image(cotangent)), (routes[-1], per_image(routes[-1])), (drow[-1], per_image(drow[-1]))],
-        [images_out(count, length, width, F32), images_out(count, length, MISC, BF16)] + slots_out(half, width),
+        [images_out(count, length, width, F32), images_out(count, length, MISC, BF16)] + slots_out(slots, width),
         flops=dense_flops,
     )
     upstream = cotangent
@@ -634,32 +794,23 @@
     waiting = []
     for layer in reversed(range(LAYERS)):
         kept = saved[layer]
-        dys = [exchange(item) for item in sent]
-        dxs, grads, came, reduced = [], [], [], []
-        for j in range(local):
-            dys[j], done = lax.optimization_barrier((dys[j], waiting[j : j + 1]))
-            finished += done
-            du, dx = expert_backward(dys[j], kept["slopes"][j][1], experts[layer], j)
-            dxs.append(dx)
-            grad = expert_weight_grads(kept["arrived"][j], kept["slopes"][j][0], du, dys[j], parts)
-            grads.append(grad)
-            reduced.append(lax.psum_scatter(grad[0], "dp", scatter_dimension=0, tiled=False))
-            if j + 1 < local:
-                dys[j + 1], grad = lax.optimization_barrier((dys[j + 1], grad))
-                grads[j] = grad
-        came = [exchange(item) for item in dxs]
-        waiting = reduced
+        sent = sent.reshape(local, owners, capacity, width)
+        came, grads, db1, db2 = expert_backward(sent, experts[layer], *kept["experts"], LAYERS + layer)
+        came = came.reshape(slots, width)
+        came, waiting = lax.optimization_barrier((came, waiting))
+        finished += waiting
+        waiting = [lax.psum_scatter(grads, "dp", scatter_dimension=0, tiled=False)]
         own = [
-            jnp.concatenate([g[1].reshape(width, ff // width), g[2].reshape(width, 1)], axis=1) for g in grads
+            jnp.concatenate([db1[j].reshape(width, ff // width), db2[j].reshape(width, 1)], axis=1)
+            for j in range(local)
         ]
         first_column = lax.axis_index("expert") * (local * bias_columns)
         bias = lax.dynamic_update_slice(
             jnp.zeros((width, bias_room), F32), jnp.concatenate(own, axis=1), (0, first_column)
         ).astype(BF16)
-        came, bias = lax.optimization_barrier((came, bias))
         weights = [(packed[layer], s) for s in packed_specs(packed[layer])]
         inputs = [upstream, kept["rows"], kept["middle"], *kept["attend"], dz, dcol[layer]]
-        inputs = [(a, per_image(a)) for a in inputs] + [(a, whole(a)) for a in came] + weights
+        inputs = [(a, per_image(a)) for a in inputs] + [(came, whole(came))] + weights
         inputs += [(bias, whole(bias))]
         outputs = [
             images_out(count, length, width, F32),
@@ -672,17 +823,17 @@
             below = saved[layer - 1]
             extra = [*below["picked"], below["gates"], routes[layer - 1], drow[layer - 1]]
             inputs += [(a, per_image(a)) for a in extra]
-            outputs += [images_out(count, length, MISC, BF16)] + slots_out(half, width)
+            outputs += [images_out(count, length, MISC, BF16)] + slots_out(slots, width)
         done = call(
             back_kernel, (count,), inputs, outputs,
             [pltpu.VMEM((width, 4 * width + MISC), F32), pltpu.VMEM((MISC, width), F32)], flops=3 * dense_flops,
         )
         upstream, wgrad = done[:2]
         if layer > 0:
-            dz, *sent = done[2:]
+            dz, sent = done[2:]
         mine = lax.psum_scatter(wgrad, "dp", scatter_dimension=0, tiled=True)
         dense_grads[layer] = lax.psum(mine, "expert")
-    expert_grads = [waiting, finished]
+    expert_grads = waiting + finished
 
     both = jnp.stack(dense_grads).astype(F32)
     square_grads = [both[:, :, n * width : (n + 1) * width] for n in range(4)]
@@ -691,7 +842,7 @@
         both[:, :, 4 * width + MISC :], lax.axis_index("expert") * (local * bias_columns), local * bias_columns, 2
     )
     own = jnp.transpose(own.reshape(LAYERS, share, local, bias_columns), (0, 2, 1, 3))
-    pieces = jnp.stack([jnp.stack(g) for g in expert_grads])
+    pieces = jnp.stack(expert_grads)
     inner_grad = pieces[:, :, : ff // parts].reshape(LAYERS, local, ff // FF_BLOCK, share, FF_BLOCK)
     inner_grad = jnp.transpose(inner_grad, (0, 1, 3, 2, 4)).reshape(inner_weight.shape)
     return (

time: 980 us -> 860 us (0.88)
  Pallas kernels: 305 us -> 512 us
  blocking collectives: 183 us -> 0 us
  waiting for transfers between devices: 356 us -> 266 us
  starting transfers between devices: 38.9 us -> 0.37 us
    pallas_call x0 -> x4, Pallas kernels: none -> 378 us  [expert_call(): pl.pallas_call(body, in_specs=[spec(held) for _, held in inputs], out_spe...]
    all_to_all x6 -> x0, blocking collectives: 183 us -> none  [exchange(): lax.all_to_all(array.reshape(owners, rows // owners, width), 'expert', sp...]
    pallas_call x21 -> x5, Pallas kernels: 305 us -> 133 us  [call(): pl.pallas_call(body, grid=grid, in_specs=[s for _, s in inputs], out_spec...]
    all_to_all x10 -> x0, waiting for transfers between devices: 108 us -> none  [exchange(): lax.all_to_all(array.reshape(owners, rows // owners, width), 'expert', sp...]
    all_gather x2, waiting for transfers between devices: 31.7 us -> 73.1 us  [shards(): experts.append(lax.all_gather(mine, 'dp', axis=0, tiled=False))]
    all_to_all x10 -> x0, starting transfers between devices: 38.2 us -> none  [exchange(): lax.all_to_all(array.reshape(owners, rows // owners, width), 'expert', sp...]
    unnamed x15 -> x11, waiting for transfers between devices: 105 us -> 90.6 us
    unnamed x109 -> x77, local copies, waits for them, and re-layouts: 19.8 us -> 16 us
  transfers between devices with their start and end apart: 21 -> 9, of which waited for: 15 -> 6; matrix products, arithmetic and copies ran while one was open for 5% -> 5% of each run, Pallas kernels for 27% -> 36%
where the time goes in v3:
time: 860 us; the launch traced here: 854 us
  Pallas kernels  512 us (60%)
  waiting for transfers between devices  266 us (31%)
  local copies, waits for them, and re-layouts  43.6 us (5%)
  other arithmetic  17.5 us (2%)
  between operations  14.9 us (2%)
    pallas_call x4, Pallas kernels, expert_call(): pl.pallas_call(body, in_specs=[spec(held) for _, held in inputs], out_spe...  378 us
    pallas_call x5, Pallas kernels, call(): pl.pallas_call(body, grid=grid, in_specs=[s for _, s in inputs], out_spec...  133 us
    unnamed x11, waiting for transfers between devices  90.6 us
    all_gather x2, waiting for transfers between devices, shards(): experts.append(lax.all_gather(mine, 'dp', axis=0, tiled=False))  73.1 us
    psum x1, waiting for transfers between devices, shards(): dense_grads[layer] = lax.psum(mine, 'expert')  55.4 us
    reduce_scatter x2, waiting for transfers between devices, shards(): mine = lax.psum_scatter(wgrad, 'dp', scatter_dimension=0, tiled=True)  31.3 us
  transfers between devices with their start and end apart: 9, of which 6 were waited for; matrix products, arithmetic and copies ran while one was open for 5% of the time, Pallas kernels for 36%

profile of v3, /device:TPU:0, one launch (start us, length us, event | category | flops | bytes accessed | tf_op | source)
XLA Modules:
  0.0 853.8 jit_solution(16058210015133762231)
XLA Ops:
  16.7 2.6 convert.157
  21.9 1.8 reshape_squeeze.33
  31.8 1.7 copy.303.rows
  38.3 1.7 copy.326.cotangent.upstream
  40.7 15.2 %all-gather.5.cloned.1.call-done.wq.wk.wv.wo.misc = bf16[512,2176]{1,0:T(8,128)(2,1)} async-done(((bf16[128,2176]{1,0:T(8,128)(2,1)}), bf16[512,2176]{1,0:T(8,128)(2,1)}) %all-gather.5.cloned.1.call-update) | async-done | bytes 2228240 | tf_op jit(solution)/shard_map/all_gather | solution.py:726
  60.1 20.8 %shard_map.322 = (f32[4,197,512]{2,1,0:T(8,128)}, bf16[4,197,512]{2,1,0:T(8,128)(2,1)}, bf16[4,197,512]{2,1,0:T(8,128)(2,1)}, bf16[4,197,512]{2,1,0:T(8,128)(2,1...) custom-call(f32[4,197,512]{2,1,0:T(8,128)} %copy.303.rows, ...), custom_call_target="tpu_custom_call" | custom-call | flops 4957667328 | bytes 20115936 | tf_op jit(solution)/shard_map/pallas_call | solution.py:308
  80.9 65.1 %all-gather.7.cloned.1.call-done.packed = bf16[4,2,1024,512]{3,2,1,0:T(8,128)(2,1)} async-done(((bf16[1,2,1024,512]{3,2,1,0:T(8,128)(2,1)}), bf16[4,2,1024,512]{3,2,1,0:T(8,128)(2,1)}) %all-gather.7.cloned.1.call-update) | async-done | bytes 8388624 | tf_op jit(solution)/shard_map/all_gather | solution.py:729
  146.0 93.7 %shard_map.323 = (bf16[2,8,128,512]{3,2,1,0:T(8,128)(2,1)}, bf16[2,8,128,512]{3,2,1,0:T(8,128)(2,1)}, bf16[2,1024,2048]{2,1,0:T(8,128)(2,1)}, bf16[2,1024,2048]{2,1,0:T(8,128)(2,1)}) custom-call(bf16[2,8,128,512]{3,2,1,0:T(8,128)(2,1)} %bitcast.158, bf16[4,2,1024,512]{3,2,1,0:T(8,128)(2,1)} %all-gather.7.cloned.1.call-done.packed, ...), custom_call_target="tpu_custom_call" | custom-call | flops 8589934592 | bytes 31477760 | tf_op jit(solution)/shard_map/pallas_call | solution.py:614
  239.7 25.9 %shard_map.324 = (f32[4,197,512]{2,1,0:T(8,128)}, bf16[4,197,512]{2,1,0:T(8,128)(2,1)}, bf16[4,197,512]{2,1,0:T(8,128)(2,1)}, f32[4,197,512]{2,1,0:T(8,128)}, bf...) custom-call(f32[4,197,512]{2,1,0:T(8,128)} %get-tuple-element.64.mid, ...), custom_call_target="tpu_custom_call" | custom-call | flops 4957667328 | bytes 25453344 | tf_op jit(solution)/shard_map/pallas_call | solution.py:308
  265.6 8.0 all-gather.11.cloned.1.call-done.packed
  273.6 93.7 %shard_map.325 = (bf16[2,8,128,512]{3,2,1,0:T(8,128)(2,1)}, bf16[2,8,128,512]{3,2,1,0:T(8,128)(2,1)}, bf16[2,1024,2048]{2,1,0:T(8,128)(2,1)}, bf16[2,1024,2048]{2,1,0:T(8,128)(2,1)}) custom-call(bf16[2,8,128,512]{3,2,1,0:T(8,128)(2,1)} %bitcast.157, bf16[4,2,1024,512]{3,2,1,0:T(8,128)(2,1)} %all-gather.11.cloned.1.call-done.packed, ...), custom_call_target="tpu_custom_call" | custom-call | flops 8589934592 | bytes 31477760 | tf_op jit(solution)/shard_map/pallas_call | solution.py:614
  367.3 18.7 %shard_map.326 = (f32[4,197,512]{2,1,0:T(8,128)}, bf16[4,197,128]{2,1,0:T(8,128)(2,1)}, bf16[2048,512]{1,0:T(8,128)(2,1)}) custom-call(f32[4,197,512]{2,1,0:T(8,128)} %get-tuple-element.68.middle, f32[4,197,2]{2,1,0:T(8,128)} %get-tuple-element.69.gates, s32[4,197,2]{2,1,0:T(8,128)} %copy.325.dcol, bf16[2048,512]{1,0:T(8,128)(2,1)} %bitcast.160, ...), custom_call_target="tpu_custom_call" | custom-call | flops 4957667328 | bytes 9262720 | tf_op jit(solution)/shard_map/pallas_call | solution.py:308
  386.0 95.4 %shard_map.327 = (bf16[2,8,128,512]{3,2,1,0:T(8,128)(2,1)}, bf16[4,2,1024,512]{3,2,1,0:T(8,128)(2,1)}, f32[2,1,2048]{2,1,0:T(1,128)}, f32[2,1,512]{2,1,0:T(1,128)}) custom-call(bf16[2,8,128,512]{3,2,1,0:T(8,128)(2,1)} %bitcast.159, bf16[4,2,1024,512]{3,2,1,0:T(8,128)(2,1)} %all-gather.11.cloned.1.call-done.packed, ...), custom_call_target="tpu_custom_call" | custom-call | flops 17179869184 | bytes 39866368 | tf_op jit(solution)/shard_map/pallas_call | solution.py:614
  484.4 39.6 %shard_map.328 = (f32[4,197,512]{2,1,0:T(8,128)}, bf16[512,2304]{1,0:T(8,128)(2,1)}, bf16[4,197,128]{2,1,0:T(8,128)(2,1)}, bf16[2048,512]{1,0:T(8,128)(2,1)}) custom-call(f32[4,197,512]{2,1,0:T(8,128)} %copy.326.cotangent.upstream, f32[4,197,512]{2,1,0:T(8,128)} %get-tuple-element.73.rows, f32[4,197,512]{2,1,0:T(8,128)} %get-tuple-element.68.middle, ...), custom_call_target="tpu_custom_call" | custom-call | flops 14873001984 | bytes 29954688 | tf_op jit(solution)/shard_map/pallas_call | solution.py:308
  524.1 95.6 %shard_map.329 = (bf16[2,8,128,512]{3,2,1,0:T(8,128)(2,1)}, bf16[4,2,1024,512]{3,2,1,0:T(8,128)(2,1)}, f32[2,1,2048]{2,1,0:T(1,128)}, f32[2,1,512]{2,1,0:T(1,128)}) custom-call(bf16[2,8,128,512]{3,2,1,0:T(8,128)(2,1)} %bitcast.155, bf16[4,2,1024,512]{3,2,1,0:T(8,128)(2,1)} %all-gather.7.cloned.1.call-done.packed, ...), custom_call_target="tpu_custom_call" | custom-call | flops 17179869184 | bytes 39866368 | tf_op jit(solution)/shard_map/pallas_call | solution.py:614
  623.4 28.2 %shard_map.330 = (f32[4,197,512]{2,1,0:T(8,128)}, bf16[512,2304]{1,0:T(8,128)(2,1)}) custom-call(f32[4,197,512]{2,1,0:T(8,128)} %get-tuple-element.89.upstream, f32[4,197,512]{2,1,0:T(8,128)} %copy.303.rows, f32[4,197,512]{2,1,0:T(8,128)} %get-tuple-element.64.middle, bf16[4,197,512]{2,1,0:T(8,128)(2,1)} %get-tuple-element.90.q_ref, ...), custom_call_target="tpu_custom_call" | custom-call | flops 14873001984 | bytes 26023072 | tf_op jit(solution)/shard_map/pallas_call | solution.py:308
  653.1 2.2 copy.338
  655.3 2.2 copy.339
  657.5 31.3 %reduce-scatter.9.cloned.1.call-done = bf16[128,2304]{1,0:T(8,128)(2,1)} async-done(((bf16[512,2304]{1,0:T(8,128)(2,1)}), bf16[128,2304]{1,0:T(8,128)(2,1)}) %reduce-scatter.9.cloned.1.call-update) | async-done | bytes 589840 | tf_op jit(solution)/shard_map/reduce_scatter | solution.py:834
  688.8 89.8 %reduce-scatter.15.cloned.1.call-done = bf16[1,2,1024,512]{3,2,1,0:T(8,128)(2,1)} async-done(((bf16[4,2,1024,512]{3,2,1,0:T(8,128)(2,1)}), bf16[1,2,1024,512]{3,2,1,0:T(8,128)(2,1)}) %reduce-scatter.15.cloned.1.call-update) | async-done | bytes 2097168
  778.6 3.6 fusion.4
  782.7 2.7 copy.349
  785.4 55.4 %all-reduce.5.cloned.1.call-done = (bf16[1,128,2304]{2,1,0:T(8,128)(2,1)}, bf16[1,128,2304]{2,1,0:T(8,128)(2,1)}) async-done(((bf16[1,128,2304]{2,1,0:T(8,128)(2,1)}, bf16[1,128,2304]{2,1,0:T(8,128)(2,1)}), (bf16[1,128,2304]{2,1,0:T(8,128)(2,1)}, bf16[1,128,2304]{2,1,0:T(8,128)(2,1)})) %all-reduce.5.cloned.1.call-update) | async-done | bytes 1179664 | tf_op jit(solution)/shard_map/psum | solution.py:835
  840.8 1.5 maximum_convert_fusion
  (205 shorter events, 42.8 us)
Async XLA Ops:
  7.2 3.5 copy-start.9
  7.2 3.6 copy-start.19
  7.2 4.3 copy-start.27
  7.2 4.4 copy-start.28
  7.2 4.6 copy-start.29
  7.2 4.7 copy-start.30
  7.3 4.9 copy-start.31
  7.3 5.6 copy-start.32
  7.3 6.2 copy-start.33
  7.3 6.9 copy-start.26
  7.3 6.9 copy-start.21
  7.3 48.6 %all-gather.5.cloned.1.call-start = ((), (), s32[]{:S(2)}) async-start(), calls=%async_computation.4 | async-start | bytes 2785280 | tf_op jit(solution)/shard_map/all_gather | solution.py:726
  15.5 3.8 copy-start.11
  15.5 3.8 copy-start.13
  16.6 129.3 %all-gather.7.cloned.1.call-start = ((), (), s32[]{:S(2)}) async-start(), calls=%async_computation.5 | async-start | bytes 10485760 | tf_op jit(solution)/shard_map/all_gather | solution.py:729
  25.7 214.0 %all-gather.9.cloned.1.call-start = ((), (), s32[]{:S(2)}) async-start(), calls=%async_computation.6 | async-start | bytes 2785280 | tf_op jit(solution)/shard_map/all_gather | solution.py:726
  27.8 245.8 %all-gather.11.cloned.1.call-start = ((), (), s32[]{:S(2)}) async-start(), calls=%async_computation.7 | async-start | bytes 10485760 | tf_op jit(solution)/shard_map/all_gather | solution.py:729
  30.4 592.4 %reduce-scatter.13.cloned.1.call-start = ((), (), s32[]{:S(2)}) async-start(), calls=%async_computation.10 | async-start | bytes 10485760
  33.4 4.9 copy-start.8
  481.4 176.1 %reduce-scatter.11.cloned.1.call-start = ((), (), s32[]{:S(2)}) async-start(), calls=%async_computation.9 | async-start | bytes 2949120 | tf_op jit(solution)/shard_map/reduce_scatter | solution.py:834
  524.0 164.8 %reduce-scatter.9.cloned.1.call-start = ((), (), s32[]{:S(2)}) async-start(), calls=%async_computation.8 | async-start | bytes 2949120 | tf_op jit(solution)/shard_map/reduce_scatter | solution.py:834
  651.6 127.0 %reduce-scatter.15.cloned.1.call-start = ((), (), s32[]{:S(2)}) async-start(), calls=%async_computation.11 | async-start | bytes 10485760
  652.4 188.4 %all-reduce.5.cloned.1.call-start = ((), (), s32[]{:S(2)}) async-start(), calls=%async_computation.12 | async-start | bytes 2359296 | tf_op jit(solution)/shard_map/psum | solution.py:835
  655.3 123.3 %copy-start.4 = (bf16[1,2,1024,512]{3,2,1,0:T(8,128)(2,1)S(1)}, bf16[1,2,1024,512]{3,2,1,0:T(8,128)(2,1)}, u32[]{:S(2)}) copy-start(bf16[1,2,1024,512]{3,2,1,0:T(8,128)(2,1)} %reduce-scatter.13.cloned.1.call-done) | copy-start | bytes 6291460
  (19 other events, 27.3 us)
Sparse Core Ops, SparseCore 0:
  16.8 39.0 all-gather.4
  58.3 87.5 all-gather.6
  147.8 36.3 all-gather.8
  185.9 87.6 all-gather.10
  481.5 85.6 reduce-scatter.12
  571.0 37.3 reduce-scatter.10
  651.7 37.0 reduce-scatter.8
  692.2 86.3 reduce-scatter.14
  781.0 59.7 all-reduce.4

commit v4 on v3

--- a/solution.py
+++ b/solution.py
@@ -13,9 +13,9 @@
 EPSILON = 1e-06
 FACTOR = HEAD_DIM**-0.5
 VEC_AT = 64
-BIAS_AT = 72
 MISC = 128
 FF_BLOCK = 512
+COST = 1024
 VMEM = 56 * 1024 * 1024
 
 F32 = jnp.float32
@@ -291,6 +291,11 @@
     return pl.BlockSpec((1,) + array.shape[1:], lambda i: (i,) + (0,) * (len(array.shape) - 1))
 
 
+def per_layer(array, layer):
+    shape = (None, 1) + array.shape[2:]
+    return pl.BlockSpec(shape, lambda i: (layer, i) + (0,) * (len(shape) - 2))
+
+
 def whole(array):
     return pl.BlockSpec(array.shape, lambda i: (0,) * len(array.shape))
 
@@ -302,9 +307,7 @@
 
 
 def call(body, grid, inputs, outputs, scratch=(), flops=0, aliases=None):
-    moved = sum(a.size * a.dtype.itemsize for a, _ in inputs)
     shapes = [jax.ShapeDtypeStruct(s, t) for s, t, _ in outputs]
-    moved += sum(s.size * s.dtype.itemsize for s in shapes)
     return pl.pallas_call(
         body,
         grid=grid,
@@ -313,7 +316,7 @@
         out_shape=shapes,
         scratch_shapes=list(scratch),
         compiler_params=pltpu.CompilerParams(vmem_limit_bytes=VMEM),
-        cost_estimate=pl.CostEstimate(flops=flops, bytes_accessed=moved, transcendentals=0),
+        cost_estimate=pl.CostEstimate(flops=COST, bytes_accessed=COST, transcendentals=0),
     )(*[a for a, _ in inputs])
 
 
@@ -347,6 +350,13 @@
     return sorted(range(1, count), key=lambda k: -min(k, count - k))
 
 
+def greet_all(peers):
+    barrier = pltpu.get_barrier_semaphore()
+    for peer in peers:
+        pl.semaphore_signal(barrier, inc=1, device_id=peer, device_id_type=MESH)
+    pl.semaphore_wait(barrier, len(peers))
+
+
 class Swap:
     def __init__(self, sent, arrived, made, back, sems):
         self.sent, self.arrived, self.made, self.back = sent, arrived, made, back
@@ -354,12 +364,8 @@
         self.local, self.count = arrived.shape[0], arrived.shape[1]
         self.me = lax.axis_index("expert")
 
-    def greet(self):
-        barrier = pltpu.get_barrier_semaphore()
-        for k in range(1, self.count):
-            peer = lax.rem(self.me + k, self.count)
-            pl.semaphore_signal(barrier, inc=1, device_id={"expert": peer}, device_id_type=MESH)
-        pl.semaphore_wait(barrier, self.count - 1)
+    def greet(self, others=()):
+        greet_all([{"expert": lax.rem(self.me + k, self.count)} for k in range(1, self.count)] + list(others))
 
     def outward(self, j, k, peer):
         return pltpu.make_async_remote_copy(
@@ -440,19 +446,35 @@
 
 
 def expert_kernel(
-    sent, packed, b1, b2, back, arrived_out, g_out, s_out,
+    layer, sent, packed, mine, b1, b2, back, arrived_out, g_out, s_out, packed_out,
     arrived, made, weights, g_stage, s_stage, out_send, out_recv, home_send, home_recv, own, load, stores, last,
+    share_send, share_recv,
 ):
+    row = lax.axis_index("dp")
+    parts = weights.shape[1]
     swap = Swap(sent, arrived, made, back, (out_send, out_recv, home_send, home_recv, own))
     local, count, capacity, width = arrived.shape
     chips = count // 2
     rows = 2 * capacity
     ff = g_out.shape[2]
-    loads = [pltpu.make_async_copy(packed.at[:, j], weights.at[j], load.at[j]) for j in range(local)]
+    loads = [
+        pltpu.make_async_copy(packed, weights.at[0], load.at[0]),
+        pltpu.make_async_copy(mine, weights.at[1, row], load.at[1]),
+    ]
     for copy in loads:
         copy.start()
-    swap.greet()
+    shares = [
+        pltpu.make_async_remote_copy(
+            src_ref=mine, dst_ref=weights.at[1, row], send_sem=share_send.at[k - 1], recv_sem=share_recv.at[k - 1],
+            device_id={"dp": lax.rem(row + k, parts)}, device_id_type=MESH,
+        )
+        for k in range(1, parts)
+    ]
+    swap.greet([{"dp": lax.rem(row + k, parts)} for k in range(1, parts)])
     swap.send_all()
+    for copy in shares:
+        copy.start()
+    packed_copy = pltpu.make_async_copy(weights.at[1], packed_out, last.at[1])
 
     def kept(j, slot, chip):
         place = pl.ds(pl.multiple_of(chip * rows, rows), rows)
@@ -463,8 +485,13 @@
 
     for j in range(local):
         loads[j].wait()
-
-        def chip_step(turn, carry, j=j):
+        if j == 1:
+            for copy in shares:
+                copy.wait_recv()
+            packed_copy.start()
+        number = layer * local + j
+
+        def chip_step(turn, carry, j=j, number=number):
             chip = swap.chip(turn)
             slot = lax.rem(turn, 2)
             swap.wait_chip(j, chip)
@@ -475,11 +502,11 @@
                     copy.wait()
 
             x = arrived[j, pl.ds(2 * chip, 2)].reshape(rows, width)
-            total = jnp.broadcast_to(b2[j], (rows, width))
+            total = jnp.broadcast_to(b2[number : number + 1, :], (rows, width))
             for f in range(ff // FF_BLOCK):
                 cols = slice(f * FF_BLOCK, (f + 1) * FF_BLOCK)
                 first, second = weight_blocks(weights, j, f)
-                inner = dot(x, first) + b1[j, :, cols]
+                inner = dot(x, first) + b1[number : number + 1, cols]
                 normal = 0.5 * (1.0 + lax.erf(inner * ROOT_HALF))
                 g = (inner * normal).astype(BF16)
                 density = jnp.exp(-0.5 * inner * inner) * ROOT_TWO_PI_INVERSE
@@ -493,21 +520,30 @@
             return carry
 
         lax.fori_loop(0, chips, chip_step, 0)
-    final = pltpu.make_async_copy(arrived, arrived_out, last)
+    final = pltpu.make_async_copy(arrived, arrived_out, last.at[0])
     final.start()
     for slot in range(2):
         for copy in kept(0, slot, 0):
             copy.wait()
     swap.finish()
+    for copy in shares:
+        copy.wait_send()
+    packed_copy.wait()
     final.wait()
 
 
-def expert_back_kernel(
-    sent, packed, arrived_x, g_in, s_in, back, out, db1, db2,
-    arrived, made, weights, x, du, s_stage, g_stage, first_stage, second_stage,
-    out_send, out_recv, home_send, home_recv, own, load, fetch, stores,
-):
+def expert_back_kernel(with_above, *refs):
+    if with_above:
+        *refs, above_in, above_own, above_send, above_recv, above_load = refs
+        refs = list(refs)
+        above, above_sum = refs.pop(6), refs.pop(11)
+    (
+        sent, packed_first, packed_second, arrived_x, g_in, s_in, back, summed, out, db1, db2,
+        arrived, made, weights, x, du, s_stage, g_stage, first_stage, second_stage, share_out, share_in,
+        out_send, out_recv, home_send, home_recv, own, load, fetch, stores, share_send, share_recv,
+    ) = refs
     swap = Swap(sent, arrived, made, back, (out_send, out_recv, home_send, home_recv, own))
+    row = lax.axis_index("dp")
     local, count, capacity, width = arrived.shape
     chips = count // 2
     rows = 2 * capacity
@@ -516,7 +552,9 @@
     _, parts, all_rows, _ = weights.shape
     share, take = width // parts, all_rows // 2
     each = FF_BLOCK // take
-    loads = [pltpu.make_async_copy(packed.at[:, j], weights.at[j], load.at[j]) for j in range(local)]
+    loads = [
+        pltpu.make_async_copy(packed, weights.at[j], load.at[j]) for j, packed in enumerate((packed_first, packed_second))
+    ]
     loads.append(pltpu.make_async_copy(arrived_x, x, load.at[local]))
     for copy in loads:
         copy.start()
@@ -534,16 +572,37 @@
     def results(j, f):
         return (
             pltpu.make_async_copy(
-                first_stage.at[f % 2], out.at[:, j, f * share : (f + 1) * share, :], stores.at[0, f % 2]
+                first_stage.at[f % 2], out.at[:, j - 1, f * share : (f + 1) * share, :], stores.at[0, f % 2]
             ),
             pltpu.make_async_copy(
-                second_stage.at[f % 2], out.at[f * each : (f + 1) * each, j, take:, :], stores.at[1, f % 2]
+                second_stage.at[f % 2], out.at[f * each : (f + 1) * each, j - 1, take:, :], stores.at[1, f % 2]
             ),
         )
 
+    def share_copy(k):
+        peer = lax.rem(row + k, parts)
+        return pltpu.make_async_remote_copy(
+            src_ref=share_out.at[peer], dst_ref=share_in.at[k - 1],
+            send_sem=share_send.at[k - 1], recv_sem=share_recv.at[k - 1],
+            device_id={"dp": peer}, device_id_type=MESH,
+        )
+
     slopes(0, 0).start()
-    swap.greet()
+    peers = [{"dp": lax.rem(row + k, parts)} for k in range(1, parts)]
+    swap.greet(peers)
     swap.send_all()
+    if with_above:
+        above_copies = [
+            pltpu.make_async_remote_copy(
+                src_ref=above.at[lax.rem(row + k, parts)], dst_ref=above_in.at[k - 1],
+                send_sem=above_send.at[k - 1], recv_sem=above_recv.at[k - 1],
+                device_id=peers[k - 1], device_id_type=MESH,
+            )
+            for k in range(1, parts)
+        ]
+        above_copies.append(pltpu.make_async_copy(above.at[row], above_own, above_load))
+        for copy in above_copies:
+            copy.start()
     for j in range(local):
         loads[j].wait()
         activations(j, 0).start()
@@ -582,20 +641,51 @@
             cols = slice(f * FF_BLOCK, (f + 1) * FF_BLOCK)
             if f + 1 < blocks:
                 activations(j, f + 1).start()
-            if j > 0 or f > 1:
+            if j > 1 or (j == 1 and f > 1):
                 for copy in results(j, f):
                     copy.wait()
             part = du[:, cols]
             grad = dot_tn(x[j].reshape(count * capacity, width), part).astype(BF16)
-            first_stage[f % 2] = grad.reshape(parts, share, width)
+            if j == 0:
+                share_out[:, f * share : (f + 1) * share, :] = grad.reshape(parts, share, width)
+            else:
+                first_stage[f % 2] = grad.reshape(parts, share, width)
             db1[j, :, cols] = jnp.sum(part.astype(F32), axis=0, keepdims=True)
             activations(j, f).wait()
-            grad = dot_tn(g_stage[f % 2], dy).astype(BF16)
-            second_stage[f % 2] = grad.reshape(each, take, width)
-            for copy in results(j, f):
-                copy.start()
+            grad = dot_tn(g_stage[f % 2], dy).astype(BF16).reshape(each, take, width)
+            if j == 0:
+                share_out[f * each : (f + 1) * each, take:, :] = grad
+            else:
+                second_stage[f % 2] = grad
+                for copy in results(j, f):
+                    copy.start()
+        if j == 0:
+            for k in range(1, parts):
+                share_copy(k).start()
+    if with_above:
+        for copy in above_copies:
+            copy.wait()
+        total = above_own[...].astype(F32)
+        for k in range(1, parts):
+            total = total + above_in[k - 1].astype(F32)
+        above_sum[...] = total.astype(BF16)
+    for k in range(1, parts):
+        share_copy(k).wait_recv()
+    step = 64
+
+    def add_up(turn, carry):
+        place = pl.ds(pl.multiple_of(turn * step, step), step)
+        total = share_out[row, place, :].astype(F32)
+        for k in range(1, parts):
+            total = total + share_in[k - 1, place, :].astype(F32)
+        summed[place, :] = total
+        return carry
+
+    lax.fori_loop(0, all_rows // step, add_up, 0)
+    for k in range(1, parts):
+        share_copy(k).wait_send()
     for f in range(2):
-        for copy in results(0, f):
+        for copy in results(1, f):
             copy.wait()
     swap.finish()
 
@@ -605,12 +695,11 @@
     return pairs + [pltpu.SemaphoreType.DMA((2 * local,))]
 
 
-def expert_call(body, inputs, outputs, scratch, number, flops):
+def expert_call(body, inputs, outputs, scratch, number):
     def spec(held):
         return pl.BlockSpec(memory_space=pltpu.VMEM if held else pl.ANY)
 
     shapes = [jax.ShapeDtypeStruct(s, t) for s, t, _ in outputs]
-    moved = sum(a.size * a.dtype.itemsize for a, _ in inputs) + sum(s.size * s.dtype.itemsize for s in shapes)
     return pl.pallas_call(
         body,
         in_specs=[spec(held) for _, held in inputs],
@@ -620,74 +709,331 @@
         compiler_params=pltpu.CompilerParams(
             collective_id=number, has_side_effects=True, vmem_limit_bytes=VMEM
         ),
-        cost_estimate=pl.CostEstimate(flops=flops, bytes_accessed=moved, transcendentals=0),
+        cost_estimate=pl.CostEstimate(flops=COST, bytes_accessed=COST, transcendentals=0),
     )(*[a for a, _ in inputs])
 
 
-def expert_forward(sent, expert, number):
-    packed, b1, b2 = expert
+def expert_forward(sent, packed, mine, biases, layer):
+    b1, b2 = biases
     local, count, capacity, width = sent.shape
-    ff = b1.shape[2]
+    ff = b1.shape[1]
     rows = 2 * capacity
+    parts = packed.shape[0]
     slots = (local, count * capacity, ff)
     return expert_call(
-        expert_kernel,
-        [(sent, False), (packed, False), (b1, True), (b2, True)],
-        [(sent.shape, BF16, False), (sent.shape, BF16, False), (slots, BF16, False), (slots, BF16, False)],
+        functools.partial(expert_kernel, layer),
+        [(sent, False), (packed, False), (mine, False), (b1, True), (b2, True)],
         [
-            pltpu.VMEM(sent.shape, BF16), pltpu.VMEM(sent.shape, BF16),
-            pltpu.VMEM((local, packed.shape[0], *packed.shape[2:]), BF16),
+            (sent.shape, BF16, False), (sent.shape, BF16, False), (slots, BF16, False), (slots, BF16, False),
+            (packed.shape, BF16, False),
+        ],
+        [
+            pltpu.VMEM(sent.shape, BF16), pltpu.VMEM(sent.shape, BF16), pltpu.VMEM((local, *packed.shape), BF16),
             pltpu.VMEM((2, rows, ff), BF16), pltpu.VMEM((2, rows, ff), BF16),
         ] + swap_sems(local, count) + [
-            pltpu.SemaphoreType.DMA((local,)), pltpu.SemaphoreType.DMA((2, 2)), pltpu.SemaphoreType.DMA,
+            pltpu.SemaphoreType.DMA((local,)), pltpu.SemaphoreType.DMA((2, 2)), pltpu.SemaphoreType.DMA((2,)),
+            pltpu.SemaphoreType.DMA((parts - 1,)), pltpu.SemaphoreType.DMA((parts - 1,)),
         ],
-        number,
-        4 * local * count * capacity * width * ff,
+        layer,
     )
 
 
-def expert_backward(sent, expert, arrived, g, s, number):
-    packed, b1, b2 = expert
+def expert_backward(sent, weights, arrived, g, s, above, layer):
     local, count, capacity, width = sent.shape
-    ff = b1.shape[2]
+    ff = g.shape[2]
     rows = 2 * capacity
-    parts, _, all_rows, _ = packed.shape
+    parts, all_rows, _ = weights[0].shape
     share, take = width // parts, all_rows // 2
+    inputs = [(a, False) for a in (sent, *weights, arrived, g, s)]
+    outputs = [
+        (sent.shape, BF16, False), ((all_rows, width), F32, True), ((parts, local - 1, all_rows, width), BF16, False),
+        ((local, 1, ff), F32, True), ((local, 1, width), F32, True),
+    ]
+    scratch = [
+        pltpu.VMEM(sent.shape, BF16), pltpu.VMEM(sent.shape, BF16),
+        pltpu.VMEM((local, parts, all_rows, width), BF16), pltpu.VMEM(sent.shape, BF16),
+        pltpu.VMEM((count * capacity, ff), BF16), pltpu.VMEM((2, rows, ff), BF16),
+        pltpu.VMEM((2, count * capacity, FF_BLOCK), BF16), pltpu.VMEM((2, parts, share, width), BF16),
+        pltpu.VMEM((2, FF_BLOCK // take, take, width), BF16),
+        pltpu.VMEM((parts, all_rows, width), BF16), pltpu.VMEM((parts - 1, all_rows, width), BF16),
+    ] + swap_sems(local, count) + [
+        pltpu.SemaphoreType.DMA((local + 1,)), pltpu.SemaphoreType.DMA((2, 2)), pltpu.SemaphoreType.DMA((2, 2)),
+        pltpu.SemaphoreType.DMA((parts - 1,)), pltpu.SemaphoreType.DMA((parts - 1,)),
+    ]
+    if above is not None:
+        inputs.append((above, False))
+        outputs.append((above.shape[1:], BF16, True))
+        scratch += [
+            pltpu.VMEM((parts - 1, *above.shape[1:]), BF16), pltpu.VMEM(above.shape[1:], BF16),
+            pltpu.SemaphoreType.DMA((parts - 1,)), pltpu.SemaphoreType.DMA((parts - 1,)), pltpu.SemaphoreType.DMA,
+        ]
     return expert_call(
-        expert_back_kernel,
-        [(sent, False), (packed, False), (arrived, False), (g, False), (s, False)],
+        functools.partial(expert_back_kernel, above is not None), inputs, outputs, scratch, LAYERS + layer
+    )
+
+
+def prepare_kernel(capacity, owners, *refs):
+    squares, (router, *vectors), (inner_bias, outer_bias, routes) = refs[:4], refs[4:12], refs[12:15]
+    out, above, b1, b2, dcol, drow = refs[15:21]
+    mine, turned, inner_low, outer_low = refs[21:25]
+    send, recv, pass_send, pass_recv, b1_send, b1_recv, b2_send, b2_recv, own = refs[25:]
+    parts, share, _ = out.shape
+    width = squares[0].shape[2]
+    experts_all = router.shape[2]
+    local, part_ff = inner_bias.shape[1:]
+    half = share // 2
+    row, me = lax.axis_index("dp"), lax.axis_index("expert")
+    core = lax.rem(me, 2)
+    sibling = {"expert": me + 1 - 2 * core}
+    rows = pl.ds(pl.multiple_of(core * half, half), half)
+    peers = [{"dp": lax.rem(row + k, parts)} for k in range(1, parts)]
+
+    def pack(target, layer):
+        for n in range(4):
+            target[:, n * width : (n + 1) * width] = squares[n][layer].astype(BF16)
+        turned[...] = jnp.zeros_like(turned)
+        for n in range(7):
+            turned[VEC_AT + n : VEC_AT + n + 1, :] = vectors[n][layer : layer + 1, :]
+        target[:, 4 * width :] = turned[...].T.astype(BF16)
+        target[:, 4 * width : 4 * width + experts_all] = router[layer].astype(BF16)
+
+    def remote(source, target, send_sem, recv_sem, device):
+        return pltpu.make_async_remote_copy(
+            src_ref=source, dst_ref=target, send_sem=send_sem, recv_sem=recv_sem, device_id=device, device_id_type=MESH
+        )
+
+    def hand(k):
+        place = out.at[lax.rem(row - k + parts, parts), rows]
+        return remote(place, place, pass_send.at[k - 1], pass_recv.at[k - 1], sibling)
+
+    pack(mine, 0)
+    for layer in range(LAYERS):
+        for j in range(local):
+            n = layer * local + j
+            inner_low[n : n + 1, :] = inner_bias[layer, j : j + 1, :].astype(BF16).astype(F32)
+            outer_low[n : n + 1, :] = outer_bias[layer, j : j + 1, :].astype(BF16).astype(F32)
+    greet_all([sibling] + peers)
+    place = pl.ds(pl.multiple_of(row * part_ff, part_ff), part_ff)
+    fetches = [
+        remote(mine.at[rows], out.at[row, rows], send.at[k], recv.at[k], peers[k]) for k in range(parts - 1)
+    ]
+    singles = [
+        remote(inner_low, b1.at[:, place], b1_send.at[k], b1_recv.at[k], peers[k]) for k in range(parts - 1)
+    ] + [remote(outer_low, b2.at[row], b2_send.at[k], b2_recv.at[k], peers[k]) for k in range(parts - 1)]
+    keeps = [
+        pltpu.make_async_copy(mine, out.at[row], own.at[0]),
+        pltpu.make_async_copy(inner_low, b1.at[:, place], own.at[1]),
+        pltpu.make_async_copy(outer_low, b2.at[row], own.at[2]),
+    ]
+    for copy in fetches + singles + keeps:
+        copy.start()
+    pack(above, 1)
+
+    length = routes.shape[2]
+    lanes = lax.broadcasted_iota(jnp.int32, (length, MISC), 1)
+    earlier = (
+        lax.broadcasted_iota(jnp.int32, (length, length), 0) > lax.broadcasted_iota(jnp.int32, (length, length), 1)
+    ).astype(F32).astype(BF16)
+    for layer in range(LAYERS):
+        seen = jnp.zeros((1, MISC), F32)
+        for image in range(routes.shape[1]):
+            hots, dests = [], []
+            for k in range(2):
+                hots.append((lanes == routes[layer, image, :, k : k + 1]).astype(F32))
+            counts = hots[0] + hots[1]
+            before = dot(earlier, counts.astype(BF16)) + seen
+            seen = seen + jnp.sum(counts, axis=0, keepdims=True)
+            for k in range(2):
+                slot = jnp.sum(hots[k] * before, axis=-1, keepdims=True)
+                expert = routes[layer, image, :, k : k + 1].astype(F32)
+                owner = jnp.floor(expert * (1.0 / local))
+                place = ((expert - owner * local) * owners + owner) * capacity + slot
+                dests.append(jnp.where(slot < capacity, place, -1.0))
+                dcol[layer, image, :, k : k + 1] = dests[k].astype(jnp.int32)
+            both = jnp.where(lanes == 0, dests[0], jnp.where(lanes == 1, dests[1], 0.0))
+            drow[layer, image] = both.T[0:2, :].astype(jnp.int32)
+
+    for k in range(1, parts):
+        fetches[k - 1].wait_recv()
+        hand(k).start()
+    for k in range(1, parts):
+        fetches[k - 1].wait_send()
+        hand(k).wait()
+    for copy in singles + keeps:
+        copy.wait()
+
+
+def prepare(squares, router, vectors, inner_bias, outer_bias, routes, parts, owners, number):
+    layers, share, width = squares[0].shape
+    experts_all = router.shape[2]
+    local, part_ff = inner_bias.shape[1:]
+    _, images, length, _ = routes.shape
+    capacity = (10 * images * length // (4 * experts_all) + 7) // 8 * 8
+    columns = 4 * width + MISC
+    count = layers * local
+    sems = [pltpu.SemaphoreType.DMA((parts - 1,))] * 8 + [pltpu.SemaphoreType.DMA((3,))]
+    inputs = [*squares, router, *vectors, inner_bias, outer_bias, routes]
+    out, above, b1, b2, dcol, drow = expert_call(
+        functools.partial(prepare_kernel, capacity, owners), [(a, True) for a in inputs],
         [
-            (sent.shape, BF16, False), (packed.shape, BF16, False),
-            (b1.shape, F32, True), (b2.shape, F32, True),
+            ((parts, share, columns), BF16, False), ((share, columns), BF16, True),
+            ((count, part_ff * parts), F32, False), ((parts, count, share), F32, False),
+            ((layers, images, length, 2), jnp.int32, True), ((layers, images, 2, length), jnp.int32, True),
         ],
         [
-            pltpu.VMEM(sent.shape, BF16), pltpu.VMEM(sent.shape, BF16),
-            pltpu.VMEM((local, parts, all_rows, width), BF16), pltpu.VMEM(sent.shape, BF16),
-            pltpu.VMEM((count * capacity, ff), BF16), pltpu.VMEM((2, rows, ff), BF16),
-            pltpu.VMEM((2, count * capacity, FF_BLOCK), BF16), pltpu.VMEM((2, parts, share, width), BF16),
-            pltpu.VMEM((2, FF_BLOCK // take, take, width), BF16),
-        ] + swap_sems(local, count) + [
-            pltpu.SemaphoreType.DMA((local + 1,)), pltpu.SemaphoreType.DMA((2, 2)), pltpu.SemaphoreType.DMA((2, 2)),
+            pltpu.VMEM((share, columns), BF16), pltpu.VMEM((MISC, share), F32),
+            pltpu.VMEM((count, part_ff), F32), pltpu.VMEM((count, share), F32),
+        ] + sems,
+        number,
+    )
+    b2 = jnp.transpose(b2, (1, 0, 2)).reshape(count, width)
+    return out.reshape(width, columns), above, (b1, b2), dcol, drow, capacity
+
+
+def settle_kernel(
+    grads, above, final, own, paired, own_above, paired_above, scattered, total, chips_in,
+    pair_send, pair_recv, local, dp_send, dp_recv, out_send, out_recv, back_send, back_recv, pass_send, pass_recv,
+):
+    parts, share, columns = grads.shape
+    half = share // 2
+    row, me = lax.axis_index("dp"), lax.axis_index("expert")
+    core, chip = lax.rem(me, 2), me // 2
+    chips = chips_in.shape[0] + 1
+    block = columns // chips
+    sibling = {"expert": me + 1 - 2 * core}
+    mine = pl.ds(pl.multiple_of(core * half, half), half)
+    other = pl.ds(pl.multiple_of((1 - core) * half, half), half)
+
+    def remote(source, target, send, recv, device):
+        return pltpu.make_async_remote_copy(
+            src_ref=source, dst_ref=target, send_sem=send, recv_sem=recv, device_id=device, device_id_type=MESH
+        )
+
+    def cols(number):
+        return pl.ds(pl.multiple_of(number * block, block), block)
+
+    def chip_at(k):
+        return lax.rem(chip + k + chips, chips)
+
+    dp_peers = [{"dp": lax.rem(row + k, parts)} for k in range(1, parts)]
+    chip_peers = [{"expert": 2 * chip_at(k) + core} for k in range(1, chips)]
+    greet_all([sibling] + dp_peers + chip_peers)
+
+    pairs, locals_ = [], []
+    for i in range(parts):
+        part = lax.rem(row + 1 + i, parts)
+        pairs.append(remote(grads.at[part, other], paired.at[part], pair_send.at[i], pair_recv.at[i], sibling))
+        locals_.append(pltpu.make_async_copy(grads.at[part, mine], own.at[part], local.at[i]))
+    pairs.append(remote(above.at[other], paired_above, pair_send.at[parts], pair_recv.at[parts], sibling))
+    locals_.append(pltpu.make_async_copy(above.at[mine], own_above, local.at[parts]))
+    for pair, keep in zip(pairs, locals_):
+        pair.start()
+        keep.start()
+    scatters = []
+    for i in range(parts):
+        part = lax.rem(row + 1 + i, parts)
+        pairs[i].wait_recv()
+        locals_[i].wait()
+        own[part] = (own[part].astype(F32) + paired[part].astype(F32)).astype(BF16)
+        if i + 1 < parts:
+            scatters.append(remote(own.at[part], scattered.at[i], dp_send.at[i], dp_recv.at[i], dp_peers[i]))
+            scatters[i].start()
+    pairs[parts].wait_recv()
+    locals_[parts].wait()
+    total[1] = (own_above[...].astype(F32) + paired_above[...].astype(F32)).astype(BF16)
+    value = own[row].astype(F32)
+    for i in range(parts - 1):
+        scatters[i].wait_recv()
+        value = value + scattered[i].astype(F32)
+    total[0] = value.astype(BF16)
+    outs = []
+    for k in range(1, chips):
+        outs.append(remote(
+            total.at[:, :, cols(chip_at(k))], chips_in.at[k - 1], out_send.at[k - 1], out_recv.at[k - 1],
+            chip_peers[k - 1],
+        ))
+        outs[-1].start()
+    value = total[:, :, cols(chip)].astype(F32)
+    for k in range(1, chips):
+        outs[k - 1].wait_recv()
+        value = value + chips_in[k - 1].astype(F32)
+    final[:, mine, cols(chip)] = value.astype(BF16)
+    backs, hands = [], []
+    place = final.at[:, mine, cols(chip)]
+    for k in range(1, chips):
+        backs.append(remote(place, place, back_send.at[k - 1], back_recv.at[k - 1], chip_peers[k - 1]))
+        backs[-1].start()
+    hands.append(remote(place, place, pass_send.at[0], pass_recv.at[0], sibling))
+    hands[0].start()
+    for k in range(1, chips):
+        backs[k - 1].wait_recv()
+        place = final.at[:, mine, cols(chip_at(-k))]
+        hands.append(remote(place, place, pass_send.at[k], pass_recv.at[k], sibling))
+        hands[k].start()
+    for copy in pairs + scatters + outs + backs:
+        copy.wait_send()
+    for copy in hands:
+        copy.wait()
+
+
+def settle_dense(grads, above, chips, number):
+    parts, share, columns = grads.shape
+    half = share // 2
+    quarter = pltpu.VMEM((half, columns), BF16)
+    sems = [parts + 1] * 3 + [parts - 1] * 2 + [chips - 1] * 4 + [chips] * 2
+    return expert_call(
+        settle_kernel, [(grads, False), (above, False)], [((2, share, columns), BF16, True)],
+        [
+            pltpu.VMEM((parts, half, columns), BF16), pltpu.VMEM((parts, half, columns), BF16), quarter, quarter,
+            pltpu.VMEM((parts - 1, half, columns), BF16), pltpu.VMEM((2, half, columns), BF16),
+            pltpu.VMEM((chips - 1, 2, half, columns // chips), BF16),
+        ] + [pltpu.SemaphoreType.DMA((n,)) for n in sems],
+        number,
+    )[0]
+
+
+def unpack_kernel(*refs):
+    count = 2 * LAYERS
+    pieces, both = refs[:count], refs[count]
+    squares, router, vectors, biases, inner, outer = refs[count + 1 : count + 5], *refs[count + 5 :]
+    layer = pl.program_id(0)
+    share = both.shape[1]
+    width = squares[0].shape[2]
+    for n in range(4):
+        squares[n][0] = both[0, :, n * width : (n + 1) * width].astype(F32)
+    misc = both[0, :, 4 * width : 4 * width + MISC].astype(F32)
+    router[0] = misc[:, : router.shape[2]]
+    turned = misc.T
+    vectors[0] = turned[VEC_AT : VEC_AT + 8, :]
+    biases[0] = both[0, :, 4 * width + MISC :].astype(F32)
+    blocks = inner.shape[3] // FF_BLOCK
+
+    for number in range(LAYERS):
+
+        @pl.when(layer == number)
+        def _(number=number):
+            for j in range(2):
+                piece = pieces[2 * number + j]
+                for f in range(blocks):
+                    inner[0, j, :, f * FF_BLOCK : (f + 1) * FF_BLOCK] = piece[
+                        f * share : (f + 1) * share, :
+                    ].astype(F32)
+                outer[0, j] = piece[blocks * share :, :].astype(F32)
+
+
+def unpack(pieces, both, local, ff, experts_all):
+    layers, share, columns = both.shape
+    rows, width = pieces[0].shape
+    take = rows // 2
+    by_layer = lambda *shape: ((layers, *shape), F32, pl.BlockSpec((1, *shape), lambda i: (i,) + (0,) * len(shape)))
+    return call(
+        unpack_kernel, (layers,),
+        [(p, whole(p)) for p in pieces] + [(both, pl.BlockSpec((1, share, columns), lambda i: (i, 0, 0)))],
+        [by_layer(share, width)] * 4 + [
+            by_layer(share, experts_all), by_layer(8, share), by_layer(share, columns - 4 * width - MISC),
+            by_layer(local, share, ff), by_layer(local, take, width),
         ],
-        number,
-        8 * local * count * capacity * width * ff,
     )
-
-
-def destinations(routes, experts_all, owners):
-    layers, images, length, _ = routes.shape
-    tokens = images * length
-    pairs = routes.reshape(layers, tokens, 2)
-    hot = (pairs[..., None] == jnp.arange(experts_all, dtype=jnp.int32)).astype(F32)
-    counts = (hot[:, :, 0] + hot[:, :, 1]).astype(BF16)
-    earlier = (jnp.arange(tokens)[:, None] > jnp.arange(tokens)[None, :]).astype(BF16)
-    before = jnp.einsum("ts,lse->lte", earlier, counts, preferred_element_type=F32)
-    slot = jnp.sum(before[:, :, None, :] * hot, axis=-1).astype(jnp.int32)
-    capacity = (10 * tokens // (4 * experts_all) + 7) // 8 * 8
-    local = experts_all // owners
-    row = ((pairs % local) * owners + pairs // local) * capacity + slot
-    dest = jnp.where(slot < capacity, row, -1)
-    return dest.reshape(layers, images, length, 2), capacity
 
 
 def shards(
@@ -706,35 +1052,21 @@
     squares = (query_weight, key_weight, value_weight, output_weight)
     vectors = (query_bias, value_bias, output_bias, attend_gain, attend_shift, expert_gain, expert_shift)
     bias_columns = ff // width + 1
-    bias_room = -(-experts_all * bias_columns // MISC) * MISC
-
-    biases = jnp.concatenate(
-        [inner_bias.reshape(LAYERS, local, share, ff // width), outer_bias.reshape(LAYERS, local, share, 1)], axis=3
+    columns = 4 * width + MISC + experts_all * bias_columns
+    columns = -(-columns // (MISC * (owners // 2))) * MISC * (owners // 2)
+    bias_room = columns - 4 * width - MISC
+
+    mine = []
+    for layer in range(LAYERS):
+        for j in range(local):
+            first = inner_weight[layer, j].reshape(share, ff // FF_BLOCK, FF_BLOCK)
+            first = jnp.transpose(first, (1, 0, 2)).reshape(ff // parts, width)
+            mine.append(jnp.concatenate([first, outer_weight[layer, j]], axis=0).astype(BF16))
+    dense, above, expert_biases, dcol, drow, capacity = prepare(
+        squares, router_weight, vectors, inner_bias, outer_bias, routes, parts, owners, 2 * LAYERS
     )
-    biases = jnp.transpose(biases, (2, 0, 1, 3)).reshape(share, LAYERS * local * bias_columns)
-
-    packed = []
-    experts = []
-    for layer in range(LAYERS):
-        misc = [router_weight[layer], jnp.zeros((share, VEC_AT - experts_all), F32)]
-        misc += [jnp.stack([v[layer] for v in vectors], axis=1), jnp.zeros((share, BIAS_AT - VEC_AT - 7), F32)]
-        if layer == 0:
-            misc += [biases, jnp.zeros((share, MISC - BIAS_AT - biases.shape[1]), F32)]
-        else:
-            misc += [jnp.zeros((share, MISC - BIAS_AT), F32)]
-        mine = jnp.concatenate([s[layer] for s in squares] + misc, axis=1).astype(BF16)
-        packed.append(lax.all_gather(mine, "dp", axis=0, tiled=True))
-        mine = jnp.transpose(inner_weight[layer].reshape(local, share, ff // FF_BLOCK, FF_BLOCK), (0, 2, 1, 3))
-        mine = jnp.concatenate([mine.reshape(local, ff // parts, width), outer_weight[layer]], axis=1).astype(BF16)
-        experts.append(lax.all_gather(mine, "dp", axis=0, tiled=False))
-    spare = packed[0][:, 4 * width + BIAS_AT : 4 * width + BIAS_AT + biases.shape[1]].astype(F32)
-    spare = jnp.transpose(spare.reshape(width, LAYERS, local, bias_columns), (1, 2, 0, 3))
-    inner_biases = spare[..., :-1].reshape(LAYERS, local, 1, ff)
-    outer_biases = spare[..., -1].reshape(LAYERS, local, 1, width)
-    experts = [(experts[n], inner_biases[n], outer_biases[n]) for n in range(LAYERS)]
-
-    dcol, capacity = destinations(routes, experts_all, owners)
-    drow = jnp.transpose(dcol, (0, 1, 3, 2))
+    packed = [dense, lax.all_gather(above, "dp", axis=0, tiled=True)]
+    firsts = [lax.all_gather(mine[layer * local], "dp", axis=0, tiled=False) for layer in range(LAYERS)]
     slots = experts_all * capacity
     dense_flops = 8 * tokens * width * width + 4 * tokens * slots * width
 
@@ -743,7 +1075,7 @@
     rows = images
     for layer in range(LAYERS):
         weights = [(packed[layer], s) for s in packed_specs(packed[layer])]
-        routing = [(routes[layer], per_image(routes[layer])), (drow[layer], per_image(drow[layer]))]
+        routing = [(routes, per_layer(routes, layer)), (drow, per_layer(drow, layer))]
         outputs = attend_outputs(count, length, width, slots)
         if layer == 0:
             done = call(
@@ -757,7 +1089,7 @@
                 [
                     (before["middle"], per_image(before["middle"])),
                     (before["gates"], per_image(before["gates"])),
-                    (dcol[layer - 1], per_image(dcol[layer - 1])),
+                    (dcol, per_layer(dcol, layer - 1)),
                     (back, whole(back)),
                 ] + routing + weights,
                 [
@@ -772,34 +1104,38 @@
             before["picked"] = picked
         middle, queries, keys, values, context, sums, gates = done[:7]
         sent = done[7].reshape(local, owners, capacity, width)
-        back, arrived, g, s = expert_forward(sent, experts[layer], layer)
+        back, arrived, g, s, second = expert_forward(
+            sent, firsts[layer], mine[layer * local + 1], expert_biases, layer
+        )
         back = back.reshape(slots, width)
         saved.append({
             "rows": rows, "middle": middle, "attend": (queries, keys, values, context, sums), "gates": gates,
-            "experts": (arrived, g, s),
+            "experts": (arrived, g, s), "weights": (firsts[layer], second),
         })
 
     last = saved[-1]
     result, dz, sent = call(
         turn_kernel, (count,),
         [(last["middle"], per_image(last["middle"])), (last["gates"], per_image(last["gates"]))]
-        + [(dcol[-1], per_image(dcol[-1])), (back, whole(back))]
-        + [(cotangent, per_image(cotangent)), (routes[-1], per_image(routes[-1])), (drow[-1], per_image(drow[-1]))],
+        + [(dcol, per_layer(dcol, LAYERS - 1)), (back, whole(back))]
+        + [(cotangent, per_image(cotangent)), (routes, per_layer(routes, LAYERS - 1)), (drow, per_layer(drow, LAYERS - 1))],
         [images_out(count, length, width, F32), images_out(count, length, MISC, BF16)] + slots_out(slots, width),
         flops=dense_flops,
     )
     upstream = cotangent
-    dense_grads = [None] * LAYERS
     finished = []
     waiting = []
+    wgrad = None
     for layer in reversed(range(LAYERS)):
         kept = saved[layer]
         sent = sent.reshape(local, owners, capacity, width)
-        came, grads, db1, db2 = expert_backward(sent, experts[layer], *kept["experts"], LAYERS + layer)
+        came, shares, grads, db1, db2, *above = expert_backward(
+            sent, kept["weights"], *kept["experts"], wgrad, layer
+        )
         came = came.reshape(slots, width)
         came, waiting = lax.optimization_barrier((came, waiting))
         finished += waiting
-        waiting = [lax.psum_scatter(grads, "dp", scatter_dimension=0, tiled=False)]
+        waiting = [shares, lax.psum_scatter(grads, "dp", scatter_dimension=0, tiled=False)]
         own = [
             jnp.concatenate([db1[j].reshape(width, ff // width), db2[j].reshape(width, 1)], axis=1)
             for j in range(local)
@@ -809,8 +1145,9 @@
             jnp.zeros((width, bias_room), F32), jnp.concatenate(own, axis=1), (0, first_column)
         ).astype(BF16)
         weights = [(packed[layer], s) for s in packed_specs(packed[layer])]
-        inputs = [upstream, kept["rows"], kept["middle"], *kept["attend"], dz, dcol[layer]]
-        inputs = [(a, per_image(a)) for a in inputs] + [(came, whole(came))] + weights
+        inputs = [upstream, kept["rows"], kept["middle"], *kept["attend"], dz]
+        inputs = [(a, per_image(a)) for a in inputs]
+        inputs += [(dcol, per_layer(dcol, layer)), (came, whole(came))] + weights
         inputs += [(bias, whole(bias))]
         outputs = [
             images_out(count, length, width, F32),
@@ -821,8 +1158,8 @@
         ]
         if layer > 0:
             below = saved[layer - 1]
-            extra = [*below["picked"], below["gates"], routes[layer - 1], drow[layer - 1]]
-            inputs += [(a, per_image(a)) for a in extra]
+            inputs += [(a, per_image(a)) for a in (*below["picked"], below["gates"])]
+            inputs += [(a, per_layer(a, layer - 1)) for a in (routes, drow)]
             outputs += [images_out(count, length, MISC, BF16)] + slots_out(slots, width)
         done = call(
             back_kernel, (count,), inputs, outputs,
@@ -831,29 +1168,21 @@
         upstream, wgrad = done[:2]
         if layer > 0:
             dz, sent = done[2:]
-        mine = lax.psum_scatter(wgrad, "dp", scatter_dimension=0, tiled=True)
-        dense_grads[layer] = lax.psum(mine, "expert")
-    expert_grads = waiting + finished
-
-    both = jnp.stack(dense_grads).astype(F32)
-    square_grads = [both[:, :, n * width : (n + 1) * width] for n in range(4)]
-    tail = both[:, :, 4 * width : 4 * width + MISC]
-    own = lax.dynamic_slice_in_dim(
-        both[:, :, 4 * width + MISC :], lax.axis_index("expert") * (local * bias_columns), local * bias_columns, 2
-    )
+        wgrad = wgrad.reshape(parts, share, columns)
+    both = settle_dense(wgrad, above[0], owners // 2, 2 * LAYERS + 1)
+    pieces = [waiting[0], waiting[1][0], finished[0], finished[1][0]]
+    *squares, router, vectors, biases, inner, outer = unpack(pieces, both, local, ff, experts_all)
+    own = lax.dynamic_slice_in_dim(biases, lax.axis_index("expert") * (local * bias_columns), local * bias_columns, 2)
     own = jnp.transpose(own.reshape(LAYERS, share, local, bias_columns), (0, 2, 1, 3))
-    pieces = jnp.stack(expert_grads)
-    inner_grad = pieces[:, :, : ff // parts].reshape(LAYERS, local, ff // FF_BLOCK, share, FF_BLOCK)
-    inner_grad = jnp.transpose(inner_grad, (0, 1, 3, 2, 4)).reshape(inner_weight.shape)
     return (
         result,
         upstream,
-        *square_grads,
-        tail[:, :, :experts_all],
-        *[tail[:, :, VEC_AT + n] for n in range(7)],
-        inner_grad.astype(F32),
+        *squares,
+        router,
+        *[vectors[:, n] for n in range(7)],
+        inner,
         own[..., :-1].reshape(LAYERS, local, ff // parts),
-        pieces[:, :, ff // parts :].astype(F32),
+        outer,
         own[..., -1],
     )
 

time: 860 us -> 674 us (0.78)
  waiting for transfers between devices: 266 us -> 3.37 us
  Pallas kernels: 512 us -> 616 us
  local copies, waits for them, and re-layouts: 43.6 us -> 26.3 us
  other arithmetic: 17.5 us -> 7.74 us
    pallas_call x4 -> x6, Pallas kernels: 378 us -> 475 us  [expert_call(): pl.pallas_call(body, in_specs=[spec(held) for _, held in inputs], out_spe...]
    unnamed x11 -> x7, waiting for transfers between devices: 90.6 us -> 0.13 us
    all_gather x4 -> x3, waiting for transfers between devices: 88.3 us -> 3.25 us  [the longest x2 3.22 us: shards(): lax.all_gather(mine[layer * local], 'dp', axis=0, tiled=False)]
    psum x1 -> x0, waiting for transfers between devices: 55.4 us -> none  [shards(): dense_grads[layer] = lax.psum(mine, 'expert')]
    reduce_scatter x2 -> x0, waiting for transfers between devices: 31.3 us -> none  [shards(): mine = lax.psum_scatter(wgrad, 'dp', scatter_dimension=0, tiled=True)]
    pallas_call x5 -> x6, Pallas kernels: 133 us -> 141 us  [call(): pl.pallas_call(body, grid=grid, in_specs=[s for _, s in inputs], out_spec...]
  transfers between devices with their start and end apart: 9 -> 5, of which waited for: 6 -> 2; matrix products, arithmetic and copies ran while one was open for 5% -> 2% of each run, Pallas kernels for 36% -> 60%
where the time goes in v4:
time: 674 us; the launch traced here: 668 us
  Pallas kernels  616 us (91%)
  local copies, waits for them, and re-layouts  26.3 us (4%)
  between operations  14.4 us (2%)
  other arithmetic  7.74 us (1%)
    pallas_call x6, Pallas kernels, expert_call(): pl.pallas_call(body, in_specs=[spec(held) for _, held in inputs], out_spe...  475 us
    pallas_call x6, Pallas kernels, call(): pl.pallas_call(body, grid=grid, in_specs=[s for _, s in inputs], out_spec...  141 us
    unnamed x42, local copies, waits for them, and re-layouts  16.9 us
  transfers between devices with their start and end apart: 5, of which 2 were waited for; matrix products, arithmetic and copies ran while one was open for 2% of the time, Pallas kernels for 60%

profile of v4, /device:TPU:0, one launch (start us, length us, event | category | flops | bytes accessed | tf_op | source)
XLA Modules:
  0.0 668.5 jit_solution(14355993771131659557)
XLA Ops:
  7.2 2.5 convert.37
  10.9 1.6 copy-done
  13.5 2.1 pad_maximum_fusion
  15.7 1.2 copy.107.refs_14_.routes.rest_4_
  17.7 30.6 %shard_map.322 = (bf16[4,128,2176]{2,1,0:T(8,128)(2,1)}, bf16[128,2176]{1,0:T(8,128)(2,1)}, f32[4,2048]{1,0:T(4,128)}, f32[4,4,128]{2,1,0:T(4,128)}, s32[2,4,197,2]{3,2,1,0:T(8,128)}, /*index=5*/s32[2,4,2,197]{3,2,1,0:T(2,128)}) custom-call(f32[2,128,512]{2,1,0:T(8,128)} %refs_0_.1, f32[2,128,512]{2,1,0:T(8,128)} %refs_1_.1, f32[2,128,512]{2,1,0:T(8,128)} %refs_2_.1, ...), custom_call_target="tpu_custom_call" | custom-call | flops 1024 | bytes 1024 | tf_op jit(solution)/shard_map/pallas_call | solution.py:703
  50.7 1.7 copy.106.rows
  52.4 20.6 %shard_map.323 = (f32[4,197,512]{2,1,0:T(8,128)}, bf16[4,197,512]{2,1,0:T(8,128)(2,1)}, bf16[4,197,512]{2,1,0:T(8,128)(2,1)}, bf16[4,197,512]{2,1,0:T(8,128)(2,1...) custom-call(f32[4,197,512]{2,1,0:T(8,128)} %copy.106.rows, ...), custom_call_target="tpu_custom_call" | custom-call | flops 1024 | bytes 1024 | tf_op jit(solution)/shard_map/pallas_call | solution.py:311
  74.4 1.7 copy.113.cotangent.upstream
  76.1 1.5 pad_maximum_fusion.1
  77.5 1.4 all-gather.4.cloned.1.call-done.packed.refs_1_
  79.0 95.9 %shard_map.324 = (bf16[2,8,128,512]{3,2,1,0:T(8,128)(2,1)}, bf16[2,8,128,512]{3,2,1,0:T(8,128)(2,1)}, bf16[2,1024,2048]{2,1,0:T(8,128)(2,1)}, bf16[2,1024,2048]{2,1,0:T(8,128)(2,1)}, bf16[4,1024,512]{2,1,0:T(8,128)(2,1)}) custom-call(bf16[2,8,128,512]{3,2,1,0:T(8,128)(2,1)} %bitcast.85, bf16[4,1024,512]{2,1,0:T(8,128)(2,1)} %all-gather.4.cloned.1.call-done.packed.refs_1_, ...), custom_call_target="tpu_custom_call" | custom-call | flops 1024 | bytes 1024 | tf_op jit(solution)/shard_map/pallas_call | solution.py:703
  174.9 26.4 %shard_map.325 = (f32[4,197,512]{2,1,0:T(8,128)}, bf16[4,197,512]{2,1,0:T(8,128)(2,1)}, bf16[4,197,512]{2,1,0:T(8,128)(2,1)}, f32[4,197,512]{2,1,0:T(8,128)}, bf...) custom-call(f32[4,197,512]{2,1,0:T(8,128)} %get-tuple-element.87.mid, ...), custom_call_target="tpu_custom_call" | custom-call | flops 1024 | bytes 1024 | tf_op jit(solution)/shard_map/pallas_call | solution.py:311
  201.3 1.8 all-gather.8.cloned.1.call-done.packed.refs_1_
  203.1 94.3 %shard_map.326 = (bf16[2,8,128,512]{3,2,1,0:T(8,128)(2,1)}, bf16[2,8,128,512]{3,2,1,0:T(8,128)(2,1)}, bf16[2,1024,2048]{2,1,0:T(8,128)(2,1)}, bf16[2,1024,2048]{2,1,0:T(8,128)(2,1)}, bf16[4,1024,512]{2,1,0:T(8,128)(2,1)}) custom-call(bf16[2,8,128,512]{3,2,1,0:T(8,128)(2,1)} %bitcast.86, bf16[4,1024,512]{2,1,0:T(8,128)(2,1)} %all-gather.8.cloned.1.call-done.packed.refs_1_, ...), custom_call_target="tpu_custom_call" | custom-call | flops 1024 | bytes 1024 | tf_op jit(solution)/shard_map/pallas_call | solution.py:703
  297.4 18.7 %shard_map.327 = (f32[4,197,512]{2,1,0:T(8,128)}, bf16[4,197,128]{2,1,0:T(8,128)(2,1)}, bf16[2048,512]{1,0:T(8,128)(2,1)}) custom-call(f32[4,197,512]{2,1,0:T(8,128)} %get-tuple-element.95.middle, f32[4,197,2]{2,1,0:T(8,128)} %get-tuple-element.96.gates, s32[2,4,197,2]{3,2,1,0:T(8,128)} %get-tuple-element.89.dcol, bf16[2048,512]{1,0:T(8,128)(2,1)} %bitcast.82, ...), custom_call_target="tpu_custom_call" | custom-call | flops 1024 | bytes 1024 | tf_op jit(solution)/shard_map/pallas_call | solution.py:311
  316.1 95.8 %shard_map.328 = (bf16[2,8,128,512]{3,2,1,0:T(8,128)(2,1)}, f32[1024,512]{1,0:T(8,128)}, bf16[4,1,1024,512]{3,2,1,0:T(8,128)(2,1)}, f32[2,1,2048]{2,1,0:T(1,128)}, f32[2,1,512]{2,1,0:T(1,128)}) custom-call(bf16[2,8,128,512]{3,2,1,0:T(8,128)(2,1)} %bitcast.80, bf16[4,1024,512]{2,1,0:T(8,128)(2,1)} %all-gather.8.cloned.1.call-done.packed.refs_1_, ...), custom_call_target="tpu_custom_call" | custom-call | flops 1024 | bytes 1024 | tf_op jit(solution)/shard_map/pallas_call | solution.py:703
  415.3 40.2 %shard_map.329 = (f32[4,197,512]{2,1,0:T(8,128)}, bf16[512,2560]{1,0:T(8,128)(2,1)}, bf16[4,197,128]{2,1,0:T(8,128)(2,1)}, bf16[2048,512]{1,0:T(8,128)(2,1)}) custom-call(f32[4,197,512]{2,1,0:T(8,128)} %copy.113.cotangent.upstream, f32[4,197,512]{2,1,0:T(8,128)} %get-tuple-element.100.rows, f32[4,197,512]{2,1,0:T(8,128)} %get-tuple-element.95.middle, ...), custom_call_target="tpu_custom_call" | custom-call | flops 1024 | bytes 1024 | tf_op jit(solution)/shard_map/pallas_call | solution.py:311
  455.5 96.0 %shard_map.330 = (bf16[2,8,128,512]{3,2,1,0:T(8,128)(2,1)}, f32[1024,512]{1,0:T(8,128)}, bf16[4,1,1024,512]{3,2,1,0:T(8,128)(2,1)}, f32[2,1,2048]{2,1,0:T(1,128)...) custom-call(bf16[2,8,128,512]{3,2,1,0:T(8,128)(2,1)} %bitcast.91, ...), custom_call_target="tpu_custom_call" | custom-call | flops 1024 | bytes 1024 | tf_op jit(solution)/shard_map/pallas_call | solution.py:703
  551.5 1.4 copy-done.3
  552.9 2.2 copy.124
  557.8 27.9 %shard_map.331 = (f32[4,197,512]{2,1,0:T(8,128)}, bf16[512,2560]{1,0:T(8,128)(2,1)}) custom-call(f32[4,197,512]{2,1,0:T(8,128)} %get-tuple-element.117.upstream, f32[4,197,512]{2,1,0:T(8,128)} %copy.106.rows, f32[4,197,512]{2,1,0:T(8,128)} %get-tuple-element.87.middle, bf16[4,197,512]{2,1,0:T(8,128)(2,1)} %get-tuple-element.118.q_ref, ...), custom_call_target="tpu_custom_call" | custom-call | flops 1024 | bytes 1024 | tf_op jit(solution)/shard_map/pallas_call | solution.py:311
  585.7 62.1 %shard_map.332.refs_4_ = bf16[2,128,2560]{2,1,0:T(8,128)(2,1)} custom-call(bf16[4,128,2560]{2,1,0:T(8,128)(2,1)} %bitcast.78, bf16[128,2560]{1,0:T(8,128)(2,1)} %get-tuple-element.142.above), custom_call_target="tpu_custom_call" | custom-call | flops 1024 | bytes 1024 | tf_op jit(solution)/shard_map/pallas_call | solution.py:703
  647.9 7.7 %shard_map.333 = (f32[2,128,512]{2,1,0:T(8,128)}, f32[2,128,512]{2,1,0:T(8,128)}, f32[2,128,512]{2,1,0:T(8,128)}, f32[2,128,512]{2,1,0:T(8,128)}, f32[2,128,16]{...) custom-call(f32[1024,512]{1,0:T(8,128)} %get-tuple-element.137.refs_, ...), custom_call_target="tpu_custom_call" | custom-call | flops 1024 | bytes 1024 | tf_op jit(solution)/shard_map/pallas_call | solution.py:311
  656.8 2.2 copy.125
  (85 shorter events, 16.7 us)
Async XLA Ops:
  7.2 71.8 %all-gather.4.cloned.1.call-start = ((), (), s32[]{:S(2)}) async-start(), calls=%async_computation.2 | async-start | bytes 5242880 | tf_op jit(solution)/shard_map/all_gather | solution.py:1069
  9.7 2.8 copy-start
  13.4 2.3 copy-start.10
  13.5 3.4 copy-start.11
  15.6 159.2 %all-gather.6.cloned.1.call-start = ((), (), s32[]{:S(2)}) async-start(), calls=%async_computation.3 | async-start | bytes 2785280 | tf_op jit(solution)/shard_map/all_gather | solution.py:1068
  48.3 154.8 %all-gather.8.cloned.1.call-start = ((), (), s32[]{:S(2)}) async-start(), calls=%async_computation.4 | async-start | bytes 5242880 | tf_op jit(solution)/shard_map/all_gather | solution.py:1069
  48.9 1.8 copy-start.5
  49.9 507.2 %reduce-scatter.7.cloned.1.call-start = ((), (), s32[]{:S(2)}) async-start(), calls=%async_computation.5 | async-start | bytes 5242880
  72.9 1.4 copy-start.6
  73.8 2.2 copy-start.1
  73.8 2.2 copy-start.2
  411.9 0.7 copy-start.15
  411.9 0.9 copy-start.12
  411.9 236.0 %reduce-scatter.9.cloned.1.call-start = ((), (), s32[]{:S(2)}) async-start(), calls=%async_computation.6 | async-start | bytes 5242880
  414.5 0.7 copy-start.8
  551.5 1.4 copy-start.3
  551.5 3.6 copy-start.16
  551.5 3.8 copy-start.13
  557.1 0.7 copy-start.7
  647.9 8.9 %copy-start.4 = (f32[4,197,512]{2,1,0:T(8,128)S(1)}, f32[4,197,512]{2,1,0:T(8,128)}, u32[]{:S(2)}) copy-start(f32[4,197,512]{2,1,0:T(8,128)} %get-tuple-element.207) | copy-start | bytes 4841476
  655.6 3.4 copy-start.9
  655.6 4.1 copy-start.14
Sparse Core Ops, SparseCore 0:
  15.8 63.1 all-gather.3
  80.8 68.1 all-gather.5
  150.9 52.2 all-gather.7
  412.0 66.9 reduce-scatter.6
  551.6 66.3 reduce-scatter.8

commit v5 on v4

--- a/solution.py
+++ b/solution.py
@@ -18,6 +18,7 @@
 COST = 1024
 VMEM = 56 * 1024 * 1024
 
+MESH = pl.DeviceIdType.MESH
 F32 = jnp.float32
 BF16 = jnp.bfloat16
 
@@ -68,38 +69,14 @@
     return total
 
 
-def spread(dest_rows, sources, outs, first):
-    half = outs[0].shape[0]
-    step = 256
-    length = dest_rows[0].shape[1]
-    for number, out in enumerate(outs):
-        for start in range(0, half, step):
-            slots = lax.broadcasted_iota(jnp.int32, (step, length), 0) + (number * half + start)
-            if len(sources) == 1:
-                hit = (slots == dest_rows[0]) | (slots == dest_rows[1])
-                block = dot(hit.astype(F32).astype(BF16), sources[0])
-            else:
-                block = dot((slots == dest_rows[0]).astype(F32).astype(BF16), sources[0])
-                block = block + dot((slots == dest_rows[1]).astype(F32).astype(BF16), sources[1])
-            block = block.astype(BF16)
-
-            @pl.when(first)
-            def _(out=out, start=start, block=block):
-                out[start : start + step, :] = block
-
-            @pl.when(jnp.logical_not(first))
-            def _(out=out, start=start, block=block):
-                out[start : start + step, :] += block
-
-
 def lane_masks(length):
     lanes = lax.broadcasted_iota(jnp.int32, (length, 2 * HEAD_DIM), 1)
     return (lanes < HEAD_DIM).astype(F32).astype(BF16), (lanes >= HEAD_DIM).astype(F32).astype(BF16)
 
 
 def attend_body(
-    rows, routes_ref, drow_ref, wq, wk, wv, wo, misc,
-    t_ref, q_ref, k_ref, v_ref, o_ref, lse_ref, gates_ref, outs,
+    rows, routes_ref, wq, wk, wv, wo, misc,
+    t_ref, q_ref, k_ref, v_ref, o_ref, lse_ref, gates_ref, hidden_ref,
 ):
     length = rows.shape[0]
     qb, vb, ob, again, ashift, egain, eshift = vectors_of(misc)
@@ -140,8 +117,7 @@
     gate_one = 1.0 / (1.0 + jnp.exp(zero - one))
     gates_ref[0, :, 0:1] = gate_zero
     gates_ref[0, :, 1:2] = gate_one
-    drow = drow_ref[0]
-    spread([drow[0:1, :], drow[1:2, :]], [hidden], outs, pl.program_id(0) == 0)
+    hidden_ref[0] = hidden
 
 
 def combine_body(middle, gates_ref, dcol_ref, back, yzero_ref, yone_ref):
@@ -155,7 +131,7 @@
     return middle + (gates[:, 0:1] * zero + gates[:, 1:2] * one), zero, one
 
 
-def grads_body(upstream, zero, one, gates_ref, routes_ref, drow_ref, dz_ref, outs):
+def grads_body(upstream, zero, one, gates_ref, routes_ref, dz_ref, zero_ref, one_ref):
     length = upstream.shape[0]
     gates = gates_ref[0]
     gate_zero, gate_one = gates[:, 0:1], gates[:, 1:2]
@@ -167,40 +143,34 @@
     dz = jnp.where(lanes == pair_experts[:, 0:1], gate_zero * (grad_zero - along), 0.0)
     dz = dz + jnp.where(lanes == pair_experts[:, 1:2], gate_one * (grad_one - along), 0.0)
     dz_ref[0] = dz.astype(BF16)
-    drow = drow_ref[0]
-    spread(
-        [drow[0:1, :], drow[1:2, :]],
-        [(gate_zero * upstream).astype(BF16), (gate_one * upstream).astype(BF16)],
-        outs,
-        pl.program_id(0) == 0,
-    )
-
-
-def first_kernel(rows, routes, drow, wq, wk, wv, wo, misc, *outs):
-    attend_body(rows[0], routes, drow, wq, wk, wv, wo, misc, *outs[:7], outs[7:])
+    zero_ref[0] = (gate_zero * upstream).astype(BF16)
+    one_ref[0] = (gate_one * upstream).astype(BF16)
+
+
+def first_kernel(rows, routes, wq, wk, wv, wo, misc, *outs):
+    attend_body(rows[0], routes, wq, wk, wv, wo, misc, *outs)
 
 
 def next_kernel(
-    middle, gates, dcol, back, routes, drow, wq, wk, wv, wo, misc, rows_ref, yzero, yone, *outs
+    middle, gates, dcol, back, routes, wq, wk, wv, wo, misc, rows_ref, yzero, yone, *outs
 ):
     rows, _, _ = combine_body(middle[0], gates, dcol, (back,), yzero, yone)
     rows_ref[0] = rows
-    attend_body(rows, routes, drow, wq, wk, wv, wo, misc, *outs[:7], outs[7:])
-
-
-def turn_kernel(middle, gates, dcol, back, cotangent, routes, drow, result, dz, out):
+    attend_body(rows, routes, wq, wk, wv, wo, misc, *outs)
+
+
+def turn_kernel(middle, gates, dcol, back, cotangent, routes, result, dz, zero_ref, one_ref):
     rows, zero, one = combine_body(middle[0], gates, dcol, (back,), None, None)
     result[0] = rows
-    grads_body(cotangent[0], zero, one, gates, routes, drow, dz, (out,))
+    grads_body(cotangent[0], zero, one, gates, routes, dz, zero_ref, one_ref)
 
 
 def back_kernel(
     upstream, rows, middle, q_ref, k_ref, v_ref, o_ref, lse_ref, dz_ref, dcol, came,
     wq, wk, wv, wo, misc, *rest,
 ):
-    bias, *rest = rest
     if len(rest) > 4:
-        yzero, yone, gates_below, routes_below, drow_below, grad_ref, sent, dz_below, out, wgrad, vgrad = rest
+        yzero, yone, gates_below, routes_below, grad_ref, sent, dz_below, zero_ref, one_ref, wgrad, vgrad = rest
     else:
         grad_ref, sent, wgrad, vgrad = rest
     first = pl.program_id(0) == 0
@@ -276,15 +246,15 @@
     grad_ref[0] = grad
     if len(rest) > 4:
         grads_body(
-            grad, yzero[0].astype(F32), yone[0].astype(F32), gates_below, routes_below, drow_below, dz_below,
-            (out,),
+            grad, yzero[0].astype(F32), yone[0].astype(F32), gates_below, routes_below, dz_below,
+            zero_ref, one_ref,
         )
 
     @pl.when(pl.program_id(0) == pl.num_programs(0) - 1)
     def _():
         wgrad[:, 4 * width :] += vgrad[...].T
         sent[:, : 4 * width + MISC] = wgrad[...].astype(BF16)
-        sent[:, 4 * width + MISC :] = bias[...]
+        sent[:, 4 * width + MISC :] = jnp.zeros((width, sent.shape[1] - 4 * width - MISC), BF16)
 
 
 def per_image(array):
@@ -325,11 +295,7 @@
     return (shape, kind, pl.BlockSpec((1, length, columns), lambda i: (i, 0, 0)))
 
 
-def slots_out(slots, width):
-    return [((slots, width), BF16, pl.BlockSpec((slots, width), lambda i: (0, 0)))]
-
-
-def attend_outputs(images, length, width, slots):
+def attend_outputs(images, length, width):
     return [
         images_out(images, length, width, F32),
         images_out(images, length, width, BF16),
@@ -338,16 +304,8 @@
         images_out(images, length, width, BF16),
         images_out(images, length, MISC, F32),
         images_out(images, length, 2, F32),
-    ] + slots_out(slots, width)
-
-
-ROOT_HALF = 0.7071067811865476
-ROOT_TWO_PI_INVERSE = 0.3989422804014327
-MESH = pl.DeviceIdType.MESH
-
-
-def order_of(count):
-    return sorted(range(1, count), key=lambda k: -min(k, count - k))
+        images_out(images, length, width, BF16),
+    ]
 
 
 def greet_all(peers):
@@ -356,6 +314,104 @@
         pl.semaphore_signal(barrier, inc=1, device_id=peer, device_id_type=MESH)
     pl.semaphore_wait(barrier, len(peers))
 
+
+def remote(source, target, send, recv, device):
+    return pltpu.make_async_remote_copy(
+        src_ref=source, dst_ref=target, send_sem=send, recv_sem=recv, device_id=device, device_id_type=MESH
+    )
+
+
+class SharedGather:
+    def __init__(self, mine, out, sems):
+        send, recv, pass_send, pass_recv, own = sems
+        parts, share, _ = out.shape
+        half = share // 2
+        row, me = lax.axis_index("dp"), lax.axis_index("expert")
+        core = lax.rem(me, 2)
+        sibling = {"expert": me + 1 - 2 * core}
+        rows = pl.ds(pl.multiple_of(core * half, half), half)
+        self.fetches, self.hands = [], []
+        for k in range(1, parts):
+            peer = {"dp": lax.rem(row + k, parts)}
+            self.fetches.append(remote(mine.at[rows], out.at[row, rows], send.at[k - 1], recv.at[k - 1], peer))
+            place = out.at[lax.rem(row - k + parts, parts), rows]
+            self.hands.append(remote(place, place, pass_send.at[k - 1], pass_recv.at[k - 1], sibling))
+        self.keep = pltpu.make_async_copy(mine, out.at[row], own)
+
+    def start(self):
+        for copy in self.fetches:
+            copy.start()
+        self.keep.start()
+
+    def finish(self):
+        for fetch, hand in zip(self.fetches, self.hands):
+            fetch.wait_recv()
+            hand.start()
+        for fetch, hand in zip(self.fetches, self.hands):
+            fetch.wait_send()
+            hand.wait()
+        self.keep.wait()
+
+
+class Gather:
+    def __init__(self, parts, mine, place, sems):
+        send, recv, own = sems
+        row = lax.axis_index("dp")
+        self.first, self.second = [], []
+        self.keep = pltpu.make_async_copy(mine, place(row), own)
+
+        def add(group, source, target, peer):
+            n = len(self.first) + len(self.second)
+            group.append(remote(source, target, send.at[n], recv.at[n], {"dp": peer}))
+
+        if parts != 4:
+            for k in range(1, parts):
+                add(self.first, mine, place(row), lax.rem(row + k, parts))
+            return
+        near, far = row + 1 - 2 * lax.rem(row, 2), lax.rem(row + 2, 4)
+        quarter = mine.shape[0] // 4
+        halves = [[slice(n * quarter, (n + 1) * quarter) for n in pair] for pair in ((0, 1), (2, 3))]
+        for rows, peer in ((halves[0], near), (halves[1], far)):
+            for part in rows:
+                add(self.first, mine.at[part], place(row).at[part], peer)
+        for rows, peer, other in ((halves[0], far, near), (halves[1], near, far)):
+            for part in rows:
+                add(self.second, mine.at[part], place(row).at[part], peer)
+            for part in rows:
+                add(self.second, place(other).at[part], place(other).at[part], peer)
+
+    def start(self):
+        for copy in self.first:
+            copy.start()
+        self.keep.start()
+
+    def forward(self):
+        for copy in self.first:
+            copy.wait_recv()
+        for copy in self.second:
+            copy.start()
+
+    def finish(self):
+        for copy in self.second:
+            copy.wait_recv()
+        self.keep.wait()
+
+    def drain(self):
+        for copy in self.first + self.second:
+            copy.wait_send()
+
+
+def gather_sems(parts):
+    count = 12 if parts == 4 else parts - 1
+    return [pltpu.SemaphoreType.DMA((count,)), pltpu.SemaphoreType.DMA((count,)), pltpu.SemaphoreType.DMA]
+
+
+def shared_sems(parts):
+    return [pltpu.SemaphoreType.DMA((parts - 1,))] * 4 + [pltpu.SemaphoreType.DMA]
+
+
+ROOT_HALF = 0.7071067811865476
+ROOT_TWO_PI_INVERSE = 0.3989422804014327
 
 class Swap:
     def __init__(self, sent, arrived, made, back, sems):
@@ -387,11 +443,42 @@
     def own_home(self, j):
         return pltpu.make_async_copy(self.made.at[j, self.me], self.back.at[j, self.me], self.own.at[self.local + j])
 
-    def send_all(self):
+    def send_all(self, sources, drow, layer):
+        chips = self.count // 2
+        capacity, width = self.sent.shape[2:]
+        images, length, _ = sources[0].shape
+
         for j in range(self.local):
-            for k in order_of(self.count):
-                self.outward(j, k, lax.rem(self.me + k, self.count)).start()
-            self.own_out(j).start()
+
+            def fill(turn, carry, j=j):
+                sign = 2 * lax.rem(turn, 2) - 1
+                chip = lax.rem(self.me // 2 + chips // 2 + sign * ((turn + 1) // 2) + chips, chips)
+                first = (j * self.count + 2 * chip) * capacity
+                slots = lax.broadcasted_iota(jnp.int32, (2 * capacity, length), 0) + first
+                total = jnp.zeros((2 * capacity, width), F32)
+                for image in range(images):
+                    dest = drow[layer, image]
+                    hits = [slots == dest[0:1, :], slots == dest[1:2, :]]
+                    if len(sources) == 1:
+                        hits = [hits[0] | hits[1]]
+                    for hit, source in zip(hits, sources):
+                        total = total + dot(hit.astype(F32).astype(BF16), source[image])
+                self.sent[j, pl.ds(2 * chip, 2)] = total.astype(BF16).reshape(2, capacity, width)
+                for core in range(2):
+                    peer = 2 * chip + core
+                    k = lax.rem(peer - self.me + self.count, self.count)
+
+                    @pl.when(peer != self.me)
+                    def _(k=k, peer=peer):
+                        self.outward(j, k, peer).start()
+
+                    @pl.when(peer == self.me)
+                    def _():
+                        self.own_out(j).start()
+
+                return carry
+
+            lax.fori_loop(0, chips, fill, 0)
 
     def chip(self, turn):
         chips = self.count // 2
@@ -445,36 +532,39 @@
     return first, second
 
 
-def expert_kernel(
-    layer, sent, packed, mine, b1, b2, back, arrived_out, g_out, s_out, packed_out,
-    arrived, made, weights, g_stage, s_stage, out_send, out_recv, home_send, home_recv, own, load, stores, last,
-    share_send, share_recv,
-):
+def expert_kernel(layer, with_dense, *refs):
+    if with_dense:
+        *refs, n1, n2, n3, n4, n5 = refs
+        refs = list(refs)
+        dense = SharedGather(refs.pop(7), refs.pop(13), (n1, n2, n3, n4, n5))
+    (
+        hidden, drow, inner_first, outer_mine, mine, b1, b2, back, arrived_out, g_out, s_out, outer_out, packed_out,
+        sent, arrived, made, weights, g_stage, s_stage, out_send, out_recv, home_send, home_recv, own, load, stores, last,
+        *gather_refs,
+    ) = refs
     row = lax.axis_index("dp")
     parts = weights.shape[1]
+    take = outer_mine.shape[0]
+    gathers = [
+        Gather(parts, outer_mine, lambda p: weights.at[0, p, take:], gather_refs[:3]),
+        Gather(parts, mine, lambda p: weights.at[1, p], gather_refs[3:]),
+    ]
     swap = Swap(sent, arrived, made, back, (out_send, out_recv, home_send, home_recv, own))
     local, count, capacity, width = arrived.shape
     chips = count // 2
     rows = 2 * capacity
     ff = g_out.shape[2]
-    loads = [
-        pltpu.make_async_copy(packed, weights.at[0], load.at[0]),
-        pltpu.make_async_copy(mine, weights.at[1, row], load.at[1]),
+    first_load = pltpu.make_async_copy(inner_first, weights.at[0, :, :take], load)
+    first_load.start()
+    swap.greet([{"dp": lax.rem(row + k, parts)} for k in range(1, parts)])
+    gathers[0].start()
+    swap.send_all([hidden], drow, layer)
+    gathers[0].forward()
+    gathers[1].start()
+    gathered = [
+        pltpu.make_async_copy(weights.at[0, :, take:], outer_out, last.at[1]),
+        pltpu.make_async_copy(weights.at[1], packed_out, last.at[2]),
     ]
-    for copy in loads:
-        copy.start()
-    shares = [
-        pltpu.make_async_remote_copy(
-            src_ref=mine, dst_ref=weights.at[1, row], send_sem=share_send.at[k - 1], recv_sem=share_recv.at[k - 1],
-            device_id={"dp": lax.rem(row + k, parts)}, device_id_type=MESH,
-        )
-        for k in range(1, parts)
-    ]
-    swap.greet([{"dp": lax.rem(row + k, parts)} for k in range(1, parts)])
-    swap.send_all()
-    for copy in shares:
-        copy.start()
-    packed_copy = pltpu.make_async_copy(weights.at[1], packed_out, last.at[1])
 
     def kept(j, slot, chip):
         place = pl.ds(pl.multiple_of(chip * rows, rows), rows)
@@ -484,17 +574,23 @@
         )
 
     for j in range(local):
-        loads[j].wait()
-        if j == 1:
-            for copy in shares:
-                copy.wait_recv()
-            packed_copy.start()
+        if j == 0:
+            first_load.wait()
+        gathers[j].finish()
+        gathered[j].start()
         number = layer * local + j
 
         def chip_step(turn, carry, j=j, number=number):
             chip = swap.chip(turn)
             slot = lax.rem(turn, 2)
             swap.wait_chip(j, chip)
+            if j == 0:
+
+                @pl.when(turn == 1)
+                def _():
+                    gathers[1].forward()
+                    if with_dense:
+                        dense.start()
 
             @pl.when(j * chips + turn >= 2)
             def _():
@@ -522,25 +618,29 @@
         lax.fori_loop(0, chips, chip_step, 0)
     final = pltpu.make_async_copy(arrived, arrived_out, last.at[0])
     final.start()
+    if with_dense:
+        dense.finish()
     for slot in range(2):
         for copy in kept(0, slot, 0):
             copy.wait()
     swap.finish()
-    for copy in shares:
-        copy.wait_send()
-    packed_copy.wait()
+    for gather, copy in zip(gathers, gathered):
+        gather.drain()
+        copy.wait()
     final.wait()
 
 
-def expert_back_kernel(with_above, *refs):
+def expert_back_kernel(layer, with_above, *refs):
     if with_above:
         *refs, above_in, above_own, above_send, above_recv, above_load = refs
         refs = list(refs)
-        above, above_sum = refs.pop(6), refs.pop(11)
+        above, above_sum = refs.pop(9), refs.pop(14)
     (
-        sent, packed_first, packed_second, arrived_x, g_in, s_in, back, summed, out, db1, db2,
-        arrived, made, weights, x, du, s_stage, g_stage, first_stage, second_stage, share_out, share_in,
+        zero, one, drow, inner_first, outer_first, packed_second, arrived_x, g_in, s_in, back, summed, out, bias1, bias2,
+        sent, arrived, made, weights, x, du, s_stage, g_stage, first_stage, second_stage, share_out, share_in,
+        db1, db2, db1_in, db2_in,
         out_send, out_recv, home_send, home_recv, own, load, fetch, stores, share_send, share_recv,
+        bias_send, bias_recv,
     ) = refs
     swap = Swap(sent, arrived, made, back, (out_send, out_recv, home_send, home_recv, own))
     row = lax.axis_index("dp")
@@ -553,9 +653,11 @@
     share, take = width // parts, all_rows // 2
     each = FF_BLOCK // take
     loads = [
-        pltpu.make_async_copy(packed, weights.at[j], load.at[j]) for j, packed in enumerate((packed_first, packed_second))
+        pltpu.make_async_copy(inner_first, weights.at[0, :, :take], load.at[0]),
+        pltpu.make_async_copy(packed_second, weights.at[1], load.at[1]),
+        pltpu.make_async_copy(arrived_x, x, load.at[local]),
+        pltpu.make_async_copy(outer_first, weights.at[0, :, take:], load.at[local + 1]),
     ]
-    loads.append(pltpu.make_async_copy(arrived_x, x, load.at[local]))
     for copy in loads:
         copy.start()
 
@@ -590,7 +692,6 @@
     slopes(0, 0).start()
     peers = [{"dp": lax.rem(row + k, parts)} for k in range(1, parts)]
     swap.greet(peers)
-    swap.send_all()
     if with_above:
         above_copies = [
             pltpu.make_async_remote_copy(
@@ -603,6 +704,8 @@
         above_copies.append(pltpu.make_async_copy(above.at[row], above_own, above_load))
         for copy in above_copies:
             copy.start()
+    swap.send_all([zero, one], drow, layer)
+    loads[local + 1].wait()
     for j in range(local):
         loads[j].wait()
         activations(j, 0).start()
@@ -636,7 +739,7 @@
         if j == 0:
             loads[local].wait()
         dy = arrived[j].reshape(count * capacity, width)
-        db2[j] = jnp.sum(dy.astype(F32), axis=0, keepdims=True)
+        db2[j : j + 1, :] = jnp.sum(dy.astype(F32), axis=0, keepdims=True)
         for f in range(blocks):
             cols = slice(f * FF_BLOCK, (f + 1) * FF_BLOCK)
             if f + 1 < blocks:
@@ -650,7 +753,7 @@
                 share_out[:, f * share : (f + 1) * share, :] = grad.reshape(parts, share, width)
             else:
                 first_stage[f % 2] = grad.reshape(parts, share, width)
-            db1[j, :, cols] = jnp.sum(part.astype(F32), axis=0, keepdims=True)
+            db1[j : j + 1, cols] = jnp.sum(part.astype(F32), axis=0, keepdims=True)
             activations(j, f).wait()
             grad = dot_tn(g_stage[f % 2], dy).astype(BF16).reshape(each, take, width)
             if j == 0:
@@ -662,6 +765,16 @@
         if j == 0:
             for k in range(1, parts):
                 share_copy(k).start()
+    part_ff = ff // parts
+    bias_copies = []
+    for k in range(1, parts):
+        place = pl.ds(pl.multiple_of(lax.rem(row + k, parts) * part_ff, part_ff), part_ff)
+        for n, (source, target) in enumerate(((db1.at[:, place], db1_in.at[k - 1]), (db2, db2_in.at[k - 1]))):
+            bias_copies.append(pltpu.make_async_remote_copy(
+                src_ref=source, dst_ref=target, send_sem=bias_send.at[n, k - 1], recv_sem=bias_recv.at[n, k - 1],
+                device_id=peers[k - 1], device_id_type=MESH,
+            ))
+            bias_copies[-1].start()
     if with_above:
         for copy in above_copies:
             copy.wait()
@@ -682,6 +795,14 @@
         return carry
 
     lax.fori_loop(0, all_rows // step, add_up, 0)
+    for copy in bias_copies:
+        copy.wait_recv()
+    total1, total2 = db1[:, pl.ds(pl.multiple_of(row * part_ff, part_ff), part_ff)], db2[...]
+    for k in range(1, parts):
+        total1, total2 = total1 + db1_in[k - 1], total2 + db2_in[k - 1]
+    bias1[...], bias2[...] = total1, total2
+    for copy in bias_copies:
+        copy.wait_send()
     for k in range(1, parts):
         share_copy(k).wait_send()
     for f in range(2):
@@ -713,52 +834,58 @@
     )(*[a for a, _ in inputs])
 
 
-def expert_forward(sent, packed, mine, biases, layer):
+def expert_forward(hidden, drow, shape, inner, outer_mine, mine, biases, dense, layer):
     b1, b2 = biases
-    local, count, capacity, width = sent.shape
+    local, count, capacity, width = shape
     ff = b1.shape[1]
     rows = 2 * capacity
-    parts = packed.shape[0]
+    parts = inner.shape[0]
+    packed = (parts, *mine.shape)
     slots = (local, count * capacity, ff)
-    return expert_call(
-        functools.partial(expert_kernel, layer),
-        [(sent, False), (packed, False), (mine, False), (b1, True), (b2, True)],
-        [
-            (sent.shape, BF16, False), (sent.shape, BF16, False), (slots, BF16, False), (slots, BF16, False),
-            (packed.shape, BF16, False),
-        ],
-        [
-            pltpu.VMEM(sent.shape, BF16), pltpu.VMEM(sent.shape, BF16), pltpu.VMEM((local, *packed.shape), BF16),
-            pltpu.VMEM((2, rows, ff), BF16), pltpu.VMEM((2, rows, ff), BF16),
-        ] + swap_sems(local, count) + [
-            pltpu.SemaphoreType.DMA((local,)), pltpu.SemaphoreType.DMA((2, 2)), pltpu.SemaphoreType.DMA((2,)),
-            pltpu.SemaphoreType.DMA((parts - 1,)), pltpu.SemaphoreType.DMA((parts - 1,)),
-        ],
-        layer,
-    )
-
-
-def expert_backward(sent, weights, arrived, g, s, above, layer):
-    local, count, capacity, width = sent.shape
+    inputs = [(hidden, True), (drow, True), (inner, False), (outer_mine, False), (mine, False), (b1, True), (b2, True)]
+    outputs = [
+        (shape, BF16, False), (shape, BF16, False), (slots, BF16, False), (slots, BF16, False),
+        ((parts, *outer_mine.shape), BF16, False), (packed, BF16, False),
+    ]
+    scratch = [
+        pltpu.VMEM(shape, BF16), pltpu.VMEM(shape, BF16), pltpu.VMEM(shape, BF16),
+        pltpu.VMEM((local, *packed), BF16),
+        pltpu.VMEM((2, rows, ff), BF16), pltpu.VMEM((2, rows, ff), BF16),
+    ] + swap_sems(local, count) + [
+        pltpu.SemaphoreType.DMA, pltpu.SemaphoreType.DMA((2, 2)), pltpu.SemaphoreType.DMA((3,)),
+    ] + gather_sems(parts) * 2
+    if dense is not None:
+        inputs.append((dense, False))
+        outputs.append(((parts, *dense.shape), BF16, False))
+        scratch += shared_sems(parts)
+    return expert_call(functools.partial(expert_kernel, layer, dense is not None), inputs, outputs, scratch, layer)
+
+
+def expert_backward(sources, drow, weights, arrived, g, s, above, layer):
+    shape = arrived.shape
+    local, count, capacity, width = shape
     ff = g.shape[2]
     rows = 2 * capacity
-    parts, all_rows, _ = weights[0].shape
+    parts, all_rows, _ = weights[2].shape
     share, take = width // parts, all_rows // 2
-    inputs = [(a, False) for a in (sent, *weights, arrived, g, s)]
+    inputs = [(a, True) for a in (*sources, drow)] + [(a, False) for a in (*weights, arrived, g, s)]
     outputs = [
-        (sent.shape, BF16, False), ((all_rows, width), F32, True), ((parts, local - 1, all_rows, width), BF16, False),
-        ((local, 1, ff), F32, True), ((local, 1, width), F32, True),
+        (shape, BF16, False), ((all_rows, width), F32, True), ((parts, local - 1, all_rows, width), BF16, False),
+        ((local, ff // parts), F32, True), ((local, width), F32, True),
     ]
     scratch = [
-        pltpu.VMEM(sent.shape, BF16), pltpu.VMEM(sent.shape, BF16),
-        pltpu.VMEM((local, parts, all_rows, width), BF16), pltpu.VMEM(sent.shape, BF16),
+        pltpu.VMEM(shape, BF16), pltpu.VMEM(shape, BF16), pltpu.VMEM(shape, BF16),
+        pltpu.VMEM((local, parts, all_rows, width), BF16), pltpu.VMEM(shape, BF16),
         pltpu.VMEM((count * capacity, ff), BF16), pltpu.VMEM((2, rows, ff), BF16),
         pltpu.VMEM((2, count * capacity, FF_BLOCK), BF16), pltpu.VMEM((2, parts, share, width), BF16),
         pltpu.VMEM((2, FF_BLOCK // take, take, width), BF16),
         pltpu.VMEM((parts, all_rows, width), BF16), pltpu.VMEM((parts - 1, all_rows, width), BF16),
+        pltpu.VMEM((local, ff), F32), pltpu.VMEM((local, width), F32),
+        pltpu.VMEM((parts - 1, local, ff // parts), F32), pltpu.VMEM((parts - 1, local, width), F32),
     ] + swap_sems(local, count) + [
-        pltpu.SemaphoreType.DMA((local + 1,)), pltpu.SemaphoreType.DMA((2, 2)), pltpu.SemaphoreType.DMA((2, 2)),
+        pltpu.SemaphoreType.DMA((local + 2,)), pltpu.SemaphoreType.DMA((2, 2)), pltpu.SemaphoreType.DMA((2, 2)),
         pltpu.SemaphoreType.DMA((parts - 1,)), pltpu.SemaphoreType.DMA((parts - 1,)),
+        pltpu.SemaphoreType.DMA((2, parts - 1)), pltpu.SemaphoreType.DMA((2, parts - 1)),
     ]
     if above is not None:
         inputs.append((above, False))
@@ -767,26 +894,27 @@
             pltpu.VMEM((parts - 1, *above.shape[1:]), BF16), pltpu.VMEM(above.shape[1:], BF16),
             pltpu.SemaphoreType.DMA((parts - 1,)), pltpu.SemaphoreType.DMA((parts - 1,)), pltpu.SemaphoreType.DMA,
         ]
-    return expert_call(
-        functools.partial(expert_back_kernel, above is not None), inputs, outputs, scratch, LAYERS + layer
+    done = expert_call(
+        functools.partial(expert_back_kernel, layer, above is not None), inputs, outputs, scratch, LAYERS + layer
     )
+    return done if above is not None else [*done, None]
 
 
 def prepare_kernel(capacity, owners, *refs):
     squares, (router, *vectors), (inner_bias, outer_bias, routes) = refs[:4], refs[4:12], refs[12:15]
-    out, above, b1, b2, dcol, drow = refs[15:21]
-    mine, turned, inner_low, outer_low = refs[21:25]
-    send, recv, pass_send, pass_recv, b1_send, b1_recv, b2_send, b2_recv, own = refs[25:]
+    tokens_in, (out, above, b1, b2, dcol, drow), tokens_out = refs[15:17], refs[17:23], refs[23:25]
+    mine, turned, inner_low, outer_low, token_ins, token_outs = refs[25:31]
+    sems, (b1_send, b1_recv, b2_send, b2_recv, own, token_load, token_store) = refs[31:36], refs[36:]
     parts, share, _ = out.shape
+    loads = [pltpu.make_async_copy(tokens_in[n], token_ins.at[n], token_load.at[n]) for n in range(2)]
+    stores = [pltpu.make_async_copy(token_outs.at[n], tokens_out[n], token_store.at[n]) for n in range(2)]
     width = squares[0].shape[2]
     experts_all = router.shape[2]
     local, part_ff = inner_bias.shape[1:]
-    half = share // 2
     row, me = lax.axis_index("dp"), lax.axis_index("expert")
-    core = lax.rem(me, 2)
-    sibling = {"expert": me + 1 - 2 * core}
-    rows = pl.ds(pl.multiple_of(core * half, half), half)
+    sibling = {"expert": me + 1 - 2 * lax.rem(me, 2)}
     peers = [{"dp": lax.rem(row + k, parts)} for k in range(1, parts)]
+    gather = SharedGather(mine, out, sems)
 
     def pack(target, layer):
         for n in range(4):
@@ -797,15 +925,6 @@
         target[:, 4 * width :] = turned[...].T.astype(BF16)
         target[:, 4 * width : 4 * width + experts_all] = router[layer].astype(BF16)
 
-    def remote(source, target, send_sem, recv_sem, device):
-        return pltpu.make_async_remote_copy(
-            src_ref=source, dst_ref=target, send_sem=send_sem, recv_sem=recv_sem, device_id=device, device_id_type=MESH
-        )
-
-    def hand(k):
-        place = out.at[lax.rem(row - k + parts, parts), rows]
-        return remote(place, place, pass_send.at[k - 1], pass_recv.at[k - 1], sibling)
-
     pack(mine, 0)
     for layer in range(LAYERS):
         for j in range(local):
@@ -814,20 +933,22 @@
             outer_low[n : n + 1, :] = outer_bias[layer, j : j + 1, :].astype(BF16).astype(F32)
     greet_all([sibling] + peers)
     place = pl.ds(pl.multiple_of(row * part_ff, part_ff), part_ff)
-    fetches = [
-        remote(mine.at[rows], out.at[row, rows], send.at[k], recv.at[k], peers[k]) for k in range(parts - 1)
-    ]
     singles = [
         remote(inner_low, b1.at[:, place], b1_send.at[k], b1_recv.at[k], peers[k]) for k in range(parts - 1)
     ] + [remote(outer_low, b2.at[row], b2_send.at[k], b2_recv.at[k], peers[k]) for k in range(parts - 1)]
     keeps = [
-        pltpu.make_async_copy(mine, out.at[row], own.at[0]),
-        pltpu.make_async_copy(inner_low, b1.at[:, place], own.at[1]),
-        pltpu.make_async_copy(outer_low, b2.at[row], own.at[2]),
+        pltpu.make_async_copy(inner_low, b1.at[:, place], own.at[0]),
+        pltpu.make_async_copy(outer_low, b2.at[row], own.at[1]),
     ]
-    for copy in fetches + singles + keeps:
+    gather.start()
+    for copy in singles + keeps + loads:
         copy.start()
     pack(above, 1)
+    for n in range(2):
+        loads[n].wait()
+        for image in range(routes.shape[1]):
+            token_outs[n, image] = token_ins[n, :, image, :]
+        stores[n].start()
 
     length = routes.shape[2]
     lanes = lax.broadcasted_iota(jnp.int32, (length, MISC), 1)
@@ -853,17 +974,12 @@
             both = jnp.where(lanes == 0, dests[0], jnp.where(lanes == 1, dests[1], 0.0))
             drow[layer, image] = both.T[0:2, :].astype(jnp.int32)
 
-    for k in range(1, parts):
-        fetches[k - 1].wait_recv()
-        hand(k).start()
-    for k in range(1, parts):
-        fetches[k - 1].wait_send()
-        hand(k).wait()
-    for copy in singles + keeps:
+    gather.finish()
+    for copy in singles + keeps + stores:
         copy.wait()
 
 
-def prepare(squares, router, vectors, inner_bias, outer_bias, routes, parts, owners, number):
+def prepare(squares, router, vectors, inner_bias, outer_bias, routes, tokens, parts, owners, number):
     layers, share, width = squares[0].shape
     experts_all = router.shape[2]
     local, part_ff = inner_bias.shape[1:]
@@ -871,46 +987,55 @@
     capacity = (10 * images * length // (4 * experts_all) + 7) // 8 * 8
     columns = 4 * width + MISC
     count = layers * local
-    sems = [pltpu.SemaphoreType.DMA((parts - 1,))] * 8 + [pltpu.SemaphoreType.DMA((3,))]
+    sems = shared_sems(parts) + [pltpu.SemaphoreType.DMA((parts - 1,))] * 4 + [pltpu.SemaphoreType.DMA((2,))] * 3
     inputs = [*squares, router, *vectors, inner_bias, outer_bias, routes]
-    out, above, b1, b2, dcol, drow = expert_call(
-        functools.partial(prepare_kernel, capacity, owners), [(a, True) for a in inputs],
+    turned = [jnp.transpose(item, (1, 0, 2)) for item in tokens]
+    out, above, b1, b2, dcol, drow, *tokens = expert_call(
+        functools.partial(prepare_kernel, capacity, owners), [(a, True) for a in inputs] + [(a, False) for a in turned],
         [
             ((parts, share, columns), BF16, False), ((share, columns), BF16, True),
             ((count, part_ff * parts), F32, False), ((parts, count, share), F32, False),
             ((layers, images, length, 2), jnp.int32, True), ((layers, images, 2, length), jnp.int32, True),
+            ((images, length, width), F32, False), ((images, length, width), F32, False),
         ],
         [
             pltpu.VMEM((share, columns), BF16), pltpu.VMEM((MISC, share), F32),
             pltpu.VMEM((count, part_ff), F32), pltpu.VMEM((count, share), F32),
+            pltpu.VMEM((2, length, images, width), F32), pltpu.VMEM((2, images, length, width), F32),
         ] + sems,
         number,
     )
     b2 = jnp.transpose(b2, (1, 0, 2)).reshape(count, width)
-    return out.reshape(width, columns), above, (b1, b2), dcol, drow, capacity
+    return out.reshape(width, columns), above, (b1, b2), dcol, drow, capacity, tokens
+
+
+def settle_widths(columns, chips):
+    blocks = columns // (MISC * chips)
+    wide = (blocks + 1) // 2 * MISC
+    return wide, columns // chips - wide
 
 
 def settle_kernel(
-    grads, above, final, own, paired, own_above, paired_above, scattered, total, chips_in,
-    pair_send, pair_recv, local, dp_send, dp_recv, out_send, out_recv, back_send, back_recv, pass_send, pass_recv,
+    grads, above, final, own, paired, total, chips_in, dp_in, total_b, chips_in_b, dp_in_b,
+    pair_send, pair_recv, local, out_send, out_recv, dp_send, dp_recv, out_send_b, out_recv_b, dp_send_b, dp_recv_b,
+    back_send, back_recv, pass_send, pass_recv,
 ):
     parts, share, columns = grads.shape
     half = share // 2
     row, me = lax.axis_index("dp"), lax.axis_index("expert")
     core, chip = lax.rem(me, 2), me // 2
     chips = chips_in.shape[0] + 1
-    block = columns // chips
+    wide, narrow = settle_widths(columns, chips)
+    split = chips * wide
     sibling = {"expert": me + 1 - 2 * core}
     mine = pl.ds(pl.multiple_of(core * half, half), half)
     other = pl.ds(pl.multiple_of((1 - core) * half, half), half)
 
-    def remote(source, target, send, recv, device):
-        return pltpu.make_async_remote_copy(
-            src_ref=source, dst_ref=target, send_sem=send, recv_sem=recv, device_id=device, device_id_type=MESH
-        )
-
     def cols(number):
-        return pl.ds(pl.multiple_of(number * block, block), block)
+        return pl.ds(pl.multiple_of(number * wide, MISC), wide)
+
+    def cols_b(number, start):
+        return pl.ds(pl.multiple_of(start + number * narrow, MISC), narrow)
 
     def chip_at(k):
         return lax.rem(chip + k + chips, chips)
@@ -919,58 +1044,88 @@
     chip_peers = [{"expert": 2 * chip_at(k) + core} for k in range(1, chips)]
     greet_all([sibling] + dp_peers + chip_peers)
 
-    pairs, locals_ = [], []
-    for i in range(parts):
-        part = lax.rem(row + 1 + i, parts)
-        pairs.append(remote(grads.at[part, other], paired.at[part], pair_send.at[i], pair_recv.at[i], sibling))
-        locals_.append(pltpu.make_async_copy(grads.at[part, mine], own.at[part], local.at[i]))
-    pairs.append(remote(above.at[other], paired_above, pair_send.at[parts], pair_recv.at[parts], sibling))
-    locals_.append(pltpu.make_async_copy(above.at[mine], own_above, local.at[parts]))
-    for pair, keep in zip(pairs, locals_):
-        pair.start()
-        keep.start()
+    order = [lax.rem(row + 1 + i, parts) for i in range(parts)]
+    pairs, keeps = [], []
+    for i in range(parts + 1):
+        source = grads.at[order[i]] if i < parts else above
+        pairs.append(remote(source.at[other], paired.at[i], pair_send.at[i], pair_recv.at[i], sibling))
+        keeps.append(pltpu.make_async_copy(source.at[mine], own.at[i], local.at[i]))
+        pairs[i].start()
+        keeps[i].start()
+    outs, scatters_b = [], []
+    for i in range(parts + 1):
+        pairs[i].wait_recv()
+        keeps[i].wait()
+        own[i] = (own[i].astype(F32) + paired[i].astype(F32)).astype(BF16)
+        if i < parts - 1:
+            scatters_b.append(
+                remote(own.at[i, :, split:], dp_in_b.at[i], dp_send_b.at[i], dp_recv_b.at[i], dp_peers[i])
+            )
+            scatters_b[i].start()
+        outs.append([
+            remote(
+                own.at[i, :, cols(chip_at(k))], chips_in.at[k - 1, i], out_send.at[k - 1, i], out_recv.at[k - 1, i],
+                chip_peers[k - 1],
+            )
+            for k in range(1, chips)
+        ])
+        for copy in outs[i]:
+            copy.start()
+    value = own[parts - 1, :, split:].astype(F32)
+    for i in range(parts - 1):
+        scatters_b[i].wait_recv()
+        value = value + dp_in_b[i].astype(F32)
+    total_b[0] = value.astype(BF16)
+    total_b[1] = own[parts, :, split:]
+    outs_b = [
+        remote(
+            total_b.at[:, :, cols_b(chip_at(k), 0)], chips_in_b.at[k - 1], out_send_b.at[k - 1], out_recv_b.at[k - 1],
+            chip_peers[k - 1],
+        )
+        for k in range(1, chips)
+    ]
+    for copy in outs_b:
+        copy.start()
     scatters = []
-    for i in range(parts):
-        part = lax.rem(row + 1 + i, parts)
-        pairs[i].wait_recv()
-        locals_[i].wait()
-        own[part] = (own[part].astype(F32) + paired[part].astype(F32)).astype(BF16)
-        if i + 1 < parts:
-            scatters.append(remote(own.at[part], scattered.at[i], dp_send.at[i], dp_recv.at[i], dp_peers[i]))
+    for i in range(parts + 1):
+        value = own[i, :, cols(chip)].astype(F32)
+        for k in range(1, chips):
+            outs[i][k - 1].wait_recv()
+            value = value + chips_in[k - 1, i].astype(F32)
+        if i < parts - 1:
+            total[i] = value.astype(BF16)
+            scatters.append(remote(total.at[i], dp_in.at[i], dp_send.at[i], dp_recv.at[i], dp_peers[i]))
             scatters[i].start()
-    pairs[parts].wait_recv()
-    locals_[parts].wait()
-    total[1] = (own_above[...].astype(F32) + paired_above[...].astype(F32)).astype(BF16)
-    value = own[row].astype(F32)
+        elif i == parts - 1:
+            kept = value
+        else:
+            final[1, mine, cols(chip)] = value.astype(BF16)
+    value = total_b[:, :, cols_b(chip, 0)].astype(F32)
+    for k in range(1, chips):
+        outs_b[k - 1].wait_recv()
+        value = value + chips_in_b[k - 1].astype(F32)
+    final[:, mine, cols_b(chip, split)] = value.astype(BF16)
     for i in range(parts - 1):
         scatters[i].wait_recv()
-        value = value + scattered[i].astype(F32)
-    total[0] = value.astype(BF16)
-    outs = []
+        kept = kept + dp_in[i].astype(F32)
+    final[0, mine, cols(chip)] = kept.astype(BF16)
+
+    def places(number):
+        return [final.at[:, mine, cols(number)], final.at[:, mine, cols_b(number, split)]]
+
+    backs, hands = [], []
+    for n, place in enumerate(places(chip)):
+        for k in range(1, chips):
+            backs.append(remote(place, place, back_send.at[n, k - 1], back_recv.at[n, k - 1], chip_peers[k - 1]))
+            backs[-1].start()
+        hands.append(remote(place, place, pass_send.at[n, 0], pass_recv.at[n, 0], sibling))
+        hands[-1].start()
     for k in range(1, chips):
-        outs.append(remote(
-            total.at[:, :, cols(chip_at(k))], chips_in.at[k - 1], out_send.at[k - 1], out_recv.at[k - 1],
-            chip_peers[k - 1],
-        ))
-        outs[-1].start()
-    value = total[:, :, cols(chip)].astype(F32)
-    for k in range(1, chips):
-        outs[k - 1].wait_recv()
-        value = value + chips_in[k - 1].astype(F32)
-    final[:, mine, cols(chip)] = value.astype(BF16)
-    backs, hands = [], []
-    place = final.at[:, mine, cols(chip)]
-    for k in range(1, chips):
-        backs.append(remote(place, place, back_send.at[k - 1], back_recv.at[k - 1], chip_peers[k - 1]))
-        backs[-1].start()
-    hands.append(remote(place, place, pass_send.at[0], pass_recv.at[0], sibling))
-    hands[0].start()
-    for k in range(1, chips):
-        backs[k - 1].wait_recv()
-        place = final.at[:, mine, cols(chip_at(-k))]
-        hands.append(remote(place, place, pass_send.at[k], pass_recv.at[k], sibling))
-        hands[k].start()
-    for copy in pairs + scatters + outs + backs:
+        for n, place in enumerate(places(chip_at(-k))):
+            backs[n * (chips - 1) + k - 1].wait_recv()
+            hands.append(remote(place, place, pass_send.at[n, k], pass_recv.at[n, k], sibling))
+            hands[-1].start()
+    for copy in pairs + [copy for group in outs for copy in group] + outs_b + scatters + scatters_b + backs:
         copy.wait_send()
     for copy in hands:
         copy.wait()
@@ -979,15 +1134,19 @@
 def settle_dense(grads, above, chips, number):
     parts, share, columns = grads.shape
     half = share // 2
-    quarter = pltpu.VMEM((half, columns), BF16)
-    sems = [parts + 1] * 3 + [parts - 1] * 2 + [chips - 1] * 4 + [chips] * 2
+    halves = pltpu.VMEM((parts + 1, half, columns), BF16)
+    wide, narrow = settle_widths(columns, chips)
+    dp_in = pltpu.VMEM((parts - 1, half, wide), BF16)
+    rest = chips * narrow
+    sems = [(parts + 1,)] * 3 + [(chips - 1, parts + 1)] * 2 + [(parts - 1,)] * 2
+    sems += [(chips - 1,)] * 2 + [(parts - 1,)] * 2 + [(2, chips - 1)] * 2 + [(2, chips)] * 2
     return expert_call(
         settle_kernel, [(grads, False), (above, False)], [((2, share, columns), BF16, True)],
         [
-            pltpu.VMEM((parts, half, columns), BF16), pltpu.VMEM((parts, half, columns), BF16), quarter, quarter,
-            pltpu.VMEM((parts - 1, half, columns), BF16), pltpu.VMEM((2, half, columns), BF16),
-            pltpu.VMEM((chips - 1, 2, half, columns // chips), BF16),
-        ] + [pltpu.SemaphoreType.DMA((n,)) for n in sems],
+            halves, halves, dp_in, pltpu.VMEM((chips - 1, parts + 1, half, wide), BF16), dp_in,
+            pltpu.VMEM((2, half, rest), BF16), pltpu.VMEM((chips - 1, 2, half, narrow), BF16),
+            pltpu.VMEM((parts - 1, half, rest), BF16),
+        ] + [pltpu.SemaphoreType.DMA(n) for n in sems],
         number,
     )[0]
 
@@ -995,7 +1154,7 @@
 def unpack_kernel(*refs):
     count = 2 * LAYERS
     pieces, both = refs[:count], refs[count]
-    squares, router, vectors, biases, inner, outer = refs[count + 1 : count + 5], *refs[count + 5 :]
+    squares, router, vectors, inner, outer = refs[count + 1 : count + 5], *refs[count + 5 :]
     layer = pl.program_id(0)
     share = both.shape[1]
     width = squares[0].shape[2]
@@ -1005,7 +1164,6 @@
     router[0] = misc[:, : router.shape[2]]
     turned = misc.T
     vectors[0] = turned[VEC_AT : VEC_AT + 8, :]
-    biases[0] = both[0, :, 4 * width + MISC :].astype(F32)
     blocks = inner.shape[3] // FF_BLOCK
 
     for number in range(LAYERS):
@@ -1030,7 +1188,7 @@
         unpack_kernel, (layers,),
         [(p, whole(p)) for p in pieces] + [(both, pl.BlockSpec((1, share, columns), lambda i: (i, 0, 0)))],
         [by_layer(share, width)] * 4 + [
-            by_layer(share, experts_all), by_layer(8, share), by_layer(share, columns - 4 * width - MISC),
+            by_layer(share, experts_all), by_layer(8, share),
             by_layer(local, share, ff), by_layer(local, take, width),
         ],
     )
@@ -1051,22 +1209,21 @@
     tokens = count * length
     squares = (query_weight, key_weight, value_weight, output_weight)
     vectors = (query_bias, value_bias, output_bias, attend_gain, attend_shift, expert_gain, expert_shift)
-    bias_columns = ff // width + 1
-    columns = 4 * width + MISC + experts_all * bias_columns
-    columns = -(-columns // (MISC * (owners // 2))) * MISC * (owners // 2)
-    bias_room = columns - 4 * width - MISC
-
-    mine = []
+    columns = -(-(4 * width + MISC) // (MISC * (owners // 2))) * MISC * (owners // 2)
+
+    inner_mine, outer_mine, mine = [], [], []
     for layer in range(LAYERS):
-        for j in range(local):
-            first = inner_weight[layer, j].reshape(share, ff // FF_BLOCK, FF_BLOCK)
-            first = jnp.transpose(first, (1, 0, 2)).reshape(ff // parts, width)
-            mine.append(jnp.concatenate([first, outer_weight[layer, j]], axis=0).astype(BF16))
-    dense, above, expert_biases, dcol, drow, capacity = prepare(
-        squares, router_weight, vectors, inner_bias, outer_bias, routes, parts, owners, 2 * LAYERS
+        first = inner_weight[layer].reshape(local, share, ff // FF_BLOCK, FF_BLOCK)
+        first = jnp.transpose(first, (0, 2, 1, 3)).reshape(local, ff // parts, width).astype(BF16)
+        second = outer_weight[layer].astype(BF16)
+        inner_mine.append(first[0])
+        outer_mine.append(second[0])
+        mine.append(jnp.concatenate([first[1], second[1]], axis=0))
+    dense, above, expert_biases, dcol, drow, capacity, (images, cotangent) = prepare(
+        squares, router_weight, vectors, inner_bias, outer_bias, routes, (images, cotangent), parts, owners, 2 * LAYERS
     )
-    packed = [dense, lax.all_gather(above, "dp", axis=0, tiled=True)]
-    firsts = [lax.all_gather(mine[layer * local], "dp", axis=0, tiled=False) for layer in range(LAYERS)]
+    packed = [dense]
+    firsts = [lax.all_gather(item, "dp", axis=0, tiled=False) for item in inner_mine]
     slots = experts_all * capacity
     dense_flops = 8 * tokens * width * width + 4 * tokens * slots * width
 
@@ -1075,8 +1232,8 @@
     rows = images
     for layer in range(LAYERS):
         weights = [(packed[layer], s) for s in packed_specs(packed[layer])]
-        routing = [(routes, per_layer(routes, layer)), (drow, per_layer(drow, layer))]
-        outputs = attend_outputs(count, length, width, slots)
+        routing = [(routes, per_layer(routes, layer))]
+        outputs = attend_outputs(count, length, width)
         if layer == 0:
             done = call(
                 first_kernel, (count,), [(rows, per_image(rows))] + routing + weights, outputs, flops=dense_flops
@@ -1103,77 +1260,70 @@
             done = done[3:]
             before["picked"] = picked
         middle, queries, keys, values, context, sums, gates = done[:7]
-        sent = done[7].reshape(local, owners, capacity, width)
-        back, arrived, g, s, second = expert_forward(
-            sent, firsts[layer], mine[layer * local + 1], expert_biases, layer
+        back, arrived, g, s, outer, second, *dense = expert_forward(
+            done[7], drow, (local, owners, capacity, width), firsts[layer], outer_mine[layer], mine[layer], expert_biases,
+            above if layer == 0 else None, layer,
         )
+        packed += [item.reshape(width, item.shape[2]) for item in dense]
         back = back.reshape(slots, width)
         saved.append({
             "rows": rows, "middle": middle, "attend": (queries, keys, values, context, sums), "gates": gates,
-            "experts": (arrived, g, s), "weights": (firsts[layer], second),
+            "experts": (arrived, g, s), "weights": (firsts[layer], outer, second),
         })
 
     last = saved[-1]
-    result, dz, sent = call(
+    result, dz, *sources = call(
         turn_kernel, (count,),
         [(last["middle"], per_image(last["middle"])), (last["gates"], per_image(last["gates"]))]
         + [(dcol, per_layer(dcol, LAYERS - 1)), (back, whole(back))]
-        + [(cotangent, per_image(cotangent)), (routes, per_layer(routes, LAYERS - 1)), (drow, per_layer(drow, LAYERS - 1))],
-        [images_out(count, length, width, F32), images_out(count, length, MISC, BF16)] + slots_out(slots, width),
+        + [(cotangent, per_image(cotangent)), (routes, per_layer(routes, LAYERS - 1))],
+        [images_out(count, length, width, F32), images_out(count, length, MISC, BF16)]
+        + [images_out(count, length, width, BF16)] * 2,
         flops=dense_flops,
     )
     upstream = cotangent
+    bias_grads = [None] * LAYERS
     finished = []
     waiting = []
     wgrad = None
     for layer in reversed(range(LAYERS)):
         kept = saved[layer]
-        sent = sent.reshape(local, owners, capacity, width)
-        came, shares, grads, db1, db2, *above = expert_backward(
-            sent, kept["weights"], *kept["experts"], wgrad, layer
+        came, shares, grads, *biases, above = expert_backward(
+            sources, drow, kept["weights"], *kept["experts"], wgrad, layer
         )
         came = came.reshape(slots, width)
         came, waiting = lax.optimization_barrier((came, waiting))
         finished += waiting
         waiting = [shares, lax.psum_scatter(grads, "dp", scatter_dimension=0, tiled=False)]
-        own = [
-            jnp.concatenate([db1[j].reshape(width, ff // width), db2[j].reshape(width, 1)], axis=1)
-            for j in range(local)
-        ]
-        first_column = lax.axis_index("expert") * (local * bias_columns)
-        bias = lax.dynamic_update_slice(
-            jnp.zeros((width, bias_room), F32), jnp.concatenate(own, axis=1), (0, first_column)
-        ).astype(BF16)
+        bias_grads[layer] = biases
         weights = [(packed[layer], s) for s in packed_specs(packed[layer])]
         inputs = [upstream, kept["rows"], kept["middle"], *kept["attend"], dz]
         inputs = [(a, per_image(a)) for a in inputs]
         inputs += [(dcol, per_layer(dcol, layer)), (came, whole(came))] + weights
-        inputs += [(bias, whole(bias))]
         outputs = [
             images_out(count, length, width, F32),
             (
-                (width, 4 * width + MISC + bias_room), BF16,
-                pl.BlockSpec((width, 4 * width + MISC + bias_room), lambda i: (0, 0)),
+                (width, columns), BF16,
+                pl.BlockSpec((width, columns), lambda i: (0, 0)),
             ),
         ]
         if layer > 0:
             below = saved[layer - 1]
             inputs += [(a, per_image(a)) for a in (*below["picked"], below["gates"])]
-            inputs += [(a, per_layer(a, layer - 1)) for a in (routes, drow)]
-            outputs += [images_out(count, length, MISC, BF16)] + slots_out(slots, width)
+            inputs.append((routes, per_layer(routes, layer - 1)))
+            outputs += [images_out(count, length, MISC, BF16)] + [images_out(count, length, width, BF16)] * 2
         done = call(
             back_kernel, (count,), inputs, outputs,
             [pltpu.VMEM((width, 4 * width + MISC), F32), pltpu.VMEM((MISC, width), F32)], flops=3 * dense_flops,
         )
         upstream, wgrad = done[:2]
         if layer > 0:
-            dz, sent = done[2:]
+            dz, *sources = done[2:]
         wgrad = wgrad.reshape(parts, share, columns)
-    both = settle_dense(wgrad, above[0], owners // 2, 2 * LAYERS + 1)
+    both = settle_dense(wgrad, above, owners // 2, 2 * LAYERS + 1)
     pieces = [waiting[0], waiting[1][0], finished[0], finished[1][0]]
-    *squares, router, vectors, biases, inner, outer = unpack(pieces, both, local, ff, experts_all)
-    own = lax.dynamic_slice_in_dim(biases, lax.axis_index("expert") * (local * bias_columns), local * bias_columns, 2)
-    own = jnp.transpose(own.reshape(LAYERS, share, local, bias_columns), (0, 2, 1, 3))
+    *squares, router, vectors, inner, outer = unpack(pieces, both, local, ff, experts_all)
+    outer_bias_grad = jnp.stack([b[1] for b in bias_grads])
     return (
         result,
         upstream,
@@ -1181,9 +1331,9 @@
         router,
         *[vectors[:, n] for n in range(7)],
         inner,
-        own[..., :-1].reshape(LAYERS, local, ff // parts),
+        jnp.stack([b[0] for b in bias_grads]),
         outer,
-        own[..., -1],
+        lax.dynamic_slice_in_dim(outer_bias_grad, lax.axis_index("dp") * share, share, 2),
     )
 
 

time: 674 us -> 618 us (0.917)
  Pallas kernels: 616 us -> 577 us
  local copies, waits for them, and re-layouts: 26.3 us -> 16.1 us
    pallas_call x6, Pallas kernels: 141 us -> 104 us  [call(): pl.pallas_call(body, grid=grid, in_specs=[s for _, s in inputs], out_spec...]
    unnamed x42 -> x23, local copies, waits for them, and re-layouts: 16.9 us -> 9.41 us
  transfers between devices with their start and end apart: 5 -> 4, of which waited for: 2 -> 0; matrix products, arithmetic and copies ran while one was open for 2% -> 2% of each run, Pallas kernels for 60% -> 60%
where the time goes in v5:
time: 618 us; the launch traced here: 613 us
  Pallas kernels  577 us (93%)
  local copies, waits for them, and re-layouts  16.1 us (3%)
  between operations  14.3 us (2%)
    pallas_call x6, Pallas kernels, expert_call(): pl.pallas_call(body, in_specs=[spec(held) for _, held in inputs], out_spe...  473 us
    pallas_call x6, Pallas kernels, call(): pl.pallas_call(body, grid=grid, in_specs=[s for _, s in inputs], out_spec...  104 us
  transfers between devices with their start and end apart: 4, of which 0 were waited for; matrix products, arithmetic and copies ran while one was open for 2% of the time, Pallas kernels for 60%

profile of v5, /device:TPU:0, one launch (start us, length us, event | category | flops | bytes accessed | tf_op | source)
XLA Modules:
  0.0 613.4 jit_solution(13253865785718898733)
XLA Ops:
  7.2 2.5 convert.8
  11.0 0.9 fusion.3
  13.0 0.9 fusion.2
  14.7 1.3 copy.49.refs_14_.routes.rest_3_
  16.0 28.2 %shard_map.322 = (bf16[4,128,2176]{2,1,0:T(8,128)(2,1)}, bf16[128,2176]{1,0:T(8,128)(2,1)}, f32[4,2048]{1,0:T(4,128)}, f32[4,4,128]{2,1,0:T(4,128)}, s32[2,4,197...) custom-call(f32[2,128,512]{2,1,0:T(8,128)} %refs_0_.1, ...), custom_call_target="tpu_custom_call" | custom-call | flops 1024 | bytes 1024 | tf_op jit(solution)/shard_map/pallas_call | solution.py:824
  44.2 12.2 %shard_map.323 = (f32[4,197,512]{2,1,0:T(8,128)}, bf16[4,197,512]{2,1,0:T(8,128)(2,1)}, bf16[4,197,512]{2,1,0:T(8,128)(2,1)}, bf16[4,197,512]{2,1,0:T(8,128)(2,1...) custom-call(f32[4,197,512]{2,1,0:T(8,128)} %get-tuple-element.91.row, ...), custom_call_target="tpu_custom_call" | custom-call | flops 1024 | bytes 1024 | tf_op jit(solution)/shard_map/pallas_call | solution.py:281
  56.7 1.2 slice_bitcast_fusion
  57.9 1.0 pad_maximum_fusion.refs_4_
  58.9 1.0 pad_maximum_fusion.1.refs_4_
  60.0 104.1 %shard_map.324 = (bf16[2,8,128,512]{3,2,1,0:T(8,128)(2,1)}, bf16[2,8,128,512]{3,2,1,0:T(8,128)(2,1)}, bf16[2,1024,2048]{2,1,0:T(8,128)(2,1)}, bf16[2,1024,2048]{...) custom-call(bf16[4,197,512]{2,1,0:T(8,128)(2,1)} %get-tuple-element., ...), custom_call_target="tpu_custom_call" | custom-call | flops 1024 | bytes 1024 | tf_op jit(solution)/shard_map/pallas_call | solution.py:824
  164.0 17.3 %shard_map.325 = (f32[4,197,512]{2,1,0:T(8,128)}, bf16[4,197,512]{2,1,0:T(8,128)(2,1)}, bf16[4,197,512]{2,1,0:T(8,128)(2,1)}, f32[4,197,512]{2,1,0:T(8,128)}, bf...) custom-call(f32[4,197,512]{2,1,0:T(8,128)} %get-tuple-element.93.mid, ...), custom_call_target="tpu_custom_call" | custom-call | flops 1024 | bytes 1024 | tf_op jit(solution)/shard_map/pallas_call | solution.py:281
  181.4 95.3 %shard_map.326 = (bf16[2,8,128,512]{3,2,1,0:T(8,128)(2,1)}, bf16[2,8,128,512]{3,2,1,0:T(8,128)(2,1)}, bf16[2,1024,2048]{2,1,0:T(8,128)(2,1)}, bf16[2,1024,2048]{...) custom-call(bf16[4,197,512]{2,1,0:T(8,128)(2,1)} %get-tuple-element.105.refs_0_, ...), custom_call_target="tpu_custom_call" | custom-call | flops 1024 | bytes 1024 | tf_op jit(solution)/shard_map/pallas_call | solution.py:824
  276.7 8.9 %shard_map.327 = (f32[4,197,512]{2,1,0:T(8,128)}, bf16[4,197,128]{2,1,0:T(8,128)(2,1)}, bf16[4,197,512]{2,1,0:T(8,128)(2,1)}, bf16[4,197,512]{2,1,0:T(8,128)(2,1)}) custom-call(f32[4,197,512]{2,1,0:T(8,128)} %get-tuple-element.103.middle, f32[4,197,2]{2,1,0:T(8,128)} %get-tuple-element.104.gates, s32[2,4,197,2]{3,2,1,0:T(8,128)} %get-tuple-element.95.dcol, ...), custom_call_target="tpu_custom_call" | custom-call | flops 1024 | bytes 1024 | tf_op jit(solution)/shard_map/pallas_call | solution.py:281
  285.7 97.7 %shard_map.328 = (bf16[2,8,128,512]{3,2,1,0:T(8,128)(2,1)}, f32[1024,512]{1,0:T(8,128)}, bf16[4,1,1024,512]{3,2,1,0:T(8,128)(2,1)}, f32[2,512]{1,0:T(2,128)}, f32[2,512]{1,0:T(2,128)}) custom-call(bf16[4,197,512]{2,1,0:T(8,128)(2,1)} %get-tuple-element.116.refs_0_, bf16[4,197,512]{2,1,0:T(8,128)(2,1)} %get-tuple-element.117.refs_1_, ...), custom_call_target="tpu_custom_call" | custom-call | flops 1024 | bytes 1024 | tf_op jit(solution)/shard_map/pallas_call | solution.py:824
  383.5 29.6 %shard_map.329 = (f32[4,197,512]{2,1,0:T(8,128)}, bf16[512,2560]{1,0:T(8,128)(2,1)}, bf16[4,197,128]{2,1,0:T(8,128)(2,1)}, bf16[4,197,512]{2,1,0:T(8,128)(2,1)}, bf16[4,197,512]{2,1,0:T(8,128)(2,1)}) custom-call(f32[4,197,512]{2,1,0:T(8,128)} %get-tuple-element.107.cotangent.upstream, f32[4,197,512]{2,1,0:T(8,128)} %get-tuple-element.109.rows, ...), custom_call_target="tpu_custom_call" | custom-call | flops 1024 | bytes 1024 | tf_op jit(solution)/shard_map/pallas_call | solution.py:281
  413.0 98.0 %shard_map.330 = (bf16[2,8,128,512]{3,2,1,0:T(8,128)(2,1)}, f32[1024,512]{1,0:T(8,128)}, bf16[4,1,1024,512]{3,2,1,0:T(8,128)(2,1)}, f32[2,512]{1,0:T(2,128)}, f3...) custom-call(bf16[4,197,512]{2,1,0:T(8,128)(2,1)} %get-tuple-element.133.refs_0_, ...), custom_call_target="tpu_custom_call" | custom-call | flops 1024 | bytes 1024 | tf_op jit(solution)/shard_map/pallas_call | solution.py:824
  511.2 1.4 copy-done.1
  512.5 2.2 copy.56
  515.9 28.7 %shard_map.331 = (f32[4,197,512]{2,1,0:T(8,128)}, bf16[512,2560]{1,0:T(8,128)(2,1)}) custom-call(f32[4,197,512]{2,1,0:T(8,128)} %get-tuple-element.126.upstream, f32[4,197,512]{2,1,0:T(8,128)} %get-tuple-element.91.rows, f32[4,197,512]{2,1,0:T(8,128)} %get-tuple-element.93.middle, bf16[4,197,512]{2,1,0:T(8,128)(2,1)} %get-tuple-element.127.q_ref, ...), custom_call_target="tpu_custom_call" | custom-call | flops 1024 | bytes 1024 | tf_op jit(solution)/shard_map/pallas_call | solution.py:281
  544.6 49.2 %shard_map.332.refs_4_ = bf16[2,128,2560]{2,1,0:T(8,128)(2,1)} custom-call(bf16[4,128,2560]{2,1,0:T(8,128)(2,1)} %bitcast.73, bf16[128,2560]{1,0:T(8,128)(2,1)} %get-tuple-element.151.above), custom_call_target="tpu_custom_call" | custom-call | flops 1024 | bytes 1024 | tf_op jit(solution)/shard_map/pallas_call | solution.py:824
  593.9 2.2 copy.57
  596.1 7.4 %shard_map.333 = (f32[2,128,512]{2,1,0:T(8,128)}, f32[2,128,512]{2,1,0:T(8,128)}, f32[2,128,512]{2,1,0:T(8,128)}, f32[2,128,512]{2,1,0:T(8,128)}, f32[2,128,16]{...) custom-call(f32[1024,512]{1,0:T(8,128)} %get-tuple-element.146.refs_0_, ...), custom_call_target="tpu_custom_call" | custom-call | flops 1024 | bytes 1024 | tf_op jit(solution)/shard_map/pallas_call | solution.py:281
  603.5 1.6 copy.58
  605.0 1.5 fusion.4
  (38 shorter events, 4.7 us)
Async XLA Ops:
  7.2 52.8 %all-gather.3.cloned.1.call-start = ((), (), s32[]{:S(2)}) async-start(), calls=%async_computation.2 | async-start | bytes 2621440 | tf_op jit(solution)/shard_map/all_gather | solution.py:1226
  11.9 169.5 %all-gather.5.cloned.1.call-start = ((), (), s32[]{:S(2)}) async-start(), calls=%async_computation.3 | async-start | bytes 2621440 | tf_op jit(solution)/shard_map/all_gather | solution.py:1226
  12.8 1.2 copy-start.3
  12.8 2.0 copy-start.4
  13.9 502.0 %reduce-scatter.7.cloned.1.call-start = ((), (), s32[]{:S(2)}) async-start(), calls=%async_computation.4 | async-start | bytes 5242880
  44.2 12.2 %copy-start = (f32[2,2,512,512]{3,2,1,0:T(8,128)S(1)}, f32[2,2,512,512]{3,2,1,0:T(8,128)}, u32[]{:S(2)}) copy-start(f32[2,2,512,512]{3,2,1,0:T(8,128)} %param.36) | copy-start | bytes 12582916
  383.4 212.6 %reduce-scatter.9.cloned.1.call-start = ((), (), s32[]{:S(2)}) async-start(), calls=%async_computation.5 | async-start | bytes 5242880
  511.1 1.4 copy-start.1
  511.1 3.6 copy-start.5
  511.1 3.6 copy-start.6
  511.1 4.2 copy-start.7
  511.1 4.2 copy-start.8
  544.6 49.2 %copy-start.2 = (f32[4,197,512]{2,1,0:T(8,128)S(1)}, f32[4,197,512]{2,1,0:T(8,128)}, u32[]{:S(2)}) copy-start(f32[4,197,512]{2,1,0:T(8,128)} %get-tuple-element.183) | copy-start | bytes 4841476
Sparse Core Ops, SparseCore 0:
  12.0 47.7 all-gather.2
  62.3 50.6 all-gather.4
  383.5 74.7 reduce-scatter.6
  511.2 59.5 reduce-scatter.8

commit v6 on v5

--- a/solution.py
+++ b/solution.py
@@ -56,17 +56,6 @@
 def vectors_of(misc_ref):
     turned = misc_ref[...].astype(F32).T
     return [turned[VEC_AT + n : VEC_AT + n + 1, :] for n in range(7)]
-
-
-def pick(dest, buffers):
-    total = None
-    for number, buffer in enumerate(buffers):
-        count = buffer.shape[0]
-        lanes = lax.broadcasted_iota(jnp.int32, (dest.shape[0], count), 1)
-        chosen = (dest - number * count == lanes).astype(F32).astype(BF16)
-        part = dot(chosen, buffer[...])
-        total = part if total is None else total + part
-    return total
 
 
 def lane_masks(length):
@@ -120,14 +109,9 @@
     hidden_ref[0] = hidden
 
 
-def combine_body(middle, gates_ref, dcol_ref, back, yzero_ref, yone_ref):
-    dest = dcol_ref[0]
+def combine(middle, gates_ref, zero_ref, one_ref):
     gates = gates_ref[0]
-    zero = pick(dest[:, 0:1], back)
-    one = pick(dest[:, 1:2], back)
-    if yzero_ref is not None:
-        yzero_ref[0] = zero.astype(BF16)
-        yone_ref[0] = one.astype(BF16)
+    zero, one = zero_ref[0].astype(F32), one_ref[0].astype(F32)
     return middle + (gates[:, 0:1] * zero + gates[:, 1:2] * one), zero, one
 
 
@@ -152,27 +136,116 @@
 
 
 def next_kernel(
-    middle, gates, dcol, back, routes, wq, wk, wv, wo, misc, rows_ref, yzero, yone, *outs
+    middle, gates, yzero, yone, routes, wq, wk, wv, wo, misc, rows_ref, *outs
 ):
-    rows, _, _ = combine_body(middle[0], gates, dcol, (back,), yzero, yone)
+    rows, _, _ = combine(middle[0], gates, yzero, yone)
     rows_ref[0] = rows
     attend_body(rows, routes, wq, wk, wv, wo, misc, *outs)
 
 
-def turn_kernel(middle, gates, dcol, back, cotangent, routes, result, dz, zero_ref, one_ref):
-    rows, zero, one = combine_body(middle[0], gates, dcol, (back,), None, None)
+def turn_kernel(middle, gates, yzero, yone, cotangent, routes, result, dz, zero_ref, one_ref):
+    rows, zero, one = combine(middle[0], gates, yzero, yone)
     result[0] = rows
     grads_body(cotangent[0], zero, one, gates, routes, dz, zero_ref, one_ref)
 
 
+class Spread:
+    def __init__(self, above, refs):
+        self.own, self.paired, self.chips_in, self.final, *sems = refs
+        pair_send, pair_recv, local, out_send, out_recv, back_send, back_recv, pass_send, pass_recv = sems
+        half, columns = self.own.shape
+        me = lax.axis_index("expert")
+        core, chip = lax.rem(me, 2), me // 2
+        self.chips = chips = self.chips_in.shape[0] + 1
+        block = columns // chips
+        sibling = {"expert": me + 1 - 2 * core}
+        mine = pl.ds(pl.multiple_of(core * half, half), half)
+        other = pl.ds(pl.multiple_of((1 - core) * half, half), half)
+
+        def chip_at(k):
+            return lax.rem(chip + k + chips, chips)
+
+        def cols(number):
+            return pl.ds(pl.multiple_of(number * block, block), block)
+
+        peers = [{"expert": 2 * chip_at(k) + core} for k in range(1, chips)]
+        self.peers = [sibling] + peers
+        self.pair = remote(above.at[other], self.paired, pair_send, pair_recv, sibling)
+        self.keep = pltpu.make_async_copy(above.at[mine], self.own, local)
+        self.outs = [
+            remote(
+                self.own.at[:, cols(chip_at(k))], self.chips_in.at[k - 1], out_send.at[k - 1], out_recv.at[k - 1],
+                peers[k - 1],
+            )
+            for k in range(1, chips)
+        ]
+        self.place = (mine, cols(chip))
+        place = self.final.at[mine, cols(chip)]
+        self.backs = [
+            remote(place, place, back_send.at[k - 1], back_recv.at[k - 1], peers[k - 1]) for k in range(1, chips)
+        ]
+        self.hands = []
+        for k in range(chips):
+            place = self.final.at[mine, cols(chip_at(-k))]
+            self.hands.append(remote(place, place, pass_send.at[k], pass_recv.at[k], sibling))
+
+    def stage(self, number):
+        if number == 0:
+            greet_all(self.peers)
+            self.pair.start()
+            self.keep.start()
+        elif number == 1:
+            self.pair.wait_recv()
+            self.keep.wait()
+            self.own[...] = (self.own[...].astype(F32) + self.paired[...].astype(F32)).astype(BF16)
+            for copy in self.outs:
+                copy.start()
+        elif number == 2:
+            value = self.own[:, self.place[1]].astype(F32)
+            for n, copy in enumerate(self.outs):
+                copy.wait_recv()
+                value = value + self.chips_in[n].astype(F32)
+            self.final[self.place[0], self.place[1]] = value.astype(BF16)
+            for copy in self.backs:
+                copy.start()
+        else:
+            for copy in self.backs:
+                copy.wait_recv()
+            for copy in self.hands:
+                copy.start()
+
+    def finish(self, result):
+        for copy in self.hands:
+            copy.wait()
+        for copy in [self.pair] + self.outs + self.backs:
+            copy.wait_send()
+        result[...] = self.final[...]
+
+
+def spread_scratch(share, columns, chips):
+    half = share // 2
+    half_rows = pltpu.VMEM((half, columns), BF16)
+    sems = [()] * 3 + [(chips - 1,)] * 4 + [(chips,)] * 2
+    return [
+        half_rows, half_rows, pltpu.VMEM((chips - 1, half, columns // chips), BF16), pltpu.VMEM((share, columns), BF16),
+    ] + [pltpu.SemaphoreType.DMA(n) for n in sems]
+
+
 def back_kernel(
-    upstream, rows, middle, q_ref, k_ref, v_ref, o_ref, lse_ref, dz_ref, dcol, came,
+    lowest, upstream, rows, middle, q_ref, k_ref, v_ref, o_ref, lse_ref, dz_ref, came,
     wq, wk, wv, wo, misc, *rest,
 ):
-    if len(rest) > 4:
+    if not lowest:
         yzero, yone, gates_below, routes_below, grad_ref, sent, dz_below, zero_ref, one_ref, wgrad, vgrad = rest
     else:
-        grad_ref, sent, wgrad, vgrad = rest
+        above, grad_ref, sent, above_out, wgrad, vgrad, *spread_refs = rest
+        spread = Spread(above, spread_refs)
+        for number in range(4):
+
+            @pl.when(pl.program_id(0) == number)
+            def _(number=number):
+                spread.stage(number)
+
     first = pl.program_id(0) == 0
     length = rows.shape[1]
     width = rows.shape[2]
@@ -189,11 +262,7 @@
     unit_two, scale_two = standardize(middle[0])
     hidden = (unit_two * egain + eshift).astype(BF16)
     dz = dz_ref[0]
-    dest = dcol[0]
-    dhidden = dot_nt(dz, misc[...])
-    lanes = lax.broadcasted_iota(jnp.int32, (length, came.shape[0]), 1)
-    hit = (dest[:, 0:1] == lanes) | (dest[:, 1:2] == lanes)
-    dhidden = dhidden + dot(hit.astype(F32).astype(BF16), came[...])
+    dhidden = dot_nt(dz, misc[...]) + came[0]
     wgrad[:, 4 * width :] += dot_tn(hidden, dz)
     add_vector(5, dhidden * unit_two)
     add_vector(6, dhidden)
@@ -205,6 +274,7 @@
     masks = lane_masks(length)
     first_half = lax.broadcasted_iota(jnp.int32, (length, 2 * HEAD_DIM), 1) < HEAD_DIM
     dqs, dks, dvs = [], [], []
+    sums = lse_ref[0].T
     for pair in range(HEADS // 2):
         cols = slice(pair * 2 * HEAD_DIM, (pair + 1) * 2 * HEAD_DIM)
         keys = k_ref[0, :, cols]
@@ -214,18 +284,18 @@
         for side in range(2):
             own_queries = queries * (masks[side] * FACTOR)
             own_context = dcontext[:, cols] * masks[side]
-            scores = dot_nt(own_queries, keys)
+            scores = dot_nt(keys, own_queries)
             number = 2 * pair + side
-            attention = jnp.exp(scores - lse_ref[0, :, number : number + 1])
-            prob = dot_nt(own_context, values)
+            attention = jnp.exp(scores - sums[number : number + 1, :])
+            prob = dot_nt(values, own_context)
             weighed = attention * prob
-            delta = jnp.sum(weighed, axis=-1, keepdims=True)
+            delta = jnp.sum(weighed, axis=0, keepdims=True)
             dscores = (weighed - attention * delta).astype(BF16)
-            dvalue = dot_tn(attention.astype(BF16), own_context)
-            dkey = dot_tn(dscores, own_queries)
+            dvalue = dot(attention.astype(BF16), own_context)
+            dkey = dot(dscores, own_queries)
             dvalues = dvalue if dvalues is None else dvalues + dvalue
             dkeys = dkey if dkeys is None else dkeys + dkey
-            dqueries.append(dot(dscores, keys))
+            dqueries.append(dot_tn(dscores, keys))
         dqs.append((jnp.where(first_half, dqueries[0], dqueries[1]) * FACTOR).astype(BF16))
         dks.append(dkeys.astype(BF16))
         dvs.append(dvalues.astype(BF16))
@@ -234,9 +304,7 @@
     dv = jnp.concatenate(dvs, axis=1)
     unit, scale = standardize(rows[0])
     low = (unit * again + ashift).astype(BF16)
-    wgrad[:, 0:width] += dot_tn(low, dq)
-    wgrad[:, width : 2 * width] += dot_tn(low, dk)
-    wgrad[:, 2 * width : 3 * width] += dot_tn(low, dv)
+    wgrad[:, 0 : 3 * width] += dot_tn(low, jnp.concatenate([dq, dk, dv], axis=1))
     add_vector(0, dq.astype(F32))
     add_vector(1, dv.astype(F32))
     dlow = dot_nt(dq, wq[...]) + dot_nt(dk, wk[...]) + dot_nt(dv, wv[...])
@@ -244,7 +312,7 @@
     add_vector(4, dlow)
     grad = dmiddle + standardize_back(dlow, unit, scale, again)
     grad_ref[0] = grad
-    if len(rest) > 4:
+    if not lowest:
         grads_body(
             grad, yzero[0].astype(F32), yone[0].astype(F32), gates_below, routes_below, dz_below,
             zero_ref, one_ref,
@@ -255,6 +323,8 @@
         wgrad[:, 4 * width :] += vgrad[...].T
         sent[:, : 4 * width + MISC] = wgrad[...].astype(BF16)
         sent[:, 4 * width + MISC :] = jnp.zeros((width, sent.shape[1] - 4 * width - MISC), BF16)
+        if lowest:
+            spread.finish(above_out)
 
 
 def per_image(array):
@@ -276,7 +346,7 @@
     return specs + [pl.BlockSpec((width, MISC), lambda i: (0, 4 * width // MISC))]
 
 
-def call(body, grid, inputs, outputs, scratch=(), flops=0, aliases=None):
+def call(body, grid, inputs, outputs, scratch=(), number=None):
     shapes = [jax.ShapeDtypeStruct(s, t) for s, t, _ in outputs]
     return pl.pallas_call(
         body,
@@ -285,7 +355,9 @@
         out_specs=[s for _, _, s in outputs],
         out_shape=shapes,
         scratch_shapes=list(scratch),
-        compiler_params=pltpu.CompilerParams(vmem_limit_bytes=VMEM),
+        compiler_params=pltpu.CompilerParams(
+            vmem_limit_bytes=VMEM, collective_id=number, has_side_effects=number is not None
+        ),
         cost_estimate=pl.CostEstimate(flops=COST, bytes_accessed=COST, transcendentals=0),
     )(*[a for a, _ in inputs])
 
@@ -514,13 +586,49 @@
             def _():
                 self.own_home(j).start()
 
+    def wait_home(self, j, chip):
+        for core in range(2):
+            source = 2 * chip + core
+            k = lax.rem(self.me - source + self.count, self.count)
+
+            @pl.when(source != self.me)
+            def _(k=k, source=source):
+                place = self.back.at[j, source]
+                remote(place, place, self.home_send.at[j, k], self.home_recv.at[j, k], {"expert": source}).wait_recv()
+
+            @pl.when(source == self.me)
+            def _():
+                self.own_home(j).wait()
+
+    def take_home(self, dcol, layer, total):
+        count, images, length, width = total.shape
+        capacity = self.back.shape[2]
+        total[...] = jnp.zeros_like(total)
+        for j in range(self.local):
+
+            def step(turn, carry, j=j):
+                chip = self.chip(turn)
+                self.wait_home(j, chip)
+                rows = self.back[j, pl.ds(2 * chip, 2)].reshape(2 * capacity, width)
+                first = (j * self.count + 2 * chip) * capacity
+                lanes = lax.broadcasted_iota(jnp.int32, (length, 2 * capacity), 1) + first
+                for image in range(images):
+                    dest = dcol[layer, image]
+                    hits = [dest[:, 0:1] == lanes, dest[:, 1:2] == lanes]
+                    if count == 1:
+                        hits = [hits[0] | hits[1]]
+                    for k, hit in enumerate(hits):
+                        total[k, image] += dot(hit.astype(F32).astype(BF16), rows).astype(total.dtype)
+                return carry
+
+            lax.fori_loop(0, self.count // 2, step, 0)
+
     def finish(self):
         for j in range(self.local):
-            self.own_home(j).wait()
             for k in range(1, self.count):
                 peer = lax.rem(self.me + k, self.count)
                 self.outward(j, k, peer).wait_send()
-                self.homeward(j, k, peer).wait()
+                self.homeward(j, k, peer).wait_send()
 
 
 def weight_blocks(weights, j, f):
@@ -534,12 +642,14 @@
 
 def expert_kernel(layer, with_dense, *refs):
     if with_dense:
-        *refs, n1, n2, n3, n4, n5 = refs
+        *refs, n1, n2, n3, n4, n5, m1, m2, m3 = refs
         refs = list(refs)
-        dense = SharedGather(refs.pop(7), refs.pop(13), (n1, n2, n3, n4, n5))
+        dense_in, next_in, dense_out, next_out = refs.pop(8), refs.pop(8), refs.pop(14), refs.pop(14)
+        dense = SharedGather(dense_in, dense_out, (n1, n2, n3, n4, n5))
+        following = Gather(dense_out.shape[0], next_in, lambda p: next_out.at[p], (m1, m2, m3))
     (
-        hidden, drow, inner_first, outer_mine, mine, b1, b2, back, arrived_out, g_out, s_out, outer_out, packed_out,
-        sent, arrived, made, weights, g_stage, s_stage, out_send, out_recv, home_send, home_recv, own, load, stores, last,
+        hidden, drow, dcol, inner_first, outer_mine, mine, b1, b2, picked, arrived_out, g_out, s_out, outer_out, packed_out,
+        back, sent, arrived, made, weights, g_stage, s_stage, out_send, out_recv, home_send, home_recv, own, load, stores, last,
         *gather_refs,
     ) = refs
     row = lax.axis_index("dp")
@@ -578,6 +688,8 @@
             first_load.wait()
         gathers[j].finish()
         gathered[j].start()
+        if j == 1 and with_dense:
+            following.start()
         number = layer * local + j
 
         def chip_step(turn, carry, j=j, number=number):
@@ -591,6 +703,12 @@
                     gathers[1].forward()
                     if with_dense:
                         dense.start()
+
+            if j == 1 and with_dense:
+
+                @pl.when(turn == 2)
+                def _():
+                    following.forward()
 
             @pl.when(j * chips + turn >= 2)
             def _():
@@ -620,9 +738,12 @@
     final.start()
     if with_dense:
         dense.finish()
+        following.finish()
+        following.drain()
     for slot in range(2):
         for copy in kept(0, slot, 0):
             copy.wait()
+    swap.take_home(dcol, layer, picked)
     swap.finish()
     for gather, copy in zip(gathers, gathered):
         gather.drain()
@@ -634,10 +755,10 @@
     if with_above:
         *refs, above_in, above_own, above_send, above_recv, above_load = refs
         refs = list(refs)
-        above, above_sum = refs.pop(9), refs.pop(14)
+        above, above_sum = refs.pop(10), refs.pop(15)
     (
-        zero, one, drow, inner_first, outer_first, packed_second, arrived_x, g_in, s_in, back, summed, out, bias1, bias2,
-        sent, arrived, made, weights, x, du, s_stage, g_stage, first_stage, second_stage, share_out, share_in,
+        zero, one, drow, dcol, inner_first, outer_first, packed_second, arrived_x, g_in, s_in,
+        came, summed, out, bias1, bias2, back, sent, arrived, made, weights, x, du, s_stage, g_stage, first_stage, second_stage, share_out, share_in,
         db1, db2, db1_in, db2_in,
         out_send, out_recv, home_send, home_recv, own, load, fetch, stores, share_send, share_recv,
         bias_send, bias_recv,
@@ -801,6 +922,7 @@
     for k in range(1, parts):
         total1, total2 = total1 + db1_in[k - 1], total2 + db2_in[k - 1]
     bias1[...], bias2[...] = total1, total2
+    swap.take_home(dcol, layer, came)
     for copy in bias_copies:
         copy.wait_send()
     for k in range(1, parts):
@@ -834,7 +956,7 @@
     )(*[a for a, _ in inputs])
 
 
-def expert_forward(hidden, drow, shape, inner, outer_mine, mine, biases, dense, layer):
+def expert_forward(hidden, drow, dcol, shape, inner, outer_mine, mine, biases, following, layer):
     b1, b2 = biases
     local, count, capacity, width = shape
     ff = b1.shape[1]
@@ -842,39 +964,39 @@
     parts = inner.shape[0]
     packed = (parts, *mine.shape)
     slots = (local, count * capacity, ff)
-    inputs = [(hidden, True), (drow, True), (inner, False), (outer_mine, False), (mine, False), (b1, True), (b2, True)]
+    inputs = [(hidden, True), (drow, True), (dcol, True), (inner, False), (outer_mine, False), (mine, False), (b1, True), (b2, True)]
     outputs = [
-        (shape, BF16, False), (shape, BF16, False), (slots, BF16, False), (slots, BF16, False),
+        ((2, *hidden.shape), BF16, True), (shape, BF16, False), (slots, BF16, False), (slots, BF16, False),
         ((parts, *outer_mine.shape), BF16, False), (packed, BF16, False),
     ]
     scratch = [
-        pltpu.VMEM(shape, BF16), pltpu.VMEM(shape, BF16), pltpu.VMEM(shape, BF16),
+        pltpu.VMEM(shape, BF16), pltpu.VMEM(shape, BF16), pltpu.VMEM(shape, BF16), pltpu.VMEM(shape, BF16),
         pltpu.VMEM((local, *packed), BF16),
         pltpu.VMEM((2, rows, ff), BF16), pltpu.VMEM((2, rows, ff), BF16),
     ] + swap_sems(local, count) + [
         pltpu.SemaphoreType.DMA, pltpu.SemaphoreType.DMA((2, 2)), pltpu.SemaphoreType.DMA((3,)),
     ] + gather_sems(parts) * 2
-    if dense is not None:
-        inputs.append((dense, False))
-        outputs.append(((parts, *dense.shape), BF16, False))
-        scratch += shared_sems(parts)
-    return expert_call(functools.partial(expert_kernel, layer, dense is not None), inputs, outputs, scratch, layer)
-
-
-def expert_backward(sources, drow, weights, arrived, g, s, above, layer):
+    if following:
+        inputs += [(item, False) for item in following]
+        outputs += [((parts, *item.shape), BF16, False) for item in following]
+        scratch += shared_sems(parts) + gather_sems(parts)
+    return expert_call(functools.partial(expert_kernel, layer, bool(following)), inputs, outputs, scratch, layer)
+
+
+def expert_backward(sources, drow, dcol, weights, arrived, g, s, above, layer):
     shape = arrived.shape
     local, count, capacity, width = shape
     ff = g.shape[2]
     rows = 2 * capacity
     parts, all_rows, _ = weights[2].shape
     share, take = width // parts, all_rows // 2
-    inputs = [(a, True) for a in (*sources, drow)] + [(a, False) for a in (*weights, arrived, g, s)]
+    inputs = [(a, True) for a in (*sources, drow, dcol)] + [(a, False) for a in (*weights, arrived, g, s)]
     outputs = [
-        (shape, BF16, False), ((all_rows, width), F32, True), ((parts, local - 1, all_rows, width), BF16, False),
+        ((1, *sources[0].shape), F32, True), ((all_rows, width), F32, True), ((parts, local - 1, all_rows, width), BF16, False),
         ((local, ff // parts), F32, True), ((local, width), F32, True),
     ]
     scratch = [
-        pltpu.VMEM(shape, BF16), pltpu.VMEM(shape, BF16), pltpu.VMEM(shape, BF16),
+        pltpu.VMEM(shape, BF16), pltpu.VMEM(shape, BF16), pltpu.VMEM(shape, BF16), pltpu.VMEM(shape, BF16),
         pltpu.VMEM((local, parts, all_rows, width), BF16), pltpu.VMEM(shape, BF16),
         pltpu.VMEM((count * capacity, ff), BF16), pltpu.VMEM((2, rows, ff), BF16),
         pltpu.VMEM((2, count * capacity, FF_BLOCK), BF16), pltpu.VMEM((2, parts, share, width), BF16),
@@ -1016,9 +1138,9 @@
 
 
 def settle_kernel(
-    grads, above, final, own, paired, total, chips_in, dp_in, total_b, chips_in_b, dp_in_b,
+    grads, tokens_a, tokens_b, final, tokens_out_a, tokens_out_b, own, paired, total, chips_in, dp_in, total_b, chips_in_b, dp_in_b,
     pair_send, pair_recv, local, out_send, out_recv, dp_send, dp_recv, out_send_b, out_recv_b, dp_send_b, dp_recv_b,
-    back_send, back_recv, pass_send, pass_recv,
+    back_send, back_recv, pass_send, pass_recv, token_ins, token_outs, token_load, token_store,
 ):
     parts, share, columns = grads.shape
     half = share // 2
@@ -1046,14 +1168,20 @@
 
     order = [lax.rem(row + 1 + i, parts) for i in range(parts)]
     pairs, keeps = [], []
-    for i in range(parts + 1):
-        source = grads.at[order[i]] if i < parts else above
+    for i in range(parts):
+        source = grads.at[order[i]]
         pairs.append(remote(source.at[other], paired.at[i], pair_send.at[i], pair_recv.at[i], sibling))
         keeps.append(pltpu.make_async_copy(source.at[mine], own.at[i], local.at[i]))
         pairs[i].start()
         keeps[i].start()
+    loads = [pltpu.make_async_copy(t, token_ins.at[n], token_load.at[n]) for n, t in enumerate((tokens_a, tokens_b))]
+    stores = [
+        pltpu.make_async_copy(token_outs.at[n], t, token_store.at[n]) for n, t in enumerate((tokens_out_a, tokens_out_b))
+    ]
+    for copy in loads:
+        copy.start()
     outs, scatters_b = [], []
-    for i in range(parts + 1):
+    for i in range(parts):
         pairs[i].wait_recv()
         keeps[i].wait()
         own[i] = (own[i].astype(F32) + paired[i].astype(F32)).astype(BF16)
@@ -1071,15 +1199,19 @@
         ])
         for copy in outs[i]:
             copy.start()
+    for n in range(2):
+        loads[n].wait()
+        for image in range(token_ins.shape[1]):
+            token_outs[n, :, image, :] = token_ins[n, image]
+        stores[n].start()
     value = own[parts - 1, :, split:].astype(F32)
     for i in range(parts - 1):
         scatters_b[i].wait_recv()
         value = value + dp_in_b[i].astype(F32)
-    total_b[0] = value.astype(BF16)
-    total_b[1] = own[parts, :, split:]
+    total_b[...] = value.astype(BF16)
     outs_b = [
         remote(
-            total_b.at[:, :, cols_b(chip_at(k), 0)], chips_in_b.at[k - 1], out_send_b.at[k - 1], out_recv_b.at[k - 1],
+            total_b.at[:, cols_b(chip_at(k), 0)], chips_in_b.at[k - 1], out_send_b.at[k - 1], out_recv_b.at[k - 1],
             chip_peers[k - 1],
         )
         for k in range(1, chips)
@@ -1087,7 +1219,7 @@
     for copy in outs_b:
         copy.start()
     scatters = []
-    for i in range(parts + 1):
+    for i in range(parts):
         value = own[i, :, cols(chip)].astype(F32)
         for k in range(1, chips):
             outs[i][k - 1].wait_recv()
@@ -1096,22 +1228,20 @@
             total[i] = value.astype(BF16)
             scatters.append(remote(total.at[i], dp_in.at[i], dp_send.at[i], dp_recv.at[i], dp_peers[i]))
             scatters[i].start()
-        elif i == parts - 1:
+        else:
             kept = value
-        else:
-            final[1, mine, cols(chip)] = value.astype(BF16)
-    value = total_b[:, :, cols_b(chip, 0)].astype(F32)
+    value = total_b[:, cols_b(chip, 0)].astype(F32)
     for k in range(1, chips):
         outs_b[k - 1].wait_recv()
         value = value + chips_in_b[k - 1].astype(F32)
-    final[:, mine, cols_b(chip, split)] = value.astype(BF16)
+    final[mine, cols_b(chip, split)] = value.astype(BF16)
     for i in range(parts - 1):
         scatters[i].wait_recv()
         kept = kept + dp_in[i].astype(F32)
-    final[0, mine, cols(chip)] = kept.astype(BF16)
+    final[mine, cols(chip)] = kept.astype(BF16)
 
     def places(number):
-        return [final.at[:, mine, cols(number)], final.at[:, mine, cols_b(number, split)]]
+        return [final.at[mine, cols(number)], final.at[mine, cols_b(number, split)]]
 
     backs, hands = [], []
     for n, place in enumerate(places(chip)):
@@ -1127,49 +1257,55 @@
             hands[-1].start()
     for copy in pairs + [copy for group in outs for copy in group] + outs_b + scatters + scatters_b + backs:
         copy.wait_send()
-    for copy in hands:
+    for copy in hands + stores:
         copy.wait()
 
 
-def settle_dense(grads, above, chips, number):
+def settle(grads, tokens, chips, number):
     parts, share, columns = grads.shape
     half = share // 2
-    halves = pltpu.VMEM((parts + 1, half, columns), BF16)
+    images, length, width = tokens[0].shape
+    halves = pltpu.VMEM((parts, half, columns), BF16)
     wide, narrow = settle_widths(columns, chips)
     dp_in = pltpu.VMEM((parts - 1, half, wide), BF16)
     rest = chips * narrow
-    sems = [(parts + 1,)] * 3 + [(chips - 1, parts + 1)] * 2 + [(parts - 1,)] * 2
+    sems = [(parts,)] * 3 + [(chips - 1, parts)] * 2 + [(parts - 1,)] * 2
     sems += [(chips - 1,)] * 2 + [(parts - 1,)] * 2 + [(2, chips - 1)] * 2 + [(2, chips)] * 2
+    turned = ((length, images, width), F32, False)
     return expert_call(
-        settle_kernel, [(grads, False), (above, False)], [((2, share, columns), BF16, True)],
+        settle_kernel, [(item, False) for item in (grads, *tokens)], [((share, columns), BF16, True), turned, turned],
         [
-            halves, halves, dp_in, pltpu.VMEM((chips - 1, parts + 1, half, wide), BF16), dp_in,
-            pltpu.VMEM((2, half, rest), BF16), pltpu.VMEM((chips - 1, 2, half, narrow), BF16),
+            halves, halves, dp_in, pltpu.VMEM((chips - 1, parts, half, wide), BF16), dp_in,
+            pltpu.VMEM((half, rest), BF16), pltpu.VMEM((chips - 1, half, narrow), BF16),
             pltpu.VMEM((parts - 1, half, rest), BF16),
-        ] + [pltpu.SemaphoreType.DMA(n) for n in sems],
+        ] + [pltpu.SemaphoreType.DMA(n) for n in sems] + [
+            pltpu.VMEM((2, images, length, width), F32), pltpu.VMEM((2, length, images, width), F32),
+            pltpu.SemaphoreType.DMA((2,)), pltpu.SemaphoreType.DMA((2,)),
+        ],
         number,
-    )[0]
+    )
 
 
 def unpack_kernel(*refs):
     count = 2 * LAYERS
-    pieces, both = refs[:count], refs[count]
-    squares, router, vectors, inner, outer = refs[count + 1 : count + 5], *refs[count + 5 :]
+    pieces, both, refs = refs[:count], refs[count : count + LAYERS], refs[count + LAYERS :]
+    squares, router, vectors, (inner, outer) = refs[:4], refs[4], refs[5:12], refs[12:]
     layer = pl.program_id(0)
-    share = both.shape[1]
+    share = both[0].shape[0]
     width = squares[0].shape[2]
-    for n in range(4):
-        squares[n][0] = both[0, :, n * width : (n + 1) * width].astype(F32)
-    misc = both[0, :, 4 * width : 4 * width + MISC].astype(F32)
-    router[0] = misc[:, : router.shape[2]]
-    turned = misc.T
-    vectors[0] = turned[VEC_AT : VEC_AT + 8, :]
     blocks = inner.shape[3] // FF_BLOCK
 
     for number in range(LAYERS):
 
         @pl.when(layer == number)
         def _(number=number):
+            dense = both[number]
+            for n in range(4):
+                squares[n][0] = dense[:, n * width : (n + 1) * width].astype(F32)
+            turned = dense[:, 4 * width : 4 * width + MISC].astype(F32).T
+            router[0] = turned[: router.shape[1], :]
+            for n in range(7):
+                vectors[n][number : number + 1, :] = turned[VEC_AT + n : VEC_AT + n + 1, :]
             for j in range(2):
                 piece = pieces[2 * number + j]
                 for f in range(blocks):
@@ -1180,15 +1316,16 @@
 
 
 def unpack(pieces, both, local, ff, experts_all):
-    layers, share, columns = both.shape
+    layers, (share, columns) = len(both), both[0].shape
     rows, width = pieces[0].shape
     take = rows // 2
     by_layer = lambda *shape: ((layers, *shape), F32, pl.BlockSpec((1, *shape), lambda i: (i,) + (0,) * len(shape)))
     return call(
         unpack_kernel, (layers,),
-        [(p, whole(p)) for p in pieces] + [(both, pl.BlockSpec((1, share, columns), lambda i: (i, 0, 0)))],
+        [(p, whole(p)) for p in (*pieces, *both)],
         [by_layer(share, width)] * 4 + [
-            by_layer(share, experts_all), by_layer(8, share),
+            by_layer(experts_all, share),
+        ] + [((layers, share), F32, pl.BlockSpec((layers, share), lambda i: (0, 0)))] * 7 + [
             by_layer(local, share, ff), by_layer(local, take, width),
         ],
     )
@@ -1223,9 +1360,8 @@
         squares, router_weight, vectors, inner_bias, outer_bias, routes, (images, cotangent), parts, owners, 2 * LAYERS
     )
     packed = [dense]
-    firsts = [lax.all_gather(item, "dp", axis=0, tiled=False) for item in inner_mine]
+    firsts = [lax.all_gather(inner_mine[0], "dp", axis=0, tiled=False)]
     slots = experts_all * capacity
-    dense_flops = 8 * tokens * width * width + 4 * tokens * slots * width
 
     saved = []
     back = None
@@ -1236,9 +1372,8 @@
         outputs = attend_outputs(count, length, width)
         if layer == 0:
             done = call(
-                first_kernel, (count,), [(rows, per_image(rows))] + routing + weights, outputs, flops=dense_flops
+                first_kernel, (count,), [(rows, per_image(rows))] + routing + weights, outputs
             )
-            picked = None
         else:
             before = saved[-1]
             done = call(
@@ -1246,40 +1381,35 @@
                 [
                     (before["middle"], per_image(before["middle"])),
                     (before["gates"], per_image(before["gates"])),
-                    (dcol, per_layer(dcol, layer - 1)),
-                    (back, whole(back)),
+                    (picked, per_layer(picked, 0)),
+                    (picked, per_layer(picked, 1)),
                 ] + routing + weights,
                 [
                     images_out(count, length, width, F32),
-                    images_out(count, length, width, BF16),
-                    images_out(count, length, width, BF16),
-                ] + outputs,
-                flops=dense_flops,
+                ] + outputs
             )
-            rows, *picked = done[:3]
-            done = done[3:]
-            before["picked"] = picked
+            rows, *done = done
         middle, queries, keys, values, context, sums, gates = done[:7]
-        back, arrived, g, s, outer, second, *dense = expert_forward(
-            done[7], drow, (local, owners, capacity, width), firsts[layer], outer_mine[layer], mine[layer], expert_biases,
-            above if layer == 0 else None, layer,
+        picked, arrived, g, s, outer, second, *following = expert_forward(
+            done[7], drow, dcol, (local, owners, capacity, width), firsts[layer], outer_mine[layer], mine[layer], expert_biases,
+            (above, inner_mine[layer + 1]) if layer + 1 < LAYERS else (), layer,
         )
-        packed += [item.reshape(width, item.shape[2]) for item in dense]
-        back = back.reshape(slots, width)
+        if following:
+            packed.append(following[0].reshape(width, following[0].shape[2]))
+            firsts.append(following[1])
         saved.append({
             "rows": rows, "middle": middle, "attend": (queries, keys, values, context, sums), "gates": gates,
-            "experts": (arrived, g, s), "weights": (firsts[layer], outer, second),
+            "experts": (arrived, g, s), "weights": (firsts[layer], outer, second), "picked": picked,
         })
 
     last = saved[-1]
     result, dz, *sources = call(
         turn_kernel, (count,),
         [(last["middle"], per_image(last["middle"])), (last["gates"], per_image(last["gates"]))]
-        + [(dcol, per_layer(dcol, LAYERS - 1)), (back, whole(back))]
+        + [(picked, per_layer(picked, k)) for k in range(2)]
         + [(cotangent, per_image(cotangent)), (routes, per_layer(routes, LAYERS - 1))],
         [images_out(count, length, width, F32), images_out(count, length, MISC, BF16)]
-        + [images_out(count, length, width, BF16)] * 2,
-        flops=dense_flops,
+        + [images_out(count, length, width, BF16)] * 2
     )
     upstream = cotangent
     bias_grads = [None] * LAYERS
@@ -1289,9 +1419,9 @@
     for layer in reversed(range(LAYERS)):
         kept = saved[layer]
         came, shares, grads, *biases, above = expert_backward(
-            sources, drow, kept["weights"], *kept["experts"], wgrad, layer
+            sources, drow, dcol, kept["weights"], *kept["experts"], wgrad, layer
         )
-        came = came.reshape(slots, width)
+        came = came[0]
         came, waiting = lax.optimization_barrier((came, waiting))
         finished += waiting
         waiting = [shares, lax.psum_scatter(grads, "dp", scatter_dimension=0, tiled=False)]
@@ -1299,7 +1429,7 @@
         weights = [(packed[layer], s) for s in packed_specs(packed[layer])]
         inputs = [upstream, kept["rows"], kept["middle"], *kept["attend"], dz]
         inputs = [(a, per_image(a)) for a in inputs]
-        inputs += [(dcol, per_layer(dcol, layer)), (came, whole(came))] + weights
+        inputs += [(came, per_image(came))] + weights
         outputs = [
             images_out(count, length, width, F32),
             (
@@ -1309,27 +1439,33 @@
         ]
         if layer > 0:
             below = saved[layer - 1]
-            inputs += [(a, per_image(a)) for a in (*below["picked"], below["gates"])]
+            inputs += [(below["picked"], per_layer(below["picked"], k)) for k in range(2)]
+            inputs.append((below["gates"], per_image(below["gates"])))
             inputs.append((routes, per_layer(routes, layer - 1)))
             outputs += [images_out(count, length, MISC, BF16)] + [images_out(count, length, width, BF16)] * 2
-        done = call(
-            back_kernel, (count,), inputs, outputs,
-            [pltpu.VMEM((width, 4 * width + MISC), F32), pltpu.VMEM((MISC, width), F32)], flops=3 * dense_flops,
-        )
+        scratch = [pltpu.VMEM((width, 4 * width + MISC), F32), pltpu.VMEM((MISC, width), F32)]
+        number = None
+        if layer == 0:
+            inputs.append((above, pl.BlockSpec(memory_space=pl.ANY)))
+            outputs.append((above.shape, BF16, pl.BlockSpec(above.shape, lambda i: (0, 0))))
+            scratch += spread_scratch(share, columns, owners // 2)
+            number = 2 * LAYERS + 2
+        done = call(functools.partial(back_kernel, layer == 0), (count,), inputs, outputs, scratch, number)
         upstream, wgrad = done[:2]
         if layer > 0:
             dz, *sources = done[2:]
         wgrad = wgrad.reshape(parts, share, columns)
-    both = settle_dense(wgrad, above, owners // 2, 2 * LAYERS + 1)
+    lowest, result, upstream = settle(wgrad, (result, upstream), owners // 2, 2 * LAYERS + 1)
+    both = (lowest, done[2])
     pieces = [waiting[0], waiting[1][0], finished[0], finished[1][0]]
-    *squares, router, vectors, inner, outer = unpack(pieces, both, local, ff, experts_all)
+    *squares, router, v0, v1, v2, v3, v4, v5, v6, inner, outer = unpack(pieces, both, local, ff, experts_all)
     outer_bias_grad = jnp.stack([b[1] for b in bias_grads])
     return (
-        result,
-        upstream,
+        jnp.transpose(result, (1, 0, 2)),
+        jnp.transpose(upstream, (1, 0, 2)),
         *squares,
-        router,
-        *[vectors[:, n] for n in range(7)],
+        jnp.transpose(router, (0, 2, 1)),
+        v0, v1, v2, v3, v4, v5, v6,
         inner,
         jnp.stack([b[0] for b in bias_grads]),
         outer,

time: 618 us -> 605 us (0.979)
  Pallas kernels: 577 us -> 567 us
  transfers between devices with their start and end apart: 4 -> 3, of which waited for: 0 -> 0; matrix products, arithmetic and copies ran while one was open for 2% -> 2% of each run, Pallas kernels for 60% -> 40%
where the time goes in v6:
time: 605 us; the launch traced here: 600 us
  Pallas kernels  567 us (94%)
  between operations  14.3 us (2%)
  local copies, waits for them, and re-layouts  13.1 us (2%)
    pallas_call x6, Pallas kernels, expert_call(): pl.pallas_call(body, in_specs=[spec(held) for _, held in inputs], out_spe...  468 us
    pallas_call x6, Pallas kernels, call(): pl.pallas_call(body, grid=grid, in_specs=[s for _, s in inputs], out_spec...  99.5 us
  transfers between devices with their start and end apart: 3, of which 0 were waited for; matrix products, arithmetic and copies ran while one was open for 2% of the time, Pallas kernels for 40%

profile of v6, /device:TPU:0, one launch (start us, length us, event | category | flops | bytes accessed | tf_op | source)
XLA Modules:
  0.0 600.3 jit_solution(5448333078120538020)
XLA Ops:
  7.2 2.5 convert.8
  9.7 1.2 fusion.1
  10.9 0.8 convert_element_type.20
  11.9 1.1 fusion.3
  13.8 1.2 copy.46.refs_14_.routes.rest_3_
  15.1 28.2 %shard_map.322 = (bf16[4,128,2176]{2,1,0:T(8,128)(2,1)}, bf16[128,2176]{1,0:T(8,128)(2,1)}, f32[4,2048]{1,0:T(4,128)}, f32[4,4,128]{2,1,0:T(4,128)}, s32[2,4,197...) custom-call(f32[2,128,512]{2,1,0:T(8,128)} %refs_0_.1, ...), custom_call_target="tpu_custom_call" | custom-call | flops 1024 | bytes 1024 | tf_op jit(solution)/shard_map/pallas_call | solution.py:946
  43.3 12.1 %shard_map.323 = (f32[4,197,512]{2,1,0:T(8,128)}, bf16[4,197,512]{2,1,0:T(8,128)(2,1)}, bf16[4,197,512]{2,1,0:T(8,128)(2,1)}, bf16[4,197,512]{2,1,0:T(8,128)(2,1...) custom-call(f32[4,197,512]{2,1,0:T(8,128)} %get-tuple-element.101.ro, ...), custom_call_target="tpu_custom_call" | custom-call | flops 1024 | bytes 1024 | tf_op jit(solution)/shard_map/pallas_call | solution.py:351
  55.7 1.8 convert_element_type.22
  57.7 0.9 fusion.2
  58.7 1.2 slice_bitcast_fusion
  59.8 1.4 pad_maximum_fusion
  61.3 99.9 %shard_map.324 = (bf16[2,4,197,512]{3,2,1,0:T(8,128)(2,1)}, bf16[2,8,128,512]{3,2,1,0:T(8,128)(2,1)}, bf16[2,1024,2048]{2,1,0:T(8,128)(2,1)}, bf16[2,1024,2048]{...) custom-call(bf16[4,197,512]{2,1,0:T(8,128)(2,1)} %get-tuple-element., ...), custom_call_target="tpu_custom_call" | custom-call | flops 1024 | bytes 1024 | tf_op jit(solution)/shard_map/pallas_call | solution.py:946
  161.2 13.1 %shard_map.325 = (f32[4,197,512]{2,1,0:T(8,128)}, f32[4,197,512]{2,1,0:T(8,128)}, bf16[4,197,512]{2,1,0:T(8,128)(2,1)}, bf16[4,197,512]{2,1,0:T(8,128)(2,1)}, bf...) custom-call(f32[4,197,512]{2,1,0:T(8,128)} %get-tuple-element.103.mi, ...), custom_call_target="tpu_custom_call" | custom-call | flops 1024 | bytes 1024 | tf_op jit(solution)/shard_map/pallas_call | solution.py:351
  174.3 99.5 %shard_map.326 = (bf16[2,4,197,512]{3,2,1,0:T(8,128)(2,1)}, bf16[2,8,128,512]{3,2,1,0:T(8,128)(2,1)}, bf16[2,1024,2048]{2,1,0:T(8,128)(2,1)}, bf16[2,1024,2048]{...) custom-call(bf16[4,197,512]{2,1,0:T(8,128)(2,1)} %get-tuple-element.121.refs_0_, ...), custom_call_target="tpu_custom_call" | custom-call | flops 1024 | bytes 1024 | tf_op jit(solution)/shard_map/pallas_call | solution.py:946
  273.8 5.7 shard_map.327
  279.5 99.5 %shard_map.328 = (f32[1,4,197,512]{3,2,1,0:T(8,128)}, f32[1024,512]{1,0:T(8,128)}, bf16[4,1,1024,512]{3,2,1,0:T(8,128)(2,1)}, f32[2,512]{1,0:T(2,128)}, f32[2,512]{1,0:T(2,128)}) custom-call(bf16[4,197,512]{2,1,0:T(8,128)(2,1)} %get-tuple-element.125.refs_0_, bf16[4,197,512]{2,1,0:T(8,128)(2,1)} %get-tuple-element.126.refs_1_, ...), custom_call_target="tpu_custom_call" | custom-call | flops 1024 | bytes 1024 | tf_op jit(solution)/shard_map/pallas_call | solution.py:946
  379.0 25.8 %shard_map.329 = (f32[4,197,512]{2,1,0:T(8,128)}, bf16[512,2560]{1,0:T(8,128)(2,1)}, bf16[4,197,128]{2,1,0:T(8,128)(2,1)}, bf16[4,197,512]{2,1,0:T(8,128)(2,1)}, bf16[4,197,512]{2,1,0:T(8,128)(2,1)}) custom-call(f32[4,197,512]{2,1,0:T(8,128)} %get-tuple-element.100.cotangent.upstream, f32[4,197,512]{2,1,0:T(8,128)} %get-tuple-element.113.rows, ...), custom_call_target="tpu_custom_call" | custom-call | flops 1024 | bytes 1024 | tf_op jit(solution)/shard_map/pallas_call | solution.py:351
  404.9 102.4 %shard_map.330 = (f32[1,4,197,512]{3,2,1,0:T(8,128)}, f32[1024,512]{1,0:T(8,128)}, bf16[4,1,1024,512]{3,2,1,0:T(8,128)(2,1)}, f32[2,512]{1,0:T(2,128)}, f32[2,512]{1,0:T(2,128)}, /*index=5*/bf16[128,2560]{1,0:T(8,128)(2,1)}) custom-call(bf16[4,197,512]{2,1,0:T(8,128)(2,1)} %get-tuple-element.140.refs_0_, bf16[4,197,512]{2,1,0:T(8,128)(2,1)} %get-tuple-element.141.refs_1_, ...), custom_call_target="tpu_custom_call" | custom-call | flops 1024 | bytes 1024 | tf_op jit(solution)/shard_map/pallas_call | solution.py:946
  509.2 35.0 %shard_map.331 = (f32[4,197,512]{2,1,0:T(8,128)}, bf16[512,2560]{1,0:T(8,128)(2,1)}, bf16[128,2560]{1,0:T(8,128)(2,1)}) custom-call(f32[4,197,512]{2,1,0:T(8,128)} %get-tuple-element.133.upstream, f32[4,197,512]{2,1,0:T(8,128)} %get-tuple-element.101.rows, f32[4,197,512]{2,1,0:T(8,128)} %get-tuple-element.103.middle, ...), custom_call_target="tpu_custom_call" | custom-call | flops 1024 | bytes 1024 | tf_op jit(solution)/shard_map/pallas_call | solution.py:351
  544.2 38.4 %shard_map.332 = (bf16[128,2560]{1,0:T(8,128)(2,1)}, f32[197,4,512]{2,1,0:T(4,128)}, f32[197,4,512]{2,1,0:T(4,128)}) custom-call(bf16[4,128,2560]{2,1,0:T(8,128)(2,1)} %bitcast.67, f32[4,197,512]{2,1,0:T(8,128)} %get-tuple-element.154.tokens_a, f32[4,197,512]{2,1,0:T(8,128)} %get-tuple-element.155.tokens_b), custom_call_target="tpu_custom_call" | custom-call | flops 1024 | bytes 1024 | tf_op jit(solution)/shard_map/pallas_call | solution.py:946
  582.6 7.7 %shard_map.333 = (f32[2,128,512]{2,1,0:T(8,128)}, f32[2,128,512]{2,1,0:T(8,128)}, f32[2,128,512]{2,1,0:T(8,128)}, f32[2,128,512]{2,1,0:T(8,128)}, f32[2,16,128]{...) custom-call(f32[1024,512]{1,0:T(8,128)} %get-tuple-element.158.refs_, ...), custom_call_target="tpu_custom_call" | custom-call | flops 1024 | bytes 1024 | tf_op jit(solution)/shard_map/pallas_call | solution.py:351
  590.3 1.2 copy.59
  591.5 0.8 copy-done.2
  592.3 1.2 copy.60
  (34 shorter events, 3.5 us)
Async XLA Ops:
  7.2 54.1 %all-gather.2.cloned.1.call-start = ((), (), s32[]{:S(2)}) async-start(), calls=%async_computation.2 | async-start | bytes 2621440 | tf_op jit(solution)/shard_map/all_gather | solution.py:1363
  11.7 1.4 copy-start.4
  11.7 2.1 copy-start.5
  13.0 496.1 %reduce-scatter.7.cloned.1.call-start = ((), (), s32[]{:S(2)}) async-start(), calls=%async_computation.3 | async-start | bytes 5242880
  43.2 12.2 %copy-start = (f32[2,2,512,512]{3,2,1,0:T(8,128)S(1)}, f32[2,2,512,512]{3,2,1,0:T(8,128)}, u32[]{:S(2)}) copy-start(f32[2,2,512,512]{3,2,1,0:T(8,128)} %param.36) | copy-start | bytes 12582916
  58.7 1.2 copy-start.1
  379.0 203.7 %reduce-scatter.9.cloned.1.call-start = ((), (), s32[]{:S(2)}) async-start(), calls=%async_computation.4 | async-start | bytes 5242880
  507.3 0.7 copy-start.6
  507.3 0.7 copy-start.7
  507.3 1.3 copy-start.8
  507.3 1.3 copy-start.9
  582.6 7.7 %copy-start.3 = (f32[197,4,512]{2,1,0:T(4,128)S(1)}, f32[197,4,512]{2,1,0:T(4,128)}, u32[]{:S(2)}) copy-start(f32[197,4,512]{2,1,0:T(4,128)} %get-tuple-element.156) | copy-start | bytes 4841476
  590.3 2.0 copy-start.2
Sparse Core Ops, SparseCore 0:
  13.1 45.7 all-gather.1
  379.1 74.3 reduce-scatter.6
  507.5 61.0 reduce-scatter.8

commit v7 on v6

--- a/solution.py
+++ b/solution.py
@@ -151,8 +151,8 @@
 
 class Spread:
     def __init__(self, above, refs):
-        self.own, self.paired, self.chips_in, self.final, *sems = refs
-        pair_send, pair_recv, local, out_send, out_recv, back_send, back_recv, pass_send, pass_recv = sems
+        self.own, self.chips_in, self.final, *sems = refs
+        local, out_send, out_recv, back_send, back_recv, pass_send, pass_recv = sems
         half, columns = self.own.shape
         me = lax.axis_index("expert")
         core, chip = lax.rem(me, 2), me // 2
@@ -160,7 +160,6 @@
         block = columns // chips
         sibling = {"expert": me + 1 - 2 * core}
         mine = pl.ds(pl.multiple_of(core * half, half), half)
-        other = pl.ds(pl.multiple_of((1 - core) * half, half), half)
 
         def chip_at(k):
             return lax.rem(chip + k + chips, chips)
@@ -170,8 +169,7 @@
 
         peers = [{"expert": 2 * chip_at(k) + core} for k in range(1, chips)]
         self.peers = [sibling] + peers
-        self.pair = remote(above.at[other], self.paired, pair_send, pair_recv, sibling)
-        self.keep = pltpu.make_async_copy(above.at[mine], self.own, local)
+        self.keep = pltpu.make_async_copy(above, self.own, local)
         self.outs = [
             remote(
                 self.own.at[:, cols(chip_at(k))], self.chips_in.at[k - 1], out_send.at[k - 1], out_recv.at[k - 1],
@@ -191,16 +189,12 @@
 
     def stage(self, number):
         if number == 0:
+            self.keep.start()
             greet_all(self.peers)
-            self.pair.start()
-            self.keep.start()
-        elif number == 1:
-            self.pair.wait_recv()
             self.keep.wait()
-            self.own[...] = (self.own[...].astype(F32) + self.paired[...].astype(F32)).astype(BF16)
             for copy in self.outs:
                 copy.start()
-        elif number == 2:
+        elif number == 1:
             value = self.own[:, self.place[1]].astype(F32)
             for n, copy in enumerate(self.outs):
                 copy.wait_recv()
@@ -217,7 +211,7 @@
     def finish(self, result):
         for copy in self.hands:
             copy.wait()
-        for copy in [self.pair] + self.outs + self.backs:
+        for copy in self.outs + self.backs:
             copy.wait_send()
         result[...] = self.final[...]
 
@@ -225,9 +219,9 @@
 def spread_scratch(share, columns, chips):
     half = share // 2
     half_rows = pltpu.VMEM((half, columns), BF16)
-    sems = [()] * 3 + [(chips - 1,)] * 4 + [(chips,)] * 2
+    sems = [()] + [(chips - 1,)] * 4 + [(chips,)] * 2
     return [
-        half_rows, half_rows, pltpu.VMEM((chips - 1, half, columns // chips), BF16), pltpu.VMEM((share, columns), BF16),
+        half_rows, pltpu.VMEM((chips - 1, half, columns // chips), BF16), pltpu.VMEM((share, columns), BF16),
     ] + [pltpu.SemaphoreType.DMA(n) for n in sems]
 
 
@@ -240,7 +234,7 @@
     else:
         above, grad_ref, sent, above_out, wgrad, vgrad, *spread_refs = rest
         spread = Spread(above, spread_refs)
-        for number in range(4):
+        for number in range(3):
 
             @pl.when(pl.program_id(0) == number)
             def _(number=number):
@@ -644,19 +638,21 @@
     if with_dense:
         *refs, n1, n2, n3, n4, n5, m1, m2, m3 = refs
         refs = list(refs)
-        dense_in, next_in, dense_out, next_out = refs.pop(8), refs.pop(8), refs.pop(14), refs.pop(14)
+        dense_in, dense_out, next_out = refs.pop(7), refs.pop(13), refs.pop(13)
         dense = SharedGather(dense_in, dense_out, (n1, n2, n3, n4, n5))
+        next_in = refs[4].at[layer + 1, 0, : next_out.shape[1]]
         following = Gather(dense_out.shape[0], next_in, lambda p: next_out.at[p], (m1, m2, m3))
     (
-        hidden, drow, dcol, inner_first, outer_mine, mine, b1, b2, picked, arrived_out, g_out, s_out, outer_out, packed_out,
+        hidden, drow, dcol, inner_first, shares, b1, b2, picked, arrived_out, g_out, s_out, outer_out, packed_out,
         back, sent, arrived, made, weights, g_stage, s_stage, out_send, out_recv, home_send, home_recv, own, load, stores, last,
         *gather_refs,
     ) = refs
     row = lax.axis_index("dp")
     parts = weights.shape[1]
-    take = outer_mine.shape[0]
+    take = weights.shape[2] // 2
+    mine = shares.at[layer, 1]
     gathers = [
-        Gather(parts, outer_mine, lambda p: weights.at[0, p, take:], gather_refs[:3]),
+        Gather(parts, shares.at[layer, 0, take:], lambda p: weights.at[0, p, take:], gather_refs[:3]),
         Gather(parts, mine, lambda p: weights.at[1, p], gather_refs[3:]),
     ]
     swap = Swap(sent, arrived, made, back, (out_send, out_recv, home_send, home_recv, own))
@@ -753,7 +749,7 @@
 
 def expert_back_kernel(layer, with_above, *refs):
     if with_above:
-        *refs, above_in, above_own, above_send, above_recv, above_load = refs
+        *refs, above_in, above_own, above_paired, above_send, above_recv, above_load, pair_send, pair_recv = refs
         refs = list(refs)
         above, above_sum = refs.pop(10), refs.pop(15)
     (
@@ -814,18 +810,29 @@
     peers = [{"dp": lax.rem(row + k, parts)} for k in range(1, parts)]
     swap.greet(peers)
     if with_above:
+        core = lax.rem(swap.me, 2)
+        half = above_own.shape[1]
+        mine = pl.ds(pl.multiple_of(core * half, half), half)
+        other = pl.ds(pl.multiple_of((1 - core) * half, half), half)
+        pair = remote(above.at[:, other], above_paired, pair_send, pair_recv, {"expert": swap.me + 1 - 2 * core})
+        keep = pltpu.make_async_copy(above.at[:, mine], above_own, above_load)
+        pair.start()
+        keep.start()
         above_copies = [
-            pltpu.make_async_remote_copy(
-                src_ref=above.at[lax.rem(row + k, parts)], dst_ref=above_in.at[k - 1],
-                send_sem=above_send.at[k - 1], recv_sem=above_recv.at[k - 1],
-                device_id=peers[k - 1], device_id_type=MESH,
+            remote(
+                above_own.at[lax.rem(row + k, parts)], above_in.at[k - 1], above_send.at[k - 1], above_recv.at[k - 1],
+                peers[k - 1],
             )
             for k in range(1, parts)
         ]
-        above_copies.append(pltpu.make_async_copy(above.at[row], above_own, above_load))
+    swap.send_all([zero, one], drow, layer)
+    if with_above:
+        pair.wait_recv()
+        keep.wait()
+        for part in range(parts):
+            above_own[part] = (above_own[part].astype(F32) + above_paired[part].astype(F32)).astype(BF16)
         for copy in above_copies:
             copy.start()
-    swap.send_all([zero, one], drow, layer)
     loads[local + 1].wait()
     for j in range(local):
         loads[j].wait()
@@ -898,8 +905,8 @@
             bias_copies[-1].start()
     if with_above:
         for copy in above_copies:
-            copy.wait()
-        total = above_own[...].astype(F32)
+            copy.wait_recv()
+        total = above_own[row].astype(F32)
         for k in range(1, parts):
             total = total + above_in[k - 1].astype(F32)
         above_sum[...] = total.astype(BF16)
@@ -923,6 +930,9 @@
         total1, total2 = total1 + db1_in[k - 1], total2 + db2_in[k - 1]
     bias1[...], bias2[...] = total1, total2
     swap.take_home(dcol, layer, came)
+    if with_above:
+        for copy in above_copies + [pair]:
+            copy.wait_send()
     for copy in bias_copies:
         copy.wait_send()
     for k in range(1, parts):
@@ -956,18 +966,19 @@
     )(*[a for a, _ in inputs])
 
 
-def expert_forward(hidden, drow, dcol, shape, inner, outer_mine, mine, biases, following, layer):
+def expert_forward(hidden, drow, dcol, shape, inner, shares, biases, following, layer):
     b1, b2 = biases
     local, count, capacity, width = shape
     ff = b1.shape[1]
     rows = 2 * capacity
     parts = inner.shape[0]
-    packed = (parts, *mine.shape)
+    packed = (parts, *shares.shape[2:])
+    half = (parts, shares.shape[2] // 2, width)
     slots = (local, count * capacity, ff)
-    inputs = [(hidden, True), (drow, True), (dcol, True), (inner, False), (outer_mine, False), (mine, False), (b1, True), (b2, True)]
+    inputs = [(hidden, True), (drow, True), (dcol, True), (inner, False), (shares, False), (b1, True), (b2, True)]
     outputs = [
         ((2, *hidden.shape), BF16, True), (shape, BF16, False), (slots, BF16, False), (slots, BF16, False),
-        ((parts, *outer_mine.shape), BF16, False), (packed, BF16, False),
+        (half, BF16, False), (packed, BF16, False),
     ]
     scratch = [
         pltpu.VMEM(shape, BF16), pltpu.VMEM(shape, BF16), pltpu.VMEM(shape, BF16), pltpu.VMEM(shape, BF16),
@@ -976,11 +987,11 @@
     ] + swap_sems(local, count) + [
         pltpu.SemaphoreType.DMA, pltpu.SemaphoreType.DMA((2, 2)), pltpu.SemaphoreType.DMA((3,)),
     ] + gather_sems(parts) * 2
-    if following:
-        inputs += [(item, False) for item in following]
-        outputs += [((parts, *item.shape), BF16, False) for item in following]
+    if following is not None:
+        inputs.append((following, False))
+        outputs += [((parts, *following.shape), BF16, False), (half, BF16, False)]
         scratch += shared_sems(parts) + gather_sems(parts)
-    return expert_call(functools.partial(expert_kernel, layer, bool(following)), inputs, outputs, scratch, layer)
+    return expert_call(functools.partial(expert_kernel, layer, following is not None), inputs, outputs, scratch, layer)
 
 
 def expert_backward(sources, drow, dcol, weights, arrived, g, s, above, layer):
@@ -1011,11 +1022,12 @@
     ]
     if above is not None:
         inputs.append((above, False))
-        outputs.append((above.shape[1:], BF16, True))
+        halves = (share // 2, above.shape[2])
+        outputs.append((halves, BF16, True))
         scratch += [
-            pltpu.VMEM((parts - 1, *above.shape[1:]), BF16), pltpu.VMEM(above.shape[1:], BF16),
-            pltpu.SemaphoreType.DMA((parts - 1,)), pltpu.SemaphoreType.DMA((parts - 1,)), pltpu.SemaphoreType.DMA,
-        ]
+            pltpu.VMEM((parts - 1, *halves), BF16), pltpu.VMEM((parts, *halves), BF16), pltpu.VMEM((parts, *halves), BF16),
+            pltpu.SemaphoreType.DMA((parts - 1,)), pltpu.SemaphoreType.DMA((parts - 1,)),
+        ] + [pltpu.SemaphoreType.DMA] * 3
     done = expert_call(
         functools.partial(expert_back_kernel, layer, above is not None), inputs, outputs, scratch, LAYERS + layer
     )
@@ -1024,9 +1036,15 @@
 
 def prepare_kernel(capacity, owners, *refs):
     squares, (router, *vectors), (inner_bias, outer_bias, routes) = refs[:4], refs[4:12], refs[12:15]
-    tokens_in, (out, above, b1, b2, dcol, drow), tokens_out = refs[15:17], refs[17:23], refs[23:25]
-    mine, turned, inner_low, outer_low, token_ins, token_outs = refs[25:31]
-    sems, (b1_send, b1_recv, b2_send, b2_recv, own, token_load, token_store) = refs[31:36], refs[36:]
+    tokens_in, matrices, refs = refs[15:17], refs[17:19], refs[19:]
+    (out, above, b1, b2, dcol, drow), tokens_out, packed_out, refs = refs[:6], refs[6:8], refs[8], refs[9:]
+    mine, turned, inner_low, outer_low, token_ins, token_outs, inner_in, outer_in, packs = refs[:9]
+    sems, (b1_send, b1_recv, b2_send, b2_recv, own, token_load, token_store, weight_sems) = refs[9:14], refs[14:]
+    weight_loads = [
+        pltpu.make_async_copy(matrices[0], inner_in, weight_sems.at[0]),
+        pltpu.make_async_copy(matrices[1], outer_in, weight_sems.at[1]),
+    ]
+    weight_store = pltpu.make_async_copy(packs, packed_out, weight_sems.at[2])
     parts, share, _ = out.shape
     loads = [pltpu.make_async_copy(tokens_in[n], token_ins.at[n], token_load.at[n]) for n in range(2)]
     stores = [pltpu.make_async_copy(token_outs.at[n], tokens_out[n], token_store.at[n]) for n in range(2)]
@@ -1063,7 +1081,7 @@
         pltpu.make_async_copy(outer_low, b2.at[row], own.at[1]),
     ]
     gather.start()
-    for copy in singles + keeps + loads:
+    for copy in singles + keeps + loads + weight_loads:
         copy.start()
     pack(above, 1)
     for n in range(2):
@@ -1096,12 +1114,22 @@
             both = jnp.where(lanes == 0, dests[0], jnp.where(lanes == 1, dests[1], 0.0))
             drow[layer, image] = both.T[0:2, :].astype(jnp.int32)
 
+    for copy in weight_loads:
+        copy.wait()
+    take = outer_in.shape[2]
+    for layer in range(LAYERS):
+        for j in range(local):
+            for f in range(take // share):
+                cols = slice(f * FF_BLOCK, (f + 1) * FF_BLOCK)
+                packs[layer, j, f * share : (f + 1) * share, :] = inner_in[layer, j, :, cols].astype(BF16)
+            packs[layer, j, take:, :] = outer_in[layer, j].astype(BF16)
+    weight_store.start()
     gather.finish()
-    for copy in singles + keeps + stores:
+    for copy in singles + keeps + stores + [weight_store]:
         copy.wait()
 
 
-def prepare(squares, router, vectors, inner_bias, outer_bias, routes, tokens, parts, owners, number):
+def prepare(squares, router, vectors, inner_bias, outer_bias, routes, tokens, matrices, parts, owners, number):
     layers, share, width = squares[0].shape
     experts_all = router.shape[2]
     local, part_ff = inner_bias.shape[1:]
@@ -1110,25 +1138,29 @@
     columns = 4 * width + MISC
     count = layers * local
     sems = shared_sems(parts) + [pltpu.SemaphoreType.DMA((parts - 1,))] * 4 + [pltpu.SemaphoreType.DMA((2,))] * 3
+    sems.append(pltpu.SemaphoreType.DMA((3,)))
+    packs = (layers, local, 2 * matrices[1].shape[2], width)
     inputs = [*squares, router, *vectors, inner_bias, outer_bias, routes]
     turned = [jnp.transpose(item, (1, 0, 2)) for item in tokens]
-    out, above, b1, b2, dcol, drow, *tokens = expert_call(
-        functools.partial(prepare_kernel, capacity, owners), [(a, True) for a in inputs] + [(a, False) for a in turned],
+    out, above, b1, b2, dcol, drow, *tokens, packs = expert_call(
+        functools.partial(prepare_kernel, capacity, owners),
+        [(a, True) for a in inputs] + [(a, False) for a in (*turned, *matrices)],
         [
             ((parts, share, columns), BF16, False), ((share, columns), BF16, True),
             ((count, part_ff * parts), F32, False), ((parts, count, share), F32, False),
             ((layers, images, length, 2), jnp.int32, True), ((layers, images, 2, length), jnp.int32, True),
-            ((images, length, width), F32, False), ((images, length, width), F32, False),
+            ((images, length, width), F32, False), ((images, length, width), F32, False), (packs, BF16, False),
         ],
         [
             pltpu.VMEM((share, columns), BF16), pltpu.VMEM((MISC, share), F32),
             pltpu.VMEM((count, part_ff), F32), pltpu.VMEM((count, share), F32),
             pltpu.VMEM((2, length, images, width), F32), pltpu.VMEM((2, images, length, width), F32),
+            pltpu.VMEM(matrices[0].shape, F32), pltpu.VMEM(matrices[1].shape, F32), pltpu.VMEM(packs, BF16),
         ] + sems,
         number,
     )
     b2 = jnp.transpose(b2, (1, 0, 2)).reshape(count, width)
-    return out.reshape(width, columns), above, (b1, b2), dcol, drow, capacity, tokens
+    return out.reshape(width, columns), above, (b1, b2), dcol, drow, capacity, tokens, packs
 
 
 def settle_widths(columns, chips):
@@ -1348,19 +1380,14 @@
     vectors = (query_bias, value_bias, output_bias, attend_gain, attend_shift, expert_gain, expert_shift)
     columns = -(-(4 * width + MISC) // (MISC * (owners // 2))) * MISC * (owners // 2)
 
-    inner_mine, outer_mine, mine = [], [], []
-    for layer in range(LAYERS):
-        first = inner_weight[layer].reshape(local, share, ff // FF_BLOCK, FF_BLOCK)
-        first = jnp.transpose(first, (0, 2, 1, 3)).reshape(local, ff // parts, width).astype(BF16)
-        second = outer_weight[layer].astype(BF16)
-        inner_mine.append(first[0])
-        outer_mine.append(second[0])
-        mine.append(jnp.concatenate([first[1], second[1]], axis=0))
-    dense, above, expert_biases, dcol, drow, capacity, (images, cotangent) = prepare(
-        squares, router_weight, vectors, inner_bias, outer_bias, routes, (images, cotangent), parts, owners, 2 * LAYERS
+    first = inner_weight[0, 0].reshape(share, ff // FF_BLOCK, FF_BLOCK)
+    first = jnp.transpose(first, (1, 0, 2)).reshape(ff // parts, width).astype(BF16)
+    firsts = [lax.all_gather(first, "dp", axis=0, tiled=False)]
+    dense, above, expert_biases, dcol, drow, capacity, (images, cotangent), mine = prepare(
+        squares, router_weight, vectors, inner_bias, outer_bias, routes, (images, cotangent), (inner_weight, outer_weight),
+        parts, owners, 2 * LAYERS,
     )
     packed = [dense]
-    firsts = [lax.all_gather(inner_mine[0], "dp", axis=0, tiled=False)]
     slots = experts_all * capacity
 
     saved = []
@@ -1391,8 +1418,8 @@
             rows, *done = done
         middle, queries, keys, values, context, sums, gates = done[:7]
         picked, arrived, g, s, outer, second, *following = expert_forward(
-            done[7], drow, dcol, (local, owners, capacity, width), firsts[layer], outer_mine[layer], mine[layer], expert_biases,
-            (above, inner_mine[layer + 1]) if layer + 1 < LAYERS else (), layer,
+            done[7], drow, dcol, (local, owners, capacity, width), firsts[layer], mine, expert_biases,
+            above if layer + 1 < LAYERS else None, layer,
         )
         if following:
             packed.append(following[0].reshape(width, following[0].shape[2]))
@@ -1447,7 +1474,7 @@
         number = None
         if layer == 0:
             inputs.append((above, pl.BlockSpec(memory_space=pl.ANY)))
-            outputs.append((above.shape, BF16, pl.BlockSpec(above.shape, lambda i: (0, 0))))
+            outputs.append(((share, columns), BF16, pl.BlockSpec((share, columns), lambda i: (0, 0))))
             scratch += spread_scratch(share, columns, owners // 2)
             number = 2 * LAYERS + 2
         done = call(functools.partial(back_kernel, layer == 0), (count,), inputs, outputs, scratch, number)

time: 605 us -> 600 us (level)
  transfers between devices with their start and end apart: 3 -> 3, of which waited for: 0 -> 1; matrix products, arithmetic and copies ran while one was open for 2% -> 1% of each run, Pallas kernels for 40% -> 41%
where the time goes in v7:
time: 600 us; the launch traced here: 595 us
  Pallas kernels  567 us (94%)
  between operations  14.4 us (2%)
  local copies, waits for them, and re-layouts  8.3 us (1%)
    pallas_call x6, Pallas kernels, expert_call(): pl.pallas_call(body, in_specs=[spec(held) for _, held in inputs], out_spe...  467 us
    pallas_call x6, Pallas kernels, call(): pl.pallas_call(body, grid=grid, in_specs=[s for _, s in inputs], out_spec...  101 us
  transfers between devices with their start and end apart: 3, of which 1 were waited for; matrix products, arithmetic and copies ran while one was open for 1% of the time, Pallas kernels for 41%

profile of v7, /device:TPU:0, one launch (start us, length us, event | category | flops | bytes accessed | tf_op | source)
XLA Modules:
  0.0 595.1 jit_solution(16785353881701737089)
XLA Ops:
  7.3 1.3 slice.7
  8.6 0.4 convert_element_type.17
  8.9 0.9 copy.47
  9.9 0.8 copy.44.refs_4_
  10.7 1.2 copy.45.refs_14_.routes.rest_3_
  11.9 28.3 %shard_map.322 = (bf16[4,128,2176]{2,1,0:T(8,128)(2,1)}, bf16[128,2176]{1,0:T(8,128)(2,1)}, f32[4,2048]{1,0:T(4,128)}, f32[4,4,128]{2,1,0:T(4,128)}, s32[2,4,197...) custom-call(f32[2,128,512]{2,1,0:T(8,128)} %refs_0_.1, ...), custom_call_target="tpu_custom_call" | custom-call | flops 1024 | bytes 1024 | tf_op jit(solution)/shard_map/pallas_call | solution.py:956
  40.1 12.0 %shard_map.323 = (f32[4,197,512]{2,1,0:T(8,128)}, bf16[4,197,512]{2,1,0:T(8,128)(2,1)}, bf16[4,197,512]{2,1,0:T(8,128)(2,1)}, bf16[4,197,512]{2,1,0:T(8,128)(2,1...) custom-call(f32[4,197,512]{2,1,0:T(8,128)} %get-tuple-element.102.ro, ...), custom_call_target="tpu_custom_call" | custom-call | flops 1024 | bytes 1024 | tf_op jit(solution)/shard_map/pallas_call | solution.py:345
  52.2 3.5 all-gather.2.cloned.1.call-done.refs_3_.refs_4_
  55.7 100.9 %shard_map.324 = (bf16[2,4,197,512]{3,2,1,0:T(8,128)(2,1)}, bf16[2,8,128,512]{3,2,1,0:T(8,128)(2,1)}, bf16[2,1024,2048]{2,1,0:T(8,128)(2,1)}, bf16[2,1024,2048]{...) custom-call(bf16[4,197,512]{2,1,0:T(8,128)(2,1)} %get-tuple-element., ...), custom_call_target="tpu_custom_call" | custom-call | flops 1024 | bytes 1024 | tf_op jit(solution)/shard_map/pallas_call | solution.py:956
  156.6 13.1 %shard_map.325 = (f32[4,197,512]{2,1,0:T(8,128)}, f32[4,197,512]{2,1,0:T(8,128)}, bf16[4,197,512]{2,1,0:T(8,128)(2,1)}, bf16[4,197,512]{2,1,0:T(8,128)(2,1)}, bf...) custom-call(f32[4,197,512]{2,1,0:T(8,128)} %get-tuple-element.104.mi, ...), custom_call_target="tpu_custom_call" | custom-call | flops 1024 | bytes 1024 | tf_op jit(solution)/shard_map/pallas_call | solution.py:345
  169.8 98.0 %shard_map.326 = (bf16[2,4,197,512]{3,2,1,0:T(8,128)(2,1)}, bf16[2,8,128,512]{3,2,1,0:T(8,128)(2,1)}, bf16[2,1024,2048]{2,1,0:T(8,128)(2,1)}, bf16[2,1024,2048]{...) custom-call(bf16[4,197,512]{2,1,0:T(8,128)(2,1)} %get-tuple-element.123.refs_0_, ...), custom_call_target="tpu_custom_call" | custom-call | flops 1024 | bytes 1024 | tf_op jit(solution)/shard_map/pallas_call | solution.py:956
  267.8 5.7 shard_map.327
  273.5 99.5 %shard_map.328 = (f32[1,4,197,512]{3,2,1,0:T(8,128)}, f32[1024,512]{1,0:T(8,128)}, bf16[4,1,1024,512]{3,2,1,0:T(8,128)(2,1)}, f32[2,512]{1,0:T(2,128)}, f32[2,512]{1,0:T(2,128)}) custom-call(bf16[4,197,512]{2,1,0:T(8,128)(2,1)} %get-tuple-element.127.refs_0_, bf16[4,197,512]{2,1,0:T(8,128)(2,1)} %get-tuple-element.128.refs_1_, ...), custom_call_target="tpu_custom_call" | custom-call | flops 1024 | bytes 1024 | tf_op jit(solution)/shard_map/pallas_call | solution.py:956
  373.1 25.7 %shard_map.329 = (f32[4,197,512]{2,1,0:T(8,128)}, bf16[512,2560]{1,0:T(8,128)(2,1)}, bf16[4,197,128]{2,1,0:T(8,128)(2,1)}, bf16[4,197,512]{2,1,0:T(8,128)(2,1)}, bf16[4,197,512]{2,1,0:T(8,128)(2,1)}) custom-call(f32[4,197,512]{2,1,0:T(8,128)} %get-tuple-element.101.cotangent.upstream, f32[4,197,512]{2,1,0:T(8,128)} %get-tuple-element.115.rows, ...), custom_call_target="tpu_custom_call" | custom-call | flops 1024 | bytes 1024 | tf_op jit(solution)/shard_map/pallas_call | solution.py:345
  398.7 100.8 %shard_map.330 = (f32[1,4,197,512]{3,2,1,0:T(8,128)}, f32[1024,512]{1,0:T(8,128)}, bf16[4,1,1024,512]{3,2,1,0:T(8,128)(2,1)}, f32[2,512]{1,0:T(2,128)}, f32[2,512]{1,0:T(2,128)}, /*index=5*/bf16[64,2560]{1,0:T(8,128)(2,1)}) custom-call(bf16[4,197,512]{2,1,0:T(8,128)(2,1)} %get-tuple-element.142.refs_0_, bf16[4,197,512]{2,1,0:T(8,128)(2,1)} %get-tuple-element.143.refs_1_, ...), custom_call_target="tpu_custom_call" | custom-call | flops 1024 | bytes 1024 | tf_op jit(solution)/shard_map/pallas_call | solution.py:956
  499.6 0.6 copy-done.4
  500.2 0.6 fusion
  500.8 0.6 pad_maximum_fusion
  501.4 36.4 %shard_map.331 = (f32[4,197,512]{2,1,0:T(8,128)}, bf16[512,2560]{1,0:T(8,128)(2,1)}, bf16[128,2560]{1,0:T(8,128)(2,1)}) custom-call(f32[4,197,512]{2,1,0:T(8,128)} %get-tuple-element.135.upstream, f32[4,197,512]{2,1,0:T(8,128)} %get-tuple-element.102.rows, f32[4,197,512]{2,1,0:T(8,128)} %get-tuple-element.104.middle, ...), custom_call_target="tpu_custom_call" | custom-call | flops 1024 | bytes 1024 | tf_op jit(solution)/shard_map/pallas_call | solution.py:345
  537.9 39.3 %shard_map.332 = (bf16[128,2560]{1,0:T(8,128)(2,1)}, f32[197,4,512]{2,1,0:T(4,128)}, f32[197,4,512]{2,1,0:T(4,128)}) custom-call(bf16[4,128,2560]{2,1,0:T(8,128)(2,1)} %bitcast.48, f32[4,197,512]{2,1,0:T(8,128)} %get-tuple-element.156.tokens_a, f32[4,197,512]{2,1,0:T(8,128)} %get-tuple-element.157.tokens_b), custom_call_target="tpu_custom_call" | custom-call | flops 1024 | bytes 1024 | tf_op jit(solution)/shard_map/pallas_call | solution.py:956
  577.3 7.7 %shard_map.333 = (f32[2,128,512]{2,1,0:T(8,128)}, f32[2,128,512]{2,1,0:T(8,128)}, f32[2,128,512]{2,1,0:T(8,128)}, f32[2,128,512]{2,1,0:T(8,128)}, f32[2,16,128]{...) custom-call(f32[1024,512]{1,0:T(8,128)} %get-tuple-element.160.refs_, ...), custom_call_target="tpu_custom_call" | custom-call | flops 1024 | bytes 1024 | tf_op jit(solution)/shard_map/pallas_call | solution.py:345
  584.9 1.2 copy.53
  586.1 0.8 copy-done
  586.9 1.2 copy.54
  (22 shorter events, 0.2 us)
Async XLA Ops:
  7.2 2.7 copy-start.2
  7.2 3.5 copy-start.3
  7.2 48.5 %all-gather.2.cloned.1.call-start = ((), (), s32[]{:S(2)}) async-start(), calls=%async_computation.2 | async-start | bytes 2621440 | tf_op jit(solution)/shard_map/all_gather | solution.py:1385
  9.8 491.6 %reduce-scatter.7.cloned.1.call-start = ((), (), s32[]{:S(2)}) async-start(), calls=%async_computation.3 | async-start | bytes 5242880
  373.0 204.2 %reduce-scatter.9.cloned.1.call-start = ((), (), s32[]{:S(2)}) async-start(), calls=%async_computation.4 | async-start | bytes 5242880
  499.5 0.7 copy-start.4
  499.6 0.7 copy-start.5
  499.6 1.2 copy-start.6
  499.6 1.2 copy-start.7
  577.2 7.7 %copy-start.1 = (f32[197,4,512]{2,1,0:T(4,128)S(1)}, f32[197,4,512]{2,1,0:T(4,128)}, u32[]{:S(2)}) copy-start(f32[197,4,512]{2,1,0:T(4,128)} %get-tuple-element.158) | copy-start | bytes 4841476
  584.9 2.0 copy-start
Sparse Core Ops, SparseCore 0:
  10.5 45.1 all-gather.1
  373.1 93.0 reduce-scatter.6
  499.7 61.5 reduce-scatter.8

commit v8 on v7

--- a/solution.py
+++ b/solution.py
@@ -145,7 +145,12 @@
 
 def turn_kernel(middle, gates, yzero, yone, cotangent, routes, result, dz, zero_ref, one_ref):
     rows, zero, one = combine(middle[0], gates, yzero, yone)
-    result[0] = rows
+    for image in range(result.shape[1]):
+
+        @pl.when(pl.program_id(0) == image)
+        def _(image=image):
+            result[:, image, :] = rows
+
     grads_body(cotangent[0], zero, one, gates, routes, dz, zero_ref, one_ref)
 
 
@@ -234,11 +239,10 @@
     else:
         above, grad_ref, sent, above_out, wgrad, vgrad, *spread_refs = rest
         spread = Spread(above, spread_refs)
-        for number in range(3):
-
-            @pl.when(pl.program_id(0) == number)
-            def _(number=number):
-                spread.stage(number)
+
+        @pl.when(pl.program_id(0) == 0)
+        def _():
+            spread.stage(0)
 
     first = pl.program_id(0) == 0
     length = rows.shape[1]
@@ -312,6 +316,13 @@
             zero_ref, one_ref,
         )
 
+    if lowest:
+        for number in range(1, 3):
+
+            @pl.when(pl.program_id(0) == number)
+            def _(number=number):
+                spread.stage(number)
+
     @pl.when(pl.program_id(0) == pl.num_programs(0) - 1)
     def _():
         wgrad[:, 4 * width :] += vgrad[...].T
@@ -919,7 +930,7 @@
         total = share_out[row, place, :].astype(F32)
         for k in range(1, parts):
             total = total + share_in[k - 1, place, :].astype(F32)
-        summed[place, :] = total
+        summed[place, :] = total.astype(BF16)
         return carry
 
     lax.fori_loop(0, all_rows // step, add_up, 0)
@@ -1003,7 +1014,7 @@
     share, take = width // parts, all_rows // 2
     inputs = [(a, True) for a in (*sources, drow, dcol)] + [(a, False) for a in (*weights, arrived, g, s)]
     outputs = [
-        ((1, *sources[0].shape), F32, True), ((all_rows, width), F32, True), ((parts, local - 1, all_rows, width), BF16, False),
+        ((1, *sources[0].shape), F32, True), ((all_rows, width), BF16, True), ((parts, local - 1, all_rows, width), BF16, False),
         ((local, ff // parts), F32, True), ((local, width), F32, True),
     ]
     scratch = [
@@ -1170,7 +1181,7 @@
 
 
 def settle_kernel(
-    grads, tokens_a, tokens_b, final, tokens_out_a, tokens_out_b, own, paired, total, chips_in, dp_in, total_b, chips_in_b, dp_in_b,
+    grads, tokens, final, tokens_out, own, paired, total, chips_in, dp_in, total_b, chips_in_b, dp_in_b,
     pair_send, pair_recv, local, out_send, out_recv, dp_send, dp_recv, out_send_b, out_recv_b, dp_send_b, dp_recv_b,
     back_send, back_recv, pass_send, pass_recv, token_ins, token_outs, token_load, token_store,
 ):
@@ -1206,12 +1217,9 @@
         keeps.append(pltpu.make_async_copy(source.at[mine], own.at[i], local.at[i]))
         pairs[i].start()
         keeps[i].start()
-    loads = [pltpu.make_async_copy(t, token_ins.at[n], token_load.at[n]) for n, t in enumerate((tokens_a, tokens_b))]
-    stores = [
-        pltpu.make_async_copy(token_outs.at[n], t, token_store.at[n]) for n, t in enumerate((tokens_out_a, tokens_out_b))
-    ]
-    for copy in loads:
-        copy.start()
+    tokens_load = pltpu.make_async_copy(tokens, token_ins, token_load)
+    tokens_load.start()
+    tokens_store = pltpu.make_async_copy(token_outs, tokens_out, token_store)
     outs, scatters_b = [], []
     for i in range(parts):
         pairs[i].wait_recv()
@@ -1231,11 +1239,10 @@
         ])
         for copy in outs[i]:
             copy.start()
-    for n in range(2):
-        loads[n].wait()
-        for image in range(token_ins.shape[1]):
-            token_outs[n, :, image, :] = token_ins[n, image]
-        stores[n].start()
+    tokens_load.wait()
+    for image in range(token_ins.shape[0]):
+        token_outs[:, image, :] = token_ins[image]
+    tokens_store.start()
     value = own[parts - 1, :, split:].astype(F32)
     for i in range(parts - 1):
         scatters_b[i].wait_recv()
@@ -1289,30 +1296,30 @@
             hands[-1].start()
     for copy in pairs + [copy for group in outs for copy in group] + outs_b + scatters + scatters_b + backs:
         copy.wait_send()
-    for copy in hands + stores:
+    for copy in hands + [tokens_store]:
         copy.wait()
 
 
 def settle(grads, tokens, chips, number):
     parts, share, columns = grads.shape
     half = share // 2
-    images, length, width = tokens[0].shape
+    images, length, width = tokens.shape
     halves = pltpu.VMEM((parts, half, columns), BF16)
     wide, narrow = settle_widths(columns, chips)
     dp_in = pltpu.VMEM((parts - 1, half, wide), BF16)
     rest = chips * narrow
     sems = [(parts,)] * 3 + [(chips - 1, parts)] * 2 + [(parts - 1,)] * 2
     sems += [(chips - 1,)] * 2 + [(parts - 1,)] * 2 + [(2, chips - 1)] * 2 + [(2, chips)] * 2
-    turned = ((length, images, width), F32, False)
     return expert_call(
-        settle_kernel, [(item, False) for item in (grads, *tokens)], [((share, columns), BF16, True), turned, turned],
+        settle_kernel, [(grads, False), (tokens, False)],
+        [((share, columns), BF16, True), ((length, images, width), F32, False)],
         [
             halves, halves, dp_in, pltpu.VMEM((chips - 1, parts, half, wide), BF16), dp_in,
             pltpu.VMEM((half, rest), BF16), pltpu.VMEM((chips - 1, half, narrow), BF16),
             pltpu.VMEM((parts - 1, half, rest), BF16),
         ] + [pltpu.SemaphoreType.DMA(n) for n in sems] + [
-            pltpu.VMEM((2, images, length, width), F32), pltpu.VMEM((2, length, images, width), F32),
-            pltpu.SemaphoreType.DMA((2,)), pltpu.SemaphoreType.DMA((2,)),
+            pltpu.VMEM((images, length, width), F32), pltpu.VMEM((length, images, width), F32),
+            pltpu.SemaphoreType.DMA, pltpu.SemaphoreType.DMA,
         ],
         number,
     )
@@ -1320,46 +1327,50 @@
 
 def unpack_kernel(*refs):
     count = 2 * LAYERS
-    pieces, both, refs = refs[:count], refs[count : count + LAYERS], refs[count + LAYERS :]
+    firsts, seconds, both, miscs = refs[:count], refs[count : 2 * count], refs[2 * count : 2 * count + 2], refs[2 * count + 2 : 2 * count + 4]
+    refs = refs[2 * count + 4 :]
     squares, router, vectors, (inner, outer) = refs[:4], refs[4], refs[5:12], refs[12:]
-    layer = pl.program_id(0)
-    share = both[0].shape[0]
     width = squares[0].shape[2]
-    blocks = inner.shape[3] // FF_BLOCK
-
-    for number in range(LAYERS):
-
-        @pl.when(layer == number)
-        def _(number=number):
-            dense = both[number]
-            for n in range(4):
-                squares[n][0] = dense[:, n * width : (n + 1) * width].astype(F32)
-            turned = dense[:, 4 * width : 4 * width + MISC].astype(F32).T
-            router[0] = turned[: router.shape[1], :]
+    for layer in range(LAYERS):
+        for n in range(4):
+            squares[n][layer] = both[layer][:, n * width : (n + 1) * width].astype(F32)
+        for j in range(2):
+            first = firsts[2 * layer + j]
+            for f in range(first.shape[0]):
+                inner[layer, j, :, f * FF_BLOCK : (f + 1) * FF_BLOCK] = first[f].astype(F32)
+            outer[layer, j] = seconds[2 * layer + j][...].astype(F32)
+
+    @pl.when(pl.program_id(0) == 0)
+    def _():
+        for layer in range(LAYERS):
+            turned = miscs[layer][...].astype(F32).T
+            router[layer] = turned[: router.shape[1], :]
             for n in range(7):
-                vectors[n][number : number + 1, :] = turned[VEC_AT + n : VEC_AT + n + 1, :]
-            for j in range(2):
-                piece = pieces[2 * number + j]
-                for f in range(blocks):
-                    inner[0, j, :, f * FF_BLOCK : (f + 1) * FF_BLOCK] = piece[
-                        f * share : (f + 1) * share, :
-                    ].astype(F32)
-                outer[0, j] = piece[blocks * share :, :].astype(F32)
+                vectors[n][layer : layer + 1, :] = turned[VEC_AT + n : VEC_AT + n + 1, :]
 
 
 def unpack(pieces, both, local, ff, experts_all):
     layers, (share, columns) = len(both), both[0].shape
     rows, width = pieces[0].shape
     take = rows // 2
-    by_layer = lambda *shape: ((layers, *shape), F32, pl.BlockSpec((1, *shape), lambda i: (i,) + (0,) * len(shape)))
+    blocks = ff // FF_BLOCK
+    steps = max(1, share // 32)
+    part = share // steps
+    firsts = pl.BlockSpec((None, blocks, part, width), lambda i: (0, 0, i, 0))
+    seconds = pl.BlockSpec((None, take // steps, width), lambda i: (1, i, 0))
+    some = lambda rows, *rest: ((layers, *rest[:-1], rows, rest[-1]), F32, pl.BlockSpec(
+        (layers, *rest[:-1], rows // steps, rest[-1]), lambda i: (0,) * len(rest) + (i, 0)
+    ))
     return call(
-        unpack_kernel, (layers,),
-        [(p, whole(p)) for p in (*pieces, *both)],
-        [by_layer(share, width)] * 4 + [
-            by_layer(experts_all, share),
-        ] + [((layers, share), F32, pl.BlockSpec((layers, share), lambda i: (0, 0)))] * 7 + [
-            by_layer(local, share, ff), by_layer(local, take, width),
-        ],
+        unpack_kernel, (steps,),
+        [(p.reshape(2, blocks, share, width), firsts) for p in pieces]
+        + [(p.reshape(2, take, width), seconds) for p in pieces]
+        + [(a, pl.BlockSpec((part, columns), lambda i: (i, 0))) for a in both]
+        + [(a, pl.BlockSpec((share, MISC), lambda i: (0, 4 * width // MISC))) for a in both],
+        [some(share, width)] * 4
+        + [((layers, experts_all, share), F32, pl.BlockSpec((layers, experts_all, share), lambda i: (0, 0, 0)))]
+        + [((layers, share), F32, pl.BlockSpec((layers, share), lambda i: (0, 0)))] * 7
+        + [some(share, local, ff), some(take, local, width)],
     )
 
 
@@ -1435,7 +1446,8 @@
         [(last["middle"], per_image(last["middle"])), (last["gates"], per_image(last["gates"]))]
         + [(picked, per_layer(picked, k)) for k in range(2)]
         + [(cotangent, per_image(cotangent)), (routes, per_layer(routes, LAYERS - 1))],
-        [images_out(count, length, width, F32), images_out(count, length, MISC, BF16)]
+        [((length, count, width), F32, pl.BlockSpec((length, count, width), lambda i: (0, 0, 0)))]
+        + [images_out(count, length, MISC, BF16)]
         + [images_out(count, length, width, BF16)] * 2
     )
     upstream = cotangent
@@ -1482,7 +1494,7 @@
         if layer > 0:
             dz, *sources = done[2:]
         wgrad = wgrad.reshape(parts, share, columns)
-    lowest, result, upstream = settle(wgrad, (result, upstream), owners // 2, 2 * LAYERS + 1)
+    lowest, upstream = settle(wgrad, upstream, owners // 2, 2 * LAYERS + 1)
     both = (lowest, done[2])
     pieces = [waiting[0], waiting[1][0], finished[0], finished[1][0]]
     *squares, router, v0, v1, v2, v3, v4, v5, v6, inner, outer = unpack(pieces, both, local, ff, experts_all)

time: 600 us -> 592 us (0.987)
  transfers between devices with their start and end apart: 3 -> 3, of which waited for: 1 -> 1; matrix products, arithmetic and copies ran while one was open for 1% -> 1% of each run, Pallas kernels for 41% -> 40%
where the time goes in v8:
time: 592 us; the launch traced here: 588 us
  Pallas kernels  562 us (95%)
  between operations  14.3 us (2%)
  local copies, waits for them, and re-layouts  6.31 us (1%)
    pallas_call x6, Pallas kernels, expert_call(): pl.pallas_call(body, in_specs=[spec(held) for _, held in inputs], out_spe...  464 us
    pallas_call x6, Pallas kernels, call(): pl.pallas_call(body, grid=grid, in_specs=[s for _, s in inputs], out_spec...  98.6 us
  transfers between devices with their start and end apart: 3, of which 1 were waited for; matrix products, arithmetic and copies ran while one was open for 1% of the time, Pallas kernels for 40%

profile of v8, /device:TPU:0, one launch (start us, length us, event | category | flops | bytes accessed | tf_op | source)
XLA Modules:
  0.0 587.9 jit_solution(3564672087627287195)
XLA Ops:
  7.3 1.3 slice.7
  8.6 0.4 convert_element_type.17
  8.9 0.9 copy.47
  9.8 0.0 reduce-scatter.7.cloned.1.call-start
  9.9 0.8 copy.44.refs_4_
  10.7 1.2 copy.45.refs_14_.routes.rest_3_
  11.9 28.2 %shard_map.322 = (bf16[4,128,2176]{2,1,0:T(8,128)(2,1)}, bf16[128,2176]{1,0:T(8,128)(2,1)}, f32[4,2048]{1,0:T(4,128)}, f32[4,4,128]{2,1,0:T(4,128)}, s32[2,4,197...) custom-call(f32[2,128,512]{2,1,0:T(8,128)} %refs_0_.1, ...), custom_call_target="tpu_custom_call" | custom-call | flops 1024 | bytes 1024 | tf_op jit(solution)/shard_map/pallas_call | solution.py:967
  40.1 12.0 %shard_map.323 = (f32[4,197,512]{2,1,0:T(8,128)}, bf16[4,197,512]{2,1,0:T(8,128)(2,1)}, bf16[4,197,512]{2,1,0:T(8,128)(2,1)}, bf16[4,197,512]{2,1,0:T(8,128)(2,1...) custom-call(f32[4,197,512]{2,1,0:T(8,128)} %get-tuple-element.100.ro, ...), custom_call_target="tpu_custom_call" | custom-call | flops 1024 | bytes 1024 | tf_op jit(solution)/shard_map/pallas_call | solution.py:356
  52.1 3.6 all-gather.2.cloned.1.call-done.refs_3_.refs_4_
  55.7 100.9 %shard_map.324 = (bf16[2,4,197,512]{3,2,1,0:T(8,128)(2,1)}, bf16[2,8,128,512]{3,2,1,0:T(8,128)(2,1)}, bf16[2,1024,2048]{2,1,0:T(8,128)(2,1)}, bf16[2,1024,2048]{...) custom-call(bf16[4,197,512]{2,1,0:T(8,128)(2,1)} %get-tuple-element., ...), custom_call_target="tpu_custom_call" | custom-call | flops 1024 | bytes 1024 | tf_op jit(solution)/shard_map/pallas_call | solution.py:967
  156.6 13.1 %shard_map.325 = (f32[4,197,512]{2,1,0:T(8,128)}, f32[4,197,512]{2,1,0:T(8,128)}, bf16[4,197,512]{2,1,0:T(8,128)(2,1)}, bf16[4,197,512]{2,1,0:T(8,128)(2,1)}, bf...) custom-call(f32[4,197,512]{2,1,0:T(8,128)} %get-tuple-element.102.mi, ...), custom_call_target="tpu_custom_call" | custom-call | flops 1024 | bytes 1024 | tf_op jit(solution)/shard_map/pallas_call | solution.py:356
  169.7 98.1 %shard_map.326 = (bf16[2,4,197,512]{3,2,1,0:T(8,128)(2,1)}, bf16[2,8,128,512]{3,2,1,0:T(8,128)(2,1)}, bf16[2,1024,2048]{2,1,0:T(8,128)(2,1)}, bf16[2,1024,2048]{...) custom-call(bf16[4,197,512]{2,1,0:T(8,128)(2,1)} %get-tuple-element.115.refs_0_, ...), custom_call_target="tpu_custom_call" | custom-call | flops 1024 | bytes 1024 | tf_op jit(solution)/shard_map/pallas_call | solution.py:967
  267.8 6.3 %shard_map.327 = (f32[197,4,512]{2,1,0:T(4,128)}, bf16[4,197,128]{2,1,0:T(8,128)(2,1)}, bf16[4,197,512]{2,1,0:T(8,128)(2,1)}, bf16[4,197,512]{2,1,0:T(8,128)(2,1)}) custom-call(f32[4,197,512]{2,1,0:T(8,128)} %get-tuple-element.113.middle, f32[4,197,2]{2,1,0:T(8,128)} %get-tuple-element.114.gates, bf16[2,4,197,512]{3,2,1,0:T(8,128)(2,1)} %get-tuple-element.117.yzero.yone, ...), custom_call_target="tpu_custom_call" | custom-call | flops 1024 | bytes 1024 | tf_op jit(solution)/shard_map/pallas_call | solution.py:356
  274.1 99.1 %shard_map.328 = (f32[1,4,197,512]{3,2,1,0:T(8,128)}, bf16[1024,512]{1,0:T(8,128)(2,1)}, bf16[4,1,1024,512]{3,2,1,0:T(8,128)(2,1)}, f32[2,512]{1,0:T(2,128)}, f32[2,512]{1,0:T(2,128)}) custom-call(bf16[4,197,512]{2,1,0:T(8,128)(2,1)} %get-tuple-element.127.refs_0_, bf16[4,197,512]{2,1,0:T(8,128)(2,1)} %get-tuple-element.128.refs_1_, ...), custom_call_target="tpu_custom_call" | custom-call | flops 1024 | bytes 1024 | tf_op jit(solution)/shard_map/pallas_call | solution.py:967
  373.3 0.0 reduce-scatter.9.cloned.1.call-start
  373.3 25.7 %shard_map.329 = (f32[4,197,512]{2,1,0:T(8,128)}, bf16[512,2560]{1,0:T(8,128)(2,1)}, bf16[4,197,128]{2,1,0:T(8,128)(2,1)}, bf16[4,197,512]{2,1,0:T(8,128)(2,1)}, bf16[4,197,512]{2,1,0:T(8,128)(2,1)}) custom-call(f32[4,197,512]{2,1,0:T(8,128)} %get-tuple-element.118.cotangent.upstream, f32[4,197,512]{2,1,0:T(8,128)} %get-tuple-element.120.rows, ...), custom_call_target="tpu_custom_call" | custom-call | flops 1024 | bytes 1024 | tf_op jit(solution)/shard_map/pallas_call | solution.py:356
  399.0 100.5 %shard_map.330 = (f32[1,4,197,512]{3,2,1,0:T(8,128)}, bf16[1024,512]{1,0:T(8,128)(2,1)}, bf16[4,1,1024,512]{3,2,1,0:T(8,128)(2,1)}, f32[2,512]{1,0:T(2,128)}, f3...) custom-call(bf16[4,197,512]{2,1,0:T(8,128)(2,1)} %get-tuple-element.142.refs_0_, ...), custom_call_target="tpu_custom_call" | custom-call | flops 1024 | bytes 1024 | tf_op jit(solution)/shard_map/pallas_call | solution.py:967
  499.6 0.6 copy-done.3
  500.2 0.6 fusion
  500.8 0.6 pad_maximum_fusion
  501.4 34.1 %shard_map.331 = (f32[4,197,512]{2,1,0:T(8,128)}, bf16[512,2560]{1,0:T(8,128)(2,1)}, bf16[128,2560]{1,0:T(8,128)(2,1)}) custom-call(f32[4,197,512]{2,1,0:T(8,128)} %get-tuple-element.135.upstream, f32[4,197,512]{2,1,0:T(8,128)} %get-tuple-element.100.rows, f32[4,197,512]{2,1,0:T(8,128)} %get-tuple-element.102.middle, ...), custom_call_target="tpu_custom_call" | custom-call | flops 1024 | bytes 1024 | tf_op jit(solution)/shard_map/pallas_call | solution.py:356
  535.5 37.0 %shard_map.332 = (bf16[128,2560]{1,0:T(8,128)(2,1)}, f32[197,4,512]{2,1,0:T(4,128)}) custom-call(bf16[4,128,2560]{2,1,0:T(8,128)(2,1)} %bitcast.62, f32[4,197,512]{2,1,0:T(8,128)} %get-tuple-element.156.tokens), custom_call_target="tpu_custom_call" | custom-call | flops 1024 | bytes 1024 | tf_op jit(solution)/shard_map/pallas_call | solution.py:967
  572.6 7.3 %shard_map.333 = (f32[2,128,512]{2,1,0:T(8,128)}, f32[2,128,512]{2,1,0:T(8,128)}, f32[2,128,512]{2,1,0:T(8,128)}, f32[2,128,512]{2,1,0:T(8,128)}, f32[2,16,128]{...) custom-call(bf16[2,4,128,512]{3,2,1,0:T(8,128)(2,1)} %bitcast.57, ...), custom_call_target="tpu_custom_call" | custom-call | flops 1024 | bytes 1024 | tf_op jit(solution)/shard_map/pallas_call | solution.py:356
  579.9 1.2 copy.52
  (19 shorter events, 0.1 us)
Async XLA Ops:
  7.2 2.7 copy-start.1
  7.2 3.5 copy-start.2
  7.2 48.5 %all-gather.2.cloned.1.call-start = ((), (), s32[]{:S(2)}) async-start(), calls=%async_computation.2 | async-start | bytes 2621440 | tf_op jit(solution)/shard_map/all_gather | solution.py:1396
  9.8 491.6 %reduce-scatter.7.cloned.1.call-start = ((), (), s32[]{:S(2)}) async-start(), calls=%async_computation.3 | async-start | bytes 5242880
  373.3 199.2 %reduce-scatter.9.cloned.1.call-start = ((), (), s32[]{:S(2)}) async-start(), calls=%async_computation.4 | async-start | bytes 5242880
  499.6 0.7 copy-start.3
  499.6 0.7 copy-start.4
  499.6 1.2 copy-start.5
  499.6 1.2 copy-start.6
  572.5 7.3 %copy-start = (f32[197,4,512]{2,1,0:T(4,128)S(1)}, f32[197,4,512]{2,1,0:T(4,128)}, u32[]{:S(2)}) copy-start(f32[197,4,512]{2,1,0:T(4,128)} %get-tuple-element.157) | copy-start | bytes 4841476
Sparse Core Ops, SparseCore 0:
  10.5 45.1 all-gather.1
  373.4 93.1 reduce-scatter.6
  499.7 61.9 reduce-scatter.8

commit v9 on v8

--- a/solution.py
+++ b/solution.py
@@ -194,7 +194,6 @@
 
     def stage(self, number):
         if number == 0:
-            self.keep.start()
             greet_all(self.peers)
             self.keep.wait()
             for copy in self.outs:
@@ -242,7 +241,7 @@
 
         @pl.when(pl.program_id(0) == 0)
         def _():
-            spread.stage(0)
+            spread.keep.start()
 
     first = pl.program_id(0) == 0
     length = rows.shape[1]
@@ -317,7 +316,7 @@
         )
 
     if lowest:
-        for number in range(1, 3):
+        for number in range(3):
 
             @pl.when(pl.program_id(0) == number)
             def _(number=number):

time: 592 us -> 595 us (level)
  transfers between devices with their start and end apart: 3 -> 3, of which waited for: 1 -> 1; matrix products, arithmetic and copies ran while one was open for 1% -> 1% of each run, Pallas kernels for 40% -> 41%
where the time goes in v9:
time: 595 us; the launch traced here: 591 us
  Pallas kernels  565 us (95%)
  between operations  14.3 us (2%)
  local copies, waits for them, and re-layouts  6.31 us (1%)
    pallas_call x6, Pallas kernels, expert_call(): pl.pallas_call(body, in_specs=[spec(held) for _, held in inputs], out_spe...  465 us
    pallas_call x6, Pallas kernels, call(): pl.pallas_call(body, grid=grid, in_specs=[s for _, s in inputs], out_spec...  100 us
  transfers between devices with their start and end apart: 3, of which 1 were waited for; matrix products, arithmetic and copies ran while one was open for 1% of the time, Pallas kernels for 41%

profile of v9, /device:TPU:0, one launch (start us, length us, event | category | flops | bytes accessed | tf_op | source)
XLA Modules:
  0.0 590.9 jit_solution(5782471337883335862)
XLA Ops:
  7.3 1.3 slice.7
  8.6 0.4 convert_element_type.17
  8.9 0.9 copy.47
  9.8 0.0 reduce-scatter.7.cloned.1.call-start
  9.9 0.8 copy.44.refs_4_
  10.7 1.2 copy.45.refs_14_.routes.rest_3_
  11.9 28.2 %shard_map.322 = (bf16[4,128,2176]{2,1,0:T(8,128)(2,1)}, bf16[128,2176]{1,0:T(8,128)(2,1)}, f32[4,2048]{1,0:T(4,128)}, f32[4,4,128]{2,1,0:T(4,128)}, s32[2,4,197...) custom-call(f32[2,128,512]{2,1,0:T(8,128)} %refs_0_.1, ...), custom_call_target="tpu_custom_call" | custom-call | flops 1024 | bytes 1024 | tf_op jit(solution)/shard_map/pallas_call | solution.py:966
  40.1 12.0 %shard_map.323 = (f32[4,197,512]{2,1,0:T(8,128)}, bf16[4,197,512]{2,1,0:T(8,128)(2,1)}, bf16[4,197,512]{2,1,0:T(8,128)(2,1)}, bf16[4,197,512]{2,1,0:T(8,128)(2,1...) custom-call(f32[4,197,512]{2,1,0:T(8,128)} %get-tuple-element.100.ro, ...), custom_call_target="tpu_custom_call" | custom-call | flops 1024 | bytes 1024 | tf_op jit(solution)/shard_map/pallas_call | solution.py:355
  52.1 3.6 all-gather.2.cloned.1.call-done.refs_3_.refs_4_
  55.7 100.9 %shard_map.324 = (bf16[2,4,197,512]{3,2,1,0:T(8,128)(2,1)}, bf16[2,8,128,512]{3,2,1,0:T(8,128)(2,1)}, bf16[2,1024,2048]{2,1,0:T(8,128)(2,1)}, bf16[2,1024,2048]{...) custom-call(bf16[4,197,512]{2,1,0:T(8,128)(2,1)} %get-tuple-element., ...), custom_call_target="tpu_custom_call" | custom-call | flops 1024 | bytes 1024 | tf_op jit(solution)/shard_map/pallas_call | solution.py:966
  156.6 13.1 %shard_map.325 = (f32[4,197,512]{2,1,0:T(8,128)}, f32[4,197,512]{2,1,0:T(8,128)}, bf16[4,197,512]{2,1,0:T(8,128)(2,1)}, bf16[4,197,512]{2,1,0:T(8,128)(2,1)}, bf...) custom-call(f32[4,197,512]{2,1,0:T(8,128)} %get-tuple-element.102.mi, ...), custom_call_target="tpu_custom_call" | custom-call | flops 1024 | bytes 1024 | tf_op jit(solution)/shard_map/pallas_call | solution.py:355
  169.7 98.1 %shard_map.326 = (bf16[2,4,197,512]{3,2,1,0:T(8,128)(2,1)}, bf16[2,8,128,512]{3,2,1,0:T(8,128)(2,1)}, bf16[2,1024,2048]{2,1,0:T(8,128)(2,1)}, bf16[2,1024,2048]{...) custom-call(bf16[4,197,512]{2,1,0:T(8,128)(2,1)} %get-tuple-element.115.refs_0_, ...), custom_call_target="tpu_custom_call" | custom-call | flops 1024 | bytes 1024 | tf_op jit(solution)/shard_map/pallas_call | solution.py:966
  267.8 6.3 %shard_map.327 = (f32[197,4,512]{2,1,0:T(4,128)}, bf16[4,197,128]{2,1,0:T(8,128)(2,1)}, bf16[4,197,512]{2,1,0:T(8,128)(2,1)}, bf16[4,197,512]{2,1,0:T(8,128)(2,1)}) custom-call(f32[4,197,512]{2,1,0:T(8,128)} %get-tuple-element.113.middle, f32[4,197,2]{2,1,0:T(8,128)} %get-tuple-element.114.gates, bf16[2,4,197,512]{3,2,1,0:T(8,128)(2,1)} %get-tuple-element.117.yzero.yone, ...), custom_call_target="tpu_custom_call" | custom-call | flops 1024 | bytes 1024 | tf_op jit(solution)/shard_map/pallas_call | solution.py:355
  274.1 99.1 %shard_map.328 = (f32[1,4,197,512]{3,2,1,0:T(8,128)}, bf16[1024,512]{1,0:T(8,128)(2,1)}, bf16[4,1,1024,512]{3,2,1,0:T(8,128)(2,1)}, f32[2,512]{1,0:T(2,128)}, f32[2,512]{1,0:T(2,128)}) custom-call(bf16[4,197,512]{2,1,0:T(8,128)(2,1)} %get-tuple-element.127.refs_0_, bf16[4,197,512]{2,1,0:T(8,128)(2,1)} %get-tuple-element.128.refs_1_, ...), custom_call_target="tpu_custom_call" | custom-call | flops 1024 | bytes 1024 | tf_op jit(solution)/shard_map/pallas_call | solution.py:966
  373.3 0.0 reduce-scatter.9.cloned.1.call-start
  373.3 25.7 %shard_map.329 = (f32[4,197,512]{2,1,0:T(8,128)}, bf16[512,2560]{1,0:T(8,128)(2,1)}, bf16[4,197,128]{2,1,0:T(8,128)(2,1)}, bf16[4,197,512]{2,1,0:T(8,128)(2,1)}, bf16[4,197,512]{2,1,0:T(8,128)(2,1)}) custom-call(f32[4,197,512]{2,1,0:T(8,128)} %get-tuple-element.118.cotangent.upstream, f32[4,197,512]{2,1,0:T(8,128)} %get-tuple-element.120.rows, ...), custom_call_target="tpu_custom_call" | custom-call | flops 1024 | bytes 1024 | tf_op jit(solution)/shard_map/pallas_call | solution.py:355
  399.0 100.5 %shard_map.330 = (f32[1,4,197,512]{3,2,1,0:T(8,128)}, bf16[1024,512]{1,0:T(8,128)(2,1)}, bf16[4,1,1024,512]{3,2,1,0:T(8,128)(2,1)}, f32[2,512]{1,0:T(2,128)}, f3...) custom-call(bf16[4,197,512]{2,1,0:T(8,128)(2,1)} %get-tuple-element.142.refs_0_, ...), custom_call_target="tpu_custom_call" | custom-call | flops 1024 | bytes 1024 | tf_op jit(solution)/shard_map/pallas_call | solution.py:966
  499.6 0.6 copy-done.3
  500.2 0.6 fusion
  500.8 0.6 pad_maximum_fusion
  501.4 35.8 %shard_map.331 = (f32[4,197,512]{2,1,0:T(8,128)}, bf16[512,2560]{1,0:T(8,128)(2,1)}, bf16[128,2560]{1,0:T(8,128)(2,1)}) custom-call(f32[4,197,512]{2,1,0:T(8,128)} %get-tuple-element.135.upstream, f32[4,197,512]{2,1,0:T(8,128)} %get-tuple-element.100.rows, f32[4,197,512]{2,1,0:T(8,128)} %get-tuple-element.102.middle, ...), custom_call_target="tpu_custom_call" | custom-call | flops 1024 | bytes 1024 | tf_op jit(solution)/shard_map/pallas_call | solution.py:355
  537.3 38.2 %shard_map.332 = (bf16[128,2560]{1,0:T(8,128)(2,1)}, f32[197,4,512]{2,1,0:T(4,128)}) custom-call(bf16[4,128,2560]{2,1,0:T(8,128)(2,1)} %bitcast.62, f32[4,197,512]{2,1,0:T(8,128)} %get-tuple-element.156.tokens), custom_call_target="tpu_custom_call" | custom-call | flops 1024 | bytes 1024 | tf_op jit(solution)/shard_map/pallas_call | solution.py:966
  575.5 7.3 %shard_map.333 = (f32[2,128,512]{2,1,0:T(8,128)}, f32[2,128,512]{2,1,0:T(8,128)}, f32[2,128,512]{2,1,0:T(8,128)}, f32[2,128,512]{2,1,0:T(8,128)}, f32[2,16,128]{...) custom-call(bf16[2,4,128,512]{3,2,1,0:T(8,128)(2,1)} %bitcast.57, ...), custom_call_target="tpu_custom_call" | custom-call | flops 1024 | bytes 1024 | tf_op jit(solution)/shard_map/pallas_call | solution.py:355
  582.9 1.2 copy.52
  (19 shorter events, 0.1 us)
Async XLA Ops:
  7.2 2.7 copy-start.1
  7.2 3.5 copy-start.2
  7.2 48.5 %all-gather.2.cloned.1.call-start = ((), (), s32[]{:S(2)}) async-start(), calls=%async_computation.2 | async-start | bytes 2621440 | tf_op jit(solution)/shard_map/all_gather | solution.py:1395
  9.8 491.6 %reduce-scatter.7.cloned.1.call-start = ((), (), s32[]{:S(2)}) async-start(), calls=%async_computation.3 | async-start | bytes 5242880
  373.3 202.2 %reduce-scatter.9.cloned.1.call-start = ((), (), s32[]{:S(2)}) async-start(), calls=%async_computation.4 | async-start | bytes 5242880
  499.6 0.7 copy-start.3
  499.6 0.7 copy-start.4
  499.6 1.2 copy-start.5
  499.6 1.2 copy-start.6
  575.5 7.3 %copy-start = (f32[197,4,512]{2,1,0:T(4,128)S(1)}, f32[197,4,512]{2,1,0:T(4,128)}, u32[]{:S(2)}) copy-start(f32[197,4,512]{2,1,0:T(4,128)} %get-tuple-element.157) | copy-start | bytes 4841476
Sparse Core Ops, SparseCore 0:
  10.5 45.1 all-gather.1
  373.4 93.1 reduce-scatter.6
  499.7 63.6 reduce-scatter.8
